TPU v7x, 128 devices: a whole 4x4x4 slice. The times are simulated.
128 devices in a mesh: row: 8 (over z_hi, x), col: 16 (over z_lo, y, core).
Axes of the slice: x: 4, y: 4, z: 4 (z_hi: 2, z_lo: 2; z = z_hi * 2 + z_lo), core: 2. Of those that a mesh axis runs over, the one named last changes fastest.
Arguments:
- samples: bfloat16 [16, 8, 256, 16384], P('col', 'row'), may hold values from -6 to 6
- w_start: float32 [32768, 256], P(('row', 'col')), may hold values from 0.005 to 2
- h_start: float32 [256, 8192], P('row', 'col'), may hold values from 0.005 to 2
Outputs:
- w_final: float32 [32768, 256], P(('row', 'col'))
- h_final: float32 [256, 8192], P('row', 'col')
All inputs are finite; a program needn't handle non-finite values.
Results may differ from a plain program's by a relative error of at most 0.0013.
Values may be sent and summed in bfloat16 or wider, within the bound.
No kernel may reach another device: no remote copies, remote signals or barrier semaphores. Data moves between devices by JAX's collectives and lax.ppermute only.
A program may use at most 128 MiB of HBM per device.

v0:
```python
import math

import jax
import jax.numpy as jnp
from jax import lax
from jax.sharding import PartitionSpec as P

BINS = 128
ITERS = 2
WIN = 256


def in_order(parts, dim):
    lengths = list(parts.shape[1:])
    lengths[dim] *= parts.shape[0]
    return jnp.moveaxis(parts, 0, dim).reshape(lengths)


def from_everyone(x, axis):
    peers = lax.axis_size(axis)
    return lax.all_to_all(jnp.broadcast_to(x[None], (peers, *x.shape)), axis, 0, 0, tiled=True)


def gather_directly(x, axis, dim):
    return in_order(from_everyone(x, axis), dim)


def cut_along(x, dim, peers):
    before, after = (x.shape[:dim], x.shape[dim + 1 :])
    return jnp.moveaxis(x.reshape(*before, peers, -1, *after), dim, 0)


def summed_on_arrival(x, axis, dim):
    peers = lax.axis_size(axis)
    parts = lax.all_to_all(cut_along(x, dim, peers), axis, 0, 0, tiled=True)
    return jnp.sum(parts, axis=0)


def sent_together(arrays, axis, dim, along):
    columns = [a.reshape(*a.shape[:along], -1) for a in arrays]
    both = jnp.concatenate(columns, axis=along)
    whole, at, gathered = (summed_on_arrival(both, axis, dim), 0, [])
    for a, column in zip(arrays, columns):
        piece = whole[..., at : at + column.shape[along]]
        gathered.append(piece.reshape(*piece.shape[:along], *a.shape[along:]))
        at += column.shape[along]
    return tuple(gathered)


def taken_together(x, axis):
    return from_everyone(x, axis).sum(axis=0)


def dft_table():
    sample_idx = jnp.arange(WIN, dtype=jnp.int32)
    bin_idx = jnp.arange(BINS, dtype=jnp.int32)
    phases = sample_idx[:, None] * bin_idx[None, :] % WIN
    phases = phases.astype(jnp.float32) * (2.0 * math.pi / WIN)
    shaping = 0.5 - 0.5 * jnp.cos(sample_idx.astype(jnp.float32) * (2.0 * math.pi / WIN))
    shaping = shaping / math.sqrt(3.0 * WIN / 8.0)
    both = jnp.concatenate(
        [shaping[:, None] * jnp.cos(phases), -shaping[:, None] * jnp.sin(phases)], axis=1
    )
    return both.astype(jnp.bfloat16)


def frame_energy(record, table):
    channels = record.shape[0]
    frames = record.reshape(channels, record.shape[1] // WIN, WIN)
    spectrum = jnp.einsum("cfn,nk->fck", frames, table, preferred_element_type=jnp.float32)
    real_part = spectrum[:, :, :BINS]
    imag_part = spectrum[:, :, BINS:]
    energy = (real_part * real_part + imag_part * imag_part).astype(jnp.bfloat16)
    return energy.reshape(energy.shape[0], channels * BINS)


def local_terms(spectra_tile, w_block, h_block):
    recon = jnp.einsum("kf,rk->fr", h_block, w_block, preferred_element_type=jnp.float32)
    quotient = (spectra_tile / recon).astype(jnp.bfloat16)
    h_numer = jnp.einsum("rk,fr->kf", w_block, quotient, preferred_element_type=jnp.float32)
    w_numer = jnp.einsum("fr,kf->rk", quotient, h_block, preferred_element_type=jnp.float32)
    w_colsum = jnp.sum(w_block, axis=0, dtype=jnp.float32)
    h_rowsum = jnp.sum(h_block, axis=1, dtype=jnp.float32)
    return (h_numer, w_numer, w_colsum, h_rowsum)


def local(samples, w_start, h_start):
    table = dft_table()
    record = samples.reshape(samples.shape[2], samples.shape[3])
    energy = frame_energy(record, table)
    spectra_tile = lax.all_to_all(energy, "row", split_axis=1, concat_axis=0, tiled=True)
    w_state = w_start
    h_state = h_start
    for sweep in range(ITERS):
        w_block = lax.all_gather(w_state.astype(jnp.bfloat16), "col", axis=0, tiled=True)
        h_block = gather_directly(h_state.astype(jnp.bfloat16), "row", 0)
        h_numer, w_numer, w_colsum, h_rowsum = local_terms(spectra_tile, w_block, h_block)
        h_numer, w_colsum = sent_together((h_numer, w_colsum), "row", 0, 1)
        w_numer = lax.psum_scatter(w_numer, "col", scatter_dimension=0, tiled=True)
        h_rowsum = taken_together(h_rowsum, "col")
        h_state = h_state * h_numer / w_colsum[:, None]
        w_state = w_state * w_numer / h_rowsum[None, :]
    return (w_state, h_state)


def solution(mesh):
    placed = (P("col", "row", None, None), P(("row", "col"), None), P("row", "col"))
    return jax.shard_map(
        local,
        mesh=mesh,
        in_specs=placed,
        out_specs=(P(("row", "col"), None), P("row", "col")),
        check_vma=False,
    )
```

profile of v0, /device:TPU:0, one launch (start us, length us, event | category | flops | bytes accessed | tf_op | source)
XLA Modules:
  0.0 333.0 jit_solution(8128198583981182468)
XLA Ops:
  7.2 0.8 convert_element_type.69
  8.0 0.7 broadcast_in_dim.12
  8.7 7.7 %all-to-all-start.1 = ((bf16[8,32,512]{2,1,0:T(8,128)(2,1)}), bf16[8,32,512]{2,1,0:T(8,128)(2,1)S(1)}, u32[]{:S(2)}, u32[]{:S(2)}) async-start(bf16[8,32,512]{2,1,0:T(8,128)(2,1)} %broadcast_in_dim.12), calls=%async_computation.1 | async-start | bytes 524288 | tf_op jit(solution)/shard_map/all_to_all | solution.py:21
  16.4 0.0 all-gather.3.cloned.1.call-start
  16.5 1.6 convert_element_type.70
  18.1 0.0 all-gather.3.cloned.1.call-update
  18.1 0.0 reduce-scatter.3.cloned.1.call-start
  18.3 9.4 %copy.30 = bf16[32,8,64,256]{3,2,1,0:T(8,128)(2,1)} copy(bf16[32,8,64,256]{3,1,2,0:T(8,128)(2,1)} %bitcast.37) | data formatting | bytes 16777216
  27.6 0.5 multiply_convert_fusion
  28.2 15.2 %convolution_bitcast_fusion = f32[64,256,256]{1,2,0:T(8,128)} fusion(bf16[256,64,256]{2,1,0:T(8,128)(2,1)} %bitcast.36, bf16[256,128]{0,1:T(8,128)(2,1)S(1)} %get-tuple-element.2, bf16[256,128]{0,1:T(8,128)(2,1)S(1)} %get-tuple-element.3), kind=kOutput, calls=%fused_computation | convolution fusion | flops 2147745792 | bytes 25296896 | tf_op jit(solution)/shard_map/cfn,nk->fck/dot_general | solution.py:70
  43.4 9.0 %fusion.1 = bf16[64,256,128]{1,2,0:T(8,128)(2,1)} fusion(f32[64,256,256]{1,2,0:T(8,128)} %convolution_bitcast_fusion), kind=kLoop, calls=%fused_computation.3 | loop fusion | flops 8388608 | bytes 20971520 | tf_op jit(solution)/shard_map/convert_element_type | solution.py:73
  52.4 6.4 %copy.22 = bf16[64,256,128]{2,1,0:T(8,128)(2,1)} copy(bf16[64,256,128]{1,2,0:T(8,128)(2,1)} %fusion.1) | data formatting | bytes 8388608 | tf_op jit(solution)/shard_map/convert_element_type | solution.py:73
  58.8 7.3 %all_to_all.30 = bf16[64,8,4096]{2,1,0:T(8,128)(2,1)} reshape(bf16[64,256,128]{2,1,0:T(8,128)(2,1)} %copy.22) | data formatting | bytes 8388608 | tf_op jit(solution)/shard_map/all_to_all | solution.py:91
  66.1 6.5 %copy.23 = bf16[64,8,4096]{2,0,1:T(8,128)(2,1)} copy(bf16[64,8,4096]{2,1,0:T(8,128)(2,1)} %all_to_all.30) | data formatting | bytes 8388608 | tf_op jit(solution)/shard_map/all_to_all | solution.py:91
  72.5 0.0 all-to-all-done.1
  72.5 57.6 %all_to_all.45 = bf16[64,8,4096]{2,0,1:T(8,128)(2,1)} all-to-all(bf16[64,8,4096]{2,0,1:T(8,128)(2,1)} %copy.23), channel_id=1, replica_groups=mesh['row'=8,'col'=16] {'row'}, dimensions={1} | all-to-all | bytes 8388608 | tf_op jit(solution)/shard_map/all_to_all | solution.py:91
  130.2 4.6 %fusion.2 = bf16[512,4096]{1,0:T(8,128)(2,1)S(1)} fusion(bf16[64,8,4096]{2,0,1:T(8,128)(2,1)} %all_to_all.45, bf16[256,512]{1,0:T(8,128)(2,1)S(1)} %bitcast.38, bf16[4096,256]{1,0:T(8,128)(2,1)} %all-gather.3.cloned.1.call-done), kind=kOutput, calls=%fused_computation.7 | convolution fusion | flops 1080033280 | bytes 10747904 | tf_op jit(solution)/shard_map/kf,rk->fr/dot_general | solution.py:78
  134.7 0.0 copy-start
  134.7 2.0 copy-done
  136.7 3.3 fusion.19
  140.0 0.0 reduce-scatter.3.cloned.1.call-update
  140.0 0.0 all-gather.5.cloned.1.call-start
  140.1 0.1 convert_reduce_fusion.3
  140.2 0.1 broadcast_in_dim.13
  140.3 11.0 %all_to_all.46 = f32[16,1,256]{2,1,0:T(1,128)S(1)} all-to-all(f32[16,1,256]{2,1,0:T(1,128)S(1)} %broadcast_in_dim.14), channel_id=1, replica_groups=mesh['row'=8,'col'=16] {'col'}, dimensions={0} | all-to-all | bytes 32768 | tf_op jit(solution)/shard_map/all_to_all | solution.py:21
  151.3 53.2 %reduce-scatter.3.cloned.1.call-done = f32[256,256]{1,0:T(8,128)} async-done(((f32[4096,256]{1,0:T(8,128)}), f32[256,256]{1,0:T(8,128)}) %reduce-scatter.3.cloned.1.call-update) | async-done | bytes 262160 | tf_op jit(solution)/shard_map/reduce_scatter | solution.py:99
  204.6 0.0 copy-done.2
  204.6 1.6 fusion.18
  206.2 0.0 all-gather.5.cloned.1.call-update
  206.2 0.0 reduce-scatter.5.cloned.1.call-start
  206.3 0.0 copy-done.3
  206.3 0.6 convert_reduce_fusion.1
  206.9 0.2 concatenate.27
  207.1 0.0 copy-start.6
  207.1 3.5 %fusion.20 = f32[512,256]{0,1:T(8,128)S(1)} fusion(bf16[512,4096]{1,0:T(8,128)(2,1)} %copy-done, bf16[4096,256]{1,0:T(8,128)(2,1)S(1)} %copy-done.3), kind=kOutput, calls=%fused_computation.44 | convolution fusion | flops 1073741824 | bytes 6815744 | tf_op jit(solution)/shard_map/rk,fr->kf/dot_general | solution.py:80
  210.6 0.1 pad_maximum_fusion
  210.7 17.3 %all_to_all.47 = f32[8,32,513]{2,1,0:T(8,128)S(1)} all-to-all(f32[8,32,513]{2,1,0:T(8,128)S(1)} %pad_maximum_fusion), channel_id=1, replica_groups=mesh['row'=8,'col'=16] {'row'}, dimensions={0} | all-to-all | bytes 1050624 | tf_op jit(solution)/shard_map/all_to_all | solution.py:35
  228.0 0.1 slice_reduce_fusion.1
  228.1 0.0 copy-done.6
  228.1 0.1 fusion.17
  228.2 11.9 %all_to_all.48 = bf16[8,32,512]{2,1,0:T(8,128)(2,1)S(1)} all-to-all(bf16[8,32,512]{2,1,0:T(8,128)(2,1)S(1)} %broadcast_in_dim.15), channel_id=1, replica_groups=mesh['row'=8,'col'=16] {'row'}, dimensions={0} | all-to-all | bytes 524288 | tf_op jit(solution)/shard_map/all_to_all | solution.py:21
  240.1 2.8 all-gather.5.cloned.1.call-done
  242.9 4.5 %fusion.3 = bf16[512,4096]{1,0:T(8,128)(2,1)S(1)} fusion(bf16[64,8,4096]{2,0,1:T(8,128)(2,1)} %all_to_all.45, bf16[256,512]{1,0:T(8,128)(2,1)S(1)} %bitcast.40, bf16[4096,256]{1,0:T(8,128)(2,1)} %all-gather.5.cloned.1.call-done), kind=kOutput, calls=%fused_computation.8 | convolution fusion | flops 1080033280 | bytes 10747904 | tf_op jit(solution)/shard_map/kf,rk->fr/dot_general | solution.py:78
  247.5 0.0 copy-start.1
  247.5 2.0 copy-done.1
  249.5 3.2 fusion.21
  252.7 0.0 reduce-scatter.5.cloned.1.call-update
  252.7 0.1 convert_reduce_fusion.2
  252.8 0.1 broadcast_in_dim.16
  252.9 0.6 broadcast_in_dim.17
  253.5 5.2 %all-to-all-start.5 = ((f32[16,1,256]{2,1,0:T(1,128)}), f32[16,1,256]{2,1,0:T(1,128)S(1)}, u32[]{:S(2)}, u32[]{:S(2)}) async-start(f32[16,1,256]{2,1,0:T(1,128)} %broadcast_in_dim.17), calls=%async_computation.7 | async-start | bytes 32768 | tf_op jit(solution)/shard_map/all_to_all | solution.py:21
  258.8 0.0 copy-done.4
  258.8 0.6 convert_reduce_fusion
  259.3 0.2 concatenate.28
  259.6 3.5 %fusion.22 = f32[256,512]{1,0:T(8,128)S(1)} fusion(bf16[4096,256]{1,0:T(8,128)(2,1)S(1)} %copy-done.4, bf16[512,4096]{1,0:T(8,128)(2,1)} %copy-done.1), kind=kOutput, calls=%fused_computation.46 | convolution fusion | flops 1073741824 | bytes 6815744 | tf_op jit(solution)/shard_map/rk,fr->kf/dot_general | solution.py:80
  263.1 0.9 pad_maximum_fusion.1
  264.0 0.9 all-to-all-done.5
  264.8 9.7 %all-to-all-start.6 = ((f32[8,32,513]{2,1,0:T(8,128)}), f32[8,32,513]{2,1,0:T(8,128)S(1)}, u32[]{:S(2)}, u32[]{:S(2)}) async-start(f32[8,32,513]{2,1,0:T(8,128)} %pad_maximum_fusion.1), calls=%async_computation.8 | async-start | bytes 1310720 | tf_op jit(solution)/shard_map/all_to_all | solution.py:35
  274.6 15.0 %all-to-all-done.6 = f32[8,32,513]{2,1,0:T(8,128)S(1)} async-done(((f32[8,32,513]{2,1,0:T(8,128)}), f32[8,32,513]{2,1,0:T(8,128)S(1)}, u32[]{:S(2)}, u32[]{:S(2)}) %all-to-all-start.6) | async-done | bytes 525344 | tf_op jit(solution)/shard_map/all_to_all | solution.py:35
  289.6 0.1 slice_reduce_fusion
  289.7 0.7 fusion.13
  290.4 34.4 %reduce-scatter.5.cloned.1.call-done = f32[256,256]{1,0:T(8,128)} async-done(((f32[4096,256]{1,0:T(8,128)}), f32[256,256]{1,0:T(8,128)}) %reduce-scatter.5.cloned.1.call-update) | async-done | bytes 262160 | tf_op jit(solution)/shard_map/reduce_scatter | solution.py:99
  324.8 0.0 copy-done.5
  324.8 1.7 multiply_divide_fusion
  (13 shorter events, 0.3 us)
Async XLA Ops:
  8.7 63.8 %all-to-all-start.1 = ((bf16[8,32,512]{2,1,0:T(8,128)(2,1)}), bf16[8,32,512]{2,1,0:T(8,128)(2,1)S(1)}, u32[]{:S(2)}, u32[]{:S(2)}) async-start(bf16[8,32,512]{2,1,0:T(8,128)(2,1)} %broadcast_in_dim.12), calls=%async_computation.1 | async-start | bytes 524288 | tf_op jit(solution)/shard_map/all_to_all | solution.py:21
  16.4 113.7 %all-gather.3.cloned.1.call-start = ((), (), s32[]{:S(2)}) async-start(), calls=%async_computation.9 | async-start | bytes 2228224 | tf_op jit(solution)/shard_map/all_gather | solution.py:95
  18.1 186.5 %reduce-scatter.3.cloned.1.call-start = ((), (), s32[]{:S(2)}) async-start(), calls=%async_computation.10 | async-start | bytes 4456448 | tf_op jit(solution)/shard_map/reduce_scatter | solution.py:99
  134.7 2.0 copy-start
  140.0 64.6 %copy-start.2 = (f32[256,256]{1,0:T(8,128)S(1)}, f32[256,256]{1,0:T(8,128)}, u32[]{:S(2)}) copy-start(f32[256,256]{1,0:T(8,128)} %param.4) | copy-start | bytes 786436
  140.0 66.3 %copy-start.3 = (bf16[4096,256]{1,0:T(8,128)(2,1)S(1)}, bf16[4096,256]{1,0:T(8,128)(2,1)}, u32[]{:S(2)}) copy-start(bf16[4096,256]{1,0:T(8,128)(2,1)} %all-gather.3.cloned.1.call-done) | copy-start | bytes 6291460
  140.0 102.9 %all-gather.5.cloned.1.call-start = ((), (), s32[]{:S(2)}) async-start(), calls=%async_computation.11 | async-start | bytes 2228224 | tf_op jit(solution)/shard_map/all_gather | solution.py:95
  206.2 118.5 %reduce-scatter.5.cloned.1.call-start = ((), (), s32[]{:S(2)}) async-start(), calls=%async_computation.12 | async-start | bytes 4456448 | tf_op jit(solution)/shard_map/reduce_scatter | solution.py:99
  207.1 21.0 %copy-start.6 = (f32[32,512]{1,0:T(8,128)S(1)}, f32[32,512]{1,0:T(8,128)}, u32[]{:S(2)}) copy-start(f32[32,512]{1,0:T(8,128)} %param.5) | copy-start | bytes 196612
  247.5 2.0 copy-start.1
  252.7 6.1 %copy-start.4 = (bf16[4096,256]{1,0:T(8,128)(2,1)S(1)}, bf16[4096,256]{1,0:T(8,128)(2,1)}, u32[]{:S(2)}) copy-start(bf16[4096,256]{1,0:T(8,128)(2,1)} %all-gather.5.cloned.1.call-done) | copy-start | bytes 6291460
  253.5 11.3 %all-to-all-start.5 = ((f32[16,1,256]{2,1,0:T(1,128)}), f32[16,1,256]{2,1,0:T(1,128)S(1)}, u32[]{:S(2)}, u32[]{:S(2)}) async-start(f32[16,1,256]{2,1,0:T(1,128)} %broadcast_in_dim.17), calls=%async_computation.7 | async-start | bytes 32768 | tf_op jit(solution)/shard_map/all_to_all | solution.py:21
  259.5 65.2 %copy-start.5 = (f32[256,256]{1,0:T(8,128)S(1)}, f32[256,256]{1,0:T(8,128)}, u32[]{:S(2)}) copy-start(f32[256,256]{1,0:T(8,128)} %reduce-scatter.3.cloned.1.call-done) | copy-start | bytes 786436
  264.8 24.7 %all-to-all-start.6 = ((f32[8,32,513]{2,1,0:T(8,128)}), f32[8,32,513]{2,1,0:T(8,128)S(1)}, u32[]{:S(2)}, u32[]{:S(2)}) async-start(f32[8,32,513]{2,1,0:T(8,128)} %pad_maximum_fusion.1), calls=%async_computation.8 | async-start | bytes 1310720 | tf_op jit(solution)/shard_map/all_to_all | solution.py:35
Sparse Core Ops, SparseCore 0:
  19.0 35.8 all-gather.2
  140.1 64.3 reduce-scatter.2
  206.9 36.0 all-gather.4
  252.9 71.8 reduce-scatter.4
where the time goes:
time: 335 us; the launch traced here: 333 us
  waiting for transfers between devices  106 us (32%)
  blocking collectives  97.8 us (29%)
  matrix products  37.8 us (11%)
  local copies, waits for them, and re-layouts  35.6 us (11%)
  starting transfers between devices  22.8 us (7%)
  other arithmetic  18.7 us (6%)
  between operations  13.9 us (4%)
    reduce_scatter x2, waiting for transfers between devices, local(): w_numer = lax.psum_scatter(w_numer, 'col', scatter_dimension=0, tiled=True)  87.6 us
    all_to_all x1, blocking collectives, local(): lax.all_to_all(energy, 'row', split_axis=1, concat_axis=0, tiled=True)  57.6 us
    all_to_all x2, blocking collectives, from_everyone(): lax.all_to_all(jnp.broadcast_to(x[None], (peers, *x.shape)), axis, 0, 0,...  22.9 us
    all_to_all x1, blocking collectives, summed_on_arrival(): parts = lax.all_to_all(cut_along(x, dim, peers), axis, 0, 0, tiled=True)  17.3 us
    dot_general x1, matrix products, frame_energy(): jnp.einsum('cfn,nk->fck', frames, table, preferred_element_type=jnp.float32)  15.2 us
    all_to_all x1, waiting for transfers between devices, summed_on_arrival(): parts = lax.all_to_all(cut_along(x, dim, peers), axis, 0, 0, tiled=True)  15 us
    all_to_all x2, local copies, waits for them, and re-layouts, local(): lax.all_to_all(energy, 'row', split_axis=1, concat_axis=0, tiled=True)  13.8 us
    unnamed x15, local copies, waits for them, and re-layouts  13.3 us
  transfers between devices with their start and end apart: 7, of which 5 were waited for; matrix products, arithmetic and copies ran while one was open for 18% of the time, Pallas kernels for 0%

commit v1 on v0

v1 whole, which is shorter than its diff:
```python
import math

import jax
import jax.numpy as jnp
import numpy as np
from jax import lax
from jax.experimental import pallas as pl
from jax.experimental.pallas import tpu as pltpu
from jax.sharding import Mesh
from jax.sharding import PartitionSpec as P

BINS = 128
ITERS = 2
WIN = 256

AXES = ("zh", "x", "zl", "y", "core")
SIZES = (2, 4, 2, 4, 2)
ROWS = ("core", "zh", "x")
COLS = ("zl", "y")
N_ROWS = 16
N_COLS = 8


def dft_table():
    n = np.arange(WIN, dtype=np.int32)
    k = np.arange(BINS, dtype=np.int32)
    phases = (n[:, None] * k[None, :] % WIN).astype(np.float32) * np.float32(2.0 * math.pi / WIN)
    taper = np.float32(0.5) - np.float32(0.5) * np.cos(n.astype(np.float32) * np.float32(2.0 * math.pi / WIN))
    taper = (taper / np.float32(math.sqrt(3.0 * WIN / 8.0))).astype(np.float32)
    both = np.concatenate([taper[:, None] * np.cos(phases), -taper[:, None] * np.sin(phases)], axis=1)
    return jnp.asarray(both.astype(np.float32)).astype(jnp.bfloat16)


def energy_kernel(x_ref, table_ref, out_ref, flat_ref):
    chans = x_ref.shape[0]
    frames = x_ref.shape[1] // WIN
    table = table_ref[...]
    group = 16
    for g in range(frames // group):
        x = jnp.concatenate(
            [x_ref[:, (g * group + f) * WIN : (g * group + f + 1) * WIN] for f in range(group)], axis=0
        )
        spec = jnp.dot(x, table, preferred_element_type=jnp.float32)
        re, im = spec[:, :BINS], spec[:, BINS:]
        flat_ref[g * group * chans : (g + 1) * group * chans, :] = re * re + im * im
    for c in range(chans):
        q, core, j = c // 4, (c // 2) % 2, c % 2
        at = (q * 2 + j) * BINS
        out_ref[core, 0, :, at : at + BINS] = flat_ref[pl.ds(c, frames, stride=chans), :].astype(jnp.bfloat16)


def energies(record, table):
    channels, samples = record.shape
    frames = samples // WIN
    per_row = channels // (N_ROWS // 2)
    rows = channels * BINS // N_ROWS
    return pl.pallas_call(
        energy_kernel,
        grid=(N_ROWS // 2,),
        in_specs=[
            pl.BlockSpec((per_row, samples), lambda r: (r, 0)),
            pl.BlockSpec((WIN, 2 * BINS), lambda r: (0, 0)),
        ],
        out_specs=pl.BlockSpec((2, 1, frames, rows), lambda r: (0, r, 0, 0)),
        out_shape=jax.ShapeDtypeStruct((2, N_ROWS // 2, frames, rows), jnp.bfloat16),
        scratch_shapes=[pltpu.VMEM((frames * per_row, BINS), jnp.float32)],
        compiler_params=pltpu.CompilerParams(vmem_limit_bytes=40 << 20),
        cost_estimate=pl.CostEstimate(
            flops=2 * channels * frames * WIN * WIN, bytes_accessed=12 << 20, transcendentals=0
        ),
        name="energy",
    )(record, table)


def split(x):
    hi = x.astype(jnp.bfloat16)
    return hi, (x - hi.astype(jnp.float32)).astype(jnp.bfloat16)


def sweep_kernel(s_ref, h_ref, w_ref, wn_ref, hn_ref, ht_ref, acc_ref, cs_ref, rs_ref):
    q = pl.program_id(0)
    rank = w_ref.shape[2]
    half = h_ref.shape[2]

    @pl.when(q == 0)
    def _():
        for c in range(2):
            ht_ref[c * half : (c + 1) * half, :] = h_ref[c].T
        ones = jnp.ones((16, 2 * half), jnp.bfloat16)
        rs_ref[...] = jnp.dot(ones, ht_ref[...], preferred_element_type=jnp.float32)
        cs_ref[...] = jnp.zeros_like(cs_ref)

    w = w_ref[0]
    recon = lax.dot_general(ht_ref[...], w, (((1,), (1,)), ((), ())), preferred_element_type=jnp.float32)
    quotient = (s_ref[...].astype(jnp.float32) / recon).astype(jnp.bfloat16)
    wn = jnp.dot(h_ref[0], quotient[:half], preferred_element_type=jnp.float32)
    wn = wn + jnp.dot(h_ref[1], quotient[half:], preferred_element_type=jnp.float32)
    wn_ref[0, :rank, :] = wn.astype(jnp.bfloat16)
    hi, lo = split(rs_ref[...])
    wn_ref[0, rank:, :] = jnp.where(lax.broadcasted_iota(jnp.int32, hi.shape, 0) == 0, hi, lo)
    cs_ref[...] += jnp.sum(w.astype(jnp.float32), axis=0, keepdims=True)
    hn = jnp.dot(quotient, w, preferred_element_type=jnp.float32)

    @pl.when(q == 0)
    def _():
        acc_ref[...] = hn

    @pl.when(q > 0)
    def _():
        acc_ref[...] += hn

    @pl.when(q == N_COLS - 1)
    def _():
        column = jnp.broadcast_to(cs_ref[0:1, :], (128, rank)).T
        hi, lo = split(column)
        sums = jnp.where(lax.broadcasted_iota(jnp.int32, hi.shape, 1) == 0, hi, lo)
        each = rank // (N_ROWS // 2)
        for c in range(2):
            hn = acc_ref[c * half : (c + 1) * half, :].T.astype(jnp.bfloat16)
            for r in range(N_ROWS // 2):
                hn_ref[c * 8 + r, :, :half] = hn[r * each : (r + 1) * each, :]
                hn_ref[c * 8 + r, :, half:] = sums[r * each : (r + 1) * each, :]


def sweep(spectra, h, w):
    frames, rows = spectra.shape
    rank, half = h.shape[1], h.shape[2]
    block = rows // N_COLS
    each = rank // (N_ROWS // 2)
    return pl.pallas_call(
        sweep_kernel,
        grid=(N_COLS,),
        in_specs=[
            pl.BlockSpec((frames, block), lambda q: (0, q)),
            pl.BlockSpec((2, rank, half), lambda q: (0, 0, 0)),
            pl.BlockSpec((1, block, rank), lambda q: (q, 0, 0)),
        ],
        out_specs=[
            pl.BlockSpec((1, rank + 16, block), lambda q: (q, 0, 0)),
            pl.BlockSpec((N_ROWS, each, half + 128), lambda q: (0, 0, 0)),
        ],
        out_shape=[
            jax.ShapeDtypeStruct((N_COLS, rank + 16, block), jnp.bfloat16),
            jax.ShapeDtypeStruct((N_ROWS, each, half + 128), jnp.bfloat16),
        ],
        scratch_shapes=[
            pltpu.VMEM((frames, rank), jnp.bfloat16),
            pltpu.VMEM((frames, rank), jnp.float32),
            pltpu.VMEM((8, rank), jnp.float32),
            pltpu.VMEM((16, rank), jnp.float32),
        ],
        compiler_params=pltpu.CompilerParams(vmem_limit_bytes=48 << 20),
        cost_estimate=pl.CostEstimate(flops=6 * frames * rows * rank, bytes_accessed=8 << 20, transcendentals=0),
        name="sweep",
    )(spectra, h, w)


def w_update_kernel(parts_ref, w_ref, new_ref, low_ref):
    rank = w_ref.shape[1]
    total = parts_ref[0].astype(jnp.float32)
    for i in range(1, N_COLS):
        total = total + parts_ref[i].astype(jnp.float32)
    rowsum = total[rank : rank + 1, :] + total[rank + 1 : rank + 2, :]
    new = w_ref[...] * total[:rank, :].T / rowsum
    new_ref[...] = new
    low_ref[...] = new.astype(jnp.bfloat16)


def w_update(parts, w):
    return pl.pallas_call(
        w_update_kernel,
        out_shape=[jax.ShapeDtypeStruct(w.shape, jnp.float32), jax.ShapeDtypeStruct(w.shape, jnp.bfloat16)],
        name="w_update",
    )(parts, w)


def h_update_kernel(parts_ref, h_ref, new_ref, low_ref):
    half = h_ref.shape[1]
    total = parts_ref[0].astype(jnp.float32)
    for i in range(1, N_ROWS):
        total = total + parts_ref[i].astype(jnp.float32)
    colsum = total[:, half : half + 1] + total[:, half + 1 : half + 2]
    new = h_ref[...] * total[:, :half] / colsum
    new_ref[...] = new
    low_ref[...] = new.astype(jnp.bfloat16)


def h_update(parts, h):
    return pl.pallas_call(
        h_update_kernel,
        out_shape=[jax.ShapeDtypeStruct(h.shape, jnp.float32), jax.ShapeDtypeStruct(h.shape, jnp.bfloat16)],
        name="h_update",
    )(parts, h)


def exchange(x, axes):
    return lax.all_to_all(x, axes, 0, 0, tiled=True)


def spread(x, axes, peers):
    return exchange(jnp.broadcast_to(x[None], (peers, *x.shape)), axes)


def local(samples, w, h):
    rank = w.shape[1]
    record = samples.reshape(samples.shape[2], samples.shape[3])
    h_all = lax.all_gather(h.astype(jnp.bfloat16), ROWS, axis=0, tiled=False)
    w_all = lax.all_gather(w.astype(jnp.bfloat16), COLS, axis=0, tiled=False)
    energy = energies(record, dft_table())
    frames, rows = energy.shape[2:]
    spectra = exchange(energy.reshape(N_ROWS, frames, rows), ROWS).reshape(N_ROWS * frames, rows)
    for step in range(ITERS):
        w_parts, h_parts = sweep(spectra, h_all.reshape(2, rank, -1), w_all)
        h_parts = exchange(h_parts, ROWS)
        w_parts = exchange(w_parts, COLS)
        h, h_low = h_update(h_parts, h)
        w, w_low = w_update(w_parts, w)
        if step + 1 < ITERS:
            h_all = spread(h_low, ROWS, N_ROWS)
            w_all = spread(w_low, COLS, N_COLS)
    return (w, h)


def solution(mesh):
    fine = Mesh(mesh.devices.reshape(SIZES), AXES)
    row, col = ("zh", "x"), ("zl", "y", "core")
    return jax.shard_map(
        local,
        mesh=fine,
        in_specs=(P(col, row, None, None), P(row + col, None), P(row, col)),
        out_specs=(P(row + col, None), P(row, col)),
        check_vma=False,
    )
```

time: 335 us -> 274 us (0.82)
  waiting for transfers between devices: 106 us -> 40.1 us
  blocking collectives: 97.8 us -> 147 us
  Pallas kernels: 0 us -> 39.5 us
  matrix products: 37.8 us -> 0 us
  local copies, waits for them, and re-layouts: 35.6 us -> 11.1 us
  other arithmetic: 18.7 us -> 0.68 us
    all_gather x0 -> x1, blocking collectives: none -> 91.3 us  [local(): h_all = lax.all_gather(h.astype(jnp.bfloat16), ROWS, axis=0, tiled=False)]
    reduce_scatter x2 -> x0, waiting for transfers between devices: 87.6 us -> none  [local(): w_numer = lax.psum_scatter(w_numer, 'col', scatter_dimension=0, tiled=True)]
    all_to_all x4 -> x3, blocking collectives: 97.8 us -> 55.8 us  [exchange(): return lax.all_to_all(x, axes, 0, 0, tiled=True)]
    pallas_call x0 -> x7, Pallas kernels: none -> 39.5 us  [the longest x2 21.6 us: sweep(): pl.pallas_call(sweep_kernel, grid=(N_COLS,), in_specs=[pl.BlockSpec((fram...]
    dot_general x7 -> x0, matrix products: 37.8 us -> none  [the longest x1 15.2 us: frame_energy(): jnp.einsum('cfn,nk->fck', frames, table, preferred_element_type=jnp.float32)]
    all_to_all x3 -> x4, waiting for transfers between devices: 15.8 us -> 40 us  [exchange(): return lax.all_to_all(x, axes, 0, 0, tiled=True)]
    all_to_all x2 -> x0, local copies, waits for them, and re-layouts: 13.8 us -> none  [local(): lax.all_to_all(energy, 'row', split_axis=1, concat_axis=0, tiled=True)]
    convert_element_type x5 -> x2, other arithmetic: 13.2 us -> 0.68 us  [the longest x1 0.67 us: local(): w_all = lax.all_gather(w.astype(jnp.bfloat16), COLS, axis=0, tiled=False)]
  transfers between devices with their start and end apart: 7 -> 5, of which waited for: 5 -> 3; matrix products, arithmetic and copies ran while one was open for 18% -> 0% of each run, Pallas kernels for 0% -> 2%
where the time goes in v1:
time: 274 us; the launch traced here: 272 us
  blocking collectives  147 us (54%)
  waiting for transfers between devices  40.1 us (15%)
  Pallas kernels  39.5 us (14%)
  starting transfers between devices  19.5 us (7%)
  between operations  14.1 us (5%)
  local copies, waits for them, and re-layouts  11.1 us (4%)
    all_gather x1, blocking collectives, local(): h_all = lax.all_gather(h.astype(jnp.bfloat16), ROWS, axis=0, tiled=False)  91.3 us
    all_to_all x3, blocking collectives, exchange(): return lax.all_to_all(x, axes, 0, 0, tiled=True)  55.8 us
    all_to_all x4, waiting for transfers between devices, exchange(): return lax.all_to_all(x, axes, 0, 0, tiled=True)  40 us
    pallas_call x2, Pallas kernels, sweep(): pl.pallas_call(sweep_kernel, grid=(N_COLS,), in_specs=[pl.BlockSpec((fram...  21.6 us
    all_to_all x4, starting transfers between devices, exchange(): return lax.all_to_all(x, axes, 0, 0, tiled=True)  19.5 us
    pallas_call x1, Pallas kernels, energies(): pl.pallas_call(energy_kernel, grid=(N_ROWS // 2,), in_specs=[pl.BlockSpec...  9.71 us
    unnamed x16, local copies, waits for them, and re-layouts  8.53 us
  transfers between devices with their start and end apart: 5, of which 3 were waited for; matrix products, arithmetic and copies ran while one was open for 0% of the time, Pallas kernels for 2%

profile of v1, /device:TPU:0, one launch (start us, length us, event | category | flops | bytes accessed | tf_op | source)
XLA Modules:
  0.0 272.2 jit_solution(2157985850196642622)
XLA Ops:
  7.2 0.0 copy-start.1
  7.2 3.4 %copy-done.1 = bf16[1,1,256,16384]{3,2,1,0:T(8,128)(2,1)S(1)} copy-done((bf16[1,1,256,16384]{3,2,1,0:T(8,128)(2,1)S(1)}, bf16[1,1,256,16384]{3,2,1,0:T(8,128)(2,1)}, u32[]{:S(2)}) %copy-start.1) | copy-done | bytes 8388632
  10.5 0.0 copy-start.2
  10.5 0.9 copy-done.2
  11.5 9.7 %energy.1 = bf16[2,8,64,2048]{3,2,1,0:T(8,128)(2,1)S(1)} custom-call(bf16[256,16384]{1,0:T(8,128)(2,1)S(1)} %bitcast.7, bf16[256,256]{1,0:T(8,128)(2,1)S(1)} %copy-done.2), custom_call_target="tpu_custom_call" | custom-call | flops 2147483648 | bytes 12582912 | tf_op jit(solution)/shard_map/energy/pallas_call | solution.py:57
  21.2 0.0 copy-start
  21.2 2.0 copy-done
  23.2 0.0 copy-start.6
  23.2 0.0 copy-start.7
  23.2 8.0 %all-to-all-start = ((bf16[16,64,2048]{2,1,0:T(8,128)(2,1)}), bf16[16,64,2048]{2,1,0:T(8,128)(2,1)}, u32[]{:S(2)}, u32[]{:S(2)}) async-start(bf16[16,64,2048]{2,1,0:T(8,128)(2,1)} %bitcast.6), calls=%async_computation | async-start | bytes 8388608 | tf_op jit(solution)/shard_map/all_to_all | solution.py:197
  31.2 0.0 all-gather.4.cloned.1.call-start
  31.2 0.0 copy-done.6
  31.2 0.7 convert_element_type.11
  31.9 0.0 all-gather.4.cloned.1.call-update
  31.9 0.0 copy-done.7
  31.9 91.3 %all-gather = bf16[512,512]{1,0:T(8,128)(2,1)S(1)} all-gather(bf16[32,512]{1,0:T(8,128)(2,1)S(1)} %convert_element_type.10), channel_id=2, replica_groups=mesh['zh'=2,'x'=4,'zl'=2,'y'=4,'core'=2] {'core','zh','x'}, dimensions={0}, use_global_device_ids=true | all-gather | bytes 557056 | tf_op jit(solution)/shard_map/all_gather | solution.py:207
  123.3 0.0 all-gather.4.cloned.1.call-done
  123.3 0.0 all-to-all-done
  123.3 0.0 copy-start.3
  123.3 1.2 copy-done.3
  124.5 10.8 %sweep.2 = (bf16[8,272,256]{2,1,0:T(8,128)(2,1)}, bf16[16,32,640]{2,1,0:T(8,128)(2,1)S(1)}) custom-call(bf16[1024,2048]{1,0:T(8,128)(2,1)} %bitcast.2.s_ref, bf16[2,256,512]{2,1,0:T(8,128)(2,1)S(1)} %bitcast.9, bf16[8,256,256]{2,1,0:T(8,128)(2,1)S(1)} %bitcast.10), custom_call_target="tpu_custom_call" | custom-call | flops 3221225472 | bytes 8388608 | tf_op jit(solution)/shard_map/sweep/pallas_call | solution.py:130
  135.3 20.1 %all_to_all.35.parts_ref = bf16[16,32,640]{2,1,0:T(8,128)(2,1)} all-to-all(bf16[16,32,640]{2,1,0:T(8,128)(2,1)S(1)} %get-tuple-element.12), channel_id=1, replica_groups=mesh['zh'=2,'x'=4,'zl'=2,'y'=4,'core'=2] {'core','zh','x'}, dimensions={0} | all-to-all | bytes 1310720 | tf_op jit(solution)/shard_map/all_to_all | solution.py:197
  155.4 4.4 %all-to-all-start.3 = ((bf16[8,272,256]{2,1,0:T(8,128)(2,1)}), bf16[8,272,256]{2,1,0:T(8,128)(2,1)S(1)}, u32[]{:S(2)}, u32[]{:S(2)}) async-start(bf16[8,272,256]{2,1,0:T(8,128)(2,1)} %get-tuple-element.14), calls=%async_computation.3 | async-start | bytes 2228224 | tf_op jit(solution)/shard_map/all_to_all | solution.py:197
  159.7 1.9 h_update.2
  161.6 15.0 %all-to-all-done.3.parts_ref = bf16[8,272,256]{2,1,0:T(8,128)(2,1)S(1)} async-done(((bf16[8,272,256]{2,1,0:T(8,128)(2,1)}), bf16[8,272,256]{2,1,0:T(8,128)(2,1)S(1)}, u32[]{:S(2)}, u32[]{:S(2)}) %all-to-all-start.3) | async-done | bytes 1114144 | tf_op jit(solution)/shard_map/all_to_all | solution.py:197
  176.6 0.0 copy-start.4
  176.6 1.6 broadcast_in_dim.4
  178.2 3.6 %all-to-all-start.2 = ((bf16[16,32,512]{2,1,0:T(8,128)(2,1)}), bf16[16,32,512]{2,1,0:T(8,128)(2,1)S(1)}, u32[]{:S(2)}, u32[]{:S(2)}) async-start(bf16[16,32,512]{2,1,0:T(8,128)(2,1)} %broadcast_in_dim.4), calls=%async_computation.2 | async-start | bytes 1048576 | tf_op jit(solution)/shard_map/all_to_all | solution.py:197
  181.8 0.0 copy-done.4
  181.8 2.2 w_update.2
  184.0 9.9 %all-to-all-done.2 = bf16[16,32,512]{2,1,0:T(8,128)(2,1)S(1)} async-done(((bf16[16,32,512]{2,1,0:T(8,128)(2,1)}), bf16[16,32,512]{2,1,0:T(8,128)(2,1)S(1)}, u32[]{:S(2)}, u32[]{:S(2)}) %all-to-all-start.2) | async-done | bytes 524320 | tf_op jit(solution)/shard_map/all_to_all | solution.py:197
  194.0 1.0 broadcast_in_dim.5
  194.9 18.8 %all_to_all.36.w_ref = bf16[8,256,256]{2,1,0:T(8,128)(2,1)S(1)} all-to-all(bf16[8,256,256]{2,1,0:T(8,128)(2,1)S(1)} %broadcast_in_dim.5), channel_id=1, replica_groups=mesh['zh'=2,'x'=4,'zl'=2,'y'=4,'core'=2] {'zl','y'}, dimensions={0} | all-to-all | bytes 2097152 | tf_op jit(solution)/shard_map/all_to_all | solution.py:197
  213.8 10.8 %sweep.3 = (bf16[8,272,256]{2,1,0:T(8,128)(2,1)}, bf16[16,32,640]{2,1,0:T(8,128)(2,1)S(1)}) custom-call(bf16[1024,2048]{1,0:T(8,128)(2,1)} %bitcast.2.s_ref, bf16[2,256,512]{2,1,0:T(8,128)(2,1)S(1)} %bitcast.8, bf16[8,256,256]{2,1,0:T(8,128)(2,1)S(1)} %all_to_all.36.w_ref), custom_call_target="tpu_custom_call" | custom-call | flops 3221225472 | bytes 8388608 | tf_op jit(solution)/shard_map/sweep/pallas_call | solution.py:130
  224.6 16.9 %all_to_all.37.parts_ref = bf16[16,32,640]{2,1,0:T(8,128)(2,1)} all-to-all(bf16[16,32,640]{2,1,0:T(8,128)(2,1)S(1)} %get-tuple-element.19), channel_id=1, replica_groups=mesh['zh'=2,'x'=4,'zl'=2,'y'=4,'core'=2] {'core','zh','x'}, dimensions={0} | all-to-all | bytes 1310720 | tf_op jit(solution)/shard_map/all_to_all | solution.py:197
  241.5 3.6 %all-to-all-start.5 = ((bf16[8,272,256]{2,1,0:T(8,128)(2,1)}), bf16[8,272,256]{2,1,0:T(8,128)(2,1)S(1)}, u32[]{:S(2)}, u32[]{:S(2)}) async-start(bf16[8,272,256]{2,1,0:T(8,128)(2,1)} %get-tuple-element.16), calls=%async_computation.5 | async-start | bytes 2228224 | tf_op jit(solution)/shard_map/all_to_all | solution.py:197
  245.1 1.9 h_update.3
  247.0 15.1 %all-to-all-done.5.parts_ref = bf16[8,272,256]{2,1,0:T(8,128)(2,1)S(1)} async-done(((bf16[8,272,256]{2,1,0:T(8,128)(2,1)}), bf16[8,272,256]{2,1,0:T(8,128)(2,1)S(1)}, u32[]{:S(2)}, u32[]{:S(2)}) %all-to-all-start.5) | async-done | bytes 1114144 | tf_op jit(solution)/shard_map/all_to_all | solution.py:197
  262.1 0.0 copy-start.5
  262.1 1.0 copy-done.5
  263.1 2.2 w_update.3
  (1 shorter events, 0.0 us)
Async XLA Ops:
  7.2 3.4 %copy-start.1 = (bf16[1,1,256,16384]{3,2,1,0:T(8,128)(2,1)S(1)}, bf16[1,1,256,16384]{3,2,1,0:T(8,128)(2,1)}, u32[]{:S(2)}) copy-start(bf16[1,1,256,16384]{3,2,1,0:T(8,128)(2,1)} %param.4) | copy-start | bytes 25165828
  10.5 0.9 copy-start.2
  21.2 2.0 copy-start
  23.2 8.0 %copy-start.6 = (f32[256,256]{1,0:T(8,128)S(1)}, f32[256,256]{1,0:T(8,128)}, u32[]{:S(2)}) copy-start(f32[256,256]{1,0:T(8,128)} %w_ref.1) | copy-start | bytes 786436
  23.2 8.7 %copy-start.7 = (f32[32,512]{1,0:T(8,128)S(1)}, f32[32,512]{1,0:T(8,128)}, u32[]{:S(2)}) copy-start(f32[32,512]{1,0:T(8,128)} %h_ref.1) | copy-start | bytes 196612
  23.2 100.1 %all-to-all-start = ((bf16[16,64,2048]{2,1,0:T(8,128)(2,1)}), bf16[16,64,2048]{2,1,0:T(8,128)(2,1)}, u32[]{:S(2)}, u32[]{:S(2)}) async-start(bf16[16,64,2048]{2,1,0:T(8,128)(2,1)} %bitcast.6), calls=%async_computation | async-start | bytes 8388608 | tf_op jit(solution)/shard_map/all_to_all | solution.py:197
  31.2 92.1 %all-gather.4.cloned.1.call-start = ((), (), s32[]{:S(2)}) async-start(), calls=%async_computation.7 | async-start | bytes 1179648 | tf_op jit(solution)/shard_map/all_gather | solution.py:208
  123.3 1.2 copy-start.3
  155.4 21.2 %all-to-all-start.3 = ((bf16[8,272,256]{2,1,0:T(8,128)(2,1)}), bf16[8,272,256]{2,1,0:T(8,128)(2,1)S(1)}, u32[]{:S(2)}, u32[]{:S(2)}) async-start(bf16[8,272,256]{2,1,0:T(8,128)(2,1)} %get-tuple-element.14), calls=%async_computation.3 | async-start | bytes 2228224 | tf_op jit(solution)/shard_map/all_to_all | solution.py:197
  176.6 5.2 %copy-start.4 = (bf16[8,272,256]{2,1,0:T(8,128)(2,1)}, bf16[8,272,256]{2,1,0:T(8,128)(2,1)S(1)}, u32[]{:S(2)}) copy-start(bf16[8,272,256]{2,1,0:T(8,128)(2,1)S(1)} %all-to-all-done.3.parts_ref) | copy-start | bytes 3342340
  178.2 15.8 %all-to-all-start.2 = ((bf16[16,32,512]{2,1,0:T(8,128)(2,1)}), bf16[16,32,512]{2,1,0:T(8,128)(2,1)S(1)}, u32[]{:S(2)}, u32[]{:S(2)}) async-start(bf16[16,32,512]{2,1,0:T(8,128)(2,1)} %broadcast_in_dim.4), calls=%async_computation.2 | async-start | bytes 1048576 | tf_op jit(solution)/shard_map/all_to_all | solution.py:197
  241.5 20.6 %all-to-all-start.5 = ((bf16[8,272,256]{2,1,0:T(8,128)(2,1)}), bf16[8,272,256]{2,1,0:T(8,128)(2,1)S(1)}, u32[]{:S(2)}, u32[]{:S(2)}) async-start(bf16[8,272,256]{2,1,0:T(8,128)(2,1)} %get-tuple-element.16), calls=%async_computation.5 | async-start | bytes 2228224 | tf_op jit(solution)/shard_map/all_to_all | solution.py:197
  262.1 1.0 copy-start.5
Sparse Core Ops, SparseCore 0:
  34.2 48.6 all-gather.3

commit v2 on v1

v2 whole, which is shorter than its diff:
```python
import math

import jax
import jax.numpy as jnp
import numpy as np
from jax import lax
from jax.experimental import pallas as pl
from jax.experimental.pallas import tpu as pltpu
from jax.sharding import Mesh
from jax.sharding import PartitionSpec as P

BINS = 128
ITERS = 2
WIN = 256

AXES = ("zh", "x", "zl", "y", "core")
SIZES = (2, 4, 2, 4, 2)
TILE = ("core", "zl", "zh", "x")
RANKS = ("zl", "zh", "x")
N_Y = 4
N_R = 8
N_P = 16
PAD = 128


def dft_table():
    n = np.arange(WIN, dtype=np.int32)
    k = np.arange(BINS, dtype=np.int32)
    phases = (n[:, None] * k[None, :] % WIN).astype(np.float32) * np.float32(2.0 * math.pi / WIN)
    taper = np.float32(0.5) - np.float32(0.5) * np.cos(n.astype(np.float32) * np.float32(2.0 * math.pi / WIN))
    taper = (taper / np.float32(math.sqrt(3.0 * WIN / 8.0))).astype(np.float32)
    both = np.concatenate([taper[:, None] * np.cos(phases), -taper[:, None] * np.sin(phases)], axis=1)
    return jnp.asarray(both.astype(np.float32)).astype(jnp.bfloat16)


def whole(n, space=pltpu.VMEM):
    return [pl.BlockSpec(memory_space=space)] * n


def energy_kernel(x_ref, table_ref, out_ref, flat_ref):
    chans = x_ref.shape[0]
    frames = x_ref.shape[1] // WIN
    table = table_ref[...]
    group = 16
    for g in range(frames // group):
        x = jnp.concatenate(
            [x_ref[:, (g * group + f) * WIN : (g * group + f + 1) * WIN] for f in range(group)], axis=0
        )
        spec = jnp.dot(x, table, preferred_element_type=jnp.float32)
        re, im = spec[:, :BINS], spec[:, BINS:]
        flat_ref[g * group * chans : (g + 1) * group * chans, :] = re * re + im * im
    for c in range(chans):
        zl, y, core, j = c // 16, (c // 4) % 4, (c // 2) % 2, c % 2
        at = (y * 2 + j) * BINS
        out_ref[core, zl, 0, :, at : at + BINS] = flat_ref[pl.ds(c, frames, stride=chans), :].astype(jnp.bfloat16)


def energies(record, table):
    channels, samples = record.shape
    frames = samples // WIN
    per_row = channels // N_R
    rows = channels * BINS // (2 * N_P)
    return pl.pallas_call(
        energy_kernel,
        grid=(N_R,),
        in_specs=[
            pl.BlockSpec((per_row, samples), lambda r: (r, 0)),
            pl.BlockSpec((WIN, 2 * BINS), lambda r: (0, 0)),
        ],
        out_specs=pl.BlockSpec((2, 2, 1, frames, rows), lambda r: (0, 0, r, 0, 0)),
        out_shape=jax.ShapeDtypeStruct((2, 2, N_R, frames, rows), jnp.bfloat16),
        scratch_shapes=[pltpu.VMEM((frames * per_row, BINS), jnp.float32)],
        compiler_params=pltpu.CompilerParams(vmem_limit_bytes=58 << 20),
        cost_estimate=pl.CostEstimate(
            flops=2 * channels * frames * WIN * WIN, bytes_accessed=12 << 20, transcendentals=0
        ),
        name="energy",
    )(record, table)


def hi_lo(x, axis):
    hi = x.astype(jnp.bfloat16)
    lo = (x - hi.astype(jnp.float32)).astype(jnp.bfloat16)
    return jnp.where(lax.broadcasted_iota(jnp.int32, x.shape, axis) == 0, hi, lo)


def sweep_kernel(at_ref, s_ref, own_ref, oth_ref, w0, w1, w2, w3, n0, n1, n2, n3, hown_ref, hoth_ref, ht_ref):
    core, y = at_ref[0], at_ref[1]
    blocks, rank, half = own_ref.shape
    span = blocks * half
    h_refs, n_refs, out_refs = (own_ref, oth_ref), (n0, n1, n2, n3), (hown_ref, hoth_ref)
    for i, ref in enumerate(h_refs):
        for b in range(blocks):
            ht_ref[i, b * half : (b + 1) * half, :] = ref[b].T
    ones = jnp.ones((16, span), jnp.bfloat16)
    rowsum = jnp.dot(ones, ht_ref[0], preferred_element_type=jnp.float32)
    rowsum = rowsum + jnp.dot(ones, ht_ref[1], preferred_element_type=jnp.float32)
    colsum = jnp.zeros((rank, 1), jnp.float32)
    for p in range(2):
        wt = jnp.concatenate([w[...] for w in ((w0, w1), (w2, w3))[p]], axis=0).T
        colsum = colsum + jnp.sum(wt.astype(jnp.float32), axis=1, keepdims=True)
        wn = None
        for i in range(2):
            rows = pl.ds(pl.multiple_of((core if i == 0 else 1 - core) * span, span), span)
            columns = [
                pl.ds(pl.multiple_of(lax.rem(y + 2 * p + t, N_Y) * rank, rank), rank) for t in range(2)
            ]
            s = jnp.concatenate([s_ref[rows, c] for c in columns], axis=1)
            recon = jnp.dot(ht_ref[i], wt, preferred_element_type=jnp.float32)
            quotient = (s.astype(jnp.float32) / recon).astype(jnp.bfloat16)
            hn = lax.dot_general(wt, quotient, (((1,), (1,)), ((), ())), preferred_element_type=jnp.float32)
            if p == 0:
                out_refs[i][:, :span] = hn
            else:
                out_refs[i][:, :span] += hn
            for b in range(blocks):
                part = jnp.dot(
                    h_refs[i][b], quotient[b * half : (b + 1) * half], preferred_element_type=jnp.float32
                )
                wn = part if wn is None else wn + part
        for t in range(2):
            ref = n_refs[2 * p + t]
            ref[:rank, :] = wn[:, t * rank : (t + 1) * rank].astype(ref.dtype)
            if ref.dtype == jnp.float32:
                keep = lax.broadcasted_iota(jnp.int32, rowsum.shape, 0) == 0
                ref[rank:, :] = jnp.where(keep, rowsum, 0.0)
            else:
                ref[rank:, :] = hi_lo(rowsum, 0)
    for ref in out_refs:
        ref[:, span:] = jnp.broadcast_to(colsum, (rank, PAD))


def sweep(at, spectra, h_own, h_oth, ws):
    frames, rows = spectra.shape
    blocks, rank, half = h_own.shape
    part = (rank + 16, rank)
    sums = jax.ShapeDtypeStruct((rank, blocks * half + PAD), jnp.float32)
    return pl.pallas_call(
        sweep_kernel,
        in_specs=whole(1, pltpu.SMEM) + whole(7),
        out_specs=whole(6),
        out_shape=[jax.ShapeDtypeStruct(part, jnp.float32)]
        + [jax.ShapeDtypeStruct(part, jnp.bfloat16)] * 3
        + [sums, sums],
        scratch_shapes=[pltpu.VMEM((2, blocks * half, rank), jnp.bfloat16)],
        compiler_params=pltpu.CompilerParams(vmem_limit_bytes=32 << 20),
        cost_estimate=pl.CostEstimate(flops=6 * frames * rows * rank, bytes_accessed=8 << 20, transcendentals=0),
        name="sweep",
    )(at, spectra, h_own, h_oth, *ws)


def pair_kernel(a_ref, b_ref, out_ref):
    each, half = out_ref.shape[1], out_ref.shape[2] - PAD
    span = a_ref.shape[1] - PAD
    total = a_ref[...] + b_ref[...]
    sums = hi_lo(total[:, span:], 1)
    for zl in range(2):
        part = total[:, zl * half : (zl + 1) * half].astype(jnp.bfloat16)
        for r in range(N_R):
            out_ref[zl * N_R + r, :, :half] = part[r * each : (r + 1) * each, :]
            out_ref[zl * N_R + r, :, half:] = sums[r * each : (r + 1) * each, :]


def pair(a, b, each, half):
    return pl.pallas_call(
        pair_kernel,
        in_specs=whole(2),
        out_specs=whole(1)[0],
        out_shape=jax.ShapeDtypeStruct((N_P, each, half + PAD), jnp.bfloat16),
        compiler_params=pltpu.CompilerParams(vmem_limit_bytes=12 << 20),
        name="pair",
    )(a, b)


def h_update_kernel(parts_ref, h_ref, new_ref, low_ref):
    half = h_ref.shape[1]
    total = parts_ref[0].astype(jnp.float32)
    for i in range(1, N_P):
        total = total + parts_ref[i].astype(jnp.float32)
    colsum = total[:, half : half + 1] + total[:, half + 1 : half + 2]
    new = h_ref[...] * total[:, :half] / colsum
    new_ref[...] = new
    low = new.astype(jnp.bfloat16)
    for i in range(N_P):
        low_ref[i] = low


def h_update(parts, h):
    return pl.pallas_call(
        h_update_kernel,
        in_specs=whole(2),
        out_specs=whole(2),
        out_shape=[jax.ShapeDtypeStruct(h.shape, jnp.float32), jax.ShapeDtypeStruct((N_P, *h.shape), jnp.bfloat16)],
        compiler_params=pltpu.CompilerParams(vmem_limit_bytes=12 << 20),
        name="h_update",
    )(parts, h)


def w_update_kernel(p0, p1, p2, p3, w_ref, new_ref, low_ref):
    rank = w_ref.shape[1]
    total = p0[...] + p1[...].astype(jnp.float32) + p2[...].astype(jnp.float32) + p3[...].astype(jnp.float32)
    rowsum = total[rank : rank + 1, :] + total[rank + 1 : rank + 2, :]
    new = w_ref[...] * total[:rank, :].T / rowsum
    new_ref[...] = new
    low_ref[...] = new.astype(jnp.bfloat16)


def w_update(parts, w):
    return pl.pallas_call(
        w_update_kernel,
        in_specs=whole(5),
        out_specs=whole(2),
        out_shape=[jax.ShapeDtypeStruct(w.shape, jnp.float32), jax.ShapeDtypeStruct(w.shape, jnp.bfloat16)],
        compiler_params=pltpu.CompilerParams(vmem_limit_bytes=12 << 20),
        name="w_update",
    )(*parts, w)


def exchange(x, axes):
    return lax.all_to_all(x, axes, 0, 0, tiled=True)


def from_sibling(x):
    return lax.ppermute(x, "core", [(0, 1), (1, 0)])


def sent_ahead(x, t):
    return lax.ppermute(x, "y", [(i, (i + t) % N_Y) for i in range(N_Y)])


def taken_ahead(x):
    return [x] + [lax.ppermute(x, "y", [(i, (i - t) % N_Y) for i in range(N_Y)]) for t in range(1, N_Y)]


def gathered(low, rank):
    own = exchange(low, RANKS).reshape(2, rank, -1)
    return own, from_sibling(own)


def local(samples, w, h):
    rank = w.shape[1]
    record = samples.reshape(samples.shape[2], samples.shape[3])
    at = jnp.stack([lax.axis_index("core"), lax.axis_index("y")]).astype(jnp.int32)
    h_own, h_oth = gathered(jnp.broadcast_to(h.astype(jnp.bfloat16)[None], (N_P, *h.shape)), rank)
    energy = energies(record, dft_table())
    frames, rows = energy.shape[3:]
    energy, w_low = lax.optimization_barrier((energy, w.astype(jnp.bfloat16)))
    ws = taken_ahead(w_low)
    spectra = exchange(energy.reshape(2 * N_P, frames, rows), TILE).reshape(2 * N_P * frames, rows)
    for step in range(ITERS):
        n0, n1, n2, n3, s_own, s_oth = sweep(at, spectra, h_own, h_oth, ws)
        s_own = pair(s_own, from_sibling(s_oth), *h.shape)
        h_parts = exchange(s_own, RANKS)
        w_parts = [n0] + [sent_ahead(n, t + 1) for t, n in enumerate((n1, n2, n3))]
        h, low = h_update(h_parts, h)
        w, w_low = w_update(w_parts, w)
        if step + 1 < ITERS:
            h_own, h_oth = gathered(low, rank)
            ws = taken_ahead(w_low)
    return (w, h)


def solution(mesh):
    fine = Mesh(mesh.devices.reshape(SIZES), AXES)
    row, col = ("zh", "x"), ("zl", "y", "core")
    return jax.shard_map(
        local,
        mesh=fine,
        in_specs=(P(col, row, None, None), P(row + col, None), P(row, col)),
        out_specs=(P(row + col, None), P(row, col)),
        check_vma=False,
    )
```

time: 274 us -> 181 us (0.66)
  blocking collectives: 147 us -> 33.1 us
  waiting for transfers between devices: 40.1 us -> 74.3 us
  starting transfers between devices: 19.5 us -> 40.6 us
  between operations: 14.1 us -> 0.74 us
  local copies, waits for them, and re-layouts: 11.1 us -> 0.87 us
  Pallas kernels: 39.5 us -> 29.3 us
    all_gather x1 -> x0, blocking collectives: 91.3 us -> none  [local(): h_all = lax.all_gather(h.astype(jnp.bfloat16), ROWS, axis=0, tiled=False)]
    ppermute x0 -> x16, waiting for transfers between devices: none -> 29.2 us  [the longest x6 12 us: sent_ahead(): return lax.ppermute(x, 'y', [(i, (i + t) % N_Y) for i in range(N_Y)])]
    all_to_all x3 -> x2, blocking collectives: 55.8 us -> 33.1 us  [exchange(): return lax.all_to_all(x, axes, 0, 0, tiled=True)]
    ppermute x0 -> x16, starting transfers between devices: none -> 21.4 us  [the longest x6 10.5 us: taken_ahead(): lax.ppermute(x, 'y', [(i, (i - t) % N_Y) for i in range(N_Y)])]
    pallas_call x7 -> x9, Pallas kernels: 39.5 us -> 29.3 us  [the longest x2 13.6 us: sweep(): pl.pallas_call(sweep_kernel, in_specs=whole(1, pltpu.SMEM) + whole(7), ou...]
    unnamed x16 -> x4, local copies, waits for them, and re-layouts: 8.53 us -> 0.01 us
    all_to_all x4 -> x3, waiting for transfers between devices: 40 us -> 45 us  [exchange(): return lax.all_to_all(x, axes, 0, 0, tiled=True)]
    all_to_all x4 -> x3, starting transfers between devices: 19.5 us -> 19.2 us  [exchange(): return lax.all_to_all(x, axes, 0, 0, tiled=True)]
  transfers between devices with their start and end apart: 5 -> 19, of which waited for: 3 -> 13; matrix products, arithmetic and copies ran while one was open for 0% -> 0% of each run, Pallas kernels for 2% -> 7%
where the time goes in v2:
time: 181 us; the launch traced here: 180 us
  waiting for transfers between devices  74.3 us (41%)
  starting transfers between devices  40.6 us (22%)
  blocking collectives  33.1 us (18%)
  Pallas kernels  29.3 us (16%)
    all_to_all x3, waiting for transfers between devices, exchange(): return lax.all_to_all(x, axes, 0, 0, tiled=True)  45 us
    all_to_all x2, blocking collectives, exchange(): return lax.all_to_all(x, axes, 0, 0, tiled=True)  33.1 us
    all_to_all x3, starting transfers between devices, exchange(): return lax.all_to_all(x, axes, 0, 0, tiled=True)  19.2 us
    pallas_call x2, Pallas kernels, sweep(): pl.pallas_call(sweep_kernel, in_specs=whole(1, pltpu.SMEM) + whole(7), ou...  13.6 us
    pallas_call x1, Pallas kernels, energies(): pl.pallas_call(energy_kernel, grid=(N_R,), in_specs=[pl.BlockSpec((per_ro...  12.3 us
    ppermute x6, waiting for transfers between devices, sent_ahead(): return lax.ppermute(x, 'y', [(i, (i + t) % N_Y) for i in range(N_Y)])  12 us
    ppermute x6, waiting for transfers between devices, taken_ahead(): lax.ppermute(x, 'y', [(i, (i - t) % N_Y) for i in range(N_Y)])  11.8 us
    ppermute x6, starting transfers between devices, taken_ahead(): lax.ppermute(x, 'y', [(i, (i - t) % N_Y) for i in range(N_Y)])  10.5 us
  transfers between devices with their start and end apart: 19, of which 13 were waited for; matrix products, arithmetic and copies ran while one was open for 0% of the time, Pallas kernels for 7%

profile of v2, /device:TPU:0, one launch (start us, length us, event | category | flops | bytes accessed | tf_op | source)
XLA Modules:
  0.0 179.9 jit_solution(4007551378840094719)
XLA Ops:
  0.6 0.0 copy-start
  0.6 0.9 convert_element_type.11
  1.5 0.9 broadcast_in_dim.2
  2.4 8.0 %all-to-all-start.1 = ((bf16[16,32,512]{2,1,0:T(8,128)(2,1)}), bf16[16,32,512]{2,1,0:T(8,128)(2,1)S(1)}, u32[]{:S(2)}, u32[]{:S(2)}) async-start(bf16[16,32,512]{2,1,0:T(8,128)(2,1)} %broadcast_in_dim.2), calls=%async_computation.1 | async-start | bytes 1048576 | tf_op jit(solution)/shard_map/all_to_all | solution.py:220
  10.4 0.0 copy-done
  10.4 12.3 %energy.1 = bf16[2,2,8,64,1024]{4,3,2,1,0:T(8,128)(2,1)} custom-call(bf16[256,16384]{1,0:T(8,128)(2,1)} %bitcast.12, bf16[256,256]{1,0:T(8,128)(2,1)} %constant.12.table_ref), custom_call_target="tpu_custom_call" | custom-call | flops 2147483648 | bytes 12582912 | tf_op jit(solution)/shard_map/energy/pallas_call | solution.py:63
  22.7 0.0 all-to-all-done.1
  22.7 7.6 %all-to-all-start = ((bf16[32,64,1024]{2,1,0:T(8,128)(2,1)}), bf16[32,64,1024]{2,1,0:T(8,128)(2,1)}, u32[]{:S(2)}, u32[]{:S(2)}) async-start(bf16[32,64,1024]{2,1,0:T(8,128)(2,1)} %bitcast.11), calls=%async_computation | async-start | bytes 8388608 | tf_op jit(solution)/shard_map/all_to_all | solution.py:220
  30.4 0.3 collective-permute-start
  30.7 3.0 %collective-permute-start.1 = (bf16[256,256]{1,0:T(8,128)(2,1)S(1)}, bf16[256,256]{1,0:T(8,128)(2,1)S(1)}, u32[]{:S(2)}, u32[]{:S(2)}) collective-permute-start(bf16[256,256]{1,0:T(8,128)(2,1)S(1)} %convert_element_type.10.w0), channel_id=1, source_target_pairs={{0,6},{2,0},{4,2},{6,4},{1,7},{3,1},{5,3},{7,5},{8,14},{10,8},{12,... | collective-permute-start | bytes 393224 | tf_op jit(solution)/shard_map/ppermute | solution.py:232
  33.7 0.6 collective-permute-start.2
  34.3 1.0 collective-permute-start.3
  35.3 0.1 pad_add_fusion.at_ref
  35.4 4.4 %collective-permute-done.1.w1 = bf16[256,256]{1,0:T(8,128)(2,1)S(1)} collective-permute-done((bf16[256,256]{1,0:T(8,128)(2,1)S(1)}, bf16[256,256]{1,0:T(8,128)(2,1)S(1)}, u32[]{:S(2)}, u32[]{:S(2)}) %collective-permute-start.1) | collective-permute-done | bytes 131104 | tf_op jit(solution)/shard_map/ppermute | solution.py:232
  39.7 1.9 %collective-permute-done.2.w2 = bf16[256,256]{1,0:T(8,128)(2,1)S(1)} collective-permute-done((bf16[256,256]{1,0:T(8,128)(2,1)S(1)}, bf16[256,256]{1,0:T(8,128)(2,1)S(1)}, u32[]{:S(2)}, u32[]{:S(2)}) %collective-permute-start.2) | collective-permute-done | bytes 131104 | tf_op jit(solution)/shard_map/ppermute | solution.py:232
  41.6 1.8 %collective-permute-done.3.w3 = bf16[256,256]{1,0:T(8,128)(2,1)S(1)} collective-permute-done((bf16[256,256]{1,0:T(8,128)(2,1)S(1)}, bf16[256,256]{1,0:T(8,128)(2,1)S(1)}, u32[]{:S(2)}, u32[]{:S(2)}) %collective-permute-start.3) | collective-permute-done | bytes 131104 | tf_op jit(solution)/shard_map/ppermute | solution.py:232
  43.4 0.0 collective-permute-done.oth_ref
  43.4 43.1 %all-to-all-done = bf16[32,64,1024]{2,1,0:T(8,128)(2,1)} async-done(((bf16[32,64,1024]{2,1,0:T(8,128)(2,1)}), bf16[32,64,1024]{2,1,0:T(8,128)(2,1)}, u32[]{:S(2)}, u32[]{:S(2)}) %all-to-all-start) | async-done | bytes 4194336 | tf_op jit(solution)/shard_map/all_to_all | solution.py:220
  86.6 6.8 %sweep.2 = (f32[272,256]{1,0:T(8,128)S(1)}, bf16[272,256]{1,0:T(8,128)(2,1)S(1)}, bf16[272,256]{1,0:T(8,128)(2,1)S(1)}, bf16[272,256]{1,0:T(8,128)(2,1)S(1)}, f3...) custom-call(s32[2]{0:T(128)S(1)} %pad_add_fusion.at_ref, bf16[2048,1024]{1,0:T(8,128)(2,1)} %bitcast.4.s_ref, ...), custom_call_target="tpu_custom_call" | custom-call | flops 3221225472 | bytes 8388608 | tf_op jit(solution)/shard_map/sweep/pallas_call | solution.py:138
  93.4 0.3 collective-permute-start.4
  93.7 2.6 %collective-permute-done.4.b_ref = f32[256,1152]{1,0:T(8,128)S(1)} collective-permute-done((f32[256,1152]{1,0:T(8,128)S(1)}, f32[256,1152]{1,0:T(8,128)S(1)}, u32[]{:S(2)}, u32[]{:S(2)}) %collective-permute-start.4) | collective-permute-done | bytes 1179680 | tf_op jit(solution)/shard_map/ppermute | solution.py:224
  96.3 0.2 pair.2
  96.5 0.0 copy-start.1
  96.5 19.5 %all_to_all.25.parts_ref = bf16[16,32,640]{2,1,0:T(8,128)(2,1)S(1)} all-to-all(bf16[16,32,640]{2,1,0:T(8,128)(2,1)S(1)} %pair.2), channel_id=1, replica_groups=mesh['zh'=2,'x'=4,'zl'=2,'y'=4,'core'=2] {'zl','zh','x'}, dimensions={0} | all-to-all | bytes 1310720 | tf_op jit(solution)/shard_map/all_to_all | solution.py:220
  116.0 0.0 copy-done.1
  116.0 0.2 h_update.2
  116.2 13.7 %all_to_all.26 = bf16[16,32,512]{2,1,0:T(8,128)(2,1)S(1)} all-to-all(bf16[16,32,512]{2,1,0:T(8,128)(2,1)S(1)} %get-tuple-element.26), channel_id=1, replica_groups=mesh['zh'=2,'x'=4,'zl'=2,'y'=4,'core'=2] {'zl','zh','x'}, dimensions={0} | all-to-all | bytes 1048576 | tf_op jit(solution)/shard_map/all_to_all | solution.py:220
  129.8 0.0 collective-permute-start.5
  129.9 1.6 collective-permute-start.6
  131.4 2.9 %collective-permute-start.7 = (bf16[272,256]{1,0:T(8,128)(2,1)S(1)}, bf16[272,256]{1,0:T(8,128)(2,1)S(1)}, u32[]{:S(2)}, u32[]{:S(2)}) collective-permute-start(bf16[272,256]{1,0:T(8,128)(2,1)S(1)} %get-tuple-element.29), channel_id=1, source_target_pairs={{0,4},{2,6},{4,0},{6,2},{1,5},{3,7},{5,1},{7,3},{8,12},{10,14},{12... | collective-permute-start | bytes 417800 | tf_op jit(solution)/shard_map/ppermute | solution.py:228
  134.3 1.4 collective-permute-start.8
  135.7 1.5 collective-permute-done.6.p1
  137.2 4.2 %collective-permute-done.7.p2 = bf16[272,256]{1,0:T(8,128)(2,1)S(1)} collective-permute-done((bf16[272,256]{1,0:T(8,128)(2,1)S(1)}, bf16[272,256]{1,0:T(8,128)(2,1)S(1)}, u32[]{:S(2)}, u32[]{:S(2)}) %collective-permute-start.7) | collective-permute-done | bytes 139296 | tf_op jit(solution)/shard_map/ppermute | solution.py:228
  141.4 0.0 collective-permute-done.8.p3
  141.4 0.2 w_update.2
  141.5 2.7 %collective-permute-start.10 = (bf16[256,256]{1,0:T(8,128)(2,1)S(1)}, bf16[256,256]{1,0:T(8,128)(2,1)S(1)}, u32[]{:S(2)}, u32[]{:S(2)}) collective-permute-start(bf16[256,256]{1,0:T(8,128)(2,1)S(1)} %get-tuple-element.31.w0), channel_id=1, source_target_pairs={{0,4},{2,6},{4,0},{6,2},{1,5},{3,7},{5,1},{7,3},{8,12},{10,14},{12... | collective-permute-start | bytes 393224 | tf_op jit(solution)/shard_map/ppermute | solution.py:232
  144.2 0.3 collective-permute-start.11
  144.5 2.9 %collective-permute-start.9 = (bf16[256,256]{1,0:T(8,128)(2,1)S(1)}, bf16[256,256]{1,0:T(8,128)(2,1)S(1)}, u32[]{:S(2)}, u32[]{:S(2)}) collective-permute-start(bf16[256,256]{1,0:T(8,128)(2,1)S(1)} %get-tuple-element.31.w0), channel_id=1, source_target_pairs={{0,6},{2,0},{4,2},{6,4},{1,7},{3,1},{5,3},{7,5},{8,14},{10,8},{12,... | collective-permute-start | bytes 393224 | tf_op jit(solution)/shard_map/ppermute | solution.py:232
  147.4 2.1 %collective-permute-done.10.w2 = bf16[256,256]{1,0:T(8,128)(2,1)S(1)} collective-permute-done((bf16[256,256]{1,0:T(8,128)(2,1)S(1)}, bf16[256,256]{1,0:T(8,128)(2,1)S(1)}, u32[]{:S(2)}, u32[]{:S(2)}) %collective-permute-start.10) | collective-permute-done | bytes 131104 | tf_op jit(solution)/shard_map/ppermute | solution.py:232
  149.5 1.6 collective-permute-done.11.w3
  151.1 0.0 collective-permute-done.9.w1
  151.1 0.0 collective-permute-done.5.oth_ref
  151.1 6.8 %sweep.3 = (f32[272,256]{1,0:T(8,128)S(1)}, bf16[272,256]{1,0:T(8,128)(2,1)S(1)}, bf16[272,256]{1,0:T(8,128)(2,1)S(1)}, bf16[272,256]{1,0:T(8,128)(2,1)S(1)}, f3...) custom-call(s32[2]{0:T(128)S(1)} %pad_add_fusion.at_ref, bf16[2048,1024]{1,0:T(8,128)(2,1)} %bitcast.4.s_ref, ...), custom_call_target="tpu_custom_call" | custom-call | flops 3221225472 | bytes 8388608 | tf_op jit(solution)/shard_map/sweep/pallas_call | solution.py:138
  157.9 0.1 collective-permute-start.15
  158.0 2.8 %collective-permute-done.15.b_ref = f32[256,1152]{1,0:T(8,128)S(1)} collective-permute-done((f32[256,1152]{1,0:T(8,128)S(1)}, f32[256,1152]{1,0:T(8,128)S(1)}, u32[]{:S(2)}, u32[]{:S(2)}) %collective-permute-start.15) | collective-permute-done | bytes 1179680 | tf_op jit(solution)/shard_map/ppermute | solution.py:224
  160.8 0.9 pair.3
  161.8 3.6 %all-to-all-start.4 = ((bf16[16,32,640]{2,1,0:T(8,128)(2,1)}), bf16[16,32,640]{2,1,0:T(8,128)(2,1)S(1)}, u32[]{:S(2)}, u32[]{:S(2)}) async-start(bf16[16,32,640]{2,1,0:T(8,128)(2,1)} %pair.3), calls=%async_computation.4 | async-start | bytes 1310720 | tf_op jit(solution)/shard_map/all_to_all | solution.py:220
  165.4 0.8 collective-permute-start.12
  166.2 3.2 %collective-permute-start.13 = (bf16[272,256]{1,0:T(8,128)(2,1)S(1)}, bf16[272,256]{1,0:T(8,128)(2,1)S(1)}, u32[]{:S(2)}, u32[]{:S(2)}) collective-permute-start(bf16[272,256]{1,0:T(8,128)(2,1)S(1)} %get-tuple-element.34), channel_id=1, source_target_pairs={{0,4},{2,6},{4,0},{6,2},{1,5},{3,7},{5,1},{7,3},{8,12},{10,14},{12... | collective-permute-start | bytes 417800 | tf_op jit(solution)/shard_map/ppermute | solution.py:228
  169.4 0.3 collective-permute-start.14
  169.8 2.7 %collective-permute-done.12.p1 = bf16[272,256]{1,0:T(8,128)(2,1)S(1)} collective-permute-done((bf16[272,256]{1,0:T(8,128)(2,1)S(1)}, bf16[272,256]{1,0:T(8,128)(2,1)S(1)}, u32[]{:S(2)}, u32[]{:S(2)}) %collective-permute-start.12) | collective-permute-done | bytes 139296 | tf_op jit(solution)/shard_map/ppermute | solution.py:228
  172.4 3.7 %collective-permute-done.13.p2 = bf16[272,256]{1,0:T(8,128)(2,1)S(1)} collective-permute-done((bf16[272,256]{1,0:T(8,128)(2,1)S(1)}, bf16[272,256]{1,0:T(8,128)(2,1)S(1)}, u32[]{:S(2)}, u32[]{:S(2)}) %collective-permute-start.13) | collective-permute-done | bytes 139296 | tf_op jit(solution)/shard_map/ppermute | solution.py:228
  176.1 0.0 collective-permute-done.14.p3
  176.1 0.9 w_update.3
  177.0 1.9 %all-to-all-done.4.parts_ref = bf16[16,32,640]{2,1,0:T(8,128)(2,1)S(1)} async-done(((bf16[16,32,640]{2,1,0:T(8,128)(2,1)}), bf16[16,32,640]{2,1,0:T(8,128)(2,1)S(1)}, u32[]{:S(2)}, u32[]{:S(2)}) %all-to-all-start.4) | async-done | bytes 655392 | tf_op jit(solution)/shard_map/all_to_all | solution.py:220
  178.9 1.0 h_update.3
  (1 shorter events, 0.0 us)
Async XLA Ops:
  0.6 9.7 %copy-start = (f32[256,256]{1,0:T(8,128)S(1)}, f32[256,256]{1,0:T(8,128)}, u32[]{:S(2)}) copy-start(f32[256,256]{1,0:T(8,128)} %w_ref.1) | copy-start | bytes 786436
  2.4 20.4 %all-to-all-start.1 = ((bf16[16,32,512]{2,1,0:T(8,128)(2,1)}), bf16[16,32,512]{2,1,0:T(8,128)(2,1)S(1)}, u32[]{:S(2)}, u32[]{:S(2)}) async-start(bf16[16,32,512]{2,1,0:T(8,128)(2,1)} %broadcast_in_dim.2), calls=%async_computation.1 | async-start | bytes 1048576 | tf_op jit(solution)/shard_map/all_to_all | solution.py:220
  22.7 63.8 %all-to-all-start = ((bf16[32,64,1024]{2,1,0:T(8,128)(2,1)}), bf16[32,64,1024]{2,1,0:T(8,128)(2,1)}, u32[]{:S(2)}, u32[]{:S(2)}) async-start(bf16[32,64,1024]{2,1,0:T(8,128)(2,1)} %bitcast.11), calls=%async_computation | async-start | bytes 8388608 | tf_op jit(solution)/shard_map/all_to_all | solution.py:220
  30.4 13.0 %collective-permute-start = (bf16[2,256,512]{2,1,0:T(8,128)(2,1)S(1)}, bf16[2,256,512]{2,1,0:T(8,128)(2,1)S(1)}, u32[]{:S(2)}, u32[]{:S(2)}) collective-permute-start(bf16[2,256,512]{2,1,0:T(8,128)(2,1)S(1)} %bitcast.7), channel_id=1, source_target_pairs={{0,1},{1,0},{2,3},{3,2},{4,5},{5,4},{6,7},{7,6},{8,9},{9,8},{10,11... | collective-permute-start | bytes 1572872 | tf_op jit(solution)/shard_map/ppermute | solution.py:224
  30.7 9.0 %collective-permute-start.1 = (bf16[256,256]{1,0:T(8,128)(2,1)S(1)}, bf16[256,256]{1,0:T(8,128)(2,1)S(1)}, u32[]{:S(2)}, u32[]{:S(2)}) collective-permute-start(bf16[256,256]{1,0:T(8,128)(2,1)S(1)} %convert_element_type.10.w0), channel_id=1, source_target_pairs={{0,6},{2,0},{4,2},{6,4},{1,7},{3,1},{5,3},{7,5},{8,14},{10,8},{12,... | collective-permute-start | bytes 393224 | tf_op jit(solution)/shard_map/ppermute | solution.py:232
  33.7 7.9 %collective-permute-start.2 = (bf16[256,256]{1,0:T(8,128)(2,1)S(1)}, bf16[256,256]{1,0:T(8,128)(2,1)S(1)}, u32[]{:S(2)}, u32[]{:S(2)}) collective-permute-start(bf16[256,256]{1,0:T(8,128)(2,1)S(1)} %convert_element_type.10.w0), channel_id=1, source_target_pairs={{0,4},{2,6},{4,0},{6,2},{1,5},{3,7},{5,1},{7,3},{8,12},{10,14},{12... | collective-permute-start | bytes 393224 | tf_op jit(solution)/shard_map/ppermute | solution.py:232
  34.3 9.1 %collective-permute-start.3 = (bf16[256,256]{1,0:T(8,128)(2,1)S(1)}, bf16[256,256]{1,0:T(8,128)(2,1)S(1)}, u32[]{:S(2)}, u32[]{:S(2)}) collective-permute-start(bf16[256,256]{1,0:T(8,128)(2,1)S(1)} %convert_element_type.10.w0), channel_id=1, source_target_pairs={{0,2},{2,4},{4,6},{6,0},{1,3},{3,5},{5,7},{7,1},{8,10},{10,12},{12... | collective-permute-start | bytes 393224 | tf_op jit(solution)/shard_map/ppermute | solution.py:232
  93.4 2.9 %collective-permute-start.4 = (f32[256,1152]{1,0:T(8,128)S(1)}, f32[256,1152]{1,0:T(8,128)S(1)}, u32[]{:S(2)}, u32[]{:S(2)}) collective-permute-start(f32[256,1152]{1,0:T(8,128)S(1)} %get-tuple-element.25), channel_id=1, source_target_pairs={{0,1},{1,0},{2,3},{3,2},{4,5},{5,4},{6,7},{7,6},{8,9},{9,8},{10,11... | collective-permute-start | bytes 3538952 | tf_op jit(solution)/shard_map/ppermute | solution.py:224
  96.5 19.5 %copy-start.1 = (f32[32,512]{1,0:T(8,128)S(1)}, f32[32,512]{1,0:T(8,128)}, u32[]{:S(2)}) copy-start(f32[32,512]{1,0:T(8,128)} %h_ref.1) | copy-start | bytes 196612
  129.8 21.3 %collective-permute-start.5 = (bf16[2,256,512]{2,1,0:T(8,128)(2,1)S(1)}, bf16[2,256,512]{2,1,0:T(8,128)(2,1)S(1)}, u32[]{:S(2)}, u32[]{:S(2)}) collective-permute-start(bf16[2,256,512]{2,1,0:T(8,128)(2,1)S(1)} %bitcast.9), channel_id=1, source_target_pairs={{0,1},{1,0},{2,3},{3,2},{4,5},{5,4},{6,7},{7,6},{8,9},{9,8},{10,11... | collective-permute-start | bytes 1572872 | tf_op jit(solution)/shard_map/ppermute | solution.py:224
  129.9 7.4 %collective-permute-start.6 = (bf16[272,256]{1,0:T(8,128)(2,1)S(1)}, bf16[272,256]{1,0:T(8,128)(2,1)S(1)}, u32[]{:S(2)}, u32[]{:S(2)}) collective-permute-start(bf16[272,256]{1,0:T(8,128)(2,1)S(1)} %get-tuple-element.28), channel_id=1, source_target_pairs={{0,2},{2,4},{4,6},{6,0},{1,3},{3,5},{5,7},{7,1},{8,10},{10,12},{12... | collective-permute-start | bytes 417800 | tf_op jit(solution)/shard_map/ppermute | solution.py:228
  131.4 9.9 %collective-permute-start.7 = (bf16[272,256]{1,0:T(8,128)(2,1)S(1)}, bf16[272,256]{1,0:T(8,128)(2,1)S(1)}, u32[]{:S(2)}, u32[]{:S(2)}) collective-permute-start(bf16[272,256]{1,0:T(8,128)(2,1)S(1)} %get-tuple-element.29), channel_id=1, source_target_pairs={{0,4},{2,6},{4,0},{6,2},{1,5},{3,7},{5,1},{7,3},{8,12},{10,14},{12... | collective-permute-start | bytes 417800 | tf_op jit(solution)/shard_map/ppermute | solution.py:228
  134.3 7.0 %collective-permute-start.8 = (bf16[272,256]{1,0:T(8,128)(2,1)S(1)}, bf16[272,256]{1,0:T(8,128)(2,1)S(1)}, u32[]{:S(2)}, u32[]{:S(2)}) collective-permute-start(bf16[272,256]{1,0:T(8,128)(2,1)S(1)} %get-tuple-element.30), channel_id=1, source_target_pairs={{0,6},{2,0},{4,2},{6,4},{1,7},{3,1},{5,3},{7,5},{8,14},{10,8},{12,... | collective-permute-start | bytes 417800 | tf_op jit(solution)/shard_map/ppermute | solution.py:228
  141.5 8.0 %collective-permute-start.10 = (bf16[256,256]{1,0:T(8,128)(2,1)S(1)}, bf16[256,256]{1,0:T(8,128)(2,1)S(1)}, u32[]{:S(2)}, u32[]{:S(2)}) collective-permute-start(bf16[256,256]{1,0:T(8,128)(2,1)S(1)} %get-tuple-element.31.w0), channel_id=1, source_target_pairs={{0,4},{2,6},{4,0},{6,2},{1,5},{3,7},{5,1},{7,3},{8,12},{10,14},{12... | collective-permute-start | bytes 393224 | tf_op jit(solution)/shard_map/ppermute | solution.py:232
  144.2 6.9 %collective-permute-start.11 = (bf16[256,256]{1,0:T(8,128)(2,1)S(1)}, bf16[256,256]{1,0:T(8,128)(2,1)S(1)}, u32[]{:S(2)}, u32[]{:S(2)}) collective-permute-start(bf16[256,256]{1,0:T(8,128)(2,1)S(1)} %get-tuple-element.31.w0), channel_id=1, source_target_pairs={{0,2},{2,4},{4,6},{6,0},{1,3},{3,5},{5,7},{7,1},{8,10},{10,12},{12... | collective-permute-start | bytes 393224 | tf_op jit(solution)/shard_map/ppermute | solution.py:232
  144.5 6.6 %collective-permute-start.9 = (bf16[256,256]{1,0:T(8,128)(2,1)S(1)}, bf16[256,256]{1,0:T(8,128)(2,1)S(1)}, u32[]{:S(2)}, u32[]{:S(2)}) collective-permute-start(bf16[256,256]{1,0:T(8,128)(2,1)S(1)} %get-tuple-element.31.w0), channel_id=1, source_target_pairs={{0,6},{2,0},{4,2},{6,4},{1,7},{3,1},{5,3},{7,5},{8,14},{10,8},{12,... | collective-permute-start | bytes 393224 | tf_op jit(solution)/shard_map/ppermute | solution.py:232
  157.9 2.9 %collective-permute-start.15 = (f32[256,1152]{1,0:T(8,128)S(1)}, f32[256,1152]{1,0:T(8,128)S(1)}, u32[]{:S(2)}, u32[]{:S(2)}) collective-permute-start(f32[256,1152]{1,0:T(8,128)S(1)} %get-tuple-element.39), channel_id=1, source_target_pairs={{0,1},{1,0},{2,3},{3,2},{4,5},{5,4},{6,7},{7,6},{8,9},{9,8},{10,11... | collective-permute-start | bytes 3538952 | tf_op jit(solution)/shard_map/ppermute | solution.py:224
  161.8 17.1 %all-to-all-start.4 = ((bf16[16,32,640]{2,1,0:T(8,128)(2,1)}), bf16[16,32,640]{2,1,0:T(8,128)(2,1)S(1)}, u32[]{:S(2)}, u32[]{:S(2)}) async-start(bf16[16,32,640]{2,1,0:T(8,128)(2,1)} %pair.3), calls=%async_computation.4 | async-start | bytes 1310720 | tf_op jit(solution)/shard_map/all_to_all | solution.py:220
  165.4 7.1 %collective-permute-start.12 = (bf16[272,256]{1,0:T(8,128)(2,1)S(1)}, bf16[272,256]{1,0:T(8,128)(2,1)S(1)}, u32[]{:S(2)}, u32[]{:S(2)}) collective-permute-start(bf16[272,256]{1,0:T(8,128)(2,1)S(1)} %get-tuple-element.33), channel_id=1, source_target_pairs={{0,2},{2,4},{4,6},{6,0},{1,3},{3,5},{5,7},{7,1},{8,10},{10,12},{12... | collective-permute-start | bytes 417800 | tf_op jit(solution)/shard_map/ppermute | solution.py:228
  166.2 9.9 %collective-permute-start.13 = (bf16[272,256]{1,0:T(8,128)(2,1)S(1)}, bf16[272,256]{1,0:T(8,128)(2,1)S(1)}, u32[]{:S(2)}, u32[]{:S(2)}) collective-permute-start(bf16[272,256]{1,0:T(8,128)(2,1)S(1)} %get-tuple-element.34), channel_id=1, source_target_pairs={{0,4},{2,6},{4,0},{6,2},{1,5},{3,7},{5,1},{7,3},{8,12},{10,14},{12... | collective-permute-start | bytes 417800 | tf_op jit(solution)/shard_map/ppermute | solution.py:228
  169.4 6.7 %collective-permute-start.14 = (bf16[272,256]{1,0:T(8,128)(2,1)S(1)}, bf16[272,256]{1,0:T(8,128)(2,1)S(1)}, u32[]{:S(2)}, u32[]{:S(2)}) collective-permute-start(bf16[272,256]{1,0:T(8,128)(2,1)S(1)} %get-tuple-element.35), channel_id=1, source_target_pairs={{0,6},{2,0},{4,2},{6,4},{1,7},{3,1},{5,3},{7,5},{8,14},{10,8},{12,... | collective-permute-start | bytes 417800 | tf_op jit(solution)/shard_map/ppermute | solution.py:228

commit v3 on v2

--- a/solution.py
+++ b/solution.py
@@ -37,22 +37,40 @@
     return [pl.BlockSpec(memory_space=space)] * n
 
 
-def energy_kernel(x_ref, table_ref, out_ref, flat_ref):
-    chans = x_ref.shape[0]
-    frames = x_ref.shape[1] // WIN
+def energy_kernel(x_hbm, table_ref, out_hbm, x_ref, out_ref, in_sem, out_sem):
+    blocks, chans, samples = x_ref.shape
+    frames = samples // WIN
+    group = 16
+
+    def fetch(r):
+        return pltpu.make_async_copy(x_hbm.at[pl.ds(r * chans, chans), :], x_ref.at[r], in_sem.at[r])
+
+    def put(r):
+        return pltpu.make_async_copy(out_ref.at[r], out_hbm.at[:, :, r], out_sem.at[r])
+
+    for r in range(blocks):
+        fetch(r).start()
     table = table_ref[...]
-    group = 16
-    for g in range(frames // group):
-        x = jnp.concatenate(
-            [x_ref[:, (g * group + f) * WIN : (g * group + f + 1) * WIN] for f in range(group)], axis=0
-        )
-        spec = jnp.dot(x, table, preferred_element_type=jnp.float32)
-        re, im = spec[:, :BINS], spec[:, BINS:]
-        flat_ref[g * group * chans : (g + 1) * group * chans, :] = re * re + im * im
-    for c in range(chans):
-        zl, y, core, j = c // 16, (c // 4) % 4, (c // 2) % 2, c % 2
-        at = (y * 2 + j) * BINS
-        out_ref[core, zl, 0, :, at : at + BINS] = flat_ref[pl.ds(c, frames, stride=chans), :].astype(jnp.bfloat16)
+
+    @pl.loop(0, blocks)
+    def _(r):
+        fetch(r).wait()
+        for g in range(frames // group):
+            x = jnp.concatenate(
+                [x_ref[r, :, (g * group + f) * WIN : (g * group + f + 1) * WIN] for f in range(group)], axis=0
+            )
+            spec = jnp.dot(x, table, preferred_element_type=jnp.float32)
+            re, im = spec[:, :BINS], spec[:, BINS:]
+            energy = (re * re + im * im).reshape(group, chans, BINS)
+            energy = pltpu.einshape("fcb->cfb", energy).astype(jnp.bfloat16)
+            for c in range(chans):
+                zl, y, core, j = c // 16, (c // 4) % 4, (c // 2) % 2, c % 2
+                at = (y * 2 + j) * BINS
+                out_ref[r, core, zl, g * group : (g + 1) * group, at : at + BINS] = energy[c]
+        put(r).start()
+
+    for r in range(blocks):
+        put(r).wait()
 
 
 def energies(record, table):
@@ -62,14 +80,15 @@
     rows = channels * BINS // (2 * N_P)
     return pl.pallas_call(
         energy_kernel,
-        grid=(N_R,),
-        in_specs=[
-            pl.BlockSpec((per_row, samples), lambda r: (r, 0)),
-            pl.BlockSpec((WIN, 2 * BINS), lambda r: (0, 0)),
+        in_specs=[pl.BlockSpec(memory_space=pl.ANY), pl.BlockSpec(memory_space=pltpu.VMEM)],
+        out_specs=pl.BlockSpec(memory_space=pl.ANY),
+        out_shape=jax.ShapeDtypeStruct((2, 2, N_R, frames, rows), jnp.bfloat16),
+        scratch_shapes=[
+            pltpu.VMEM((N_R, per_row, samples), jnp.bfloat16),
+            pltpu.VMEM((N_R, 2, 2, frames, rows), jnp.bfloat16),
+            pltpu.SemaphoreType.DMA((N_R,)),
+            pltpu.SemaphoreType.DMA((N_R,)),
         ],
-        out_specs=pl.BlockSpec((2, 2, 1, frames, rows), lambda r: (0, 0, r, 0, 0)),
-        out_shape=jax.ShapeDtypeStruct((2, 2, N_R, frames, rows), jnp.bfloat16),
-        scratch_shapes=[pltpu.VMEM((frames * per_row, BINS), jnp.float32)],
         compiler_params=pltpu.CompilerParams(vmem_limit_bytes=58 << 20),
         cost_estimate=pl.CostEstimate(
             flops=2 * channels * frames * WIN * WIN, bytes_accessed=12 << 20, transcendentals=0
@@ -92,7 +111,7 @@
     for i, ref in enumerate(h_refs):
         for b in range(blocks):
             ht_ref[i, b * half : (b + 1) * half, :] = ref[b].T
-    ones = jnp.ones((16, span), jnp.bfloat16)
+    ones = jnp.ones((8, span), jnp.bfloat16)
     rowsum = jnp.dot(ones, ht_ref[0], preferred_element_type=jnp.float32)
     rowsum = rowsum + jnp.dot(ones, ht_ref[1], preferred_element_type=jnp.float32)
     colsum = jnp.zeros((rank, 1), jnp.float32)
@@ -120,12 +139,8 @@
                 wn = part if wn is None else wn + part
         for t in range(2):
             ref = n_refs[2 * p + t]
-            ref[:rank, :] = wn[:, t * rank : (t + 1) * rank].astype(ref.dtype)
-            if ref.dtype == jnp.float32:
-                keep = lax.broadcasted_iota(jnp.int32, rowsum.shape, 0) == 0
-                ref[rank:, :] = jnp.where(keep, rowsum, 0.0)
-            else:
-                ref[rank:, :] = hi_lo(rowsum, 0)
+            ref[:rank, :] = wn[:, t * rank : (t + 1) * rank]
+            ref[rank:, :] = rowsum
     for ref in out_refs:
         ref[:, span:] = jnp.broadcast_to(colsum, (rank, PAD))
 
@@ -133,15 +148,13 @@
 def sweep(at, spectra, h_own, h_oth, ws):
     frames, rows = spectra.shape
     blocks, rank, half = h_own.shape
-    part = (rank + 16, rank)
+    part = (rank + 8, rank)
     sums = jax.ShapeDtypeStruct((rank, blocks * half + PAD), jnp.float32)
     return pl.pallas_call(
         sweep_kernel,
         in_specs=whole(1, pltpu.SMEM) + whole(7),
         out_specs=whole(6),
-        out_shape=[jax.ShapeDtypeStruct(part, jnp.float32)]
-        + [jax.ShapeDtypeStruct(part, jnp.bfloat16)] * 3
-        + [sums, sums],
+        out_shape=[jax.ShapeDtypeStruct(part, jnp.float32)] * 4 + [sums, sums],
         scratch_shapes=[pltpu.VMEM((2, blocks * half, rank), jnp.bfloat16)],
         compiler_params=pltpu.CompilerParams(vmem_limit_bytes=32 << 20),
         cost_estimate=pl.CostEstimate(flops=6 * frames * rows * rank, bytes_accessed=8 << 20, transcendentals=0),
@@ -198,9 +211,8 @@
 
 def w_update_kernel(p0, p1, p2, p3, w_ref, new_ref, low_ref):
     rank = w_ref.shape[1]
-    total = p0[...] + p1[...].astype(jnp.float32) + p2[...].astype(jnp.float32) + p3[...].astype(jnp.float32)
-    rowsum = total[rank : rank + 1, :] + total[rank + 1 : rank + 2, :]
-    new = w_ref[...] * total[:rank, :].T / rowsum
+    total = (p0[...] + p1[...]) + (p2[...] + p3[...])
+    new = w_ref[...] * total[:rank, :].T / total[rank : rank + 1, :]
     new_ref[...] = new
     low_ref[...] = new.astype(jnp.bfloat16)
 
@@ -232,31 +244,30 @@
     return [x] + [lax.ppermute(x, "y", [(i, (i - t) % N_Y) for i in range(N_Y)]) for t in range(1, N_Y)]
 
 
-def gathered(low, rank):
-    own = exchange(low, RANKS).reshape(2, rank, -1)
-    return own, from_sibling(own)
-
-
 def local(samples, w, h):
     rank = w.shape[1]
     record = samples.reshape(samples.shape[2], samples.shape[3])
     at = jnp.stack([lax.axis_index("core"), lax.axis_index("y")]).astype(jnp.int32)
-    h_own, h_oth = gathered(jnp.broadcast_to(h.astype(jnp.bfloat16)[None], (N_P, *h.shape)), rank)
+    h_own = exchange(jnp.broadcast_to(h.astype(jnp.bfloat16)[None], (N_P, *h.shape)), RANKS)
     energy = energies(record, dft_table())
     frames, rows = energy.shape[3:]
     energy, w_low = lax.optimization_barrier((energy, w.astype(jnp.bfloat16)))
     ws = taken_ahead(w_low)
+    h_own = h_own.reshape(2, rank, -1)
+    h_oth = from_sibling(h_own)
     spectra = exchange(energy.reshape(2 * N_P, frames, rows), TILE).reshape(2 * N_P * frames, rows)
     for step in range(ITERS):
         n0, n1, n2, n3, s_own, s_oth = sweep(at, spectra, h_own, h_oth, ws)
-        s_own = pair(s_own, from_sibling(s_oth), *h.shape)
-        h_parts = exchange(s_own, RANKS)
         w_parts = [n0] + [sent_ahead(n, t + 1) for t, n in enumerate((n1, n2, n3))]
+        h_parts = exchange(pair(s_own, from_sibling(s_oth), *h.shape), RANKS)
+        w_parts, h_parts = lax.optimization_barrier((w_parts, h_parts))
         h, low = h_update(h_parts, h)
         w, w_low = w_update(w_parts, w)
         if step + 1 < ITERS:
-            h_own, h_oth = gathered(low, rank)
             ws = taken_ahead(w_low)
+            ws, h_own = lax.optimization_barrier((ws, exchange(low, RANKS)))
+            h_own = h_own.reshape(2, rank, -1)
+            h_oth = from_sibling(h_own)
     return (w, h)
 
 

time: 181 us -> 174 us (0.961)
  blocking collectives: 33.1 us -> 0 us
  waiting for transfers between devices: 74.3 us -> 91.1 us
  starting transfers between devices: 40.6 us -> 53.3 us
  Pallas kernels: 29.3 us -> 26 us
    all_to_all x2 -> x0, blocking collectives: 33.1 us -> none  [exchange(): return lax.all_to_all(x, axes, 0, 0, tiled=True)]
    all_to_all x3 -> x5, starting transfers between devices: 19.2 us -> 33.3 us  [exchange(): return lax.all_to_all(x, axes, 0, 0, tiled=True)]
    ppermute x6, waiting for transfers between devices: 12 us -> 22.5 us  [sent_ahead(): return lax.ppermute(x, 'y', [(i, (i + t) % N_Y) for i in range(N_Y)])]
    pallas_call x1, Pallas kernels: 12.3 us -> 7.42 us  [energies(): pl.pallas_call(energy_kernel, in_specs=[pl.BlockSpec(memory_space=pl.ANY)...]
    all_to_all x3 -> x5, waiting for transfers between devices: 45 us -> 48.1 us  [exchange(): return lax.all_to_all(x, axes, 0, 0, tiled=True)]
    ppermute x4, waiting for transfers between devices: 5.43 us -> 7.26 us  [from_sibling(): return lax.ppermute(x, 'core', [(0, 1), (1, 0)])]
  transfers between devices with their start and end apart: 19 -> 21, of which waited for: 13 -> 17; matrix products, arithmetic and copies ran while one was open for 0% -> 0% of each run, Pallas kernels for 7% -> 4%
where the time goes in v3:
time: 174 us; the launch traced here: 173 us
  waiting for transfers between devices  91.1 us (52%)
  starting transfers between devices  53.3 us (31%)
  Pallas kernels  26 us (15%)
    all_to_all x5, waiting for transfers between devices, exchange(): return lax.all_to_all(x, axes, 0, 0, tiled=True)  48.1 us
    all_to_all x5, starting transfers between devices, exchange(): return lax.all_to_all(x, axes, 0, 0, tiled=True)  33.3 us
    ppermute x6, waiting for transfers between devices, sent_ahead(): return lax.ppermute(x, 'y', [(i, (i + t) % N_Y) for i in range(N_Y)])  22.5 us
    pallas_call x2, Pallas kernels, sweep(): pl.pallas_call(sweep_kernel, in_specs=whole(1, pltpu.SMEM) + whole(7), ou...  13.6 us
    ppermute x6, waiting for transfers between devices, taken_ahead(): lax.ppermute(x, 'y', [(i, (i - t) % N_Y) for i in range(N_Y)])  13.2 us
    ppermute x6, starting transfers between devices, sent_ahead(): return lax.ppermute(x, 'y', [(i, (i + t) % N_Y) for i in range(N_Y)])  9.95 us
    ppermute x6, starting transfers between devices, taken_ahead(): lax.ppermute(x, 'y', [(i, (i - t) % N_Y) for i in range(N_Y)])  9.28 us
    pallas_call x1, Pallas kernels, energies(): pl.pallas_call(energy_kernel, in_specs=[pl.BlockSpec(memory_space=pl.ANY)...  7.42 us
  transfers between devices with their start and end apart: 21, of which 17 were waited for; matrix products, arithmetic and copies ran while one was open for 0% of the time, Pallas kernels for 4%

profile of v3, /device:TPU:0, one launch (start us, length us, event | category | flops | bytes accessed | tf_op | source)
XLA Modules:
  0.0 173.1 jit_solution(8097745891622398215)
XLA Ops:
  0.6 0.0 copy-start
  0.6 0.9 convert_element_type.11
  1.5 0.8 broadcast_in_dim.2
  2.4 8.0 %all-to-all-start.1 = ((bf16[16,32,512]{2,1,0:T(8,128)(2,1)}), bf16[16,32,512]{2,1,0:T(8,128)(2,1)S(1)}, u32[]{:S(2)}, u32[]{:S(2)}) async-start(bf16[16,32,512]{2,1,0:T(8,128)(2,1)} %broadcast_in_dim.2), calls=%async_computation.1 | async-start | bytes 1048576 | tf_op jit(solution)/shard_map/all_to_all | solution.py:232
  10.3 0.0 copy-done
  10.4 7.4 %energy.1 = bf16[2,2,8,64,1024]{4,3,2,1,0:T(8,128)(2,1)} custom-call(bf16[256,16384]{1,0:T(8,128)(2,1)} %bitcast.12, bf16[256,256]{1,0:T(8,128)(2,1)} %constant.12.table_ref), custom_call_target="tpu_custom_call" | custom-call | flops 2147483648 | bytes 12582912 | tf_op jit(solution)/shard_map/energy/pallas_call | solution.py:81
  17.8 4.1 %all-to-all-done.1 = bf16[16,32,512]{2,1,0:T(8,128)(2,1)S(1)} async-done(((bf16[16,32,512]{2,1,0:T(8,128)(2,1)}), bf16[16,32,512]{2,1,0:T(8,128)(2,1)S(1)}, u32[]{:S(2)}, u32[]{:S(2)}) %all-to-all-start.1) | async-done | bytes 524320 | tf_op jit(solution)/shard_map/all_to_all | solution.py:232
  21.9 4.9 %all-to-all-start = ((bf16[32,64,1024]{2,1,0:T(8,128)(2,1)}), bf16[32,64,1024]{2,1,0:T(8,128)(2,1)}, u32[]{:S(2)}, u32[]{:S(2)}) async-start(bf16[32,64,1024]{2,1,0:T(8,128)(2,1)} %bitcast.11), calls=%async_computation | async-start | bytes 8388608 | tf_op jit(solution)/shard_map/all_to_all | solution.py:232
  26.7 0.3 collective-permute-start
  27.0 3.0 %collective-permute-start.1 = (bf16[256,256]{1,0:T(8,128)(2,1)S(1)}, bf16[256,256]{1,0:T(8,128)(2,1)S(1)}, u32[]{:S(2)}, u32[]{:S(2)}) collective-permute-start(bf16[256,256]{1,0:T(8,128)(2,1)S(1)} %convert_element_type.10.w0), channel_id=1, source_target_pairs={{0,6},{2,0},{4,2},{6,4},{1,7},{3,1},{5,3},{7,5},{8,14},{10,8},{12,... | collective-permute-start | bytes 393224 | tf_op jit(solution)/shard_map/ppermute | solution.py:244
  30.0 0.6 collective-permute-start.2
  30.7 1.0 collective-permute-start.3
  31.6 0.1 pad_add_fusion.at_ref
  31.7 4.4 %collective-permute-done.1.w1 = bf16[256,256]{1,0:T(8,128)(2,1)S(1)} collective-permute-done((bf16[256,256]{1,0:T(8,128)(2,1)S(1)}, bf16[256,256]{1,0:T(8,128)(2,1)S(1)}, u32[]{:S(2)}, u32[]{:S(2)}) %collective-permute-start.1) | collective-permute-done | bytes 131104 | tf_op jit(solution)/shard_map/ppermute | solution.py:244
  36.1 1.9 %collective-permute-done.2.w2 = bf16[256,256]{1,0:T(8,128)(2,1)S(1)} collective-permute-done((bf16[256,256]{1,0:T(8,128)(2,1)S(1)}, bf16[256,256]{1,0:T(8,128)(2,1)S(1)}, u32[]{:S(2)}, u32[]{:S(2)}) %collective-permute-start.2) | collective-permute-done | bytes 131104 | tf_op jit(solution)/shard_map/ppermute | solution.py:244
  37.9 1.9 %collective-permute-done.3.w3 = bf16[256,256]{1,0:T(8,128)(2,1)S(1)} collective-permute-done((bf16[256,256]{1,0:T(8,128)(2,1)S(1)}, bf16[256,256]{1,0:T(8,128)(2,1)S(1)}, u32[]{:S(2)}, u32[]{:S(2)}) %collective-permute-start.3) | collective-permute-done | bytes 131104 | tf_op jit(solution)/shard_map/ppermute | solution.py:244
  39.8 0.0 collective-permute-done.oth_ref
  39.8 43.6 %all-to-all-done = bf16[32,64,1024]{2,1,0:T(8,128)(2,1)} async-done(((bf16[32,64,1024]{2,1,0:T(8,128)(2,1)}), bf16[32,64,1024]{2,1,0:T(8,128)(2,1)}, u32[]{:S(2)}, u32[]{:S(2)}) %all-to-all-start) | async-done | bytes 4194336 | tf_op jit(solution)/shard_map/all_to_all | solution.py:232
  83.4 6.8 %sweep.2 = (f32[264,256]{1,0:T(8,128)S(1)}, f32[264,256]{1,0:T(8,128)S(1)}, f32[264,256]{1,0:T(8,128)S(1)}, f32[264,256]{1,0:T(8,128)S(1)}, f32[256,1152]{1,0:T(8,128)S(1)}, /*index=5*/f32[256,1152]{1,0:T(8,128)S(1)}) custom-call(s32[2]{0:T(128)S(1)} %pad_add_fusion.at_ref, bf16[2048,1024]{1,0:T(8,128)(2,1)} %bitcast.4.s_ref, ...), custom_call_target="tpu_custom_call" | custom-call | flops 3221225472 | bytes 8388608 | tf_op jit(solution)/shard_map/sweep/pallas_call | solution.py:153
  90.2 0.3 collective-permute-start.7
  90.5 2.6 %collective-permute-done.7.b_ref = f32[256,1152]{1,0:T(8,128)S(1)} collective-permute-done((f32[256,1152]{1,0:T(8,128)S(1)}, f32[256,1152]{1,0:T(8,128)S(1)}, u32[]{:S(2)}, u32[]{:S(2)}) %collective-permute-start.7) | collective-permute-done | bytes 1179680 | tf_op jit(solution)/shard_map/ppermute | solution.py:236
  93.1 1.0 pair.2
  94.1 0.0 copy-start.1
  94.1 6.9 %all-to-all-start.2 = ((bf16[16,32,640]{2,1,0:T(8,128)(2,1)}), bf16[16,32,640]{2,1,0:T(8,128)(2,1)S(1)}, u32[]{:S(2)}, u32[]{:S(2)}) async-start(bf16[16,32,640]{2,1,0:T(8,128)(2,1)} %pair.2), calls=%async_computation.2 | async-start | bytes 1310720 | tf_op jit(solution)/shard_map/all_to_all | solution.py:232
  101.0 1.7 collective-permute-start.4
  102.6 2.9 %collective-permute-start.5 = (f32[264,256]{1,0:T(8,128)S(1)}, f32[264,256]{1,0:T(8,128)S(1)}, u32[]{:S(2)}, u32[]{:S(2)}) collective-permute-start(f32[264,256]{1,0:T(8,128)S(1)} %get-tuple-element.41), channel_id=1, source_target_pairs={{0,4},{2,6},{4,0},{6,2},{1,5},{3,7},{5,1},{7,3},{8,12},{10,14},{12... | collective-permute-start | bytes 811016 | tf_op jit(solution)/shard_map/ppermute | solution.py:240
  105.5 1.3 collective-permute-start.6
  106.9 3.7 %collective-permute-done.4.p1 = f32[264,256]{1,0:T(8,128)S(1)} collective-permute-done((f32[264,256]{1,0:T(8,128)S(1)}, f32[264,256]{1,0:T(8,128)S(1)}, u32[]{:S(2)}, u32[]{:S(2)}) %collective-permute-start.4) | collective-permute-done | bytes 270368 | tf_op jit(solution)/shard_map/ppermute | solution.py:240
  110.6 7.0 %collective-permute-done.5.p2 = f32[264,256]{1,0:T(8,128)S(1)} collective-permute-done((f32[264,256]{1,0:T(8,128)S(1)}, f32[264,256]{1,0:T(8,128)S(1)}, u32[]{:S(2)}, u32[]{:S(2)}) %collective-permute-start.5) | collective-permute-done | bytes 270368 | tf_op jit(solution)/shard_map/ppermute | solution.py:240
  117.5 0.0 collective-permute-done.6.p3
  117.5 0.0 all-to-all-done.2.parts_ref
  117.5 0.0 copy-done.1
  117.5 1.0 h_update.2
  118.6 6.9 %all-to-all-start.3 = ((bf16[16,32,512]{2,1,0:T(8,128)(2,1)}), bf16[16,32,512]{2,1,0:T(8,128)(2,1)S(1)}, u32[]{:S(2)}, u32[]{:S(2)}) async-start(bf16[16,32,512]{2,1,0:T(8,128)(2,1)} %get-tuple-element.51), calls=%async_computation.3 | async-start | bytes 1048576 | tf_op jit(solution)/shard_map/all_to_all | solution.py:232
  125.4 0.2 w_update.2
  125.6 1.3 collective-permute-start.10
  126.9 2.0 %collective-permute-start.8 = (bf16[256,256]{1,0:T(8,128)(2,1)S(1)}, bf16[256,256]{1,0:T(8,128)(2,1)S(1)}, u32[]{:S(2)}, u32[]{:S(2)}) collective-permute-start(bf16[256,256]{1,0:T(8,128)(2,1)S(1)} %get-tuple-element.53.w0), channel_id=1, source_target_pairs={{0,6},{2,0},{4,2},{6,4},{1,7},{3,1},{5,3},{7,5},{8,14},{10,8},{12,... | collective-permute-start | bytes 393224 | tf_op jit(solution)/shard_map/ppermute | solution.py:244
  128.9 1.4 collective-permute-start.9
  130.3 2.0 %collective-permute-done.10.w3 = bf16[256,256]{1,0:T(8,128)(2,1)S(1)} collective-permute-done((bf16[256,256]{1,0:T(8,128)(2,1)S(1)}, bf16[256,256]{1,0:T(8,128)(2,1)S(1)}, u32[]{:S(2)}, u32[]{:S(2)}) %collective-permute-start.10) | collective-permute-done | bytes 131104 | tf_op jit(solution)/shard_map/ppermute | solution.py:244
  132.3 1.0 collective-permute-done.8.w1
  133.2 2.1 %collective-permute-done.9.w2 = bf16[256,256]{1,0:T(8,128)(2,1)S(1)} collective-permute-done((bf16[256,256]{1,0:T(8,128)(2,1)S(1)}, bf16[256,256]{1,0:T(8,128)(2,1)S(1)}, u32[]{:S(2)}, u32[]{:S(2)}) %collective-permute-start.9) | collective-permute-done | bytes 131104 | tf_op jit(solution)/shard_map/ppermute | solution.py:244
  135.4 0.5 all-to-all-done.3
  135.8 0.0 collective-permute-start.11
  135.8 1.9 %collective-permute-done.11.oth_ref = bf16[2,256,512]{2,1,0:T(8,128)(2,1)S(1)} collective-permute-done((bf16[2,256,512]{2,1,0:T(8,128)(2,1)S(1)}, bf16[2,256,512]{2,1,0:T(8,128)(2,1)S(1)}, u32[]{:S(2)}, u32[]{:S(2)}) %collective-permute-start.11) | collective-permute-done | bytes 524320 | tf_op jit(solution)/shard_map/ppermute | solution.py:236
  137.8 6.8 %sweep.3 = (f32[264,256]{1,0:T(8,128)S(1)}, f32[264,256]{1,0:T(8,128)S(1)}, f32[264,256]{1,0:T(8,128)S(1)}, f32[264,256]{1,0:T(8,128)S(1)}, f32[256,1152]{1,0:T(8,128)S(1)}, /*index=5*/f32[256,1152]{1,0:T(8,128)S(1)}) custom-call(s32[2]{0:T(128)S(1)} %pad_add_fusion.at_ref, bf16[2048,1024]{1,0:T(8,128)(2,1)} %bitcast.4.s_ref, ...), custom_call_target="tpu_custom_call" | custom-call | flops 3221225472 | bytes 8388608 | tf_op jit(solution)/shard_map/sweep/pallas_call | solution.py:153
  144.5 0.2 collective-permute-start.15
  144.8 2.7 %collective-permute-done.15.b_ref = f32[256,1152]{1,0:T(8,128)S(1)} collective-permute-done((f32[256,1152]{1,0:T(8,128)S(1)}, f32[256,1152]{1,0:T(8,128)S(1)}, u32[]{:S(2)}, u32[]{:S(2)}) %collective-permute-start.15) | collective-permute-done | bytes 1179680 | tf_op jit(solution)/shard_map/ppermute | solution.py:236
  147.5 1.0 pair.3
  148.5 6.8 %all-to-all-start.4 = ((bf16[16,32,640]{2,1,0:T(8,128)(2,1)}), bf16[16,32,640]{2,1,0:T(8,128)(2,1)S(1)}, u32[]{:S(2)}, u32[]{:S(2)}) async-start(bf16[16,32,640]{2,1,0:T(8,128)(2,1)} %pair.3), calls=%async_computation.4 | async-start | bytes 1310720 | tf_op jit(solution)/shard_map/all_to_all | solution.py:232
  155.2 0.8 collective-permute-start.12
  156.0 2.7 %collective-permute-start.13 = (f32[264,256]{1,0:T(8,128)S(1)}, f32[264,256]{1,0:T(8,128)S(1)}, u32[]{:S(2)}, u32[]{:S(2)}) collective-permute-start(f32[264,256]{1,0:T(8,128)S(1)} %get-tuple-element.59), channel_id=1, source_target_pairs={{0,4},{2,6},{4,0},{6,2},{1,5},{3,7},{5,1},{7,3},{8,12},{10,14},{12... | collective-permute-start | bytes 811016 | tf_op jit(solution)/shard_map/ppermute | solution.py:240
  158.7 0.6 collective-permute-start.14
  159.3 6.4 %collective-permute-done.12.p1 = f32[264,256]{1,0:T(8,128)S(1)} collective-permute-done((f32[264,256]{1,0:T(8,128)S(1)}, f32[264,256]{1,0:T(8,128)S(1)}, u32[]{:S(2)}, u32[]{:S(2)}) %collective-permute-start.12) | collective-permute-done | bytes 270368 | tf_op jit(solution)/shard_map/ppermute | solution.py:240
  165.7 5.0 %collective-permute-done.13.p2 = f32[264,256]{1,0:T(8,128)S(1)} collective-permute-done((f32[264,256]{1,0:T(8,128)S(1)}, f32[264,256]{1,0:T(8,128)S(1)}, u32[]{:S(2)}, u32[]{:S(2)}) %collective-permute-start.13) | collective-permute-done | bytes 270368 | tf_op jit(solution)/shard_map/ppermute | solution.py:240
  170.7 0.4 collective-permute-done.14.p3
  171.2 0.0 all-to-all-done.4.parts_ref
  171.2 1.0 h_update.3
  172.2 0.9 w_update.3
  (1 shorter events, 0.0 us)
Async XLA Ops:
  0.6 9.7 %copy-start = (f32[256,256]{1,0:T(8,128)S(1)}, f32[256,256]{1,0:T(8,128)}, u32[]{:S(2)}) copy-start(f32[256,256]{1,0:T(8,128)} %w_ref.1) | copy-start | bytes 786436
  2.4 19.5 %all-to-all-start.1 = ((bf16[16,32,512]{2,1,0:T(8,128)(2,1)}), bf16[16,32,512]{2,1,0:T(8,128)(2,1)S(1)}, u32[]{:S(2)}, u32[]{:S(2)}) async-start(bf16[16,32,512]{2,1,0:T(8,128)(2,1)} %broadcast_in_dim.2), calls=%async_computation.1 | async-start | bytes 1048576 | tf_op jit(solution)/shard_map/all_to_all | solution.py:232
  21.9 61.5 %all-to-all-start = ((bf16[32,64,1024]{2,1,0:T(8,128)(2,1)}), bf16[32,64,1024]{2,1,0:T(8,128)(2,1)}, u32[]{:S(2)}, u32[]{:S(2)}) async-start(bf16[32,64,1024]{2,1,0:T(8,128)(2,1)} %bitcast.11), calls=%async_computation | async-start | bytes 8388608 | tf_op jit(solution)/shard_map/all_to_all | solution.py:232
  26.7 13.0 %collective-permute-start = (bf16[2,256,512]{2,1,0:T(8,128)(2,1)S(1)}, bf16[2,256,512]{2,1,0:T(8,128)(2,1)S(1)}, u32[]{:S(2)}, u32[]{:S(2)}) collective-permute-start(bf16[2,256,512]{2,1,0:T(8,128)(2,1)S(1)} %bitcast.7), channel_id=1, source_target_pairs={{0,1},{1,0},{2,3},{3,2},{4,5},{5,4},{6,7},{7,6},{8,9},{9,8},{10,11... | collective-permute-start | bytes 1572872 | tf_op jit(solution)/shard_map/ppermute | solution.py:236
  27.0 9.1 %collective-permute-start.1 = (bf16[256,256]{1,0:T(8,128)(2,1)S(1)}, bf16[256,256]{1,0:T(8,128)(2,1)S(1)}, u32[]{:S(2)}, u32[]{:S(2)}) collective-permute-start(bf16[256,256]{1,0:T(8,128)(2,1)S(1)} %convert_element_type.10.w0), channel_id=1, source_target_pairs={{0,6},{2,0},{4,2},{6,4},{1,7},{3,1},{5,3},{7,5},{8,14},{10,8},{12,... | collective-permute-start | bytes 393224 | tf_op jit(solution)/shard_map/ppermute | solution.py:244
  30.0 7.9 %collective-permute-start.2 = (bf16[256,256]{1,0:T(8,128)(2,1)S(1)}, bf16[256,256]{1,0:T(8,128)(2,1)S(1)}, u32[]{:S(2)}, u32[]{:S(2)}) collective-permute-start(bf16[256,256]{1,0:T(8,128)(2,1)S(1)} %convert_element_type.10.w0), channel_id=1, source_target_pairs={{0,4},{2,6},{4,0},{6,2},{1,5},{3,7},{5,1},{7,3},{8,12},{10,14},{12... | collective-permute-start | bytes 393224 | tf_op jit(solution)/shard_map/ppermute | solution.py:244
  30.7 9.1 %collective-permute-start.3 = (bf16[256,256]{1,0:T(8,128)(2,1)S(1)}, bf16[256,256]{1,0:T(8,128)(2,1)S(1)}, u32[]{:S(2)}, u32[]{:S(2)}) collective-permute-start(bf16[256,256]{1,0:T(8,128)(2,1)S(1)} %convert_element_type.10.w0), channel_id=1, source_target_pairs={{0,2},{2,4},{4,6},{6,0},{1,3},{3,5},{5,7},{7,1},{8,10},{10,12},{12... | collective-permute-start | bytes 393224 | tf_op jit(solution)/shard_map/ppermute | solution.py:244
  90.2 2.9 %collective-permute-start.7 = (f32[256,1152]{1,0:T(8,128)S(1)}, f32[256,1152]{1,0:T(8,128)S(1)}, u32[]{:S(2)}, u32[]{:S(2)}) collective-permute-start(f32[256,1152]{1,0:T(8,128)S(1)} %get-tuple-element.44), channel_id=1, source_target_pairs={{0,1},{1,0},{2,3},{3,2},{4,5},{5,4},{6,7},{7,6},{8,9},{9,8},{10,11... | collective-permute-start | bytes 3538952 | tf_op jit(solution)/shard_map/ppermute | solution.py:236
  94.1 23.4 %copy-start.1 = (f32[32,512]{1,0:T(8,128)S(1)}, f32[32,512]{1,0:T(8,128)}, u32[]{:S(2)}) copy-start(f32[32,512]{1,0:T(8,128)} %h_ref.1) | copy-start | bytes 196612
  94.1 23.4 %all-to-all-start.2 = ((bf16[16,32,640]{2,1,0:T(8,128)(2,1)}), bf16[16,32,640]{2,1,0:T(8,128)(2,1)S(1)}, u32[]{:S(2)}, u32[]{:S(2)}) async-start(bf16[16,32,640]{2,1,0:T(8,128)(2,1)} %pair.2), calls=%async_computation.2 | async-start | bytes 1310720 | tf_op jit(solution)/shard_map/all_to_all | solution.py:232
  101.0 9.6 %collective-permute-start.4 = (f32[264,256]{1,0:T(8,128)S(1)}, f32[264,256]{1,0:T(8,128)S(1)}, u32[]{:S(2)}, u32[]{:S(2)}) collective-permute-start(f32[264,256]{1,0:T(8,128)S(1)} %get-tuple-element.40), channel_id=1, source_target_pairs={{0,2},{2,4},{4,6},{6,0},{1,3},{3,5},{5,7},{7,1},{8,10},{10,12},{12... | collective-permute-start | bytes 811016 | tf_op jit(solution)/shard_map/ppermute | solution.py:240
  102.6 14.9 %collective-permute-start.5 = (f32[264,256]{1,0:T(8,128)S(1)}, f32[264,256]{1,0:T(8,128)S(1)}, u32[]{:S(2)}, u32[]{:S(2)}) collective-permute-start(f32[264,256]{1,0:T(8,128)S(1)} %get-tuple-element.41), channel_id=1, source_target_pairs={{0,4},{2,6},{4,0},{6,2},{1,5},{3,7},{5,1},{7,3},{8,12},{10,14},{12... | collective-permute-start | bytes 811016 | tf_op jit(solution)/shard_map/ppermute | solution.py:240
  105.5 12.0 %collective-permute-start.6 = (f32[264,256]{1,0:T(8,128)S(1)}, f32[264,256]{1,0:T(8,128)S(1)}, u32[]{:S(2)}, u32[]{:S(2)}) collective-permute-start(f32[264,256]{1,0:T(8,128)S(1)} %get-tuple-element.42), channel_id=1, source_target_pairs={{0,6},{2,0},{4,2},{6,4},{1,7},{3,1},{5,3},{7,5},{8,14},{10,8},{12,... | collective-permute-start | bytes 811016 | tf_op jit(solution)/shard_map/ppermute | solution.py:240
  118.6 17.3 %all-to-all-start.3 = ((bf16[16,32,512]{2,1,0:T(8,128)(2,1)}), bf16[16,32,512]{2,1,0:T(8,128)(2,1)S(1)}, u32[]{:S(2)}, u32[]{:S(2)}) async-start(bf16[16,32,512]{2,1,0:T(8,128)(2,1)} %get-tuple-element.51), calls=%async_computation.3 | async-start | bytes 1048576 | tf_op jit(solution)/shard_map/all_to_all | solution.py:232
  125.6 6.7 %collective-permute-start.10 = (bf16[256,256]{1,0:T(8,128)(2,1)S(1)}, bf16[256,256]{1,0:T(8,128)(2,1)S(1)}, u32[]{:S(2)}, u32[]{:S(2)}) collective-permute-start(bf16[256,256]{1,0:T(8,128)(2,1)S(1)} %get-tuple-element.53.w0), channel_id=1, source_target_pairs={{0,2},{2,4},{4,6},{6,0},{1,3},{3,5},{5,7},{7,1},{8,10},{10,12},{12... | collective-permute-start | bytes 393224 | tf_op jit(solution)/shard_map/ppermute | solution.py:244
  126.9 6.4 %collective-permute-start.8 = (bf16[256,256]{1,0:T(8,128)(2,1)S(1)}, bf16[256,256]{1,0:T(8,128)(2,1)S(1)}, u32[]{:S(2)}, u32[]{:S(2)}) collective-permute-start(bf16[256,256]{1,0:T(8,128)(2,1)S(1)} %get-tuple-element.53.w0), channel_id=1, source_target_pairs={{0,6},{2,0},{4,2},{6,4},{1,7},{3,1},{5,3},{7,5},{8,14},{10,8},{12,... | collective-permute-start | bytes 393224 | tf_op jit(solution)/shard_map/ppermute | solution.py:244
  128.9 6.5 %collective-permute-start.9 = (bf16[256,256]{1,0:T(8,128)(2,1)S(1)}, bf16[256,256]{1,0:T(8,128)(2,1)S(1)}, u32[]{:S(2)}, u32[]{:S(2)}) collective-permute-start(bf16[256,256]{1,0:T(8,128)(2,1)S(1)} %get-tuple-element.53.w0), channel_id=1, source_target_pairs={{0,4},{2,6},{4,0},{6,2},{1,5},{3,7},{5,1},{7,3},{8,12},{10,14},{12... | collective-permute-start | bytes 393224 | tf_op jit(solution)/shard_map/ppermute | solution.py:244
  135.8 1.9 %collective-permute-start.11 = (bf16[2,256,512]{2,1,0:T(8,128)(2,1)S(1)}, bf16[2,256,512]{2,1,0:T(8,128)(2,1)S(1)}, u32[]{:S(2)}, u32[]{:S(2)}) collective-permute-start(bf16[2,256,512]{2,1,0:T(8,128)(2,1)S(1)} %bitcast.9), channel_id=1, source_target_pairs={{0,1},{1,0},{2,3},{3,2},{4,5},{5,4},{6,7},{7,6},{8,9},{9,8},{10,11... | collective-permute-start | bytes 1572872 | tf_op jit(solution)/shard_map/ppermute | solution.py:236
  144.5 2.9 %collective-permute-start.15 = (f32[256,1152]{1,0:T(8,128)S(1)}, f32[256,1152]{1,0:T(8,128)S(1)}, u32[]{:S(2)}, u32[]{:S(2)}) collective-permute-start(f32[256,1152]{1,0:T(8,128)S(1)} %get-tuple-element.62), channel_id=1, source_target_pairs={{0,1},{1,0},{2,3},{3,2},{4,5},{5,4},{6,7},{7,6},{8,9},{9,8},{10,11... | collective-permute-start | bytes 3538952 | tf_op jit(solution)/shard_map/ppermute | solution.py:236
  148.5 22.7 %all-to-all-start.4 = ((bf16[16,32,640]{2,1,0:T(8,128)(2,1)}), bf16[16,32,640]{2,1,0:T(8,128)(2,1)S(1)}, u32[]{:S(2)}, u32[]{:S(2)}) async-start(bf16[16,32,640]{2,1,0:T(8,128)(2,1)} %pair.3), calls=%async_computation.4 | async-start | bytes 1310720 | tf_op jit(solution)/shard_map/all_to_all | solution.py:232
  155.2 10.5 %collective-permute-start.12 = (f32[264,256]{1,0:T(8,128)S(1)}, f32[264,256]{1,0:T(8,128)S(1)}, u32[]{:S(2)}, u32[]{:S(2)}) collective-permute-start(f32[264,256]{1,0:T(8,128)S(1)} %get-tuple-element.58), channel_id=1, source_target_pairs={{0,2},{2,4},{4,6},{6,0},{1,3},{3,5},{5,7},{7,1},{8,10},{10,12},{12... | collective-permute-start | bytes 811016 | tf_op jit(solution)/shard_map/ppermute | solution.py:240
  156.0 14.7 %collective-permute-start.13 = (f32[264,256]{1,0:T(8,128)S(1)}, f32[264,256]{1,0:T(8,128)S(1)}, u32[]{:S(2)}, u32[]{:S(2)}) collective-permute-start(f32[264,256]{1,0:T(8,128)S(1)} %get-tuple-element.59), channel_id=1, source_target_pairs={{0,4},{2,6},{4,0},{6,2},{1,5},{3,7},{5,1},{7,3},{8,12},{10,14},{12... | collective-permute-start | bytes 811016 | tf_op jit(solution)/shard_map/ppermute | solution.py:240
  158.7 12.4 %collective-permute-start.14 = (f32[264,256]{1,0:T(8,128)S(1)}, f32[264,256]{1,0:T(8,128)S(1)}, u32[]{:S(2)}, u32[]{:S(2)}) collective-permute-start(f32[264,256]{1,0:T(8,128)S(1)} %get-tuple-element.60), channel_id=1, source_target_pairs={{0,6},{2,0},{4,2},{6,4},{1,7},{3,1},{5,3},{7,5},{8,14},{10,8},{12,... | collective-permute-start | bytes 811016 | tf_op jit(solution)/shard_map/ppermute | solution.py:240

commit v4 on v3

--- a/solution.py
+++ b/solution.py
@@ -1,3 +1,4 @@
+import functools
 import math
 
 import jax
@@ -103,63 +104,59 @@
     return jnp.where(lax.broadcasted_iota(jnp.int32, x.shape, axis) == 0, hi, lo)
 
 
-def sweep_kernel(at_ref, s_ref, own_ref, oth_ref, w0, w1, w2, w3, n0, n1, n2, n3, hown_ref, hoth_ref, ht_ref):
-    core, y = at_ref[0], at_ref[1]
-    blocks, rank, half = own_ref.shape
+def sweep_kernel(first, at_ref, s_ref, h_ref, w0, w1, w2, w3, *refs):
+    before, (n0, n1, n2, n3, sums_ref, ht_ref) = (() if first else refs[:4]), refs[-6:]
+    blocks, rank, half = h_ref.shape
     span = blocks * half
-    h_refs, n_refs, out_refs = (own_ref, oth_ref), (n0, n1, n2, n3), (hown_ref, hoth_ref)
-    for i, ref in enumerate(h_refs):
-        for b in range(blocks):
-            ht_ref[i, b * half : (b + 1) * half, :] = ref[b].T
-    ones = jnp.ones((8, span), jnp.bfloat16)
-    rowsum = jnp.dot(ones, ht_ref[0], preferred_element_type=jnp.float32)
-    rowsum = rowsum + jnp.dot(ones, ht_ref[1], preferred_element_type=jnp.float32)
+    for b in range(blocks):
+        ht_ref[b * half : (b + 1) * half, :] = h_ref[b].T
+    rowsum = jnp.dot(jnp.ones((8, span), jnp.bfloat16), ht_ref[...], preferred_element_type=jnp.float32)
     colsum = jnp.zeros((rank, 1), jnp.float32)
+    rows = pl.ds(pl.multiple_of(at_ref[0 if first else 1] * span, span), span)
     for p in range(2):
         wt = jnp.concatenate([w[...] for w in ((w0, w1), (w2, w3))[p]], axis=0).T
         colsum = colsum + jnp.sum(wt.astype(jnp.float32), axis=1, keepdims=True)
+        columns = [
+            pl.ds(pl.multiple_of(lax.rem(at_ref[2] + 2 * p + t, N_Y) * rank, rank), rank) for t in range(2)
+        ]
+        s = jnp.concatenate([s_ref[rows, c] for c in columns], axis=1)
+        recon = jnp.dot(ht_ref[...], wt, preferred_element_type=jnp.float32)
+        quotient = (s.astype(jnp.float32) / recon).astype(jnp.bfloat16)
+        hn = lax.dot_general(wt, quotient, (((1,), (1,)), ((), ())), preferred_element_type=jnp.float32)
+        if p == 0:
+            sums_ref[:, :span] = hn
+        else:
+            sums_ref[:, :span] += hn
         wn = None
-        for i in range(2):
-            rows = pl.ds(pl.multiple_of((core if i == 0 else 1 - core) * span, span), span)
-            columns = [
-                pl.ds(pl.multiple_of(lax.rem(y + 2 * p + t, N_Y) * rank, rank), rank) for t in range(2)
-            ]
-            s = jnp.concatenate([s_ref[rows, c] for c in columns], axis=1)
-            recon = jnp.dot(ht_ref[i], wt, preferred_element_type=jnp.float32)
-            quotient = (s.astype(jnp.float32) / recon).astype(jnp.bfloat16)
-            hn = lax.dot_general(wt, quotient, (((1,), (1,)), ((), ())), preferred_element_type=jnp.float32)
-            if p == 0:
-                out_refs[i][:, :span] = hn
+        for b in range(blocks):
+            part = jnp.dot(h_ref[b], quotient[b * half : (b + 1) * half], preferred_element_type=jnp.float32)
+            wn = part if wn is None else wn + part
+        for t in range(2):
+            ref = (n0, n1, n2, n3)[2 * p + t]
+            part = wn[:, t * rank : (t + 1) * rank]
+            if first:
+                ref[:rank, :] = part
+                ref[rank:, :] = rowsum
             else:
-                out_refs[i][:, :span] += hn
-            for b in range(blocks):
-                part = jnp.dot(
-                    h_refs[i][b], quotient[b * half : (b + 1) * half], preferred_element_type=jnp.float32
-                )
-                wn = part if wn is None else wn + part
-        for t in range(2):
-            ref = n_refs[2 * p + t]
-            ref[:rank, :] = wn[:, t * rank : (t + 1) * rank]
-            ref[rank:, :] = rowsum
-    for ref in out_refs:
-        ref[:, span:] = jnp.broadcast_to(colsum, (rank, PAD))
-
-
-def sweep(at, spectra, h_own, h_oth, ws):
+                ref[:rank, :] = part + before[2 * p + t][:rank, :]
+                ref[rank:, :] = rowsum + before[2 * p + t][rank:, :]
+    sums_ref[:, span:] = jnp.broadcast_to(colsum, (rank, PAD))
+
+
+def half_sweep(at, spectra, h, ws, before=()):
     frames, rows = spectra.shape
-    blocks, rank, half = h_own.shape
-    part = (rank + 8, rank)
-    sums = jax.ShapeDtypeStruct((rank, blocks * half + PAD), jnp.float32)
-    return pl.pallas_call(
-        sweep_kernel,
-        in_specs=whole(1, pltpu.SMEM) + whole(7),
-        out_specs=whole(6),
-        out_shape=[jax.ShapeDtypeStruct(part, jnp.float32)] * 4 + [sums, sums],
-        scratch_shapes=[pltpu.VMEM((2, blocks * half, rank), jnp.bfloat16)],
-        compiler_params=pltpu.CompilerParams(vmem_limit_bytes=32 << 20),
-        cost_estimate=pl.CostEstimate(flops=6 * frames * rows * rank, bytes_accessed=8 << 20, transcendentals=0),
-        name="sweep",
-    )(at, spectra, h_own, h_oth, *ws)
+    blocks, rank, half = h.shape
+    return pl.pallas_call(
+        functools.partial(sweep_kernel, not before),
+        in_specs=whole(1, pltpu.SMEM) + whole(6 + len(before)),
+        out_specs=whole(5),
+        out_shape=[jax.ShapeDtypeStruct((rank + 8, rank), jnp.float32)] * 4
+        + [jax.ShapeDtypeStruct((rank, blocks * half + PAD), jnp.float32)],
+        scratch_shapes=[pltpu.VMEM((blocks * half, rank), jnp.bfloat16)],
+        compiler_params=pltpu.CompilerParams(vmem_limit_bytes=28 << 20),
+        cost_estimate=pl.CostEstimate(flops=3 * frames * rows * rank, bytes_accessed=4 << 20, transcendentals=0),
+        name="sweep_a" if not before else "sweep_b",
+    )(at, spectra, h, *ws, *before)
 
 
 def pair_kernel(a_ref, b_ref, out_ref):
@@ -247,19 +244,25 @@
 def local(samples, w, h):
     rank = w.shape[1]
     record = samples.reshape(samples.shape[2], samples.shape[3])
-    at = jnp.stack([lax.axis_index("core"), lax.axis_index("y")]).astype(jnp.int32)
-    h_own = exchange(jnp.broadcast_to(h.astype(jnp.bfloat16)[None], (N_P, *h.shape)), RANKS)
+    core, y = lax.axis_index("core"), lax.axis_index("y")
+    at = jnp.stack([1 - core, core, y]).astype(jnp.int32)
+    h_all = lax.all_gather(h.astype(jnp.bfloat16), ("zh", "x", "zl", "core"), axis=0, tiled=False)
     energy = energies(record, dft_table())
     frames, rows = energy.shape[3:]
     energy, w_low = lax.optimization_barrier((energy, w.astype(jnp.bfloat16)))
     ws = taken_ahead(w_low)
-    h_own = h_own.reshape(2, rank, -1)
-    h_oth = from_sibling(h_own)
+    h_all = h_all.reshape(N_R, 2, 2, *h.shape)
+    h_oth, h_own = [
+        lax.dynamic_index_in_dim(h_all, c, 2, keepdims=False).swapaxes(0, 1).reshape(2, rank, -1)
+        for c in (1 - core, core)
+    ]
     spectra = exchange(energy.reshape(2 * N_P, frames, rows), TILE).reshape(2 * N_P * frames, rows)
     for step in range(ITERS):
-        n0, n1, n2, n3, s_own, s_oth = sweep(at, spectra, h_own, h_oth, ws)
+        *parts, s_oth = half_sweep(at, spectra, h_oth, ws)
+        s_got = from_sibling(s_oth)
+        n0, n1, n2, n3, s_own = half_sweep(at, spectra, h_own, ws, parts)
         w_parts = [n0] + [sent_ahead(n, t + 1) for t, n in enumerate((n1, n2, n3))]
-        h_parts = exchange(pair(s_own, from_sibling(s_oth), *h.shape), RANKS)
+        h_parts = exchange(pair(s_own, s_got, *h.shape), RANKS)
         w_parts, h_parts = lax.optimization_barrier((w_parts, h_parts))
         h, low = h_update(h_parts, h)
         w, w_low = w_update(w_parts, w)

time: 174 us -> 209 us (1.20)
  waiting for transfers between devices: 91.1 us -> 113 us
  between operations: 0.75 us -> 14.2 us
  starting transfers between devices: 53.3 us -> 48.7 us
  Pallas kernels: 26 us -> 29.3 us
    all_gather x0 -> x1, waiting for transfers between devices: none -> 82.7 us  [local(): lax.all_gather(h.astype(jnp.bfloat16), ('zh', 'x', 'zl', 'core'), axis=0,...]
    all_to_all x5 -> x4, waiting for transfers between devices: 48.1 us -> 0.74 us  [exchange(): return lax.all_to_all(x, axes, 0, 0, tiled=True)]
    ppermute x6, waiting for transfers between devices: 13.2 us -> 4.42 us  [taken_ahead(): lax.ppermute(x, 'y', [(i, (i - t) % N_Y) for i in range(N_Y)])]
    all_to_all x5 -> x4, starting transfers between devices: 33.3 us -> 26.6 us  [exchange(): return lax.all_to_all(x, axes, 0, 0, tiled=True)]
    ppermute x4 -> x3, waiting for transfers between devices: 7.26 us -> 1.91 us  [from_sibling(): return lax.ppermute(x, 'core', [(0, 1), (1, 0)])]
    pallas_call x2 -> x4, Pallas kernels: 13.6 us -> 16.8 us  [half_sweep(): pl.pallas_call(functools.partial(sweep_kernel, not before), in_specs=whol...]
  transfers between devices with their start and end apart: 21 -> 20, of which waited for: 17 -> 10; matrix products, arithmetic and copies ran while one was open for 0% -> 1% of each run, Pallas kernels for 4% -> 4%
where the time goes in v4:
time: 209 us; the launch traced here: 208 us
  waiting for transfers between devices  113 us (54%)
  starting transfers between devices  48.7 us (23%)
  Pallas kernels  29.3 us (14%)
  between operations  14.2 us (7%)
    all_gather x1, waiting for transfers between devices, local(): lax.all_gather(h.astype(jnp.bfloat16), ('zh', 'x', 'zl', 'core'), axis=0,...  82.7 us
    all_to_all x4, starting transfers between devices, exchange(): return lax.all_to_all(x, axes, 0, 0, tiled=True)  26.6 us
    ppermute x6, waiting for transfers between devices, sent_ahead(): return lax.ppermute(x, 'y', [(i, (i + t) % N_Y) for i in range(N_Y)])  22.8 us
    pallas_call x4, Pallas kernels, half_sweep(): pl.pallas_call(functools.partial(sweep_kernel, not before), in_specs=whol...  16.8 us
    ppermute x6, starting transfers between devices, taken_ahead(): lax.ppermute(x, 'y', [(i, (i - t) % N_Y) for i in range(N_Y)])  11.2 us
    ppermute x6, starting transfers between devices, sent_ahead(): return lax.ppermute(x, 'y', [(i, (i + t) % N_Y) for i in range(N_Y)])  10.2 us
    pallas_call x1, Pallas kernels, energies(): pl.pallas_call(energy_kernel, in_specs=[pl.BlockSpec(memory_space=pl.ANY)...  7.41 us
    ppermute x6, waiting for transfers between devices, taken_ahead(): lax.ppermute(x, 'y', [(i, (i - t) % N_Y) for i in range(N_Y)])  4.42 us
  transfers between devices with their start and end apart: 20, of which 10 were waited for; matrix products, arithmetic and copies ran while one was open for 1% of the time, Pallas kernels for 4%

profile of v4, /device:TPU:0, one launch (start us, length us, event | category | flops | bytes accessed | tf_op | source)
XLA Modules:
  0.0 207.9 jit_solution(12451737073583727122)
XLA Ops:
  7.2 1.0 convert_element_type.10.w0
  8.1 7.4 %energy.1 = bf16[2,2,8,64,1024]{4,3,2,1,0:T(8,128)(2,1)} custom-call(bf16[256,16384]{1,0:T(8,128)(2,1)} %bitcast.23, bf16[256,256]{1,0:T(8,128)(2,1)} %constant.24.table_ref), custom_call_target="tpu_custom_call" | custom-call | flops 2147483648 | bytes 12582912 | tf_op jit(solution)/shard_map/energy/pallas_call | solution.py:82
  15.6 0.0 copy-start.1
  15.6 8.5 %all-to-all-start = ((bf16[32,64,1024]{2,1,0:T(8,128)(2,1)}), bf16[32,64,1024]{2,1,0:T(8,128)(2,1)}, u32[]{:S(2)}, u32[]{:S(2)}) async-start(bf16[32,64,1024]{2,1,0:T(8,128)(2,1)} %bitcast.22), calls=%async_computation | async-start | bytes 8388608 | tf_op jit(solution)/shard_map/all_to_all | solution.py:229
  24.1 0.0 all-gather.3.cloned.1.call-start
  24.1 0.0 copy-done.1
  24.2 0.6 convert_element_type.11
  24.8 0.0 all-gather.3.cloned.1.call-update
  24.8 1.6 collective-permute-start.2
  26.5 2.9 %collective-permute-start.1 = (bf16[256,256]{1,0:T(8,128)(2,1)S(1)}, bf16[256,256]{1,0:T(8,128)(2,1)S(1)}, u32[]{:S(2)}, u32[]{:S(2)}) collective-permute-start(bf16[256,256]{1,0:T(8,128)(2,1)S(1)} %convert_element_type.10.w0), channel_id=1, source_target_pairs={{0,4},{2,6},{4,0},{6,2},{1,5},{3,7},{5,1},{7,3},{8,12},{10,14},{12... | collective-permute-start | bytes 393224 | tf_op jit(solution)/shard_map/ppermute | solution.py:241
  29.4 1.3 collective-permute-start
  30.7 0.1 pad_add_fusion.at_ref
  30.8 82.7 %all-gather.3.cloned.1.call-done = bf16[1024,512]{1,0:T(8,128)(2,1)} async-done(((bf16[32,512]{1,0:T(8,128)(2,1)}), bf16[1024,512]{1,0:T(8,128)(2,1)}) %all-gather.3.cloned.1.call-update) | async-done | bytes 1048592 | tf_op jit(solution)/shard_map/all_gather | solution.py:249
  113.5 1.3 constant_dynamic-slice_fusion
  114.9 0.0 collective-permute-done.2.w3
  114.9 0.0 collective-permute-done.1.w2
  114.9 0.0 collective-permute-done.w1
  114.9 0.0 all-to-all-done
  114.9 4.2 %sweep_a.2 = (f32[264,256]{1,0:T(8,128)S(1)}, f32[264,256]{1,0:T(8,128)S(1)}, f32[264,256]{1,0:T(8,128)S(1)}, f32[264,256]{1,0:T(8,128)S(1)}, f32[256,1152]{1,0:T(8,128)S(1)}) custom-call(s32[3]{0:T(128)S(1)} %pad_add_fusion.at_ref, bf16[2048,1024]{1,0:T(8,128)(2,1)} %bitcast.5.s_ref, bf16[2,256,512]{2,1,0:T(8,128)(2,1)S(1)} %bitcast.21, ...), custom_call_target="tpu_custom_call" | custom-call | flops 1610612736 | bytes 4194304 | tf_op jit(solution)/shard_map/sweep_a/pallas_call | solution.py:149
  119.1 0.3 collective-permute-start.6
  119.5 4.2 %sweep_b.2 = (f32[264,256]{1,0:T(8,128)S(1)}, f32[264,256]{1,0:T(8,128)S(1)}, f32[264,256]{1,0:T(8,128)S(1)}, f32[264,256]{1,0:T(8,128)S(1)}, f32[256,1152]{1,0:T(8,128)S(1)}) custom-call(s32[3]{0:T(128)S(1)} %pad_add_fusion.at_ref, bf16[2048,1024]{1,0:T(8,128)(2,1)} %bitcast.5.s_ref, bf16[2,256,512]{2,1,0:T(8,128)(2,1)S(1)} %bitcast.20, ...), custom_call_target="tpu_custom_call" | custom-call | flops 1610612736 | bytes 4194304 | tf_op jit(solution)/shard_map/sweep_b/pallas_call | solution.py:149
  123.7 0.0 collective-permute-done.6.b_ref
  123.7 1.0 pair.2
  124.7 4.9 %all-to-all-start.1 = ((bf16[16,32,640]{2,1,0:T(8,128)(2,1)}), bf16[16,32,640]{2,1,0:T(8,128)(2,1)S(1)}, u32[]{:S(2)}, u32[]{:S(2)}) async-start(bf16[16,32,640]{2,1,0:T(8,128)(2,1)} %pair.2), calls=%async_computation.1 | async-start | bytes 1310720 | tf_op jit(solution)/shard_map/all_to_all | solution.py:229
  129.7 0.0 copy-start
  129.7 1.6 collective-permute-start.3
  131.3 2.9 %collective-permute-start.4 = (f32[264,256]{1,0:T(8,128)S(1)}, f32[264,256]{1,0:T(8,128)S(1)}, u32[]{:S(2)}, u32[]{:S(2)}) collective-permute-start(f32[264,256]{1,0:T(8,128)S(1)} %get-tuple-element.53), channel_id=1, source_target_pairs={{0,4},{2,6},{4,0},{6,2},{1,5},{3,7},{5,1},{7,3},{8,12},{10,14},{12... | collective-permute-start | bytes 811016 | tf_op jit(solution)/shard_map/ppermute | solution.py:237
  134.2 1.3 collective-permute-start.5
  135.5 3.8 %collective-permute-done.3.p1 = f32[264,256]{1,0:T(8,128)S(1)} collective-permute-done((f32[264,256]{1,0:T(8,128)S(1)}, f32[264,256]{1,0:T(8,128)S(1)}, u32[]{:S(2)}, u32[]{:S(2)}) %collective-permute-start.3) | collective-permute-done | bytes 270368 | tf_op jit(solution)/shard_map/ppermute | solution.py:237
  139.4 7.0 %collective-permute-done.4.p2 = f32[264,256]{1,0:T(8,128)S(1)} collective-permute-done((f32[264,256]{1,0:T(8,128)S(1)}, f32[264,256]{1,0:T(8,128)S(1)}, u32[]{:S(2)}, u32[]{:S(2)}) %collective-permute-start.4) | collective-permute-done | bytes 270368 | tf_op jit(solution)/shard_map/ppermute | solution.py:237
  146.4 0.0 collective-permute-done.5.p3
  146.4 0.0 all-to-all-done.1.parts_ref
  146.4 1.0 h_update.2
  147.4 6.9 %all-to-all-start.2 = ((bf16[16,32,512]{2,1,0:T(8,128)(2,1)}), bf16[16,32,512]{2,1,0:T(8,128)(2,1)S(1)}, u32[]{:S(2)}, u32[]{:S(2)}) async-start(bf16[16,32,512]{2,1,0:T(8,128)(2,1)} %get-tuple-element.63), calls=%async_computation.2 | async-start | bytes 1048576 | tf_op jit(solution)/shard_map/all_to_all | solution.py:229
  154.3 0.0 copy-done
  154.3 0.1 w_update.2
  154.5 1.3 collective-permute-start.9
  155.8 2.4 %collective-permute-start.8 = (bf16[256,256]{1,0:T(8,128)(2,1)S(1)}, bf16[256,256]{1,0:T(8,128)(2,1)S(1)}, u32[]{:S(2)}, u32[]{:S(2)}) collective-permute-start(bf16[256,256]{1,0:T(8,128)(2,1)S(1)} %get-tuple-element.65.w0), channel_id=1, source_target_pairs={{0,4},{2,6},{4,0},{6,2},{1,5},{3,7},{5,1},{7,3},{8,12},{10,14},{12... | collective-permute-start | bytes 393224 | tf_op jit(solution)/shard_map/ppermute | solution.py:241
  158.2 1.6 collective-permute-start.7
  159.8 1.7 collective-permute-done.9.w3
  161.4 2.7 %collective-permute-done.8.w2 = bf16[256,256]{1,0:T(8,128)(2,1)S(1)} collective-permute-done((bf16[256,256]{1,0:T(8,128)(2,1)S(1)}, bf16[256,256]{1,0:T(8,128)(2,1)S(1)}, u32[]{:S(2)}, u32[]{:S(2)}) %collective-permute-start.8) | collective-permute-done | bytes 131104 | tf_op jit(solution)/shard_map/ppermute | solution.py:241
  164.1 0.1 collective-permute-done.7.w1
  164.2 0.7 all-to-all-done.2
  164.9 0.0 collective-permute-start.10
  164.9 1.9 collective-permute-done.10.h_ref
  166.8 4.2 %sweep_a.3 = (f32[264,256]{1,0:T(8,128)S(1)}, f32[264,256]{1,0:T(8,128)S(1)}, f32[264,256]{1,0:T(8,128)S(1)}, f32[264,256]{1,0:T(8,128)S(1)}, f32[256,1152]{1,0:T(8,128)S(1)}) custom-call(s32[3]{0:T(128)S(1)} %pad_add_fusion.at_ref, bf16[2048,1024]{1,0:T(8,128)(2,1)} %bitcast.5.s_ref, bf16[2,256,512]{2,1,0:T(8,128)(2,1)S(1)} %collective-permute-done.10.h_ref, ...), custom_call_target="tpu_custom_call" | custom-call | flops 1610612736 | bytes 4194304 | tf_op jit(solution)/shard_map/sweep_a/pallas_call | solution.py:149
  171.0 0.4 collective-permute-start.14
  171.4 4.2 %sweep_b.3 = (f32[264,256]{1,0:T(8,128)S(1)}, f32[264,256]{1,0:T(8,128)S(1)}, f32[264,256]{1,0:T(8,128)S(1)}, f32[264,256]{1,0:T(8,128)S(1)}, f32[256,1152]{1,0:T(8,128)S(1)}) custom-call(s32[3]{0:T(128)S(1)} %pad_add_fusion.at_ref, bf16[2048,1024]{1,0:T(8,128)(2,1)} %bitcast.5.s_ref, bf16[2,256,512]{2,1,0:T(8,128)(2,1)S(1)} %bitcast.19, ...), custom_call_target="tpu_custom_call" | custom-call | flops 1610612736 | bytes 4194304 | tf_op jit(solution)/shard_map/sweep_b/pallas_call | solution.py:149
  175.6 0.0 collective-permute-done.14.b_ref
  175.6 1.0 pair.3
  176.6 6.2 %all-to-all-start.3 = ((bf16[16,32,640]{2,1,0:T(8,128)(2,1)}), bf16[16,32,640]{2,1,0:T(8,128)(2,1)S(1)}, u32[]{:S(2)}, u32[]{:S(2)}) async-start(bf16[16,32,640]{2,1,0:T(8,128)(2,1)} %pair.3), calls=%async_computation.3 | async-start | bytes 1310720 | tf_op jit(solution)/shard_map/all_to_all | solution.py:229
  182.8 1.1 collective-permute-start.11
  184.0 3.0 %collective-permute-start.12 = (f32[264,256]{1,0:T(8,128)S(1)}, f32[264,256]{1,0:T(8,128)S(1)}, u32[]{:S(2)}, u32[]{:S(2)}) collective-permute-start(f32[264,256]{1,0:T(8,128)S(1)} %get-tuple-element.75), channel_id=1, source_target_pairs={{0,4},{2,6},{4,0},{6,2},{1,5},{3,7},{5,1},{7,3},{8,12},{10,14},{12... | collective-permute-start | bytes 811016 | tf_op jit(solution)/shard_map/ppermute | solution.py:237
  186.9 0.3 collective-permute-start.13
  187.2 5.4 %collective-permute-done.11.p1 = f32[264,256]{1,0:T(8,128)S(1)} collective-permute-done((f32[264,256]{1,0:T(8,128)S(1)}, f32[264,256]{1,0:T(8,128)S(1)}, u32[]{:S(2)}, u32[]{:S(2)}) %collective-permute-start.11) | collective-permute-done | bytes 270368 | tf_op jit(solution)/shard_map/ppermute | solution.py:237
  192.6 6.5 %collective-permute-done.12.p2 = f32[264,256]{1,0:T(8,128)S(1)} collective-permute-done((f32[264,256]{1,0:T(8,128)S(1)}, f32[264,256]{1,0:T(8,128)S(1)}, u32[]{:S(2)}, u32[]{:S(2)}) %collective-permute-start.12) | collective-permute-done | bytes 270368 | tf_op jit(solution)/shard_map/ppermute | solution.py:237
  199.2 0.0 collective-permute-done.13.p3
  199.2 0.0 all-to-all-done.3.parts_ref
  199.2 1.0 h_update.3
  200.2 0.9 w_update.3
  (2 shorter events, 0.1 us)
Async XLA Ops:
  15.6 8.6 %copy-start.1 = (f32[32,512]{1,0:T(8,128)S(1)}, f32[32,512]{1,0:T(8,128)}, u32[]{:S(2)}) copy-start(f32[32,512]{1,0:T(8,128)} %h_ref.1) | copy-start | bytes 196612
  15.6 99.3 %all-to-all-start = ((bf16[32,64,1024]{2,1,0:T(8,128)(2,1)}), bf16[32,64,1024]{2,1,0:T(8,128)(2,1)}, u32[]{:S(2)}, u32[]{:S(2)}) async-start(bf16[32,64,1024]{2,1,0:T(8,128)(2,1)} %bitcast.22), calls=%async_computation | async-start | bytes 8388608 | tf_op jit(solution)/shard_map/all_to_all | solution.py:229
  24.1 89.4 %all-gather.3.cloned.1.call-start = ((), (), s32[]{:S(2)}) async-start(), calls=%async_computation.4 | async-start | bytes 1081344 | tf_op jit(solution)/shard_map/all_gather | solution.py:249
  24.8 90.0 %collective-permute-start.2 = (bf16[256,256]{1,0:T(8,128)(2,1)S(1)}, bf16[256,256]{1,0:T(8,128)(2,1)S(1)}, u32[]{:S(2)}, u32[]{:S(2)}) collective-permute-start(bf16[256,256]{1,0:T(8,128)(2,1)S(1)} %convert_element_type.10.w0), channel_id=1, source_target_pairs={{0,2},{2,4},{4,6},{6,0},{1,3},{3,5},{5,7},{7,1},{8,10},{10,12},{12... | collective-permute-start | bytes 393224 | tf_op jit(solution)/shard_map/ppermute | solution.py:241
  26.5 88.4 %collective-permute-start.1 = (bf16[256,256]{1,0:T(8,128)(2,1)S(1)}, bf16[256,256]{1,0:T(8,128)(2,1)S(1)}, u32[]{:S(2)}, u32[]{:S(2)}) collective-permute-start(bf16[256,256]{1,0:T(8,128)(2,1)S(1)} %convert_element_type.10.w0), channel_id=1, source_target_pairs={{0,4},{2,6},{4,0},{6,2},{1,5},{3,7},{5,1},{7,3},{8,12},{10,14},{12... | collective-permute-start | bytes 393224 | tf_op jit(solution)/shard_map/ppermute | solution.py:241
  29.4 85.5 %collective-permute-start = (bf16[256,256]{1,0:T(8,128)(2,1)S(1)}, bf16[256,256]{1,0:T(8,128)(2,1)S(1)}, u32[]{:S(2)}, u32[]{:S(2)}) collective-permute-start(bf16[256,256]{1,0:T(8,128)(2,1)S(1)} %convert_element_type.10.w0), channel_id=1, source_target_pairs={{0,6},{2,0},{4,2},{6,4},{1,7},{3,1},{5,3},{7,5},{8,14},{10,8},{12,... | collective-permute-start | bytes 393224 | tf_op jit(solution)/shard_map/ppermute | solution.py:241
  119.1 4.6 %collective-permute-start.6 = (f32[256,1152]{1,0:T(8,128)S(1)}, f32[256,1152]{1,0:T(8,128)S(1)}, u32[]{:S(2)}, u32[]{:S(2)}) collective-permute-start(f32[256,1152]{1,0:T(8,128)S(1)} %get-tuple-element.56), channel_id=1, source_target_pairs={{0,1},{1,0},{2,3},{3,2},{4,5},{5,4},{6,7},{7,6},{8,9},{9,8},{10,11... | collective-permute-start | bytes 3538952 | tf_op jit(solution)/shard_map/ppermute | solution.py:233
  124.7 21.6 %all-to-all-start.1 = ((bf16[16,32,640]{2,1,0:T(8,128)(2,1)}), bf16[16,32,640]{2,1,0:T(8,128)(2,1)S(1)}, u32[]{:S(2)}, u32[]{:S(2)}) async-start(bf16[16,32,640]{2,1,0:T(8,128)(2,1)} %pair.2), calls=%async_computation.1 | async-start | bytes 1310720 | tf_op jit(solution)/shard_map/all_to_all | solution.py:229
  129.7 24.6 %copy-start = (f32[256,256]{1,0:T(8,128)S(1)}, f32[256,256]{1,0:T(8,128)}, u32[]{:S(2)}) copy-start(f32[256,256]{1,0:T(8,128)} %w_ref.1) | copy-start | bytes 786436
  129.7 9.7 %collective-permute-start.3 = (f32[264,256]{1,0:T(8,128)S(1)}, f32[264,256]{1,0:T(8,128)S(1)}, u32[]{:S(2)}, u32[]{:S(2)}) collective-permute-start(f32[264,256]{1,0:T(8,128)S(1)} %get-tuple-element.52), channel_id=1, source_target_pairs={{0,2},{2,4},{4,6},{6,0},{1,3},{3,5},{5,7},{7,1},{8,10},{10,12},{12... | collective-permute-start | bytes 811016 | tf_op jit(solution)/shard_map/ppermute | solution.py:237
  131.3 15.0 %collective-permute-start.4 = (f32[264,256]{1,0:T(8,128)S(1)}, f32[264,256]{1,0:T(8,128)S(1)}, u32[]{:S(2)}, u32[]{:S(2)}) collective-permute-start(f32[264,256]{1,0:T(8,128)S(1)} %get-tuple-element.53), channel_id=1, source_target_pairs={{0,4},{2,6},{4,0},{6,2},{1,5},{3,7},{5,1},{7,3},{8,12},{10,14},{12... | collective-permute-start | bytes 811016 | tf_op jit(solution)/shard_map/ppermute | solution.py:237
  134.2 12.2 %collective-permute-start.5 = (f32[264,256]{1,0:T(8,128)S(1)}, f32[264,256]{1,0:T(8,128)S(1)}, u32[]{:S(2)}, u32[]{:S(2)}) collective-permute-start(f32[264,256]{1,0:T(8,128)S(1)} %get-tuple-element.54), channel_id=1, source_target_pairs={{0,6},{2,0},{4,2},{6,4},{1,7},{3,1},{5,3},{7,5},{8,14},{10,8},{12,... | collective-permute-start | bytes 811016 | tf_op jit(solution)/shard_map/ppermute | solution.py:237
  147.4 17.5 %all-to-all-start.2 = ((bf16[16,32,512]{2,1,0:T(8,128)(2,1)}), bf16[16,32,512]{2,1,0:T(8,128)(2,1)S(1)}, u32[]{:S(2)}, u32[]{:S(2)}) async-start(bf16[16,32,512]{2,1,0:T(8,128)(2,1)} %get-tuple-element.63), calls=%async_computation.2 | async-start | bytes 1048576 | tf_op jit(solution)/shard_map/all_to_all | solution.py:229
  154.5 7.0 %collective-permute-start.9 = (bf16[256,256]{1,0:T(8,128)(2,1)S(1)}, bf16[256,256]{1,0:T(8,128)(2,1)S(1)}, u32[]{:S(2)}, u32[]{:S(2)}) collective-permute-start(bf16[256,256]{1,0:T(8,128)(2,1)S(1)} %get-tuple-element.65.w0), channel_id=1, source_target_pairs={{0,2},{2,4},{4,6},{6,0},{1,3},{3,5},{5,7},{7,1},{8,10},{10,12},{12... | collective-permute-start | bytes 393224 | tf_op jit(solution)/shard_map/ppermute | solution.py:241
  155.8 8.3 %collective-permute-start.8 = (bf16[256,256]{1,0:T(8,128)(2,1)S(1)}, bf16[256,256]{1,0:T(8,128)(2,1)S(1)}, u32[]{:S(2)}, u32[]{:S(2)}) collective-permute-start(bf16[256,256]{1,0:T(8,128)(2,1)S(1)} %get-tuple-element.65.w0), channel_id=1, source_target_pairs={{0,4},{2,6},{4,0},{6,2},{1,5},{3,7},{5,1},{7,3},{8,12},{10,14},{12... | collective-permute-start | bytes 393224 | tf_op jit(solution)/shard_map/ppermute | solution.py:241
  158.2 6.0 %collective-permute-start.7 = (bf16[256,256]{1,0:T(8,128)(2,1)S(1)}, bf16[256,256]{1,0:T(8,128)(2,1)S(1)}, u32[]{:S(2)}, u32[]{:S(2)}) collective-permute-start(bf16[256,256]{1,0:T(8,128)(2,1)S(1)} %get-tuple-element.65.w0), channel_id=1, source_target_pairs={{0,6},{2,0},{4,2},{6,4},{1,7},{3,1},{5,3},{7,5},{8,14},{10,8},{12,... | collective-permute-start | bytes 393224 | tf_op jit(solution)/shard_map/ppermute | solution.py:241
  164.9 1.9 collective-permute-start.10
  171.0 4.6 %collective-permute-start.14 = (f32[256,1152]{1,0:T(8,128)S(1)}, f32[256,1152]{1,0:T(8,128)S(1)}, u32[]{:S(2)}, u32[]{:S(2)}) collective-permute-start(f32[256,1152]{1,0:T(8,128)S(1)} %get-tuple-element.78), channel_id=1, source_target_pairs={{0,1},{1,0},{2,3},{3,2},{4,5},{5,4},{6,7},{7,6},{8,9},{9,8},{10,11... | collective-permute-start | bytes 3538952 | tf_op jit(solution)/shard_map/ppermute | solution.py:233
  176.6 22.6 %all-to-all-start.3 = ((bf16[16,32,640]{2,1,0:T(8,128)(2,1)}), bf16[16,32,640]{2,1,0:T(8,128)(2,1)S(1)}, u32[]{:S(2)}, u32[]{:S(2)}) async-start(bf16[16,32,640]{2,1,0:T(8,128)(2,1)} %pair.3), calls=%async_computation.3 | async-start | bytes 1310720 | tf_op jit(solution)/shard_map/all_to_all | solution.py:229
  182.8 9.8 %collective-permute-start.11 = (f32[264,256]{1,0:T(8,128)S(1)}, f32[264,256]{1,0:T(8,128)S(1)}, u32[]{:S(2)}, u32[]{:S(2)}) collective-permute-start(f32[264,256]{1,0:T(8,128)S(1)} %get-tuple-element.74), channel_id=1, source_target_pairs={{0,2},{2,4},{4,6},{6,0},{1,3},{3,5},{5,7},{7,1},{8,10},{10,12},{12... | collective-permute-start | bytes 811016 | tf_op jit(solution)/shard_map/ppermute | solution.py:237
  184.0 15.2 %collective-permute-start.12 = (f32[264,256]{1,0:T(8,128)S(1)}, f32[264,256]{1,0:T(8,128)S(1)}, u32[]{:S(2)}, u32[]{:S(2)}) collective-permute-start(f32[264,256]{1,0:T(8,128)S(1)} %get-tuple-element.75), channel_id=1, source_target_pairs={{0,4},{2,6},{4,0},{6,2},{1,5},{3,7},{5,1},{7,3},{8,12},{10,14},{12... | collective-permute-start | bytes 811016 | tf_op jit(solution)/shard_map/ppermute | solution.py:237
  186.9 12.2 %collective-permute-start.13 = (f32[264,256]{1,0:T(8,128)S(1)}, f32[264,256]{1,0:T(8,128)S(1)}, u32[]{:S(2)}, u32[]{:S(2)}) collective-permute-start(f32[264,256]{1,0:T(8,128)S(1)} %get-tuple-element.76), channel_id=1, source_target_pairs={{0,6},{2,0},{4,2},{6,4},{1,7},{3,1},{5,3},{7,5},{8,14},{10,8},{12,... | collective-permute-start | bytes 811016 | tf_op jit(solution)/shard_map/ppermute | solution.py:237
Sparse Core Ops, SparseCore 0:
  27.2 86.2 all-gather.2

commit v5 on v4

--- a/solution.py
+++ b/solution.py
@@ -16,7 +16,7 @@
 
 AXES = ("zh", "x", "zl", "y", "core")
 SIZES = (2, 4, 2, 4, 2)
-TILE = ("core", "zl", "zh", "x")
+TILE = ("zh", "zl", "core", "x")
 RANKS = ("zl", "zh", "x")
 N_Y = 4
 N_R = 8
@@ -47,7 +47,7 @@
         return pltpu.make_async_copy(x_hbm.at[pl.ds(r * chans, chans), :], x_ref.at[r], in_sem.at[r])
 
     def put(r):
-        return pltpu.make_async_copy(out_ref.at[r], out_hbm.at[:, :, r], out_sem.at[r])
+        return pltpu.make_async_copy(out_ref.at[r], out_hbm.at[r // 4, :, :, r % 4], out_sem.at[r])
 
     for r in range(blocks):
         fetch(r).start()
@@ -67,7 +67,7 @@
             for c in range(chans):
                 zl, y, core, j = c // 16, (c // 4) % 4, (c // 2) % 2, c % 2
                 at = (y * 2 + j) * BINS
-                out_ref[r, core, zl, g * group : (g + 1) * group, at : at + BINS] = energy[c]
+                out_ref[r, zl, core, g * group : (g + 1) * group, at : at + BINS] = energy[c]
         put(r).start()
 
     for r in range(blocks):
@@ -83,7 +83,7 @@
         energy_kernel,
         in_specs=[pl.BlockSpec(memory_space=pl.ANY), pl.BlockSpec(memory_space=pltpu.VMEM)],
         out_specs=pl.BlockSpec(memory_space=pl.ANY),
-        out_shape=jax.ShapeDtypeStruct((2, 2, N_R, frames, rows), jnp.bfloat16),
+        out_shape=jax.ShapeDtypeStruct((2, 2, 2, 4, frames, rows), jnp.bfloat16),
         scratch_shapes=[
             pltpu.VMEM((N_R, per_row, samples), jnp.bfloat16),
             pltpu.VMEM((N_R, 2, 2, frames, rows), jnp.bfloat16),
@@ -98,12 +98,6 @@
     )(record, table)
 
 
-def hi_lo(x, axis):
-    hi = x.astype(jnp.bfloat16)
-    lo = (x - hi.astype(jnp.float32)).astype(jnp.bfloat16)
-    return jnp.where(lax.broadcasted_iota(jnp.int32, x.shape, axis) == 0, hi, lo)
-
-
 def sweep_kernel(first, at_ref, s_ref, h_ref, w0, w1, w2, w3, *refs):
     before, (n0, n1, n2, n3, sums_ref, ht_ref) = (() if first else refs[:4]), refs[-6:]
     blocks, rank, half = h_ref.shape
@@ -112,14 +106,18 @@
         ht_ref[b * half : (b + 1) * half, :] = h_ref[b].T
     rowsum = jnp.dot(jnp.ones((8, span), jnp.bfloat16), ht_ref[...], preferred_element_type=jnp.float32)
     colsum = jnp.zeros((rank, 1), jnp.float32)
-    rows = pl.ds(pl.multiple_of(at_ref[0 if first else 1] * span, span), span)
+    run = half // 2
+    core = at_ref[0 if first else 1]
+    rows = [
+        pl.ds(pl.multiple_of(((zh * blocks + b) * 2 + core) * run, run), run) for b in range(blocks) for zh in range(2)
+    ]
     for p in range(2):
         wt = jnp.concatenate([w[...] for w in ((w0, w1), (w2, w3))[p]], axis=0).T
         colsum = colsum + jnp.sum(wt.astype(jnp.float32), axis=1, keepdims=True)
         columns = [
             pl.ds(pl.multiple_of(lax.rem(at_ref[2] + 2 * p + t, N_Y) * rank, rank), rank) for t in range(2)
         ]
-        s = jnp.concatenate([s_ref[rows, c] for c in columns], axis=1)
+        s = jnp.concatenate([jnp.concatenate([s_ref[r, c] for c in columns], axis=1) for r in rows], axis=0)
         recon = jnp.dot(ht_ref[...], wt, preferred_element_type=jnp.float32)
         quotient = (s.astype(jnp.float32) / recon).astype(jnp.bfloat16)
         hn = lax.dot_general(wt, quotient, (((1,), (1,)), ((), ())), preferred_element_type=jnp.float32)
@@ -162,13 +160,13 @@
 def pair_kernel(a_ref, b_ref, out_ref):
     each, half = out_ref.shape[1], out_ref.shape[2] - PAD
     span = a_ref.shape[1] - PAD
-    total = a_ref[...] + b_ref[...]
-    sums = hi_lo(total[:, span:], 1)
-    for zl in range(2):
-        part = total[:, zl * half : (zl + 1) * half].astype(jnp.bfloat16)
-        for r in range(N_R):
-            out_ref[zl * N_R + r, :, :half] = part[r * each : (r + 1) * each, :]
-            out_ref[zl * N_R + r, :, half:] = sums[r * each : (r + 1) * each, :]
+    for r in range(N_R):
+        rows = slice(r * each, (r + 1) * each)
+        sums = a_ref[rows, span:] + b_ref[rows, span:]
+        for zl in range(2):
+            columns = slice(zl * half, (zl + 1) * half)
+            out_ref[zl * N_R + r, :, :half] = a_ref[rows, columns] + b_ref[rows, columns]
+            out_ref[zl * N_R + r, :, half:] = sums
 
 
 def pair(a, b, each, half):
@@ -176,7 +174,7 @@
         pair_kernel,
         in_specs=whole(2),
         out_specs=whole(1)[0],
-        out_shape=jax.ShapeDtypeStruct((N_P, each, half + PAD), jnp.bfloat16),
+        out_shape=jax.ShapeDtypeStruct((N_P, each, half + PAD), jnp.float32),
         compiler_params=pltpu.CompilerParams(vmem_limit_bytes=12 << 20),
         name="pair",
     )(a, b)
@@ -184,11 +182,10 @@
 
 def h_update_kernel(parts_ref, h_ref, new_ref, low_ref):
     half = h_ref.shape[1]
-    total = parts_ref[0].astype(jnp.float32)
+    total = parts_ref[0]
     for i in range(1, N_P):
-        total = total + parts_ref[i].astype(jnp.float32)
-    colsum = total[:, half : half + 1] + total[:, half + 1 : half + 2]
-    new = h_ref[...] * total[:, :half] / colsum
+        total = total + parts_ref[i]
+    new = h_ref[...] * total[:, :half] / total[:, half : half + 1]
     new_ref[...] = new
     low = new.astype(jnp.bfloat16)
     for i in range(N_P):
@@ -225,6 +222,23 @@
     )(*parts, w)
 
 
+def spread_kernel(h_ref, low_ref):
+    low = h_ref[...].astype(jnp.bfloat16)
+    for i in range(N_P):
+        low_ref[i] = low
+
+
+def spread(h):
+    return pl.pallas_call(
+        spread_kernel,
+        in_specs=whole(1),
+        out_specs=whole(1)[0],
+        out_shape=jax.ShapeDtypeStruct((N_P, *h.shape), jnp.bfloat16),
+        compiler_params=pltpu.CompilerParams(vmem_limit_bytes=12 << 20),
+        name="spread",
+    )(h)
+
+
 def exchange(x, axes):
     return lax.all_to_all(x, axes, 0, 0, tiled=True)
 
@@ -246,16 +260,13 @@
     record = samples.reshape(samples.shape[2], samples.shape[3])
     core, y = lax.axis_index("core"), lax.axis_index("y")
     at = jnp.stack([1 - core, core, y]).astype(jnp.int32)
-    h_all = lax.all_gather(h.astype(jnp.bfloat16), ("zh", "x", "zl", "core"), axis=0, tiled=False)
+    h_own = exchange(spread(h), RANKS)
     energy = energies(record, dft_table())
-    frames, rows = energy.shape[3:]
+    frames, rows = energy.shape[4:]
     energy, w_low = lax.optimization_barrier((energy, w.astype(jnp.bfloat16)))
     ws = taken_ahead(w_low)
-    h_all = h_all.reshape(N_R, 2, 2, *h.shape)
-    h_oth, h_own = [
-        lax.dynamic_index_in_dim(h_all, c, 2, keepdims=False).swapaxes(0, 1).reshape(2, rank, -1)
-        for c in (1 - core, core)
-    ]
+    h_own = h_own.reshape(2, rank, -1)
+    h_oth = from_sibling(h_own)
     spectra = exchange(energy.reshape(2 * N_P, frames, rows), TILE).reshape(2 * N_P * frames, rows)
     for step in range(ITERS):
         *parts, s_oth = half_sweep(at, spectra, h_oth, ws)
@@ -263,8 +274,8 @@
         n0, n1, n2, n3, s_own = half_sweep(at, spectra, h_own, ws, parts)
         w_parts = [n0] + [sent_ahead(n, t + 1) for t, n in enumerate((n1, n2, n3))]
         h_parts = exchange(pair(s_own, s_got, *h.shape), RANKS)
-        w_parts, h_parts = lax.optimization_barrier((w_parts, h_parts))
         h, low = h_update(h_parts, h)
+        w_parts, low, h = lax.optimization_barrier((w_parts, low, h))
         w, w_low = w_update(w_parts, w)
         if step + 1 < ITERS:
             ws = taken_ahead(w_low)

time: 209 us -> 173 us (0.83)
  waiting for transfers between devices: 113 us -> 89 us
  between operations: 14.2 us -> 0.8 us
  starting transfers between devices: 48.7 us -> 51.1 us
    all_gather x1 -> x0, waiting for transfers between devices: 82.7 us -> none  [local(): lax.all_gather(h.astype(jnp.bfloat16), ('zh', 'x', 'zl', 'core'), axis=0,...]
    all_to_all x4 -> x5, waiting for transfers between devices: 0.74 us -> 77.8 us  [exchange(): return lax.all_to_all(x, axes, 0, 0, tiled=True)]
    ppermute x6, waiting for transfers between devices: 22.8 us -> 0.02 us  [sent_ahead(): return lax.ppermute(x, 'y', [(i, (i + t) % N_Y) for i in range(N_Y)])]
    ppermute x6, waiting for transfers between devices: 4.42 us -> 9.27 us  [taken_ahead(): lax.ppermute(x, 'y', [(i, (i - t) % N_Y) for i in range(N_Y)])]
    all_to_all x4 -> x5, starting transfers between devices: 26.6 us -> 27.5 us  [exchange(): return lax.all_to_all(x, axes, 0, 0, tiled=True)]
  transfers between devices with their start and end apart: 20 -> 21, of which waited for: 10 -> 10; matrix products, arithmetic and copies ran while one was open for 1% -> 0% of each run, Pallas kernels for 4% -> 10%
where the time goes in v5:
time: 173 us; the launch traced here: 172 us
  waiting for transfers between devices  89 us (51%)
  starting transfers between devices  51.1 us (30%)
  Pallas kernels  30.5 us (18%)
    all_to_all x5, waiting for transfers between devices, exchange(): return lax.all_to_all(x, axes, 0, 0, tiled=True)  77.8 us
    all_to_all x5, starting transfers between devices, exchange(): return lax.all_to_all(x, axes, 0, 0, tiled=True)  27.5 us
    pallas_call x4, Pallas kernels, half_sweep(): pl.pallas_call(functools.partial(sweep_kernel, not before), in_specs=whol...  16.8 us
    ppermute x6, starting transfers between devices, taken_ahead(): lax.ppermute(x, 'y', [(i, (i - t) % N_Y) for i in range(N_Y)])  11.7 us
    ppermute x6, starting transfers between devices, sent_ahead(): return lax.ppermute(x, 'y', [(i, (i + t) % N_Y) for i in range(N_Y)])  11.1 us
    ppermute x6, waiting for transfers between devices, taken_ahead(): lax.ppermute(x, 'y', [(i, (i - t) % N_Y) for i in range(N_Y)])  9.27 us
    pallas_call x1, Pallas kernels, energies(): pl.pallas_call(energy_kernel, in_specs=[pl.BlockSpec(memory_space=pl.ANY)...  7.45 us
  transfers between devices with their start and end apart: 21, of which 10 were waited for; matrix products, arithmetic and copies ran while one was open for 0% of the time, Pallas kernels for 10%

profile of v5, /device:TPU:0, one launch (start us, length us, event | category | flops | bytes accessed | tf_op | source)
XLA Modules:
  0.0 172.3 jit_solution(7632178957103392534)
XLA Ops:
  0.6 0.0 copy-start
  0.6 0.0 copy-start.1
  0.7 0.9 copy-done.1
  1.5 0.9 spread.1
  2.4 8.0 %all-to-all-start.1 = ((bf16[16,32,512]{2,1,0:T(8,128)(2,1)}), bf16[16,32,512]{2,1,0:T(8,128)(2,1)S(1)}, u32[]{:S(2)}, u32[]{:S(2)}) async-start(bf16[16,32,512]{2,1,0:T(8,128)(2,1)} %spread.1), calls=%async_computation.1 | async-start | bytes 1048576 | tf_op jit(solution)/shard_map/all_to_all | solution.py:243
  10.3 0.0 copy-done
  10.4 7.4 %energy.1 = bf16[2,2,2,4,64,1024]{5,4,3,2,1,0:T(8,128)(2,1)} custom-call(bf16[256,16384]{1,0:T(8,128)(2,1)} %bitcast.13, bf16[256,256]{1,0:T(8,128)(2,1)} %constant.14.table_ref), custom_call_target="tpu_custom_call" | custom-call | flops 2147483648 | bytes 12582912 | tf_op jit(solution)/shard_map/energy/pallas_call | solution.py:82
  17.8 4.0 %all-to-all-done.1 = bf16[16,32,512]{2,1,0:T(8,128)(2,1)S(1)} async-done(((bf16[16,32,512]{2,1,0:T(8,128)(2,1)}), bf16[16,32,512]{2,1,0:T(8,128)(2,1)S(1)}, u32[]{:S(2)}, u32[]{:S(2)}) %all-to-all-start.1) | async-done | bytes 524320 | tf_op jit(solution)/shard_map/all_to_all | solution.py:243
  21.9 4.9 %all-to-all-start = ((bf16[32,64,1024]{2,1,0:T(8,128)(2,1)}), bf16[32,64,1024]{2,1,0:T(8,128)(2,1)}, u32[]{:S(2)}, u32[]{:S(2)}) async-start(bf16[32,64,1024]{2,1,0:T(8,128)(2,1)} %bitcast.12), calls=%async_computation | async-start | bytes 8388608 | tf_op jit(solution)/shard_map/all_to_all | solution.py:243
  26.7 0.2 collective-permute-start.3
  26.9 1.6 collective-permute-start.2
  28.5 2.9 %collective-permute-start.1 = (bf16[256,256]{1,0:T(8,128)(2,1)S(1)}, bf16[256,256]{1,0:T(8,128)(2,1)S(1)}, u32[]{:S(2)}, u32[]{:S(2)}) collective-permute-start(bf16[256,256]{1,0:T(8,128)(2,1)S(1)} %convert_element_type.7.w0), channel_id=1, source_target_pairs={{0,4},{2,6},{4,0},{6,2},{1,5},{3,7},{5,1},{7,3},{8,12},{10,14},{12... | collective-permute-start | bytes 393224 | tf_op jit(solution)/shard_map/ppermute | solution.py:255
  31.4 1.3 collective-permute-start
  32.8 0.1 pad_add_fusion.at_ref
  32.8 1.2 collective-permute-done.2.w3
  34.0 4.0 %collective-permute-done.1.w2 = bf16[256,256]{1,0:T(8,128)(2,1)S(1)} collective-permute-done((bf16[256,256]{1,0:T(8,128)(2,1)S(1)}, bf16[256,256]{1,0:T(8,128)(2,1)S(1)}, u32[]{:S(2)}, u32[]{:S(2)}) %collective-permute-start.1) | collective-permute-done | bytes 131104 | tf_op jit(solution)/shard_map/ppermute | solution.py:255
  38.0 0.0 collective-permute-done.w1
  38.0 0.0 collective-permute-done.3.h_ref
  38.0 39.8 %all-to-all-done = bf16[32,64,1024]{2,1,0:T(8,128)(2,1)} async-done(((bf16[32,64,1024]{2,1,0:T(8,128)(2,1)}), bf16[32,64,1024]{2,1,0:T(8,128)(2,1)}, u32[]{:S(2)}, u32[]{:S(2)}) %all-to-all-start) | async-done | bytes 4194336 | tf_op jit(solution)/shard_map/all_to_all | solution.py:243
  77.8 4.2 %sweep_a.2 = (f32[264,256]{1,0:T(8,128)S(1)}, f32[264,256]{1,0:T(8,128)S(1)}, f32[264,256]{1,0:T(8,128)S(1)}, f32[264,256]{1,0:T(8,128)S(1)}, f32[256,1152]{1,0:T(8,128)S(1)}) custom-call(s32[3]{0:T(128)S(1)} %pad_add_fusion.at_ref, bf16[2048,1024]{1,0:T(8,128)(2,1)} %bitcast.5.s_ref, bf16[2,256,512]{2,1,0:T(8,128)(2,1)S(1)} %collective-permute-done.3.h_ref, ...), custom_call_target="tpu_custom_call" | custom-call | flops 1610612736 | bytes 4194304 | tf_op jit(solution)/shard_map/sweep_a/pallas_call | solution.py:147
  82.0 0.1 collective-permute-start.7
  82.1 4.2 %sweep_b.2 = (f32[264,256]{1,0:T(8,128)S(1)}, f32[264,256]{1,0:T(8,128)}, f32[264,256]{1,0:T(8,128)S(1)}, f32[264,256]{1,0:T(8,128)S(1)}, f32[256,1152]{1,0:T(8,128)S(1)}) custom-call(s32[3]{0:T(128)S(1)} %pad_add_fusion.at_ref, bf16[2048,1024]{1,0:T(8,128)(2,1)} %bitcast.5.s_ref, bf16[2,256,512]{2,1,0:T(8,128)(2,1)S(1)} %bitcast.9, ...), custom_call_target="tpu_custom_call" | custom-call | flops 1610612736 | bytes 4194304 | tf_op jit(solution)/shard_map/sweep_b/pallas_call | solution.py:147
  86.3 0.0 collective-permute-done.7.b_ref
  86.3 1.2 pair.2
  87.6 0.0 copy-start.2
  87.6 5.3 %all-to-all-start.2 = ((f32[16,32,640]{2,1,0:T(8,128)}), f32[16,32,640]{2,1,0:T(8,128)S(1)}, u32[]{:S(2)}, u32[]{:S(2)}) async-start(f32[16,32,640]{2,1,0:T(8,128)} %pair.2), calls=%async_computation.2 | async-start | bytes 2621440 | tf_op jit(solution)/shard_map/all_to_all | solution.py:243
  92.9 1.7 collective-permute-start.4
  94.5 2.9 %collective-permute-start.5 = (f32[264,256]{1,0:T(8,128)S(1)}, f32[264,256]{1,0:T(8,128)S(1)}, u32[]{:S(2)}, u32[]{:S(2)}) collective-permute-start(f32[264,256]{1,0:T(8,128)S(1)} %get-tuple-element.54), channel_id=1, source_target_pairs={{0,4},{2,6},{4,0},{6,2},{1,5},{3,7},{5,1},{7,3},{8,12},{10,14},{12... | collective-permute-start | bytes 811016 | tf_op jit(solution)/shard_map/ppermute | solution.py:251
  97.4 1.4 collective-permute-start.6
  98.8 16.1 %all-to-all-done.2.parts_ref = f32[16,32,640]{2,1,0:T(8,128)S(1)} async-done(((f32[16,32,640]{2,1,0:T(8,128)}), f32[16,32,640]{2,1,0:T(8,128)S(1)}, u32[]{:S(2)}, u32[]{:S(2)}) %all-to-all-start.2) | async-done | bytes 1310752 | tf_op jit(solution)/shard_map/all_to_all | solution.py:243
  114.9 0.0 copy-done.2
  114.9 0.9 h_update.2
  115.8 0.0 collective-permute-done.4.p1
  115.8 0.0 collective-permute-done.5.p2
  115.9 0.0 collective-permute-done.6.p3
  115.9 3.6 %all-to-all-start.3 = ((bf16[16,32,512]{2,1,0:T(8,128)(2,1)}), bf16[16,32,512]{2,1,0:T(8,128)(2,1)S(1)}, u32[]{:S(2)}, u32[]{:S(2)}) async-start(bf16[16,32,512]{2,1,0:T(8,128)(2,1)} %get-tuple-element.65), calls=%async_computation.3 | async-start | bytes 1048576 | tf_op jit(solution)/shard_map/all_to_all | solution.py:243
  119.4 0.2 w_update.2
  119.6 1.7 collective-permute-start.10
  121.3 2.9 %collective-permute-start.9 = (bf16[256,256]{1,0:T(8,128)(2,1)S(1)}, bf16[256,256]{1,0:T(8,128)(2,1)S(1)}, u32[]{:S(2)}, u32[]{:S(2)}) collective-permute-start(bf16[256,256]{1,0:T(8,128)(2,1)S(1)} %get-tuple-element.67.w0), channel_id=1, source_target_pairs={{0,4},{2,6},{4,0},{6,2},{1,5},{3,7},{5,1},{7,3},{8,12},{10,14},{12... | collective-permute-start | bytes 393224 | tf_op jit(solution)/shard_map/ppermute | solution.py:255
  124.2 1.4 collective-permute-start.8
  125.5 1.2 collective-permute-done.10.w3
  126.7 2.9 %collective-permute-done.9.w2 = bf16[256,256]{1,0:T(8,128)(2,1)S(1)} collective-permute-done((bf16[256,256]{1,0:T(8,128)(2,1)S(1)}, bf16[256,256]{1,0:T(8,128)(2,1)S(1)}, u32[]{:S(2)}, u32[]{:S(2)}) %collective-permute-start.9) | collective-permute-done | bytes 131104 | tf_op jit(solution)/shard_map/ppermute | solution.py:255
  129.6 0.0 collective-permute-done.8.w1
  129.6 1.0 all-to-all-done.3
  130.6 0.0 collective-permute-start.11
  130.6 1.9 %collective-permute-done.11.h_ref = bf16[2,256,512]{2,1,0:T(8,128)(2,1)S(1)} collective-permute-done((bf16[2,256,512]{2,1,0:T(8,128)(2,1)S(1)}, bf16[2,256,512]{2,1,0:T(8,128)(2,1)S(1)}, u32[]{:S(2)}, u32[]{:S(2)}) %collective-permute-start.11) | collective-permute-done | bytes 524320 | tf_op jit(solution)/shard_map/ppermute | solution.py:247
  132.6 4.2 %sweep_a.3 = (f32[264,256]{1,0:T(8,128)S(1)}, f32[264,256]{1,0:T(8,128)S(1)}, f32[264,256]{1,0:T(8,128)S(1)}, f32[264,256]{1,0:T(8,128)S(1)}, f32[256,1152]{1,0:T(8,128)S(1)}) custom-call(s32[3]{0:T(128)S(1)} %pad_add_fusion.at_ref, bf16[2048,1024]{1,0:T(8,128)(2,1)} %bitcast.5.s_ref, bf16[2,256,512]{2,1,0:T(8,128)(2,1)S(1)} %collective-permute-done.11.h_ref, ...), custom_call_target="tpu_custom_call" | custom-call | flops 1610612736 | bytes 4194304 | tf_op jit(solution)/shard_map/sweep_a/pallas_call | solution.py:147
  136.7 0.4 collective-permute-start.15
  137.1 4.2 %sweep_b.3 = (f32[264,256]{1,0:T(8,128)S(1)}, f32[264,256]{1,0:T(8,128)}, f32[264,256]{1,0:T(8,128)S(1)}, f32[264,256]{1,0:T(8,128)S(1)}, f32[256,1152]{1,0:T(8,128)S(1)}) custom-call(s32[3]{0:T(128)S(1)} %pad_add_fusion.at_ref, bf16[2048,1024]{1,0:T(8,128)(2,1)} %bitcast.5.s_ref, bf16[2,256,512]{2,1,0:T(8,128)(2,1)S(1)} %bitcast.11, ...), custom_call_target="tpu_custom_call" | custom-call | flops 1610612736 | bytes 4194304 | tf_op jit(solution)/shard_map/sweep_b/pallas_call | solution.py:147
  141.3 0.0 collective-permute-done.15.b_ref
  141.4 1.2 pair.3
  142.6 5.9 %all-to-all-start.4 = ((f32[16,32,640]{2,1,0:T(8,128)}), f32[16,32,640]{2,1,0:T(8,128)S(1)}, u32[]{:S(2)}, u32[]{:S(2)}) async-start(f32[16,32,640]{2,1,0:T(8,128)} %pair.3), calls=%async_computation.4 | async-start | bytes 2621440 | tf_op jit(solution)/shard_map/all_to_all | solution.py:243
  148.4 1.3 collective-permute-start.12
  149.7 2.9 %collective-permute-start.13 = (f32[264,256]{1,0:T(8,128)S(1)}, f32[264,256]{1,0:T(8,128)S(1)}, u32[]{:S(2)}, u32[]{:S(2)}) collective-permute-start(f32[264,256]{1,0:T(8,128)S(1)} %get-tuple-element.77), channel_id=1, source_target_pairs={{0,4},{2,6},{4,0},{6,2},{1,5},{3,7},{5,1},{7,3},{8,12},{10,14},{12... | collective-permute-start | bytes 811016 | tf_op jit(solution)/shard_map/ppermute | solution.py:251
  152.6 1.1 collective-permute-start.14
  153.7 16.8 %all-to-all-done.4.parts_ref = f32[16,32,640]{2,1,0:T(8,128)S(1)} async-done(((f32[16,32,640]{2,1,0:T(8,128)}), f32[16,32,640]{2,1,0:T(8,128)S(1)}, u32[]{:S(2)}, u32[]{:S(2)}) %all-to-all-start.4) | async-done | bytes 1310752 | tf_op jit(solution)/shard_map/all_to_all | solution.py:243
  170.5 0.9 h_update.3
  171.4 0.0 collective-permute-done.12.p1
  171.4 0.0 collective-permute-done.13.p2
  171.4 0.0 collective-permute-done.14.p3
  171.4 0.9 w_update.3
  (1 shorter events, 0.0 us)
Async XLA Ops:
  0.6 9.7 %copy-start = (f32[256,256]{1,0:T(8,128)S(1)}, f32[256,256]{1,0:T(8,128)}, u32[]{:S(2)}) copy-start(f32[256,256]{1,0:T(8,128)} %w_ref.1) | copy-start | bytes 786436
  0.6 0.9 copy-start.1
  2.4 19.5 %all-to-all-start.1 = ((bf16[16,32,512]{2,1,0:T(8,128)(2,1)}), bf16[16,32,512]{2,1,0:T(8,128)(2,1)S(1)}, u32[]{:S(2)}, u32[]{:S(2)}) async-start(bf16[16,32,512]{2,1,0:T(8,128)(2,1)} %spread.1), calls=%async_computation.1 | async-start | bytes 1048576 | tf_op jit(solution)/shard_map/all_to_all | solution.py:243
  21.9 55.9 %all-to-all-start = ((bf16[32,64,1024]{2,1,0:T(8,128)(2,1)}), bf16[32,64,1024]{2,1,0:T(8,128)(2,1)}, u32[]{:S(2)}, u32[]{:S(2)}) async-start(bf16[32,64,1024]{2,1,0:T(8,128)(2,1)} %bitcast.12), calls=%async_computation | async-start | bytes 8388608 | tf_op jit(solution)/shard_map/all_to_all | solution.py:243
  26.7 11.3 %collective-permute-start.3 = (bf16[2,256,512]{2,1,0:T(8,128)(2,1)S(1)}, bf16[2,256,512]{2,1,0:T(8,128)(2,1)S(1)}, u32[]{:S(2)}, u32[]{:S(2)}) collective-permute-start(bf16[2,256,512]{2,1,0:T(8,128)(2,1)S(1)} %bitcast.8), channel_id=1, source_target_pairs={{0,1},{1,0},{2,3},{3,2},{4,5},{5,4},{6,7},{7,6},{8,9},{9,8},{10,11... | collective-permute-start | bytes 1572872 | tf_op jit(solution)/shard_map/ppermute | solution.py:247
  26.9 7.1 %collective-permute-start.2 = (bf16[256,256]{1,0:T(8,128)(2,1)S(1)}, bf16[256,256]{1,0:T(8,128)(2,1)S(1)}, u32[]{:S(2)}, u32[]{:S(2)}) collective-permute-start(bf16[256,256]{1,0:T(8,128)(2,1)S(1)} %convert_element_type.7.w0), channel_id=1, source_target_pairs={{0,2},{2,4},{4,6},{6,0},{1,3},{3,5},{5,7},{7,1},{8,10},{10,12},{12... | collective-permute-start | bytes 393224 | tf_op jit(solution)/shard_map/ppermute | solution.py:255
  28.5 9.5 %collective-permute-start.1 = (bf16[256,256]{1,0:T(8,128)(2,1)S(1)}, bf16[256,256]{1,0:T(8,128)(2,1)S(1)}, u32[]{:S(2)}, u32[]{:S(2)}) collective-permute-start(bf16[256,256]{1,0:T(8,128)(2,1)S(1)} %convert_element_type.7.w0), channel_id=1, source_target_pairs={{0,4},{2,6},{4,0},{6,2},{1,5},{3,7},{5,1},{7,3},{8,12},{10,14},{12... | collective-permute-start | bytes 393224 | tf_op jit(solution)/shard_map/ppermute | solution.py:255
  31.4 6.6 %collective-permute-start = (bf16[256,256]{1,0:T(8,128)(2,1)S(1)}, bf16[256,256]{1,0:T(8,128)(2,1)S(1)}, u32[]{:S(2)}, u32[]{:S(2)}) collective-permute-start(bf16[256,256]{1,0:T(8,128)(2,1)S(1)} %convert_element_type.7.w0), channel_id=1, source_target_pairs={{0,6},{2,0},{4,2},{6,4},{1,7},{3,1},{5,3},{7,5},{8,14},{10,8},{12,... | collective-permute-start | bytes 393224 | tf_op jit(solution)/shard_map/ppermute | solution.py:255
  82.0 4.3 %collective-permute-start.7 = (f32[256,1152]{1,0:T(8,128)S(1)}, f32[256,1152]{1,0:T(8,128)S(1)}, u32[]{:S(2)}, u32[]{:S(2)}) collective-permute-start(f32[256,1152]{1,0:T(8,128)S(1)} %get-tuple-element.57), channel_id=1, source_target_pairs={{0,1},{1,0},{2,3},{3,2},{4,5},{5,4},{6,7},{7,6},{8,9},{9,8},{10,11... | collective-permute-start | bytes 3538952 | tf_op jit(solution)/shard_map/ppermute | solution.py:247
  87.6 27.3 %copy-start.2 = (f32[32,512]{1,0:T(8,128)S(1)}, f32[32,512]{1,0:T(8,128)}, u32[]{:S(2)}) copy-start(f32[32,512]{1,0:T(8,128)} %h_ref.3) | copy-start | bytes 196612
  87.6 27.3 %all-to-all-start.2 = ((f32[16,32,640]{2,1,0:T(8,128)}), f32[16,32,640]{2,1,0:T(8,128)S(1)}, u32[]{:S(2)}, u32[]{:S(2)}) async-start(f32[16,32,640]{2,1,0:T(8,128)} %pair.2), calls=%async_computation.2 | async-start | bytes 2621440 | tf_op jit(solution)/shard_map/all_to_all | solution.py:243
  92.9 23.0 %collective-permute-start.4 = (f32[264,256]{1,0:T(8,128)}, f32[264,256]{1,0:T(8,128)S(1)}, u32[]{:S(2)}, u32[]{:S(2)}) collective-permute-start(f32[264,256]{1,0:T(8,128)} %get-tuple-element.53), channel_id=1, source_target_pairs={{0,2},{2,4},{4,6},{6,0},{1,3},{3,5},{5,7},{7,1},{8,10},{10,12},{12... | collective-permute-start | bytes 811016 | tf_op jit(solution)/shard_map/ppermute | solution.py:251
  94.5 21.3 %collective-permute-start.5 = (f32[264,256]{1,0:T(8,128)S(1)}, f32[264,256]{1,0:T(8,128)S(1)}, u32[]{:S(2)}, u32[]{:S(2)}) collective-permute-start(f32[264,256]{1,0:T(8,128)S(1)} %get-tuple-element.54), channel_id=1, source_target_pairs={{0,4},{2,6},{4,0},{6,2},{1,5},{3,7},{5,1},{7,3},{8,12},{10,14},{12... | collective-permute-start | bytes 811016 | tf_op jit(solution)/shard_map/ppermute | solution.py:251
  97.4 18.5 %collective-permute-start.6 = (f32[264,256]{1,0:T(8,128)S(1)}, f32[264,256]{1,0:T(8,128)S(1)}, u32[]{:S(2)}, u32[]{:S(2)}) collective-permute-start(f32[264,256]{1,0:T(8,128)S(1)} %get-tuple-element.55), channel_id=1, source_target_pairs={{0,6},{2,0},{4,2},{6,4},{1,7},{3,1},{5,3},{7,5},{8,14},{10,8},{12,... | collective-permute-start | bytes 811016 | tf_op jit(solution)/shard_map/ppermute | solution.py:251
  115.9 14.8 %all-to-all-start.3 = ((bf16[16,32,512]{2,1,0:T(8,128)(2,1)}), bf16[16,32,512]{2,1,0:T(8,128)(2,1)S(1)}, u32[]{:S(2)}, u32[]{:S(2)}) async-start(bf16[16,32,512]{2,1,0:T(8,128)(2,1)} %get-tuple-element.65), calls=%async_computation.3 | async-start | bytes 1048576 | tf_op jit(solution)/shard_map/all_to_all | solution.py:243
  119.6 7.1 %collective-permute-start.10 = (bf16[256,256]{1,0:T(8,128)(2,1)S(1)}, bf16[256,256]{1,0:T(8,128)(2,1)S(1)}, u32[]{:S(2)}, u32[]{:S(2)}) collective-permute-start(bf16[256,256]{1,0:T(8,128)(2,1)S(1)} %get-tuple-element.67.w0), channel_id=1, source_target_pairs={{0,2},{2,4},{4,6},{6,0},{1,3},{3,5},{5,7},{7,1},{8,10},{10,12},{12... | collective-permute-start | bytes 393224 | tf_op jit(solution)/shard_map/ppermute | solution.py:255
  121.3 8.3 %collective-permute-start.9 = (bf16[256,256]{1,0:T(8,128)(2,1)S(1)}, bf16[256,256]{1,0:T(8,128)(2,1)S(1)}, u32[]{:S(2)}, u32[]{:S(2)}) collective-permute-start(bf16[256,256]{1,0:T(8,128)(2,1)S(1)} %get-tuple-element.67.w0), channel_id=1, source_target_pairs={{0,4},{2,6},{4,0},{6,2},{1,5},{3,7},{5,1},{7,3},{8,12},{10,14},{12... | collective-permute-start | bytes 393224 | tf_op jit(solution)/shard_map/ppermute | solution.py:255
  124.2 5.4 %collective-permute-start.8 = (bf16[256,256]{1,0:T(8,128)(2,1)S(1)}, bf16[256,256]{1,0:T(8,128)(2,1)S(1)}, u32[]{:S(2)}, u32[]{:S(2)}) collective-permute-start(bf16[256,256]{1,0:T(8,128)(2,1)S(1)} %get-tuple-element.67.w0), channel_id=1, source_target_pairs={{0,6},{2,0},{4,2},{6,4},{1,7},{3,1},{5,3},{7,5},{8,14},{10,8},{12,... | collective-permute-start | bytes 393224 | tf_op jit(solution)/shard_map/ppermute | solution.py:255
  130.6 1.9 %collective-permute-start.11 = (bf16[2,256,512]{2,1,0:T(8,128)(2,1)S(1)}, bf16[2,256,512]{2,1,0:T(8,128)(2,1)S(1)}, u32[]{:S(2)}, u32[]{:S(2)}) collective-permute-start(bf16[2,256,512]{2,1,0:T(8,128)(2,1)S(1)} %bitcast.10), channel_id=1, source_target_pairs={{0,1},{1,0},{2,3},{3,2},{4,5},{5,4},{6,7},{7,6},{8,9},{9,8},{10,11... | collective-permute-start | bytes 1572872 | tf_op jit(solution)/shard_map/ppermute | solution.py:247
  136.7 4.6 %collective-permute-start.15 = (f32[256,1152]{1,0:T(8,128)S(1)}, f32[256,1152]{1,0:T(8,128)S(1)}, u32[]{:S(2)}, u32[]{:S(2)}) collective-permute-start(f32[256,1152]{1,0:T(8,128)S(1)} %get-tuple-element.80), channel_id=1, source_target_pairs={{0,1},{1,0},{2,3},{3,2},{4,5},{5,4},{6,7},{7,6},{8,9},{9,8},{10,11... | collective-permute-start | bytes 3538952 | tf_op jit(solution)/shard_map/ppermute | solution.py:247
  142.6 27.9 %all-to-all-start.4 = ((f32[16,32,640]{2,1,0:T(8,128)}), f32[16,32,640]{2,1,0:T(8,128)S(1)}, u32[]{:S(2)}, u32[]{:S(2)}) async-start(f32[16,32,640]{2,1,0:T(8,128)} %pair.3), calls=%async_computation.4 | async-start | bytes 2621440 | tf_op jit(solution)/shard_map/all_to_all | solution.py:243
  148.4 23.0 %collective-permute-start.12 = (f32[264,256]{1,0:T(8,128)}, f32[264,256]{1,0:T(8,128)S(1)}, u32[]{:S(2)}, u32[]{:S(2)}) collective-permute-start(f32[264,256]{1,0:T(8,128)} %get-tuple-element.76), channel_id=1, source_target_pairs={{0,2},{2,4},{4,6},{6,0},{1,3},{3,5},{5,7},{7,1},{8,10},{10,12},{12... | collective-permute-start | bytes 811016 | tf_op jit(solution)/shard_map/ppermute | solution.py:251
  149.7 21.7 %collective-permute-start.13 = (f32[264,256]{1,0:T(8,128)S(1)}, f32[264,256]{1,0:T(8,128)S(1)}, u32[]{:S(2)}, u32[]{:S(2)}) collective-permute-start(f32[264,256]{1,0:T(8,128)S(1)} %get-tuple-element.77), channel_id=1, source_target_pairs={{0,4},{2,6},{4,0},{6,2},{1,5},{3,7},{5,1},{7,3},{8,12},{10,14},{12... | collective-permute-start | bytes 811016 | tf_op jit(solution)/shard_map/ppermute | solution.py:251
  152.6 18.9 %collective-permute-start.14 = (f32[264,256]{1,0:T(8,128)S(1)}, f32[264,256]{1,0:T(8,128)S(1)}, u32[]{:S(2)}, u32[]{:S(2)}) collective-permute-start(f32[264,256]{1,0:T(8,128)S(1)} %get-tuple-element.78), channel_id=1, source_target_pairs={{0,6},{2,0},{4,2},{6,4},{1,7},{3,1},{5,3},{7,5},{8,14},{10,8},{12,... | collective-permute-start | bytes 811016 | tf_op jit(solution)/shard_map/ppermute | solution.py:251

commit v6 on v5

--- a/solution.py
+++ b/solution.py
@@ -21,7 +21,8 @@
 N_Y = 4
 N_R = 8
 N_P = 16
-PAD = 128
+LANES = 128
+TAIL = 8
 
 
 def dft_table():
@@ -138,7 +139,7 @@
             else:
                 ref[:rank, :] = part + before[2 * p + t][:rank, :]
                 ref[rank:, :] = rowsum + before[2 * p + t][rank:, :]
-    sums_ref[:, span:] = jnp.broadcast_to(colsum, (rank, PAD))
+    sums_ref[:, span:] = jnp.broadcast_to(colsum, (rank, LANES))
 
 
 def half_sweep(at, spectra, h, ws, before=()):
@@ -149,7 +150,7 @@
         in_specs=whole(1, pltpu.SMEM) + whole(6 + len(before)),
         out_specs=whole(5),
         out_shape=[jax.ShapeDtypeStruct((rank + 8, rank), jnp.float32)] * 4
-        + [jax.ShapeDtypeStruct((rank, blocks * half + PAD), jnp.float32)],
+        + [jax.ShapeDtypeStruct((rank, blocks * half + LANES), jnp.float32)],
         scratch_shapes=[pltpu.VMEM((blocks * half, rank), jnp.bfloat16)],
         compiler_params=pltpu.CompilerParams(vmem_limit_bytes=28 << 20),
         cost_estimate=pl.CostEstimate(flops=3 * frames * rows * rank, bytes_accessed=4 << 20, transcendentals=0),
@@ -158,34 +159,42 @@
 
 
 def pair_kernel(a_ref, b_ref, out_ref):
-    each, half = out_ref.shape[1], out_ref.shape[2] - PAD
-    span = a_ref.shape[1] - PAD
+    each = (out_ref.shape[1] - TAIL) // 4
+    half, span = 4 * LANES, a_ref.shape[1] - LANES
+    group = lax.broadcasted_iota(jnp.int32, (TAIL, LANES), 1) // each
     for r in range(N_R):
         rows = slice(r * each, (r + 1) * each)
         sums = a_ref[rows, span:] + b_ref[rows, span:]
+        tail = sums[:TAIL]
+        for j in range(1, each // TAIL):
+            tail = jnp.where(group == j, sums[j * TAIL : (j + 1) * TAIL], tail)
         for zl in range(2):
-            columns = slice(zl * half, (zl + 1) * half)
-            out_ref[zl * N_R + r, :, :half] = a_ref[rows, columns] + b_ref[rows, columns]
-            out_ref[zl * N_R + r, :, half:] = sums
-
-
-def pair(a, b, each, half):
+            for c in range(4):
+                columns = slice(zl * half + c * LANES, zl * half + (c + 1) * LANES)
+                out_ref[zl * N_R + r, c * each : (c + 1) * each, :] = a_ref[rows, columns] + b_ref[rows, columns]
+            out_ref[zl * N_R + r, 4 * each :, :] = tail
+
+
+def pair(a, b, each):
     return pl.pallas_call(
         pair_kernel,
         in_specs=whole(2),
         out_specs=whole(1)[0],
-        out_shape=jax.ShapeDtypeStruct((N_P, each, half + PAD), jnp.float32),
+        out_shape=jax.ShapeDtypeStruct((N_P, 4 * each + TAIL, LANES), jnp.float32),
         compiler_params=pltpu.CompilerParams(vmem_limit_bytes=12 << 20),
         name="pair",
     )(a, b)
 
 
 def h_update_kernel(parts_ref, h_ref, new_ref, low_ref):
-    half = h_ref.shape[1]
+    each = h_ref.shape[0]
     total = parts_ref[0]
     for i in range(1, N_P):
         total = total + parts_ref[i]
-    new = h_ref[...] * total[:, :half] / total[:, half : half + 1]
+    numer = jnp.concatenate([total[c * each : (c + 1) * each] for c in range(4)], axis=1)
+    tail = total[4 * each :]
+    colsum = jnp.concatenate([tail[:, j * each : j * each + 1] for j in range(each // TAIL)], axis=0)
+    new = h_ref[...] * numer / colsum
     new_ref[...] = new
     low = new.astype(jnp.bfloat16)
     for i in range(N_P):
@@ -222,21 +231,25 @@
     )(*parts, w)
 
 
-def spread_kernel(h_ref, low_ref):
-    low = h_ref[...].astype(jnp.bfloat16)
-    for i in range(N_P):
-        low_ref[i] = low
-
-
-def spread(h):
-    return pl.pallas_call(
-        spread_kernel,
-        in_specs=whole(1),
+def assemble_kernel(at_ref, z0, z1, z2, z3, out_ref):
+    each = z0.shape[1]
+    for i, ref in enumerate((z0, z1, z2, z3)):
+        z = lax.rem(at_ref[4] + i, 4)
+        for t in range(4):
+            r = (z // 2) * 4 + lax.rem(at_ref[3] + t, 4)
+            out_ref[lax.rem(z, 2), pl.ds(pl.multiple_of(r * each, each), each), :] = ref[t]
+
+
+def assemble(at, zs):
+    _, each, half = zs[0].shape
+    return pl.pallas_call(
+        assemble_kernel,
+        in_specs=whole(1, pltpu.SMEM) + whole(4),
         out_specs=whole(1)[0],
-        out_shape=jax.ShapeDtypeStruct((N_P, *h.shape), jnp.bfloat16),
+        out_shape=jax.ShapeDtypeStruct((2, N_R * each, half), jnp.bfloat16),
         compiler_params=pltpu.CompilerParams(vmem_limit_bytes=12 << 20),
-        name="spread",
-    )(h)
+        name="assemble",
+    )(at, *zs)
 
 
 def exchange(x, axes):
@@ -251,34 +264,34 @@
     return lax.ppermute(x, "y", [(i, (i + t) % N_Y) for i in range(N_Y)])
 
 
-def taken_ahead(x):
-    return [x] + [lax.ppermute(x, "y", [(i, (i - t) % N_Y) for i in range(N_Y)]) for t in range(1, N_Y)]
+def taken_ahead(x, axes):
+    return [x] + [lax.ppermute(x, axes, [(i, (i - t) % 4) for i in range(4)]) for t in range(1, 4)]
 
 
 def local(samples, w, h):
     rank = w.shape[1]
     record = samples.reshape(samples.shape[2], samples.shape[3])
     core, y = lax.axis_index("core"), lax.axis_index("y")
-    at = jnp.stack([1 - core, core, y]).astype(jnp.int32)
-    h_own = exchange(spread(h), RANKS)
+    x, z = lax.axis_index("x"), lax.axis_index(("zh", "zl"))
+    at = jnp.stack([1 - core, core, y, x, z]).astype(jnp.int32)
     energy = energies(record, dft_table())
     frames, rows = energy.shape[4:]
-    energy, w_low = lax.optimization_barrier((energy, w.astype(jnp.bfloat16)))
-    ws = taken_ahead(w_low)
-    h_own = h_own.reshape(2, rank, -1)
+    energy, w_low, h_low = lax.optimization_barrier((energy, w.astype(jnp.bfloat16), h.astype(jnp.bfloat16)))
+    h_own = assemble(at, taken_ahead(jnp.stack(taken_ahead(h_low, "x")), ("zh", "zl")))
     h_oth = from_sibling(h_own)
+    ws = taken_ahead(w_low, "y")
     spectra = exchange(energy.reshape(2 * N_P, frames, rows), TILE).reshape(2 * N_P * frames, rows)
     for step in range(ITERS):
         *parts, s_oth = half_sweep(at, spectra, h_oth, ws)
         s_got = from_sibling(s_oth)
         n0, n1, n2, n3, s_own = half_sweep(at, spectra, h_own, ws, parts)
         w_parts = [n0] + [sent_ahead(n, t + 1) for t, n in enumerate((n1, n2, n3))]
-        h_parts = exchange(pair(s_own, s_got, *h.shape), RANKS)
+        h_parts = exchange(pair(s_own, s_got, h.shape[0]), RANKS)
         h, low = h_update(h_parts, h)
         w_parts, low, h = lax.optimization_barrier((w_parts, low, h))
         w, w_low = w_update(w_parts, w)
         if step + 1 < ITERS:
-            ws = taken_ahead(w_low)
+            ws = taken_ahead(w_low, "y")
             ws, h_own = lax.optimization_barrier((ws, exchange(low, RANKS)))
             h_own = h_own.reshape(2, rank, -1)
             h_oth = from_sibling(h_own)

time: 173 us -> 182 us (1.052)
  starting transfers between devices: 51.1 us -> 56.3 us
  waiting for transfers between devices: 89 us -> 92.2 us
    ppermute x6 -> x12, waiting for transfers between devices: 9.27 us -> 60.3 us  [taken_ahead(): lax.ppermute(x, axes, [(i, (i - t) % 4) for i in range(4)])]
    all_to_all x5 -> x4, waiting for transfers between devices: 77.8 us -> 29.9 us  [exchange(): return lax.all_to_all(x, axes, 0, 0, tiled=True)]
    ppermute x6 -> x12, starting transfers between devices: 11.7 us -> 22.9 us  [taken_ahead(): lax.ppermute(x, axes, [(i, (i - t) % 4) for i in range(4)])]
    all_to_all x5 -> x4, starting transfers between devices: 27.5 us -> 22.4 us  [exchange(): return lax.all_to_all(x, axes, 0, 0, tiled=True)]
  transfers between devices with their start and end apart: 21 -> 26, of which waited for: 10 -> 14; matrix products, arithmetic and copies ran while one was open for 0% -> 0% of each run, Pallas kernels for 10% -> 6%
where the time goes in v6:
time: 182 us; the launch traced here: 181 us
  waiting for transfers between devices  92.2 us (51%)
  starting transfers between devices  56.3 us (31%)
  Pallas kernels  30.1 us (17%)
  other arithmetic  1.83 us (1%)
    ppermute x12, waiting for transfers between devices, taken_ahead(): lax.ppermute(x, axes, [(i, (i - t) % 4) for i in range(4)])  60.3 us
    all_to_all x4, waiting for transfers between devices, exchange(): return lax.all_to_all(x, axes, 0, 0, tiled=True)  29.9 us
    ppermute x12, starting transfers between devices, taken_ahead(): lax.ppermute(x, axes, [(i, (i - t) % 4) for i in range(4)])  22.9 us
    all_to_all x4, starting transfers between devices, exchange(): return lax.all_to_all(x, axes, 0, 0, tiled=True)  22.4 us
    pallas_call x4, Pallas kernels, half_sweep(): pl.pallas_call(functools.partial(sweep_kernel, not before), in_specs=whol...  16.8 us
    ppermute x6, starting transfers between devices, sent_ahead(): return lax.ppermute(x, 'y', [(i, (i + t) % N_Y) for i in range(N_Y)])  10.6 us
    pallas_call x1, Pallas kernels, energies(): pl.pallas_call(energy_kernel, in_specs=[pl.BlockSpec(memory_space=pl.ANY)...  7.42 us
  transfers between devices with their start and end apart: 26, of which 14 were waited for; matrix products, arithmetic and copies ran while one was open for 0% of the time, Pallas kernels for 6%

profile of v6, /device:TPU:0, one launch (start us, length us, event | category | flops | bytes accessed | tf_op | source)
XLA Modules:
  0.0 181.3 jit_solution(11637318837034078503)
XLA Ops:
  0.6 0.8 convert_element_type.11
  1.5 1.0 convert_element_type.10.w0
  2.4 7.4 %energy.1 = bf16[2,2,2,4,64,1024]{5,4,3,2,1,0:T(8,128)(2,1)} custom-call(bf16[256,16384]{1,0:T(8,128)(2,1)} %bitcast.16, bf16[256,256]{1,0:T(8,128)(2,1)} %constant.27.table_ref), custom_call_target="tpu_custom_call" | custom-call | flops 2147483648 | bytes 12582912 | tf_op jit(solution)/shard_map/energy/pallas_call | solution.py:83
  9.9 8.4 %all-to-all-start = ((bf16[32,64,1024]{2,1,0:T(8,128)(2,1)}), bf16[32,64,1024]{2,1,0:T(8,128)(2,1)}, u32[]{:S(2)}, u32[]{:S(2)}) async-start(bf16[32,64,1024]{2,1,0:T(8,128)(2,1)} %bitcast.15), calls=%async_computation | async-start | bytes 8388608 | tf_op jit(solution)/shard_map/all_to_all | solution.py:256
  18.3 1.8 collective-permute-start.2
  20.1 2.7 %collective-permute-start.1 = (bf16[32,512]{1,0:T(8,128)(2,1)S(1)}, bf16[32,512]{1,0:T(8,128)(2,1)S(1)}, u32[]{:S(2)}, u32[]{:S(2)}) collective-permute-start(bf16[32,512]{1,0:T(8,128)(2,1)S(1)} %convert_element_type.11), channel_id=1, source_target_pairs={{0,32},{16,48},{32,0},{48,16},{1,33},{17,49},{33,1},{49,17},{2,34}... | collective-permute-start | bytes 98312 | tf_op jit(solution)/shard_map/ppermute | solution.py:268
  22.7 1.5 collective-permute-start
  24.2 44.8 %collective-permute-done.2 = bf16[32,512]{1,0:T(8,128)(2,1)S(1)} collective-permute-done((bf16[32,512]{1,0:T(8,128)(2,1)S(1)}, bf16[32,512]{1,0:T(8,128)(2,1)S(1)}, u32[]{:S(2)}, u32[]{:S(2)}) %collective-permute-start.2) | collective-permute-done | bytes 32800 | tf_op jit(solution)/shard_map/ppermute | solution.py:268
  69.0 2.2 %collective-permute-done.1 = bf16[32,512]{1,0:T(8,128)(2,1)S(1)} collective-permute-done((bf16[32,512]{1,0:T(8,128)(2,1)S(1)}, bf16[32,512]{1,0:T(8,128)(2,1)S(1)}, u32[]{:S(2)}, u32[]{:S(2)}) %collective-permute-start.1) | collective-permute-done | bytes 32800 | tf_op jit(solution)/shard_map/ppermute | solution.py:268
  71.2 0.0 collective-permute-done
  71.2 1.3 collective-permute-start.5
  72.5 2.8 %collective-permute-start.4 = (bf16[4,32,512]{2,1,0:T(8,128)(2,1)S(1)}, bf16[4,32,512]{2,1,0:T(8,128)(2,1)S(1)}, u32[]{:S(2)}, u32[]{:S(2)}) collective-permute-start(bf16[4,32,512]{2,1,0:T(8,128)(2,1)S(1)} %pad_maximum_fusion.z0), channel_id=1, source_target_pairs={{0,64},{8,72},{64,0},{72,8},{1,65},{9,73},{65,1},{73,9},{2,66},{10... | collective-permute-start | bytes 393224 | tf_op jit(solution)/shard_map/ppermute | solution.py:268
  75.3 1.7 collective-permute-start.3
  77.0 0.1 stack.38.at_ref
  77.1 1.5 collective-permute-done.5.z3
  78.6 2.3 %collective-permute-done.4.z2 = bf16[4,32,512]{2,1,0:T(8,128)(2,1)S(1)} collective-permute-done((bf16[4,32,512]{2,1,0:T(8,128)(2,1)S(1)}, bf16[4,32,512]{2,1,0:T(8,128)(2,1)S(1)}, u32[]{:S(2)}, u32[]{:S(2)}) %collective-permute-start.4) | collective-permute-done | bytes 131104 | tf_op jit(solution)/shard_map/ppermute | solution.py:268
  80.9 0.1 collective-permute-done.3.z1
  80.9 0.6 assemble.1.h_ref
  81.6 0.1 collective-permute-start.9
  81.7 1.6 collective-permute-start.8
  83.3 2.9 %collective-permute-start.7 = (bf16[256,256]{1,0:T(8,128)(2,1)S(1)}, bf16[256,256]{1,0:T(8,128)(2,1)S(1)}, u32[]{:S(2)}, u32[]{:S(2)}) collective-permute-start(bf16[256,256]{1,0:T(8,128)(2,1)S(1)} %convert_element_type.10.w0), channel_id=1, source_target_pairs={{0,4},{2,6},{4,0},{6,2},{1,5},{3,7},{5,1},{7,3},{8,12},{10,14},{12... | collective-permute-start | bytes 393224 | tf_op jit(solution)/shard_map/ppermute | solution.py:268
  86.2 1.3 collective-permute-start.6
  87.5 1.3 collective-permute-done.8.w3
  88.8 4.0 %collective-permute-done.7.w2 = bf16[256,256]{1,0:T(8,128)(2,1)S(1)} collective-permute-done((bf16[256,256]{1,0:T(8,128)(2,1)S(1)}, bf16[256,256]{1,0:T(8,128)(2,1)S(1)}, u32[]{:S(2)}, u32[]{:S(2)}) %collective-permute-start.7) | collective-permute-done | bytes 131104 | tf_op jit(solution)/shard_map/ppermute | solution.py:268
  92.8 0.0 collective-permute-done.6.w1
  92.8 0.0 collective-permute-done.9.h_ref
  92.8 0.0 all-to-all-done
  92.8 4.2 %sweep_a.2 = (f32[264,256]{1,0:T(8,128)S(1)}, f32[264,256]{1,0:T(8,128)S(1)}, f32[264,256]{1,0:T(8,128)S(1)}, f32[264,256]{1,0:T(8,128)S(1)}, f32[256,1152]{1,0:T(8,128)S(1)}) custom-call(s32[5]{0:T(128)S(1)} %stack.38.at_ref, bf16[2048,1024]{1,0:T(8,128)(2,1)} %bitcast.7.s_ref, bf16[2,256,512]{2,1,0:T(8,128)(2,1)S(1)} %collective-permute-done.9.h_ref, ...), custom_call_target="tpu_custom_call" | custom-call | flops 1610612736 | bytes 4194304 | tf_op jit(solution)/shard_map/sweep_a/pallas_call | solution.py:148
  97.0 0.1 collective-permute-start.13
  97.1 4.2 %sweep_b.2 = (f32[264,256]{1,0:T(8,128)S(1)}, f32[264,256]{1,0:T(8,128)}, f32[264,256]{1,0:T(8,128)S(1)}, f32[264,256]{1,0:T(8,128)S(1)}, f32[256,1152]{1,0:T(8,128)S(1)}) custom-call(s32[5]{0:T(128)S(1)} %stack.38.at_ref, bf16[2048,1024]{1,0:T(8,128)(2,1)} %bitcast.7.s_ref, bf16[2,256,512]{2,1,0:T(8,128)(2,1)S(1)} %assemble.1.h_ref, ...), custom_call_target="tpu_custom_call" | custom-call | flops 1610612736 | bytes 4194304 | tf_op jit(solution)/shard_map/sweep_b/pallas_call | solution.py:148
  101.3 0.0 collective-permute-done.13.b_ref
  101.4 1.2 pair.2
  102.5 5.3 %all-to-all-start.1 = ((f32[16,136,128]{2,1,0:T(8,128)}), f32[16,136,128]{2,1,0:T(8,128)S(1)}, u32[]{:S(2)}, u32[]{:S(2)}) async-start(f32[16,136,128]{2,1,0:T(8,128)} %pair.2), calls=%async_computation.1 | async-start | bytes 2228224 | tf_op jit(solution)/shard_map/all_to_all | solution.py:256
  107.8 0.0 copy-start
  107.8 1.2 collective-permute-start.10
  109.0 2.4 %collective-permute-start.11 = (f32[264,256]{1,0:T(8,128)S(1)}, f32[264,256]{1,0:T(8,128)S(1)}, u32[]{:S(2)}, u32[]{:S(2)}) collective-permute-start(f32[264,256]{1,0:T(8,128)S(1)} %get-tuple-element.56), channel_id=1, source_target_pairs={{0,4},{2,6},{4,0},{6,2},{1,5},{3,7},{5,1},{7,3},{8,12},{10,14},{12... | collective-permute-start | bytes 811016 | tf_op jit(solution)/shard_map/ppermute | solution.py:264
  111.4 1.7 collective-permute-start.12
  113.1 14.4 %all-to-all-done.1.parts_ref = f32[16,136,128]{2,1,0:T(8,128)S(1)} async-done(((f32[16,136,128]{2,1,0:T(8,128)}), f32[16,136,128]{2,1,0:T(8,128)S(1)}, u32[]{:S(2)}, u32[]{:S(2)}) %all-to-all-start.1) | async-done | bytes 1114144 | tf_op jit(solution)/shard_map/all_to_all | solution.py:256
  127.5 1.0 h_update.2
  128.5 0.0 collective-permute-done.12.p3
  128.5 3.6 %all-to-all-start.2 = ((bf16[16,32,512]{2,1,0:T(8,128)(2,1)}), bf16[16,32,512]{2,1,0:T(8,128)(2,1)S(1)}, u32[]{:S(2)}, u32[]{:S(2)}) async-start(bf16[16,32,512]{2,1,0:T(8,128)(2,1)} %get-tuple-element.67), calls=%async_computation.2 | async-start | bytes 1048576 | tf_op jit(solution)/shard_map/all_to_all | solution.py:256
  132.1 0.2 w_update.2
  132.2 1.2 collective-permute-start.16
  133.4 2.4 %collective-permute-start.15 = (bf16[256,256]{1,0:T(8,128)(2,1)S(1)}, bf16[256,256]{1,0:T(8,128)(2,1)S(1)}, u32[]{:S(2)}, u32[]{:S(2)}) collective-permute-start(bf16[256,256]{1,0:T(8,128)(2,1)S(1)} %get-tuple-element.69.w0), channel_id=1, source_target_pairs={{0,4},{2,6},{4,0},{6,2},{1,5},{3,7},{5,1},{7,3},{8,12},{10,14},{12... | collective-permute-start | bytes 393224 | tf_op jit(solution)/shard_map/ppermute | solution.py:268
  135.8 1.7 collective-permute-start.14
  137.5 2.4 %collective-permute-done.16.w3 = bf16[256,256]{1,0:T(8,128)(2,1)S(1)} collective-permute-done((bf16[256,256]{1,0:T(8,128)(2,1)S(1)}, bf16[256,256]{1,0:T(8,128)(2,1)S(1)}, u32[]{:S(2)}, u32[]{:S(2)}) %collective-permute-start.16) | collective-permute-done | bytes 131104 | tf_op jit(solution)/shard_map/ppermute | solution.py:268
  139.9 1.5 collective-permute-done.15.w2
  141.4 0.3 collective-permute-done.14.w1
  141.7 1.7 all-to-all-done.2
  143.4 0.0 collective-permute-start.17
  143.4 1.9 %collective-permute-done.17.h_ref = bf16[2,256,512]{2,1,0:T(8,128)(2,1)S(1)} collective-permute-done((bf16[2,256,512]{2,1,0:T(8,128)(2,1)S(1)}, bf16[2,256,512]{2,1,0:T(8,128)(2,1)S(1)}, u32[]{:S(2)}, u32[]{:S(2)}) %collective-permute-start.17) | collective-permute-done | bytes 524320 | tf_op jit(solution)/shard_map/ppermute | solution.py:260
  145.3 4.2 %sweep_a.3 = (f32[264,256]{1,0:T(8,128)S(1)}, f32[264,256]{1,0:T(8,128)S(1)}, f32[264,256]{1,0:T(8,128)S(1)}, f32[264,256]{1,0:T(8,128)S(1)}, f32[256,1152]{1,0:T(8,128)S(1)}) custom-call(s32[5]{0:T(128)S(1)} %stack.38.at_ref, bf16[2048,1024]{1,0:T(8,128)(2,1)} %bitcast.7.s_ref, bf16[2,256,512]{2,1,0:T(8,128)(2,1)S(1)} %collective-permute-done.17.h_ref, ...), custom_call_target="tpu_custom_call" | custom-call | flops 1610612736 | bytes 4194304 | tf_op jit(solution)/shard_map/sweep_a/pallas_call | solution.py:148
  149.5 0.2 collective-permute-start.21
  149.7 4.2 %sweep_b.3 = (f32[264,256]{1,0:T(8,128)S(1)}, f32[264,256]{1,0:T(8,128)}, f32[264,256]{1,0:T(8,128)S(1)}, f32[264,256]{1,0:T(8,128)S(1)}, f32[256,1152]{1,0:T(8,128)S(1)}) custom-call(s32[5]{0:T(128)S(1)} %stack.38.at_ref, bf16[2048,1024]{1,0:T(8,128)(2,1)} %bitcast.7.s_ref, bf16[2,256,512]{2,1,0:T(8,128)(2,1)S(1)} %bitcast.14, ...), custom_call_target="tpu_custom_call" | custom-call | flops 1610612736 | bytes 4194304 | tf_op jit(solution)/shard_map/sweep_b/pallas_call | solution.py:148
  153.9 0.0 collective-permute-done.21.b_ref
  153.9 1.1 pair.3
  155.1 5.2 %all-to-all-start.3 = ((f32[16,136,128]{2,1,0:T(8,128)}), f32[16,136,128]{2,1,0:T(8,128)S(1)}, u32[]{:S(2)}, u32[]{:S(2)}) async-start(f32[16,136,128]{2,1,0:T(8,128)} %pair.3), calls=%async_computation.3 | async-start | bytes 2228224 | tf_op jit(solution)/shard_map/all_to_all | solution.py:256
  160.2 1.8 %collective-permute-start.18 = (f32[264,256]{1,0:T(8,128)}, f32[264,256]{1,0:T(8,128)S(1)}, u32[]{:S(2)}, u32[]{:S(2)}) collective-permute-start(f32[264,256]{1,0:T(8,128)} %get-tuple-element.78), channel_id=1, source_target_pairs={{0,2},{2,4},{4,6},{6,0},{1,3},{3,5},{5,7},{7,1},{8,10},{10,12},{12... | collective-permute-start | bytes 811016 | tf_op jit(solution)/shard_map/ppermute | solution.py:264
  162.1 2.4 %collective-permute-start.19 = (f32[264,256]{1,0:T(8,128)S(1)}, f32[264,256]{1,0:T(8,128)S(1)}, u32[]{:S(2)}, u32[]{:S(2)}) collective-permute-start(f32[264,256]{1,0:T(8,128)S(1)} %get-tuple-element.79), channel_id=1, source_target_pairs={{0,4},{2,6},{4,0},{6,2},{1,5},{3,7},{5,1},{7,3},{8,12},{10,14},{12... | collective-permute-start | bytes 811016 | tf_op jit(solution)/shard_map/ppermute | solution.py:264
  164.4 1.1 collective-permute-start.20
  165.6 13.9 %all-to-all-done.3.parts_ref = f32[16,136,128]{2,1,0:T(8,128)S(1)} async-done(((f32[16,136,128]{2,1,0:T(8,128)}), f32[16,136,128]{2,1,0:T(8,128)S(1)}, u32[]{:S(2)}, u32[]{:S(2)}) %all-to-all-start.3) | async-done | bytes 1114144 | tf_op jit(solution)/shard_map/all_to_all | solution.py:256
  179.4 1.0 h_update.3
  180.4 0.0 collective-permute-done.20.p3
  180.4 0.9 w_update.3
  (8 shorter events, 0.0 us)
Async XLA Ops:
  9.9 83.0 %all-to-all-start = ((bf16[32,64,1024]{2,1,0:T(8,128)(2,1)}), bf16[32,64,1024]{2,1,0:T(8,128)(2,1)}, u32[]{:S(2)}, u32[]{:S(2)}) async-start(bf16[32,64,1024]{2,1,0:T(8,128)(2,1)} %bitcast.15), calls=%async_computation | async-start | bytes 8388608 | tf_op jit(solution)/shard_map/all_to_all | solution.py:256
  18.3 50.7 %collective-permute-start.2 = (bf16[32,512]{1,0:T(8,128)(2,1)S(1)}, bf16[32,512]{1,0:T(8,128)(2,1)S(1)}, u32[]{:S(2)}, u32[]{:S(2)}) collective-permute-start(bf16[32,512]{1,0:T(8,128)(2,1)S(1)} %convert_element_type.11), channel_id=1, source_target_pairs={{0,16},{16,32},{32,48},{48,0},{1,17},{17,33},{33,49},{49,1},{2,18}... | collective-permute-start | bytes 98312 | tf_op jit(solution)/shard_map/ppermute | solution.py:268
  20.1 51.1 %collective-permute-start.1 = (bf16[32,512]{1,0:T(8,128)(2,1)S(1)}, bf16[32,512]{1,0:T(8,128)(2,1)S(1)}, u32[]{:S(2)}, u32[]{:S(2)}) collective-permute-start(bf16[32,512]{1,0:T(8,128)(2,1)S(1)} %convert_element_type.11), channel_id=1, source_target_pairs={{0,32},{16,48},{32,0},{48,16},{1,33},{17,49},{33,1},{49,17},{2,34}... | collective-permute-start | bytes 98312 | tf_op jit(solution)/shard_map/ppermute | solution.py:268
  22.7 48.5 %collective-permute-start = (bf16[32,512]{1,0:T(8,128)(2,1)S(1)}, bf16[32,512]{1,0:T(8,128)(2,1)S(1)}, u32[]{:S(2)}, u32[]{:S(2)}) collective-permute-start(bf16[32,512]{1,0:T(8,128)(2,1)S(1)} %convert_element_type.11), channel_id=1, source_target_pairs={{0,48},{16,0},{32,16},{48,32},{1,49},{17,1},{33,17},{49,33},{2,50}... | collective-permute-start | bytes 98312 | tf_op jit(solution)/shard_map/ppermute | solution.py:268
  71.2 7.3 %collective-permute-start.5 = (bf16[4,32,512]{2,1,0:T(8,128)(2,1)S(1)}, bf16[4,32,512]{2,1,0:T(8,128)(2,1)S(1)}, u32[]{:S(2)}, u32[]{:S(2)}) collective-permute-start(bf16[4,32,512]{2,1,0:T(8,128)(2,1)S(1)} %pad_maximum_fusion.z0), channel_id=1, source_target_pairs={{0,8},{8,64},{64,72},{72,0},{1,9},{9,65},{65,73},{73,1},{2,10},{10... | collective-permute-start | bytes 393224 | tf_op jit(solution)/shard_map/ppermute | solution.py:268
  72.5 8.3 %collective-permute-start.4 = (bf16[4,32,512]{2,1,0:T(8,128)(2,1)S(1)}, bf16[4,32,512]{2,1,0:T(8,128)(2,1)S(1)}, u32[]{:S(2)}, u32[]{:S(2)}) collective-permute-start(bf16[4,32,512]{2,1,0:T(8,128)(2,1)S(1)} %pad_maximum_fusion.z0), channel_id=1, source_target_pairs={{0,64},{8,72},{64,0},{72,8},{1,65},{9,73},{65,1},{73,9},{2,66},{10... | collective-permute-start | bytes 393224 | tf_op jit(solution)/shard_map/ppermute | solution.py:268
  75.3 5.6 %collective-permute-start.3 = (bf16[4,32,512]{2,1,0:T(8,128)(2,1)S(1)}, bf16[4,32,512]{2,1,0:T(8,128)(2,1)S(1)}, u32[]{:S(2)}, u32[]{:S(2)}) collective-permute-start(bf16[4,32,512]{2,1,0:T(8,128)(2,1)S(1)} %pad_maximum_fusion.z0), channel_id=1, source_target_pairs={{0,72},{8,0},{64,8},{72,64},{1,73},{9,1},{65,9},{73,65},{2,74},{10... | collective-permute-start | bytes 393224 | tf_op jit(solution)/shard_map/ppermute | solution.py:268
  81.6 11.3 %collective-permute-start.9 = (bf16[2,256,512]{2,1,0:T(8,128)(2,1)S(1)}, bf16[2,256,512]{2,1,0:T(8,128)(2,1)S(1)}, u32[]{:S(2)}, u32[]{:S(2)}) collective-permute-start(bf16[2,256,512]{2,1,0:T(8,128)(2,1)S(1)} %assemble.1.h_ref), channel_id=1, source_target_pairs={{0,1},{1,0},{2,3},{3,2},{4,5},{5,4},{6,7},{7,6},{8,9},{9,8},{10,11... | collective-permute-start | bytes 1572872 | tf_op jit(solution)/shard_map/ppermute | solution.py:260
  81.7 7.2 %collective-permute-start.8 = (bf16[256,256]{1,0:T(8,128)(2,1)S(1)}, bf16[256,256]{1,0:T(8,128)(2,1)S(1)}, u32[]{:S(2)}, u32[]{:S(2)}) collective-permute-start(bf16[256,256]{1,0:T(8,128)(2,1)S(1)} %convert_element_type.10.w0), channel_id=1, source_target_pairs={{0,2},{2,4},{4,6},{6,0},{1,3},{3,5},{5,7},{7,1},{8,10},{10,12},{12... | collective-permute-start | bytes 393224 | tf_op jit(solution)/shard_map/ppermute | solution.py:268
  83.3 9.5 %collective-permute-start.7 = (bf16[256,256]{1,0:T(8,128)(2,1)S(1)}, bf16[256,256]{1,0:T(8,128)(2,1)S(1)}, u32[]{:S(2)}, u32[]{:S(2)}) collective-permute-start(bf16[256,256]{1,0:T(8,128)(2,1)S(1)} %convert_element_type.10.w0), channel_id=1, source_target_pairs={{0,4},{2,6},{4,0},{6,2},{1,5},{3,7},{5,1},{7,3},{8,12},{10,14},{12... | collective-permute-start | bytes 393224 | tf_op jit(solution)/shard_map/ppermute | solution.py:268
  86.2 6.6 %collective-permute-start.6 = (bf16[256,256]{1,0:T(8,128)(2,1)S(1)}, bf16[256,256]{1,0:T(8,128)(2,1)S(1)}, u32[]{:S(2)}, u32[]{:S(2)}) collective-permute-start(bf16[256,256]{1,0:T(8,128)(2,1)S(1)} %convert_element_type.10.w0), channel_id=1, source_target_pairs={{0,6},{2,0},{4,2},{6,4},{1,7},{3,1},{5,3},{7,5},{8,14},{10,8},{12,... | collective-permute-start | bytes 393224 | tf_op jit(solution)/shard_map/ppermute | solution.py:268
  97.0 4.3 %collective-permute-start.13 = (f32[256,1152]{1,0:T(8,128)S(1)}, f32[256,1152]{1,0:T(8,128)S(1)}, u32[]{:S(2)}, u32[]{:S(2)}) collective-permute-start(f32[256,1152]{1,0:T(8,128)S(1)} %get-tuple-element.59), channel_id=1, source_target_pairs={{0,1},{1,0},{2,3},{3,2},{4,5},{5,4},{6,7},{7,6},{8,9},{9,8},{10,11... | collective-permute-start | bytes 3538952 | tf_op jit(solution)/shard_map/ppermute | solution.py:260
  102.5 25.0 %copy-start.1 = (f32[32,512]{1,0:T(8,128)S(1)}, f32[32,512]{1,0:T(8,128)}, u32[]{:S(2)}) copy-start(f32[32,512]{1,0:T(8,128)} %h_ref.1) | copy-start | bytes 196612
  102.5 24.9 %all-to-all-start.1 = ((f32[16,136,128]{2,1,0:T(8,128)}), f32[16,136,128]{2,1,0:T(8,128)S(1)}, u32[]{:S(2)}, u32[]{:S(2)}) async-start(f32[16,136,128]{2,1,0:T(8,128)} %pair.2), calls=%async_computation.1 | async-start | bytes 2228224 | tf_op jit(solution)/shard_map/all_to_all | solution.py:256
  107.8 24.3 %copy-start = (f32[256,256]{1,0:T(8,128)S(1)}, f32[256,256]{1,0:T(8,128)}, u32[]{:S(2)}) copy-start(f32[256,256]{1,0:T(8,128)} %w_ref.1) | copy-start | bytes 786436
  107.8 20.7 %collective-permute-start.10 = (f32[264,256]{1,0:T(8,128)}, f32[264,256]{1,0:T(8,128)S(1)}, u32[]{:S(2)}, u32[]{:S(2)}) collective-permute-start(f32[264,256]{1,0:T(8,128)} %get-tuple-element.55), channel_id=1, source_target_pairs={{0,2},{2,4},{4,6},{6,0},{1,3},{3,5},{5,7},{7,1},{8,10},{10,12},{12... | collective-permute-start | bytes 811016 | tf_op jit(solution)/shard_map/ppermute | solution.py:264
  109.0 19.4 %collective-permute-start.11 = (f32[264,256]{1,0:T(8,128)S(1)}, f32[264,256]{1,0:T(8,128)S(1)}, u32[]{:S(2)}, u32[]{:S(2)}) collective-permute-start(f32[264,256]{1,0:T(8,128)S(1)} %get-tuple-element.56), channel_id=1, source_target_pairs={{0,4},{2,6},{4,0},{6,2},{1,5},{3,7},{5,1},{7,3},{8,12},{10,14},{12... | collective-permute-start | bytes 811016 | tf_op jit(solution)/shard_map/ppermute | solution.py:264
  111.4 17.1 %collective-permute-start.12 = (f32[264,256]{1,0:T(8,128)S(1)}, f32[264,256]{1,0:T(8,128)S(1)}, u32[]{:S(2)}, u32[]{:S(2)}) collective-permute-start(f32[264,256]{1,0:T(8,128)S(1)} %get-tuple-element.57), channel_id=1, source_target_pairs={{0,6},{2,0},{4,2},{6,4},{1,7},{3,1},{5,3},{7,5},{8,14},{10,8},{12,... | collective-permute-start | bytes 811016 | tf_op jit(solution)/shard_map/ppermute | solution.py:264
  128.5 14.9 %all-to-all-start.2 = ((bf16[16,32,512]{2,1,0:T(8,128)(2,1)}), bf16[16,32,512]{2,1,0:T(8,128)(2,1)S(1)}, u32[]{:S(2)}, u32[]{:S(2)}) async-start(bf16[16,32,512]{2,1,0:T(8,128)(2,1)} %get-tuple-element.67), calls=%async_computation.2 | async-start | bytes 1048576 | tf_op jit(solution)/shard_map/all_to_all | solution.py:256
  132.2 7.7 %collective-permute-start.16 = (bf16[256,256]{1,0:T(8,128)(2,1)S(1)}, bf16[256,256]{1,0:T(8,128)(2,1)S(1)}, u32[]{:S(2)}, u32[]{:S(2)}) collective-permute-start(bf16[256,256]{1,0:T(8,128)(2,1)S(1)} %get-tuple-element.69.w0), channel_id=1, source_target_pairs={{0,2},{2,4},{4,6},{6,0},{1,3},{3,5},{5,7},{7,1},{8,10},{10,12},{12... | collective-permute-start | bytes 393224 | tf_op jit(solution)/shard_map/ppermute | solution.py:268
  133.4 8.0 %collective-permute-start.15 = (bf16[256,256]{1,0:T(8,128)(2,1)S(1)}, bf16[256,256]{1,0:T(8,128)(2,1)S(1)}, u32[]{:S(2)}, u32[]{:S(2)}) collective-permute-start(bf16[256,256]{1,0:T(8,128)(2,1)S(1)} %get-tuple-element.69.w0), channel_id=1, source_target_pairs={{0,4},{2,6},{4,0},{6,2},{1,5},{3,7},{5,1},{7,3},{8,12},{10,14},{12... | collective-permute-start | bytes 393224 | tf_op jit(solution)/shard_map/ppermute | solution.py:268
  135.8 5.9 %collective-permute-start.14 = (bf16[256,256]{1,0:T(8,128)(2,1)S(1)}, bf16[256,256]{1,0:T(8,128)(2,1)S(1)}, u32[]{:S(2)}, u32[]{:S(2)}) collective-permute-start(bf16[256,256]{1,0:T(8,128)(2,1)S(1)} %get-tuple-element.69.w0), channel_id=1, source_target_pairs={{0,6},{2,0},{4,2},{6,4},{1,7},{3,1},{5,3},{7,5},{8,14},{10,8},{12,... | collective-permute-start | bytes 393224 | tf_op jit(solution)/shard_map/ppermute | solution.py:268
  143.4 1.9 %collective-permute-start.17 = (bf16[2,256,512]{2,1,0:T(8,128)(2,1)S(1)}, bf16[2,256,512]{2,1,0:T(8,128)(2,1)S(1)}, u32[]{:S(2)}, u32[]{:S(2)}) collective-permute-start(bf16[2,256,512]{2,1,0:T(8,128)(2,1)S(1)} %bitcast.13), channel_id=1, source_target_pairs={{0,1},{1,0},{2,3},{3,2},{4,5},{5,4},{6,7},{7,6},{8,9},{9,8},{10,11... | collective-permute-start | bytes 1572872 | tf_op jit(solution)/shard_map/ppermute | solution.py:260
  149.5 4.4 %collective-permute-start.21 = (f32[256,1152]{1,0:T(8,128)S(1)}, f32[256,1152]{1,0:T(8,128)S(1)}, u32[]{:S(2)}, u32[]{:S(2)}) collective-permute-start(f32[256,1152]{1,0:T(8,128)S(1)} %get-tuple-element.82), channel_id=1, source_target_pairs={{0,1},{1,0},{2,3},{3,2},{4,5},{5,4},{6,7},{7,6},{8,9},{9,8},{10,11... | collective-permute-start | bytes 3538952 | tf_op jit(solution)/shard_map/ppermute | solution.py:260
  155.1 24.4 %all-to-all-start.3 = ((f32[16,136,128]{2,1,0:T(8,128)}), f32[16,136,128]{2,1,0:T(8,128)S(1)}, u32[]{:S(2)}, u32[]{:S(2)}) async-start(f32[16,136,128]{2,1,0:T(8,128)} %pair.3), calls=%async_computation.3 | async-start | bytes 2228224 | tf_op jit(solution)/shard_map/all_to_all | solution.py:256
  160.2 20.2 %collective-permute-start.18 = (f32[264,256]{1,0:T(8,128)}, f32[264,256]{1,0:T(8,128)S(1)}, u32[]{:S(2)}, u32[]{:S(2)}) collective-permute-start(f32[264,256]{1,0:T(8,128)} %get-tuple-element.78), channel_id=1, source_target_pairs={{0,2},{2,4},{4,6},{6,0},{1,3},{3,5},{5,7},{7,1},{8,10},{10,12},{12... | collective-permute-start | bytes 811016 | tf_op jit(solution)/shard_map/ppermute | solution.py:264
  162.1 18.4 %collective-permute-start.19 = (f32[264,256]{1,0:T(8,128)S(1)}, f32[264,256]{1,0:T(8,128)S(1)}, u32[]{:S(2)}, u32[]{:S(2)}) collective-permute-start(f32[264,256]{1,0:T(8,128)S(1)} %get-tuple-element.79), channel_id=1, source_target_pairs={{0,4},{2,6},{4,0},{6,2},{1,5},{3,7},{5,1},{7,3},{8,12},{10,14},{12... | collective-permute-start | bytes 811016 | tf_op jit(solution)/shard_map/ppermute | solution.py:264
  164.4 16.0 %collective-permute-start.20 = (f32[264,256]{1,0:T(8,128)S(1)}, f32[264,256]{1,0:T(8,128)S(1)}, u32[]{:S(2)}, u32[]{:S(2)}) collective-permute-start(f32[264,256]{1,0:T(8,128)S(1)} %get-tuple-element.80), channel_id=1, source_target_pairs={{0,6},{2,0},{4,2},{6,4},{1,7},{3,1},{5,3},{7,5},{8,14},{10,8},{12,... | collective-permute-start | bytes 811016 | tf_op jit(solution)/shard_map/ppermute | solution.py:264

commit v7 on v6

--- a/solution.py
+++ b/solution.py
@@ -17,7 +17,7 @@
 AXES = ("zh", "x", "zl", "y", "core")
 SIZES = (2, 4, 2, 4, 2)
 TILE = ("zh", "zl", "core", "x")
-RANKS = ("zl", "zh", "x")
+RANKS = ("zh", "x", "zl")
 N_Y = 4
 N_R = 8
 N_P = 16
@@ -99,28 +99,38 @@
     )(record, table)
 
 
-def sweep_kernel(first, at_ref, s_ref, h_ref, w0, w1, w2, w3, *refs):
-    before, (n0, n1, n2, n3, sums_ref, ht_ref) = (() if first else refs[:4]), refs[-6:]
-    blocks, rank, half = h_ref.shape
-    span = blocks * half
+def sweep_kernel(first, at_ref, s_hbm, h_ref, w0, w1, w2, w3, *refs):
+    before, (n0, n1, n2, n3, sums_ref, ht_ref, s_ref, sem) = (() if first else refs[:4]), refs[-8:]
+    blocks, half = h_ref.shape[1], h_ref.shape[3]
+    rank, span = ht_ref.shape[1], blocks * half
+    run = half // 2
+    core = at_ref[0 if first else 1]
+
+    def fetch(p, t, i):
+        row = ((i % 2 * blocks + i // 2) * 2 + core) * run
+        column = lax.rem(at_ref[2] + 2 * p + t, N_Y) * rank
+        return pltpu.make_async_copy(
+            s_hbm.at[pl.ds(pl.multiple_of(row, run), run), pl.ds(pl.multiple_of(column, rank), rank)],
+            s_ref.at[p, i * run : (i + 1) * run, t * rank : (t + 1) * rank],
+            sem.at[p, t, i],
+        )
+
+    pieces = [(t, i) for t in range(2) for i in range(2 * blocks)]
+    for p in range(2):
+        for t, i in pieces:
+            fetch(p, t, i).start()
+    h = [h_ref[:, b].reshape(rank, half) for b in range(blocks)]
     for b in range(blocks):
-        ht_ref[b * half : (b + 1) * half, :] = h_ref[b].T
+        ht_ref[b * half : (b + 1) * half, :] = h[b].T
     rowsum = jnp.dot(jnp.ones((8, span), jnp.bfloat16), ht_ref[...], preferred_element_type=jnp.float32)
     colsum = jnp.zeros((rank, 1), jnp.float32)
-    run = half // 2
-    core = at_ref[0 if first else 1]
-    rows = [
-        pl.ds(pl.multiple_of(((zh * blocks + b) * 2 + core) * run, run), run) for b in range(blocks) for zh in range(2)
-    ]
     for p in range(2):
         wt = jnp.concatenate([w[...] for w in ((w0, w1), (w2, w3))[p]], axis=0).T
         colsum = colsum + jnp.sum(wt.astype(jnp.float32), axis=1, keepdims=True)
-        columns = [
-            pl.ds(pl.multiple_of(lax.rem(at_ref[2] + 2 * p + t, N_Y) * rank, rank), rank) for t in range(2)
-        ]
-        s = jnp.concatenate([jnp.concatenate([s_ref[r, c] for c in columns], axis=1) for r in rows], axis=0)
         recon = jnp.dot(ht_ref[...], wt, preferred_element_type=jnp.float32)
-        quotient = (s.astype(jnp.float32) / recon).astype(jnp.bfloat16)
+        for t, i in pieces:
+            fetch(p, t, i).wait()
+        quotient = (s_ref[p].astype(jnp.float32) / recon).astype(jnp.bfloat16)
         hn = lax.dot_general(wt, quotient, (((1,), (1,)), ((), ())), preferred_element_type=jnp.float32)
         if p == 0:
             sums_ref[:, :span] = hn
@@ -128,7 +138,7 @@
             sums_ref[:, :span] += hn
         wn = None
         for b in range(blocks):
-            part = jnp.dot(h_ref[b], quotient[b * half : (b + 1) * half], preferred_element_type=jnp.float32)
+            part = jnp.dot(h[b], quotient[b * half : (b + 1) * half], preferred_element_type=jnp.float32)
             wn = part if wn is None else wn + part
         for t in range(2):
             ref = (n0, n1, n2, n3)[2 * p + t]
@@ -144,14 +154,18 @@
 
 def half_sweep(at, spectra, h, ws, before=()):
     frames, rows = spectra.shape
-    blocks, rank, half = h.shape
+    blocks, half, rank = h.shape[1], h.shape[3], ws[0].shape[1]
     return pl.pallas_call(
         functools.partial(sweep_kernel, not before),
-        in_specs=whole(1, pltpu.SMEM) + whole(6 + len(before)),
+        in_specs=whole(1, pltpu.SMEM) + whole(1, pl.ANY) + whole(5 + len(before)),
         out_specs=whole(5),
         out_shape=[jax.ShapeDtypeStruct((rank + 8, rank), jnp.float32)] * 4
         + [jax.ShapeDtypeStruct((rank, blocks * half + LANES), jnp.float32)],
-        scratch_shapes=[pltpu.VMEM((blocks * half, rank), jnp.bfloat16)],
+        scratch_shapes=[
+            pltpu.VMEM((blocks * half, rank), jnp.bfloat16),
+            pltpu.VMEM((2, blocks * half, 2 * rank), jnp.bfloat16),
+            pltpu.SemaphoreType.DMA((2, 2, 2 * blocks)),
+        ],
         compiler_params=pltpu.CompilerParams(vmem_limit_bytes=28 << 20),
         cost_estimate=pl.CostEstimate(flops=3 * frames * rows * rank, bytes_accessed=4 << 20, transcendentals=0),
         name="sweep_a" if not before else "sweep_b",
@@ -171,8 +185,8 @@
         for zl in range(2):
             for c in range(4):
                 columns = slice(zl * half + c * LANES, zl * half + (c + 1) * LANES)
-                out_ref[zl * N_R + r, c * each : (c + 1) * each, :] = a_ref[rows, columns] + b_ref[rows, columns]
-            out_ref[zl * N_R + r, 4 * each :, :] = tail
+                out_ref[r * 2 + zl, c * each : (c + 1) * each, :] = a_ref[rows, columns] + b_ref[rows, columns]
+            out_ref[r * 2 + zl, 4 * each :, :] = tail
 
 
 def pair(a, b, each):
@@ -231,59 +245,54 @@
     )(*parts, w)
 
 
-def assemble_kernel(at_ref, z0, z1, z2, z3, out_ref):
-    each = z0.shape[1]
-    for i, ref in enumerate((z0, z1, z2, z3)):
-        z = lax.rem(at_ref[4] + i, 4)
-        for t in range(4):
-            r = (z // 2) * 4 + lax.rem(at_ref[3] + t, 4)
-            out_ref[lax.rem(z, 2), pl.ds(pl.multiple_of(r * each, each), each), :] = ref[t]
-
-
-def assemble(at, zs):
-    _, each, half = zs[0].shape
-    return pl.pallas_call(
-        assemble_kernel,
-        in_specs=whole(1, pltpu.SMEM) + whole(4),
+def spread_kernel(at_ref, own_ref, oth_ref, out_ref):
+    for i in range(N_R):
+        out_ref[i, at_ref[3]] = own_ref[...]
+        out_ref[i, 1 - at_ref[3]] = oth_ref[...]
+
+
+def spread(at, own, oth):
+    return pl.pallas_call(
+        spread_kernel,
+        in_specs=whole(1, pltpu.SMEM) + whole(2),
         out_specs=whole(1)[0],
-        out_shape=jax.ShapeDtypeStruct((2, N_R * each, half), jnp.bfloat16),
+        out_shape=jax.ShapeDtypeStruct((N_R, 2, *own.shape), jnp.bfloat16),
         compiler_params=pltpu.CompilerParams(vmem_limit_bytes=12 << 20),
-        name="assemble",
-    )(at, *zs)
+        name="spread",
+    )(at, own, oth)
 
 
 def exchange(x, axes):
     return lax.all_to_all(x, axes, 0, 0, tiled=True)
 
 
-def from_sibling(x):
-    return lax.ppermute(x, "core", [(0, 1), (1, 0)])
+def from_other(x, axis):
+    return lax.ppermute(x, axis, [(0, 1), (1, 0)])
 
 
 def sent_ahead(x, t):
     return lax.ppermute(x, "y", [(i, (i + t) % N_Y) for i in range(N_Y)])
 
 
-def taken_ahead(x, axes):
-    return [x] + [lax.ppermute(x, axes, [(i, (i - t) % 4) for i in range(4)]) for t in range(1, 4)]
+def taken_ahead(x):
+    return [x] + [lax.ppermute(x, "y", [(i, (i - t) % N_Y) for i in range(N_Y)]) for t in range(1, N_Y)]
 
 
 def local(samples, w, h):
-    rank = w.shape[1]
     record = samples.reshape(samples.shape[2], samples.shape[3])
-    core, y = lax.axis_index("core"), lax.axis_index("y")
-    x, z = lax.axis_index("x"), lax.axis_index(("zh", "zl"))
-    at = jnp.stack([1 - core, core, y, x, z]).astype(jnp.int32)
+    core, y, zl = lax.axis_index("core"), lax.axis_index("y"), lax.axis_index("zl")
+    at = jnp.stack([1 - core, core, y, zl]).astype(jnp.int32)
+    h_low = h.astype(jnp.bfloat16)
+    h_own = exchange(spread(at, h_low, from_other(h_low, "zl")), ("zh", "x"))
     energy = energies(record, dft_table())
     frames, rows = energy.shape[4:]
-    energy, w_low, h_low = lax.optimization_barrier((energy, w.astype(jnp.bfloat16), h.astype(jnp.bfloat16)))
-    h_own = assemble(at, taken_ahead(jnp.stack(taken_ahead(h_low, "x")), ("zh", "zl")))
-    h_oth = from_sibling(h_own)
-    ws = taken_ahead(w_low, "y")
+    energy, w_low = lax.optimization_barrier((energy, w.astype(jnp.bfloat16)))
+    ws = taken_ahead(w_low)
+    h_oth = from_other(h_own, "core")
     spectra = exchange(energy.reshape(2 * N_P, frames, rows), TILE).reshape(2 * N_P * frames, rows)
     for step in range(ITERS):
         *parts, s_oth = half_sweep(at, spectra, h_oth, ws)
-        s_got = from_sibling(s_oth)
+        s_got = from_other(s_oth, "core")
         n0, n1, n2, n3, s_own = half_sweep(at, spectra, h_own, ws, parts)
         w_parts = [n0] + [sent_ahead(n, t + 1) for t, n in enumerate((n1, n2, n3))]
         h_parts = exchange(pair(s_own, s_got, h.shape[0]), RANKS)
@@ -291,10 +300,10 @@
         w_parts, low, h = lax.optimization_barrier((w_parts, low, h))
         w, w_low = w_update(w_parts, w)
         if step + 1 < ITERS:
-            ws = taken_ahead(w_low, "y")
+            ws = taken_ahead(w_low)
             ws, h_own = lax.optimization_barrier((ws, exchange(low, RANKS)))
-            h_own = h_own.reshape(2, rank, -1)
-            h_oth = from_sibling(h_own)
+            h_own = h_own.reshape(N_R, 2, *h.shape)
+            h_oth = from_other(h_own, "core")
     return (w, h)
 
 

time: 182 us -> 171 us (0.940)
  waiting for transfers between devices: 92.2 us -> 85.1 us
  starting transfers between devices: 56.3 us -> 52.9 us
    ppermute x16 -> x11, waiting for transfers between devices: 62.2 us -> 13.2 us  [the longest x6 9.43 us: taken_ahead(): lax.ppermute(x, 'y', [(i, (i - t) % N_Y) for i in range(N_Y)])]
    all_to_all x4 -> x5, waiting for transfers between devices: 29.9 us -> 71.9 us  [exchange(): return lax.all_to_all(x, axes, 0, 0, tiled=True)]
    ppermute x16 -> x11, starting transfers between devices: 23.3 us -> 14.3 us  [the longest x6 11.7 us: taken_ahead(): lax.ppermute(x, 'y', [(i, (i - t) % N_Y) for i in range(N_Y)])]
    all_to_all x4 -> x5, starting transfers between devices: 22.4 us -> 27.4 us  [exchange(): return lax.all_to_all(x, axes, 0, 0, tiled=True)]
  transfers between devices with their start and end apart: 26 -> 22, of which waited for: 14 -> 11; matrix products, arithmetic and copies ran while one was open for 0% -> 0% of each run, Pallas kernels for 6% -> 10%
where the time goes in v7:
time: 171 us; the launch traced here: 170 us
  waiting for transfers between devices  85.1 us (50%)
  starting transfers between devices  52.9 us (31%)
  Pallas kernels  30.2 us (18%)
    all_to_all x5, waiting for transfers between devices, exchange(): return lax.all_to_all(x, axes, 0, 0, tiled=True)  71.9 us
    all_to_all x5, starting transfers between devices, exchange(): return lax.all_to_all(x, axes, 0, 0, tiled=True)  27.4 us
    pallas_call x4, Pallas kernels, half_sweep(): pl.pallas_call(functools.partial(sweep_kernel, not before), in_specs=whol...  16.1 us
    ppermute x6, starting transfers between devices, taken_ahead(): lax.ppermute(x, 'y', [(i, (i - t) % N_Y) for i in range(N_Y)])  11.7 us
    ppermute x6, starting transfers between devices, sent_ahead(): return lax.ppermute(x, 'y', [(i, (i + t) % N_Y) for i in range(N_Y)])  11.1 us
    ppermute x6, waiting for transfers between devices, taken_ahead(): lax.ppermute(x, 'y', [(i, (i - t) % N_Y) for i in range(N_Y)])  9.43 us
    pallas_call x1, Pallas kernels, energies(): pl.pallas_call(energy_kernel, in_specs=[pl.BlockSpec(memory_space=pl.ANY)...  7.47 us
    ppermute x5, waiting for transfers between devices, from_other(): return lax.ppermute(x, axis, [(0, 1), (1, 0)])  3.75 us
  transfers between devices with their start and end apart: 22, of which 11 were waited for; matrix products, arithmetic and copies ran while one was open for 0% of the time, Pallas kernels for 10%

profile of v7, /device:TPU:0, one launch (start us, length us, event | category | flops | bytes accessed | tf_op | source)
XLA Modules:
  0.0 170.0 jit_solution(15807146182988319481)
XLA Ops:
  0.6 0.0 copy-start
  0.6 0.9 convert_element_type.11.own_ref
  1.5 2.0 %collective-permute-start = (bf16[32,512]{1,0:T(8,128)(2,1)S(1)}, bf16[32,512]{1,0:T(8,128)(2,1)S(1)}, u32[]{:S(2)}, u32[]{:S(2)}) collective-permute-start(bf16[32,512]{1,0:T(8,128)(2,1)S(1)} %convert_element_type.11.own_ref), channel_id=1, source_target_pairs={{0,8},{8,0},{1,9},{9,1},{2,10},{10,2},{3,11},{11,3},{4,12},{12,4},... | collective-permute-start | bytes 98312 | tf_op jit(solution)/shard_map/ppermute | solution.py:270
  3.5 0.1 pad_add_fusion.at_ref
  3.6 1.8 %collective-permute-done.oth_ref = bf16[32,512]{1,0:T(8,128)(2,1)S(1)} collective-permute-done((bf16[32,512]{1,0:T(8,128)(2,1)S(1)}, bf16[32,512]{1,0:T(8,128)(2,1)S(1)}, u32[]{:S(2)}, u32[]{:S(2)}) %collective-permute-start) | collective-permute-done | bytes 32800 | tf_op jit(solution)/shard_map/ppermute | solution.py:270
  5.4 1.4 spread.1
  6.8 7.7 %all-to-all-start.1 = ((bf16[8,2,32,512]{3,2,1,0:T(8,128)(2,1)}), bf16[8,2,32,512]{3,2,1,0:T(8,128)(2,1)S(1)}, u32[]{:S(2)}, u32[]{:S(2)}) async-start(bf16[8,2,32,512]{3,2,1,0:T(8,128)(2,1)} %spread.1), calls=%async_computation.1 | async-start | bytes 1048576 | tf_op jit(solution)/shard_map/all_to_all | solution.py:266
  14.5 0.0 copy-done
  14.5 7.5 %energy.1 = bf16[2,2,2,4,64,1024]{5,4,3,2,1,0:T(8,128)(2,1)} custom-call(bf16[256,16384]{1,0:T(8,128)(2,1)} %bitcast.11, bf16[256,256]{1,0:T(8,128)(2,1)} %constant.17.table_ref), custom_call_target="tpu_custom_call" | custom-call | flops 2147483648 | bytes 12582912 | tf_op jit(solution)/shard_map/energy/pallas_call | solution.py:83
  22.0 2.9 %all-to-all-done.1.h_ref = bf16[8,2,32,512]{3,2,1,0:T(8,128)(2,1)S(1)} async-done(((bf16[8,2,32,512]{3,2,1,0:T(8,128)(2,1)}), bf16[8,2,32,512]{3,2,1,0:T(8,128)(2,1)S(1)}, u32[]{:S(2)}, u32[]{:S(2)}) %all-to-all-start.1) | async-done | bytes 524320 | tf_op jit(solution)/shard_map/all_to_all | solution.py:266
  25.0 5.0 %all-to-all-start = ((bf16[32,64,1024]{2,1,0:T(8,128)(2,1)}), bf16[32,64,1024]{2,1,0:T(8,128)(2,1)}, u32[]{:S(2)}, u32[]{:S(2)}) async-start(bf16[32,64,1024]{2,1,0:T(8,128)(2,1)} %bitcast.10), calls=%async_computation | async-start | bytes 8388608 | tf_op jit(solution)/shard_map/all_to_all | solution.py:266
  29.9 0.3 collective-permute-start.4
  30.2 1.6 collective-permute-start.3
  31.8 2.9 %collective-permute-start.2 = (bf16[256,256]{1,0:T(8,128)(2,1)S(1)}, bf16[256,256]{1,0:T(8,128)(2,1)S(1)}, u32[]{:S(2)}, u32[]{:S(2)}) collective-permute-start(bf16[256,256]{1,0:T(8,128)(2,1)S(1)} %convert_element_type.10.w0), channel_id=1, source_target_pairs={{0,4},{2,6},{4,0},{6,2},{1,5},{3,7},{5,1},{7,3},{8,12},{10,14},{12... | collective-permute-start | bytes 393224 | tf_op jit(solution)/shard_map/ppermute | solution.py:278
  34.7 1.3 collective-permute-start.1
  36.0 1.2 collective-permute-done.3.w3
  37.2 4.0 %collective-permute-done.2.w2 = bf16[256,256]{1,0:T(8,128)(2,1)S(1)} collective-permute-done((bf16[256,256]{1,0:T(8,128)(2,1)S(1)}, bf16[256,256]{1,0:T(8,128)(2,1)S(1)}, u32[]{:S(2)}, u32[]{:S(2)}) %collective-permute-start.2) | collective-permute-done | bytes 131104 | tf_op jit(solution)/shard_map/ppermute | solution.py:278
  41.2 0.0 collective-permute-done.1.w1
  41.2 0.0 collective-permute-done.4.h_ref
  41.2 39.8 %all-to-all-done = bf16[32,64,1024]{2,1,0:T(8,128)(2,1)} async-done(((bf16[32,64,1024]{2,1,0:T(8,128)(2,1)}), bf16[32,64,1024]{2,1,0:T(8,128)(2,1)}, u32[]{:S(2)}, u32[]{:S(2)}) %all-to-all-start) | async-done | bytes 4194336 | tf_op jit(solution)/shard_map/all_to_all | solution.py:266
  81.0 4.0 %sweep_a.2 = (f32[264,256]{1,0:T(8,128)S(1)}, f32[264,256]{1,0:T(8,128)S(1)}, f32[264,256]{1,0:T(8,128)S(1)}, f32[264,256]{1,0:T(8,128)S(1)}, f32[256,1152]{1,0:T(8,128)S(1)}) custom-call(s32[4]{0:T(128)S(1)} %pad_add_fusion.at_ref, bf16[2048,1024]{1,0:T(8,128)(2,1)} %bitcast.6.s_hbm, bf16[8,2,32,512]{3,2,1,0:T(8,128)(2,1)S(1)} %collective-permute-done.4.h_ref, ...), custom_call_target="tpu_custom_call" | custom-call | flops 1610612736 | bytes 4194304 | tf_op jit(solution)/shard_map/sweep_a/pallas_call | solution.py:158
  85.0 0.1 collective-permute-start.8
  85.1 4.0 %sweep_b.2 = (f32[264,256]{1,0:T(8,128)S(1)}, f32[264,256]{1,0:T(8,128)}, f32[264,256]{1,0:T(8,128)S(1)}, f32[264,256]{1,0:T(8,128)S(1)}, f32[256,1152]{1,0:T(8,128)S(1)}) custom-call(s32[4]{0:T(128)S(1)} %pad_add_fusion.at_ref, bf16[2048,1024]{1,0:T(8,128)(2,1)} %bitcast.6.s_hbm, bf16[8,2,32,512]{3,2,1,0:T(8,128)(2,1)S(1)} %all-to-all-done.1.h_ref, ...), custom_call_target="tpu_custom_call" | custom-call | flops 1610612736 | bytes 4194304 | tf_op jit(solution)/shard_map/sweep_b/pallas_call | solution.py:158
  89.2 0.0 collective-permute-done.8.b_ref
  89.2 1.2 pair.2
  90.3 0.0 copy-start.1
  90.3 5.3 %all-to-all-start.2 = ((f32[16,136,128]{2,1,0:T(8,128)}), f32[16,136,128]{2,1,0:T(8,128)S(1)}, u32[]{:S(2)}, u32[]{:S(2)}) async-start(f32[16,136,128]{2,1,0:T(8,128)} %pair.2), calls=%async_computation.2 | async-start | bytes 2228224 | tf_op jit(solution)/shard_map/all_to_all | solution.py:266
  95.6 1.6 collective-permute-start.5
  97.2 2.9 %collective-permute-start.6 = (f32[264,256]{1,0:T(8,128)S(1)}, f32[264,256]{1,0:T(8,128)S(1)}, u32[]{:S(2)}, u32[]{:S(2)}) collective-permute-start(f32[264,256]{1,0:T(8,128)S(1)} %get-tuple-element.54), channel_id=1, source_target_pairs={{0,4},{2,6},{4,0},{6,2},{1,5},{3,7},{5,1},{7,3},{8,12},{10,14},{12... | collective-permute-start | bytes 811016 | tf_op jit(solution)/shard_map/ppermute | solution.py:274
  100.1 1.3 collective-permute-start.7
  101.5 13.8 %all-to-all-done.2.parts_ref = f32[16,136,128]{2,1,0:T(8,128)S(1)} async-done(((f32[16,136,128]{2,1,0:T(8,128)}), f32[16,136,128]{2,1,0:T(8,128)S(1)}, u32[]{:S(2)}, u32[]{:S(2)}) %all-to-all-start.2) | async-done | bytes 1114144 | tf_op jit(solution)/shard_map/all_to_all | solution.py:266
  115.3 0.0 copy-done.1
  115.3 1.0 h_update.2
  116.3 0.0 collective-permute-done.5.p1
  116.3 0.0 collective-permute-done.6.p2
  116.3 0.0 collective-permute-done.7.p3
  116.3 3.6 %all-to-all-start.3 = ((bf16[16,32,512]{2,1,0:T(8,128)(2,1)}), bf16[16,32,512]{2,1,0:T(8,128)(2,1)S(1)}, u32[]{:S(2)}, u32[]{:S(2)}) async-start(bf16[16,32,512]{2,1,0:T(8,128)(2,1)} %get-tuple-element.65), calls=%async_computation.3 | async-start | bytes 1048576 | tf_op jit(solution)/shard_map/all_to_all | solution.py:266
  119.9 0.2 w_update.2
  120.0 1.6 collective-permute-start.11
  121.7 2.9 %collective-permute-start.10 = (bf16[256,256]{1,0:T(8,128)(2,1)S(1)}, bf16[256,256]{1,0:T(8,128)(2,1)S(1)}, u32[]{:S(2)}, u32[]{:S(2)}) collective-permute-start(bf16[256,256]{1,0:T(8,128)(2,1)S(1)} %get-tuple-element.67.w0), channel_id=1, source_target_pairs={{0,4},{2,6},{4,0},{6,2},{1,5},{3,7},{5,1},{7,3},{8,12},{10,14},{12... | collective-permute-start | bytes 393224 | tf_op jit(solution)/shard_map/ppermute | solution.py:278
  124.6 1.3 collective-permute-start.9
  125.9 0.8 collective-permute-done.11.w3
  126.8 3.5 %collective-permute-done.10.w2 = bf16[256,256]{1,0:T(8,128)(2,1)S(1)} collective-permute-done((bf16[256,256]{1,0:T(8,128)(2,1)S(1)}, bf16[256,256]{1,0:T(8,128)(2,1)S(1)}, u32[]{:S(2)}, u32[]{:S(2)}) %collective-permute-start.10) | collective-permute-done | bytes 131104 | tf_op jit(solution)/shard_map/ppermute | solution.py:278
  130.2 0.0 collective-permute-done.9.w1
  130.2 1.0 all-to-all-done.3
  131.2 0.0 collective-permute-start.12
  131.2 1.9 %collective-permute-done.12.h_ref = bf16[8,2,32,512]{3,2,1,0:T(8,128)(2,1)S(1)} collective-permute-done((bf16[8,2,32,512]{3,2,1,0:T(8,128)(2,1)S(1)}, bf16[8,2,32,512]{3,2,1,0:T(8,128)(2,1)S(1)}, u32[]{:S(2)}, u32[]{:S(2)}) %collective-permute-start.12) | collective-permute-done | bytes 524320 | tf_op jit(solution)/shard_map/ppermute | solution.py:270
  133.1 4.0 %sweep_a.3 = (f32[264,256]{1,0:T(8,128)S(1)}, f32[264,256]{1,0:T(8,128)S(1)}, f32[264,256]{1,0:T(8,128)S(1)}, f32[264,256]{1,0:T(8,128)S(1)}, f32[256,1152]{1,0:T(8,128)S(1)}) custom-call(s32[4]{0:T(128)S(1)} %pad_add_fusion.at_ref, bf16[2048,1024]{1,0:T(8,128)(2,1)} %bitcast.6.s_hbm, bf16[8,2,32,512]{3,2,1,0:T(8,128)(2,1)S(1)} %collective-permute-done.12.h_ref, ...), custom_call_target="tpu_custom_call" | custom-call | flops 1610612736 | bytes 4194304 | tf_op jit(solution)/shard_map/sweep_a/pallas_call | solution.py:158
  137.1 0.2 collective-permute-start.16
  137.3 4.0 %sweep_b.3 = (f32[264,256]{1,0:T(8,128)S(1)}, f32[264,256]{1,0:T(8,128)}, f32[264,256]{1,0:T(8,128)S(1)}, f32[264,256]{1,0:T(8,128)S(1)}, f32[256,1152]{1,0:T(8,128)S(1)}) custom-call(s32[4]{0:T(128)S(1)} %pad_add_fusion.at_ref, bf16[2048,1024]{1,0:T(8,128)(2,1)} %bitcast.6.s_hbm, bf16[8,2,32,512]{3,2,1,0:T(8,128)(2,1)S(1)} %bitcast.9, ...), custom_call_target="tpu_custom_call" | custom-call | flops 1610612736 | bytes 4194304 | tf_op jit(solution)/shard_map/sweep_b/pallas_call | solution.py:158
  141.4 0.0 collective-permute-done.16.b_ref
  141.4 1.1 pair.3
  142.5 5.9 %all-to-all-start.4 = ((f32[16,136,128]{2,1,0:T(8,128)}), f32[16,136,128]{2,1,0:T(8,128)S(1)}, u32[]{:S(2)}, u32[]{:S(2)}) async-start(f32[16,136,128]{2,1,0:T(8,128)} %pair.3), calls=%async_computation.4 | async-start | bytes 2228224 | tf_op jit(solution)/shard_map/all_to_all | solution.py:266
  148.5 1.3 collective-permute-start.13
  149.7 2.9 %collective-permute-start.14 = (f32[264,256]{1,0:T(8,128)S(1)}, f32[264,256]{1,0:T(8,128)S(1)}, u32[]{:S(2)}, u32[]{:S(2)}) collective-permute-start(f32[264,256]{1,0:T(8,128)S(1)} %get-tuple-element.77), channel_id=1, source_target_pairs={{0,4},{2,6},{4,0},{6,2},{1,5},{3,7},{5,1},{7,3},{8,12},{10,14},{12... | collective-permute-start | bytes 811016 | tf_op jit(solution)/shard_map/ppermute | solution.py:274
  152.6 1.1 collective-permute-start.15
  153.7 14.4 %all-to-all-done.4.parts_ref = f32[16,136,128]{2,1,0:T(8,128)S(1)} async-done(((f32[16,136,128]{2,1,0:T(8,128)}), f32[16,136,128]{2,1,0:T(8,128)S(1)}, u32[]{:S(2)}, u32[]{:S(2)}) %all-to-all-start.4) | async-done | bytes 1114144 | tf_op jit(solution)/shard_map/all_to_all | solution.py:266
  168.1 1.0 h_update.3
  169.1 0.0 collective-permute-done.13.p1
  169.1 0.0 collective-permute-done.14.p2
  169.1 0.0 collective-permute-done.15.p3
  169.1 0.9 w_update.3
  (1 shorter events, 0.0 us)
Async XLA Ops:
  0.6 13.9 %copy-start = (f32[256,256]{1,0:T(8,128)S(1)}, f32[256,256]{1,0:T(8,128)}, u32[]{:S(2)}) copy-start(f32[256,256]{1,0:T(8,128)} %w_ref.1) | copy-start | bytes 786436
  1.5 3.9 %collective-permute-start = (bf16[32,512]{1,0:T(8,128)(2,1)S(1)}, bf16[32,512]{1,0:T(8,128)(2,1)S(1)}, u32[]{:S(2)}, u32[]{:S(2)}) collective-permute-start(bf16[32,512]{1,0:T(8,128)(2,1)S(1)} %convert_element_type.11.own_ref), channel_id=1, source_target_pairs={{0,8},{8,0},{1,9},{9,1},{2,10},{10,2},{3,11},{11,3},{4,12},{12,4},... | collective-permute-start | bytes 98312 | tf_op jit(solution)/shard_map/ppermute | solution.py:270
  6.8 18.1 %all-to-all-start.1 = ((bf16[8,2,32,512]{3,2,1,0:T(8,128)(2,1)}), bf16[8,2,32,512]{3,2,1,0:T(8,128)(2,1)S(1)}, u32[]{:S(2)}, u32[]{:S(2)}) async-start(bf16[8,2,32,512]{3,2,1,0:T(8,128)(2,1)} %spread.1), calls=%async_computation.1 | async-start | bytes 1048576 | tf_op jit(solution)/shard_map/all_to_all | solution.py:266
  25.0 56.1 %all-to-all-start = ((bf16[32,64,1024]{2,1,0:T(8,128)(2,1)}), bf16[32,64,1024]{2,1,0:T(8,128)(2,1)}, u32[]{:S(2)}, u32[]{:S(2)}) async-start(bf16[32,64,1024]{2,1,0:T(8,128)(2,1)} %bitcast.10), calls=%async_computation | async-start | bytes 8388608 | tf_op jit(solution)/shard_map/all_to_all | solution.py:266
  29.9 11.3 %collective-permute-start.4 = (bf16[8,2,32,512]{3,2,1,0:T(8,128)(2,1)S(1)}, bf16[8,2,32,512]{3,2,1,0:T(8,128)(2,1)S(1)}, u32[]{:S(2)}, u32[]{:S(2)}) collective-permute-start(bf16[8,2,32,512]{3,2,1,0:T(8,128)(2,1)S(1)} %all-to-all-done.1.h_ref), channel_id=1, source_target_pairs={{0,1},{1,0},{2,3},{3,2},{4,5},{5,4},{6,7},{7,6},{8,9},{9,8},{10,11... | collective-permute-start | bytes 1572872 | tf_op jit(solution)/shard_map/ppermute | solution.py:270
  30.2 7.0 %collective-permute-start.3 = (bf16[256,256]{1,0:T(8,128)(2,1)S(1)}, bf16[256,256]{1,0:T(8,128)(2,1)S(1)}, u32[]{:S(2)}, u32[]{:S(2)}) collective-permute-start(bf16[256,256]{1,0:T(8,128)(2,1)S(1)} %convert_element_type.10.w0), channel_id=1, source_target_pairs={{0,2},{2,4},{4,6},{6,0},{1,3},{3,5},{5,7},{7,1},{8,10},{10,12},{12... | collective-permute-start | bytes 393224 | tf_op jit(solution)/shard_map/ppermute | solution.py:278
  31.8 9.4 %collective-permute-start.2 = (bf16[256,256]{1,0:T(8,128)(2,1)S(1)}, bf16[256,256]{1,0:T(8,128)(2,1)S(1)}, u32[]{:S(2)}, u32[]{:S(2)}) collective-permute-start(bf16[256,256]{1,0:T(8,128)(2,1)S(1)} %convert_element_type.10.w0), channel_id=1, source_target_pairs={{0,4},{2,6},{4,0},{6,2},{1,5},{3,7},{5,1},{7,3},{8,12},{10,14},{12... | collective-permute-start | bytes 393224 | tf_op jit(solution)/shard_map/ppermute | solution.py:278
  34.7 6.5 %collective-permute-start.1 = (bf16[256,256]{1,0:T(8,128)(2,1)S(1)}, bf16[256,256]{1,0:T(8,128)(2,1)S(1)}, u32[]{:S(2)}, u32[]{:S(2)}) collective-permute-start(bf16[256,256]{1,0:T(8,128)(2,1)S(1)} %convert_element_type.10.w0), channel_id=1, source_target_pairs={{0,6},{2,0},{4,2},{6,4},{1,7},{3,1},{5,3},{7,5},{8,14},{10,8},{12,... | collective-permute-start | bytes 393224 | tf_op jit(solution)/shard_map/ppermute | solution.py:278
  85.0 4.1 %collective-permute-start.8 = (f32[256,1152]{1,0:T(8,128)S(1)}, f32[256,1152]{1,0:T(8,128)S(1)}, u32[]{:S(2)}, u32[]{:S(2)}) collective-permute-start(f32[256,1152]{1,0:T(8,128)S(1)} %get-tuple-element.57), channel_id=1, source_target_pairs={{0,1},{1,0},{2,3},{3,2},{4,5},{5,4},{6,7},{7,6},{8,9},{9,8},{10,11... | collective-permute-start | bytes 3538952 | tf_op jit(solution)/shard_map/ppermute | solution.py:270
  90.3 24.9 %copy-start.1 = (f32[32,512]{1,0:T(8,128)S(1)}, f32[32,512]{1,0:T(8,128)}, u32[]{:S(2)}) copy-start(f32[32,512]{1,0:T(8,128)} %h_ref.1) | copy-start | bytes 196612
  90.3 24.9 %all-to-all-start.2 = ((f32[16,136,128]{2,1,0:T(8,128)}), f32[16,136,128]{2,1,0:T(8,128)S(1)}, u32[]{:S(2)}, u32[]{:S(2)}) async-start(f32[16,136,128]{2,1,0:T(8,128)} %pair.2), calls=%async_computation.2 | async-start | bytes 2228224 | tf_op jit(solution)/shard_map/all_to_all | solution.py:266
  95.6 20.7 %collective-permute-start.5 = (f32[264,256]{1,0:T(8,128)}, f32[264,256]{1,0:T(8,128)S(1)}, u32[]{:S(2)}, u32[]{:S(2)}) collective-permute-start(f32[264,256]{1,0:T(8,128)} %get-tuple-element.53), channel_id=1, source_target_pairs={{0,2},{2,4},{4,6},{6,0},{1,3},{3,5},{5,7},{7,1},{8,10},{10,12},{12... | collective-permute-start | bytes 811016 | tf_op jit(solution)/shard_map/ppermute | solution.py:274
  97.2 19.0 %collective-permute-start.6 = (f32[264,256]{1,0:T(8,128)S(1)}, f32[264,256]{1,0:T(8,128)S(1)}, u32[]{:S(2)}, u32[]{:S(2)}) collective-permute-start(f32[264,256]{1,0:T(8,128)S(1)} %get-tuple-element.54), channel_id=1, source_target_pairs={{0,4},{2,6},{4,0},{6,2},{1,5},{3,7},{5,1},{7,3},{8,12},{10,14},{12... | collective-permute-start | bytes 811016 | tf_op jit(solution)/shard_map/ppermute | solution.py:274
  100.1 16.1 %collective-permute-start.7 = (f32[264,256]{1,0:T(8,128)S(1)}, f32[264,256]{1,0:T(8,128)S(1)}, u32[]{:S(2)}, u32[]{:S(2)}) collective-permute-start(f32[264,256]{1,0:T(8,128)S(1)} %get-tuple-element.55), channel_id=1, source_target_pairs={{0,6},{2,0},{4,2},{6,4},{1,7},{3,1},{5,3},{7,5},{8,14},{10,8},{12,... | collective-permute-start | bytes 811016 | tf_op jit(solution)/shard_map/ppermute | solution.py:274
  116.3 14.9 %all-to-all-start.3 = ((bf16[16,32,512]{2,1,0:T(8,128)(2,1)}), bf16[16,32,512]{2,1,0:T(8,128)(2,1)S(1)}, u32[]{:S(2)}, u32[]{:S(2)}) async-start(bf16[16,32,512]{2,1,0:T(8,128)(2,1)} %get-tuple-element.65), calls=%async_computation.3 | async-start | bytes 1048576 | tf_op jit(solution)/shard_map/all_to_all | solution.py:266
  120.0 6.7 %collective-permute-start.11 = (bf16[256,256]{1,0:T(8,128)(2,1)S(1)}, bf16[256,256]{1,0:T(8,128)(2,1)S(1)}, u32[]{:S(2)}, u32[]{:S(2)}) collective-permute-start(bf16[256,256]{1,0:T(8,128)(2,1)S(1)} %get-tuple-element.67.w0), channel_id=1, source_target_pairs={{0,2},{2,4},{4,6},{6,0},{1,3},{3,5},{5,7},{7,1},{8,10},{10,12},{12... | collective-permute-start | bytes 393224 | tf_op jit(solution)/shard_map/ppermute | solution.py:278
  121.7 8.5 %collective-permute-start.10 = (bf16[256,256]{1,0:T(8,128)(2,1)S(1)}, bf16[256,256]{1,0:T(8,128)(2,1)S(1)}, u32[]{:S(2)}, u32[]{:S(2)}) collective-permute-start(bf16[256,256]{1,0:T(8,128)(2,1)S(1)} %get-tuple-element.67.w0), channel_id=1, source_target_pairs={{0,4},{2,6},{4,0},{6,2},{1,5},{3,7},{5,1},{7,3},{8,12},{10,14},{12... | collective-permute-start | bytes 393224 | tf_op jit(solution)/shard_map/ppermute | solution.py:278
  124.6 5.6 %collective-permute-start.9 = (bf16[256,256]{1,0:T(8,128)(2,1)S(1)}, bf16[256,256]{1,0:T(8,128)(2,1)S(1)}, u32[]{:S(2)}, u32[]{:S(2)}) collective-permute-start(bf16[256,256]{1,0:T(8,128)(2,1)S(1)} %get-tuple-element.67.w0), channel_id=1, source_target_pairs={{0,6},{2,0},{4,2},{6,4},{1,7},{3,1},{5,3},{7,5},{8,14},{10,8},{12,... | collective-permute-start | bytes 393224 | tf_op jit(solution)/shard_map/ppermute | solution.py:278
  131.2 1.9 %collective-permute-start.12 = (bf16[8,2,32,512]{3,2,1,0:T(8,128)(2,1)S(1)}, bf16[8,2,32,512]{3,2,1,0:T(8,128)(2,1)S(1)}, u32[]{:S(2)}, u32[]{:S(2)}) collective-permute-start(bf16[8,2,32,512]{3,2,1,0:T(8,128)(2,1)S(1)} %bitcast.8), channel_id=1, source_target_pairs={{0,1},{1,0},{2,3},{3,2},{4,5},{5,4},{6,7},{7,6},{8,9},{9,8},{10,11... | collective-permute-start | bytes 1572872 | tf_op jit(solution)/shard_map/ppermute | solution.py:270
  137.1 4.3 %collective-permute-start.16 = (f32[256,1152]{1,0:T(8,128)S(1)}, f32[256,1152]{1,0:T(8,128)S(1)}, u32[]{:S(2)}, u32[]{:S(2)}) collective-permute-start(f32[256,1152]{1,0:T(8,128)S(1)} %get-tuple-element.80), channel_id=1, source_target_pairs={{0,1},{1,0},{2,3},{3,2},{4,5},{5,4},{6,7},{7,6},{8,9},{9,8},{10,11... | collective-permute-start | bytes 3538952 | tf_op jit(solution)/shard_map/ppermute | solution.py:270
  142.5 25.6 %all-to-all-start.4 = ((f32[16,136,128]{2,1,0:T(8,128)}), f32[16,136,128]{2,1,0:T(8,128)S(1)}, u32[]{:S(2)}, u32[]{:S(2)}) async-start(f32[16,136,128]{2,1,0:T(8,128)} %pair.3), calls=%async_computation.4 | async-start | bytes 2228224 | tf_op jit(solution)/shard_map/all_to_all | solution.py:266
  148.5 20.7 %collective-permute-start.13 = (f32[264,256]{1,0:T(8,128)}, f32[264,256]{1,0:T(8,128)S(1)}, u32[]{:S(2)}, u32[]{:S(2)}) collective-permute-start(f32[264,256]{1,0:T(8,128)} %get-tuple-element.76), channel_id=1, source_target_pairs={{0,2},{2,4},{4,6},{6,0},{1,3},{3,5},{5,7},{7,1},{8,10},{10,12},{12... | collective-permute-start | bytes 811016 | tf_op jit(solution)/shard_map/ppermute | solution.py:274
  149.7 19.4 %collective-permute-start.14 = (f32[264,256]{1,0:T(8,128)S(1)}, f32[264,256]{1,0:T(8,128)S(1)}, u32[]{:S(2)}, u32[]{:S(2)}) collective-permute-start(f32[264,256]{1,0:T(8,128)S(1)} %get-tuple-element.77), channel_id=1, source_target_pairs={{0,4},{2,6},{4,0},{6,2},{1,5},{3,7},{5,1},{7,3},{8,12},{10,14},{12... | collective-permute-start | bytes 811016 | tf_op jit(solution)/shard_map/ppermute | solution.py:274
  152.6 16.5 %collective-permute-start.15 = (f32[264,256]{1,0:T(8,128)S(1)}, f32[264,256]{1,0:T(8,128)S(1)}, u32[]{:S(2)}, u32[]{:S(2)}) collective-permute-start(f32[264,256]{1,0:T(8,128)S(1)} %get-tuple-element.78), channel_id=1, source_target_pairs={{0,6},{2,0},{4,2},{6,4},{1,7},{3,1},{5,3},{7,5},{8,14},{10,8},{12,... | collective-permute-start | bytes 811016 | tf_op jit(solution)/shard_map/ppermute | solution.py:274

commit v8 on v7

--- a/solution.py
+++ b/solution.py
@@ -1,5 +1,6 @@
 import functools
 import math
+import operator
 
 import jax
 import jax.numpy as jnp
@@ -99,6 +100,10 @@
     )(record, table)
 
 
+def added(terms):
+    return functools.reduce(operator.add, terms)
+
+
 def sweep_kernel(first, at_ref, s_hbm, h_ref, w0, w1, w2, w3, *refs):
     before, (n0, n1, n2, n3, sums_ref, ht_ref, s_ref, sem) = (() if first else refs[:4]), refs[-8:]
     blocks, half = h_ref.shape[1], h_ref.shape[3]
@@ -123,23 +128,24 @@
     for b in range(blocks):
         ht_ref[b * half : (b + 1) * half, :] = h[b].T
     rowsum = jnp.dot(jnp.ones((8, span), jnp.bfloat16), ht_ref[...], preferred_element_type=jnp.float32)
-    colsum = jnp.zeros((rank, 1), jnp.float32)
+    wts = [jnp.concatenate([w[...] for w in pair], axis=0).T for pair in ((w0, w1), (w2, w3))]
+    colsum = added(jnp.sum(wt.astype(jnp.float32), axis=1, keepdims=True) for wt in wts)
+    cuts = [slice(b * half, (b + 1) * half) for b in range(blocks)]
+    recons = [[jnp.dot(ht_ref[cut, :], wt, preferred_element_type=jnp.float32) for cut in cuts] for wt in wts]
     for p in range(2):
-        wt = jnp.concatenate([w[...] for w in ((w0, w1), (w2, w3))[p]], axis=0).T
-        colsum = colsum + jnp.sum(wt.astype(jnp.float32), axis=1, keepdims=True)
-        recon = jnp.dot(ht_ref[...], wt, preferred_element_type=jnp.float32)
         for t, i in pieces:
             fetch(p, t, i).wait()
-        quotient = (s_ref[p].astype(jnp.float32) / recon).astype(jnp.bfloat16)
-        hn = lax.dot_general(wt, quotient, (((1,), (1,)), ((), ())), preferred_element_type=jnp.float32)
-        if p == 0:
-            sums_ref[:, :span] = hn
-        else:
-            sums_ref[:, :span] += hn
-        wn = None
-        for b in range(blocks):
-            part = jnp.dot(h[b], quotient[b * half : (b + 1) * half], preferred_element_type=jnp.float32)
-            wn = part if wn is None else wn + part
+    quotients = [
+        [(s_ref[p, cut].astype(jnp.float32) / recons[p][b]).astype(jnp.bfloat16) for b, cut in enumerate(cuts)]
+        for p in range(2)
+    ]
+    for b, cut in enumerate(cuts):
+        sums_ref[:, cut] = added(
+            lax.dot_general(wts[p], quotients[p][b], (((1,), (1,)), ((), ())), preferred_element_type=jnp.float32)
+            for p in range(2)
+        )
+    for p in range(2):
+        wn = added(jnp.dot(h[b], quotients[p][b], preferred_element_type=jnp.float32) for b in range(blocks))
         for t in range(2):
             ref = (n0, n1, n2, n3)[2 * p + t]
             part = wn[:, t * rank : (t + 1) * rank]
@@ -245,29 +251,41 @@
     )(*parts, w)
 
 
-def spread_kernel(at_ref, own_ref, oth_ref, out_ref):
-    for i in range(N_R):
-        out_ref[i, at_ref[3]] = own_ref[...]
-        out_ref[i, 1 - at_ref[3]] = oth_ref[...]
-
-
-def spread(at, own, oth):
+def spread_kernel(h_hbm, out_hbm, h_ref, low_ref, in_sem, out_sem):
+    fetch = pltpu.make_async_copy(h_hbm, h_ref, in_sem)
+    fetch.start()
+    fetch.wait()
+    low_ref[...] = h_ref[...].astype(jnp.bfloat16)
+    puts = [pltpu.make_async_copy(low_ref, out_hbm.at[i], out_sem.at[i]) for i in range(N_P)]
+    for put in puts:
+        put.start()
+    for put in puts:
+        put.wait()
+
+
+def spread(h):
     return pl.pallas_call(
         spread_kernel,
-        in_specs=whole(1, pltpu.SMEM) + whole(2),
-        out_specs=whole(1)[0],
-        out_shape=jax.ShapeDtypeStruct((N_R, 2, *own.shape), jnp.bfloat16),
-        compiler_params=pltpu.CompilerParams(vmem_limit_bytes=12 << 20),
+        in_specs=whole(1, pl.ANY),
+        out_specs=whole(1, pl.ANY)[0],
+        out_shape=jax.ShapeDtypeStruct((N_P, *h.shape), jnp.bfloat16),
+        scratch_shapes=[
+            pltpu.VMEM(h.shape, jnp.float32),
+            pltpu.VMEM(h.shape, jnp.bfloat16),
+            pltpu.SemaphoreType.DMA,
+            pltpu.SemaphoreType.DMA((N_P,)),
+        ],
+        compiler_params=pltpu.CompilerParams(vmem_limit_bytes=56 << 20),
         name="spread",
-    )(at, own, oth)
+    )(h)
 
 
 def exchange(x, axes):
     return lax.all_to_all(x, axes, 0, 0, tiled=True)
 
 
-def from_other(x, axis):
-    return lax.ppermute(x, axis, [(0, 1), (1, 0)])
+def from_sibling(x):
+    return lax.ppermute(x, "core", [(0, 1), (1, 0)])
 
 
 def sent_ahead(x, t):
@@ -280,19 +298,18 @@
 
 def local(samples, w, h):
     record = samples.reshape(samples.shape[2], samples.shape[3])
-    core, y, zl = lax.axis_index("core"), lax.axis_index("y"), lax.axis_index("zl")
-    at = jnp.stack([1 - core, core, y, zl]).astype(jnp.int32)
-    h_low = h.astype(jnp.bfloat16)
-    h_own = exchange(spread(at, h_low, from_other(h_low, "zl")), ("zh", "x"))
+    core, y = lax.axis_index("core"), lax.axis_index("y")
+    at = jnp.stack([1 - core, core, y]).astype(jnp.int32)
+    h_own = exchange(spread(h), RANKS).reshape(N_R, 2, *h.shape)
     energy = energies(record, dft_table())
     frames, rows = energy.shape[4:]
     energy, w_low = lax.optimization_barrier((energy, w.astype(jnp.bfloat16)))
     ws = taken_ahead(w_low)
-    h_oth = from_other(h_own, "core")
+    h_oth = from_sibling(h_own)
     spectra = exchange(energy.reshape(2 * N_P, frames, rows), TILE).reshape(2 * N_P * frames, rows)
     for step in range(ITERS):
         *parts, s_oth = half_sweep(at, spectra, h_oth, ws)
-        s_got = from_other(s_oth, "core")
+        s_got = from_sibling(s_oth)
         n0, n1, n2, n3, s_own = half_sweep(at, spectra, h_own, ws, parts)
         w_parts = [n0] + [sent_ahead(n, t + 1) for t, n in enumerate((n1, n2, n3))]
         h_parts = exchange(pair(s_own, s_got, h.shape[0]), RANKS)
@@ -303,7 +320,7 @@
             ws = taken_ahead(w_low)
             ws, h_own = lax.optimization_barrier((ws, exchange(low, RANKS)))
             h_own = h_own.reshape(N_R, 2, *h.shape)
-            h_oth = from_other(h_own, "core")
+            h_oth = from_sibling(h_own)
     return (w, h)
 
 

time: 171 us -> 169 us (0.988)
  starting transfers between devices: 52.9 us -> 51 us
    ppermute x5 -> x4, starting transfers between devices: 2.59 us -> 0.49 us  [from_sibling(): return lax.ppermute(x, 'core', [(0, 1), (1, 0)])]
    ppermute x5 -> x4, waiting for transfers between devices: 3.75 us -> 1.92 us  [from_sibling(): return lax.ppermute(x, 'core', [(0, 1), (1, 0)])]
  transfers between devices with their start and end apart: 22 -> 21, of which waited for: 11 -> 10; matrix products, arithmetic and copies ran while one was open for 0% -> 0% of each run, Pallas kernels for 10% -> 11%
where the time goes in v8:
time: 169 us; the launch traced here: 168 us
  waiting for transfers between devices  84.4 us (50%)
  starting transfers between devices  51 us (30%)
  Pallas kernels  31.4 us (19%)
    all_to_all x5, waiting for transfers between devices, exchange(): return lax.all_to_all(x, axes, 0, 0, tiled=True)  73 us
    all_to_all x5, starting transfers between devices, exchange(): return lax.all_to_all(x, axes, 0, 0, tiled=True)  27.6 us
    pallas_call x4, Pallas kernels, half_sweep(): pl.pallas_call(functools.partial(sweep_kernel, not before), in_specs=whol...  16.8 us
    ppermute x6, starting transfers between devices, taken_ahead(): lax.ppermute(x, 'y', [(i, (i - t) % N_Y) for i in range(N_Y)])  11.7 us
    ppermute x6, starting transfers between devices, sent_ahead(): return lax.ppermute(x, 'y', [(i, (i + t) % N_Y) for i in range(N_Y)])  11.2 us
    ppermute x6, waiting for transfers between devices, taken_ahead(): lax.ppermute(x, 'y', [(i, (i - t) % N_Y) for i in range(N_Y)])  9.47 us
    pallas_call x1, Pallas kernels, energies(): pl.pallas_call(energy_kernel, in_specs=[pl.BlockSpec(memory_space=pl.ANY)...  7.46 us
  transfers between devices with their start and end apart: 21, of which 10 were waited for; matrix products, arithmetic and copies ran while one was open for 0% of the time, Pallas kernels for 11%

profile of v8, /device:TPU:0, one launch (start us, length us, event | category | flops | bytes accessed | tf_op | source)
XLA Modules:
  0.0 167.7 jit_solution(943296525264928663)
XLA Ops:
  0.6 0.0 copy-start
  0.6 1.8 %spread.1 = bf16[16,32,512]{2,1,0:T(8,128)(2,1)} custom-call(f32[32,512]{1,0:T(8,128)} %h_ref.1), custom_call_target="tpu_custom_call" | custom-call | tf_op jit(solution)/shard_map/spread/pallas_call | solution.py:267
  2.5 8.0 %all-to-all-start.1 = ((bf16[16,32,512]{2,1,0:T(8,128)(2,1)}), bf16[16,32,512]{2,1,0:T(8,128)(2,1)S(1)}, u32[]{:S(2)}, u32[]{:S(2)}) async-start(bf16[16,32,512]{2,1,0:T(8,128)(2,1)} %spread.1), calls=%async_computation.1 | async-start | bytes 1048576 | tf_op jit(solution)/shard_map/all_to_all | solution.py:284
  10.4 0.0 copy-done
  10.5 7.5 %energy.1 = bf16[2,2,2,4,64,1024]{5,4,3,2,1,0:T(8,128)(2,1)} custom-call(bf16[256,16384]{1,0:T(8,128)(2,1)} %bitcast.13, bf16[256,256]{1,0:T(8,128)(2,1)} %constant.14.table_ref), custom_call_target="tpu_custom_call" | custom-call | flops 2147483648 | bytes 12582912 | tf_op jit(solution)/shard_map/energy/pallas_call | solution.py:84
  17.9 4.0 %all-to-all-done.1 = bf16[16,32,512]{2,1,0:T(8,128)(2,1)S(1)} async-done(((bf16[16,32,512]{2,1,0:T(8,128)(2,1)}), bf16[16,32,512]{2,1,0:T(8,128)(2,1)S(1)}, u32[]{:S(2)}, u32[]{:S(2)}) %all-to-all-start.1) | async-done | bytes 524320 | tf_op jit(solution)/shard_map/all_to_all | solution.py:284
  21.9 4.9 %all-to-all-start = ((bf16[32,64,1024]{2,1,0:T(8,128)(2,1)}), bf16[32,64,1024]{2,1,0:T(8,128)(2,1)}, u32[]{:S(2)}, u32[]{:S(2)}) async-start(bf16[32,64,1024]{2,1,0:T(8,128)(2,1)} %bitcast.12), calls=%async_computation | async-start | bytes 8388608 | tf_op jit(solution)/shard_map/all_to_all | solution.py:284
  26.8 0.2 collective-permute-start.3
  27.0 1.6 collective-permute-start.2
  28.6 2.9 %collective-permute-start.1 = (bf16[256,256]{1,0:T(8,128)(2,1)S(1)}, bf16[256,256]{1,0:T(8,128)(2,1)S(1)}, u32[]{:S(2)}, u32[]{:S(2)}) collective-permute-start(bf16[256,256]{1,0:T(8,128)(2,1)S(1)} %convert_element_type.7.w0), channel_id=1, source_target_pairs={{0,4},{2,6},{4,0},{6,2},{1,5},{3,7},{5,1},{7,3},{8,12},{10,14},{12... | collective-permute-start | bytes 393224 | tf_op jit(solution)/shard_map/ppermute | solution.py:296
  31.5 1.3 collective-permute-start
  32.8 0.1 pad_add_fusion.at_ref
  32.9 1.2 collective-permute-done.2.w3
  34.1 4.0 %collective-permute-done.1.w2 = bf16[256,256]{1,0:T(8,128)(2,1)S(1)} collective-permute-done((bf16[256,256]{1,0:T(8,128)(2,1)S(1)}, bf16[256,256]{1,0:T(8,128)(2,1)S(1)}, u32[]{:S(2)}, u32[]{:S(2)}) %collective-permute-start.1) | collective-permute-done | bytes 131104 | tf_op jit(solution)/shard_map/ppermute | solution.py:296
  38.1 0.0 collective-permute-done.w1
  38.1 0.0 collective-permute-done.3.h_ref
  38.1 39.8 %all-to-all-done = bf16[32,64,1024]{2,1,0:T(8,128)(2,1)} async-done(((bf16[32,64,1024]{2,1,0:T(8,128)(2,1)}), bf16[32,64,1024]{2,1,0:T(8,128)(2,1)}, u32[]{:S(2)}, u32[]{:S(2)}) %all-to-all-start) | async-done | bytes 4194336 | tf_op jit(solution)/shard_map/all_to_all | solution.py:284
  77.9 3.9 %sweep_a.2 = (f32[264,256]{1,0:T(8,128)S(1)}, f32[264,256]{1,0:T(8,128)S(1)}, f32[264,256]{1,0:T(8,128)S(1)}, f32[264,256]{1,0:T(8,128)S(1)}, f32[256,1152]{1,0:T(8,128)S(1)}) custom-call(s32[3]{0:T(128)S(1)} %pad_add_fusion.at_ref, bf16[2048,1024]{1,0:T(8,128)(2,1)} %bitcast.5.s_hbm, bf16[8,2,32,512]{3,2,1,0:T(8,128)(2,1)S(1)} %collective-permute-done.3.h_ref, ...), custom_call_target="tpu_custom_call" | custom-call | flops 1610612736 | bytes 4194304 | tf_op jit(solution)/shard_map/sweep_a/pallas_call | solution.py:164
  81.8 0.1 collective-permute-start.7
  81.9 4.5 %sweep_b.2 = (f32[264,256]{1,0:T(8,128)S(1)}, f32[264,256]{1,0:T(8,128)}, f32[264,256]{1,0:T(8,128)S(1)}, f32[264,256]{1,0:T(8,128)S(1)}, f32[256,1152]{1,0:T(8,128)S(1)}) custom-call(s32[3]{0:T(128)S(1)} %pad_add_fusion.at_ref, bf16[2048,1024]{1,0:T(8,128)(2,1)} %bitcast.5.s_hbm, bf16[8,2,32,512]{3,2,1,0:T(8,128)(2,1)S(1)} %bitcast.9, ...), custom_call_target="tpu_custom_call" | custom-call | flops 1610612736 | bytes 4194304 | tf_op jit(solution)/shard_map/sweep_b/pallas_call | solution.py:164
  86.4 0.0 collective-permute-done.7.b_ref
  86.4 1.2 pair.2
  87.6 0.0 copy-start.1
  87.6 5.3 %all-to-all-start.2 = ((f32[16,136,128]{2,1,0:T(8,128)}), f32[16,136,128]{2,1,0:T(8,128)S(1)}, u32[]{:S(2)}, u32[]{:S(2)}) async-start(f32[16,136,128]{2,1,0:T(8,128)} %pair.2), calls=%async_computation.2 | async-start | bytes 2228224 | tf_op jit(solution)/shard_map/all_to_all | solution.py:284
  92.8 1.6 collective-permute-start.4
  94.5 2.9 %collective-permute-start.5 = (f32[264,256]{1,0:T(8,128)S(1)}, f32[264,256]{1,0:T(8,128)S(1)}, u32[]{:S(2)}, u32[]{:S(2)}) collective-permute-start(f32[264,256]{1,0:T(8,128)S(1)} %get-tuple-element.54), channel_id=1, source_target_pairs={{0,4},{2,6},{4,0},{6,2},{1,5},{3,7},{5,1},{7,3},{8,12},{10,14},{12... | collective-permute-start | bytes 811016 | tf_op jit(solution)/shard_map/ppermute | solution.py:292
  97.4 1.3 collective-permute-start.6
  98.7 13.8 %all-to-all-done.2.parts_ref = f32[16,136,128]{2,1,0:T(8,128)S(1)} async-done(((f32[16,136,128]{2,1,0:T(8,128)}), f32[16,136,128]{2,1,0:T(8,128)S(1)}, u32[]{:S(2)}, u32[]{:S(2)}) %all-to-all-start.2) | async-done | bytes 1114144 | tf_op jit(solution)/shard_map/all_to_all | solution.py:284
  112.5 0.0 copy-done.1
  112.5 1.0 h_update.2
  113.5 0.0 collective-permute-done.4.p1
  113.5 0.0 collective-permute-done.5.p2
  113.5 0.0 collective-permute-done.6.p3
  113.5 3.6 %all-to-all-start.3 = ((bf16[16,32,512]{2,1,0:T(8,128)(2,1)}), bf16[16,32,512]{2,1,0:T(8,128)(2,1)S(1)}, u32[]{:S(2)}, u32[]{:S(2)}) async-start(bf16[16,32,512]{2,1,0:T(8,128)(2,1)} %get-tuple-element.65), calls=%async_computation.3 | async-start | bytes 1048576 | tf_op jit(solution)/shard_map/all_to_all | solution.py:284
  117.1 0.2 w_update.2
  117.3 1.7 collective-permute-start.10
  118.9 2.9 %collective-permute-start.9 = (bf16[256,256]{1,0:T(8,128)(2,1)S(1)}, bf16[256,256]{1,0:T(8,128)(2,1)S(1)}, u32[]{:S(2)}, u32[]{:S(2)}) collective-permute-start(bf16[256,256]{1,0:T(8,128)(2,1)S(1)} %get-tuple-element.67.w0), channel_id=1, source_target_pairs={{0,4},{2,6},{4,0},{6,2},{1,5},{3,7},{5,1},{7,3},{8,12},{10,14},{12... | collective-permute-start | bytes 393224 | tf_op jit(solution)/shard_map/ppermute | solution.py:296
  121.9 1.3 collective-permute-start.8
  123.2 0.8 collective-permute-done.10.w3
  124.0 3.5 %collective-permute-done.9.w2 = bf16[256,256]{1,0:T(8,128)(2,1)S(1)} collective-permute-done((bf16[256,256]{1,0:T(8,128)(2,1)S(1)}, bf16[256,256]{1,0:T(8,128)(2,1)S(1)}, u32[]{:S(2)}, u32[]{:S(2)}) %collective-permute-start.9) | collective-permute-done | bytes 131104 | tf_op jit(solution)/shard_map/ppermute | solution.py:296
  127.5 0.0 collective-permute-done.8.w1
  127.5 1.0 all-to-all-done.3
  128.5 0.0 collective-permute-start.11
  128.5 1.9 %collective-permute-done.11.h_ref = bf16[8,2,32,512]{3,2,1,0:T(8,128)(2,1)S(1)} collective-permute-done((bf16[8,2,32,512]{3,2,1,0:T(8,128)(2,1)S(1)}, bf16[8,2,32,512]{3,2,1,0:T(8,128)(2,1)S(1)}, u32[]{:S(2)}, u32[]{:S(2)}) %collective-permute-start.11) | collective-permute-done | bytes 524320 | tf_op jit(solution)/shard_map/ppermute | solution.py:288
  130.4 3.9 %sweep_a.3 = (f32[264,256]{1,0:T(8,128)S(1)}, f32[264,256]{1,0:T(8,128)S(1)}, f32[264,256]{1,0:T(8,128)S(1)}, f32[264,256]{1,0:T(8,128)S(1)}, f32[256,1152]{1,0:T(8,128)S(1)}) custom-call(s32[3]{0:T(128)S(1)} %pad_add_fusion.at_ref, bf16[2048,1024]{1,0:T(8,128)(2,1)} %bitcast.5.s_hbm, bf16[8,2,32,512]{3,2,1,0:T(8,128)(2,1)S(1)} %collective-permute-done.11.h_ref, ...), custom_call_target="tpu_custom_call" | custom-call | flops 1610612736 | bytes 4194304 | tf_op jit(solution)/shard_map/sweep_a/pallas_call | solution.py:164
  134.3 0.2 collective-permute-start.15
  134.5 4.5 %sweep_b.3 = (f32[264,256]{1,0:T(8,128)S(1)}, f32[264,256]{1,0:T(8,128)}, f32[264,256]{1,0:T(8,128)S(1)}, f32[264,256]{1,0:T(8,128)S(1)}, f32[256,1152]{1,0:T(8,128)S(1)}) custom-call(s32[3]{0:T(128)S(1)} %pad_add_fusion.at_ref, bf16[2048,1024]{1,0:T(8,128)(2,1)} %bitcast.5.s_hbm, bf16[8,2,32,512]{3,2,1,0:T(8,128)(2,1)S(1)} %bitcast.11, ...), custom_call_target="tpu_custom_call" | custom-call | flops 1610612736 | bytes 4194304 | tf_op jit(solution)/shard_map/sweep_b/pallas_call | solution.py:164
  139.0 0.0 collective-permute-done.15.b_ref
  139.0 1.1 pair.3
  140.2 5.9 %all-to-all-start.4 = ((f32[16,136,128]{2,1,0:T(8,128)}), f32[16,136,128]{2,1,0:T(8,128)S(1)}, u32[]{:S(2)}, u32[]{:S(2)}) async-start(f32[16,136,128]{2,1,0:T(8,128)} %pair.3), calls=%async_computation.4 | async-start | bytes 2228224 | tf_op jit(solution)/shard_map/all_to_all | solution.py:284
  146.1 1.3 collective-permute-start.12
  147.4 2.8 %collective-permute-start.13 = (f32[264,256]{1,0:T(8,128)S(1)}, f32[264,256]{1,0:T(8,128)S(1)}, u32[]{:S(2)}, u32[]{:S(2)}) collective-permute-start(f32[264,256]{1,0:T(8,128)S(1)} %get-tuple-element.77), channel_id=1, source_target_pairs={{0,4},{2,6},{4,0},{6,2},{1,5},{3,7},{5,1},{7,3},{8,12},{10,14},{12... | collective-permute-start | bytes 811016 | tf_op jit(solution)/shard_map/ppermute | solution.py:292
  150.2 1.1 collective-permute-start.14
  151.4 14.4 %all-to-all-done.4.parts_ref = f32[16,136,128]{2,1,0:T(8,128)S(1)} async-done(((f32[16,136,128]{2,1,0:T(8,128)}), f32[16,136,128]{2,1,0:T(8,128)S(1)}, u32[]{:S(2)}, u32[]{:S(2)}) %all-to-all-start.4) | async-done | bytes 1114144 | tf_op jit(solution)/shard_map/all_to_all | solution.py:284
  165.8 1.0 h_update.3
  166.8 0.0 collective-permute-done.12.p1
  166.8 0.0 collective-permute-done.13.p2
  166.8 0.0 collective-permute-done.14.p3
  166.8 0.9 w_update.3
  (1 shorter events, 0.0 us)
Async XLA Ops:
  0.6 9.8 %copy-start = (f32[256,256]{1,0:T(8,128)S(1)}, f32[256,256]{1,0:T(8,128)}, u32[]{:S(2)}) copy-start(f32[256,256]{1,0:T(8,128)} %w_ref.1) | copy-start | bytes 786436
  2.5 19.5 %all-to-all-start.1 = ((bf16[16,32,512]{2,1,0:T(8,128)(2,1)}), bf16[16,32,512]{2,1,0:T(8,128)(2,1)S(1)}, u32[]{:S(2)}, u32[]{:S(2)}) async-start(bf16[16,32,512]{2,1,0:T(8,128)(2,1)} %spread.1), calls=%async_computation.1 | async-start | bytes 1048576 | tf_op jit(solution)/shard_map/all_to_all | solution.py:284
  21.9 55.9 %all-to-all-start = ((bf16[32,64,1024]{2,1,0:T(8,128)(2,1)}), bf16[32,64,1024]{2,1,0:T(8,128)(2,1)}, u32[]{:S(2)}, u32[]{:S(2)}) async-start(bf16[32,64,1024]{2,1,0:T(8,128)(2,1)} %bitcast.12), calls=%async_computation | async-start | bytes 8388608 | tf_op jit(solution)/shard_map/all_to_all | solution.py:284
  26.8 11.3 %collective-permute-start.3 = (bf16[8,2,32,512]{3,2,1,0:T(8,128)(2,1)S(1)}, bf16[8,2,32,512]{3,2,1,0:T(8,128)(2,1)S(1)}, u32[]{:S(2)}, u32[]{:S(2)}) collective-permute-start(bf16[8,2,32,512]{3,2,1,0:T(8,128)(2,1)S(1)} %bitcast.8), channel_id=1, source_target_pairs={{0,1},{1,0},{2,3},{3,2},{4,5},{5,4},{6,7},{7,6},{8,9},{9,8},{10,11... | collective-permute-start | bytes 1572872 | tf_op jit(solution)/shard_map/ppermute | solution.py:288
  27.0 7.1 %collective-permute-start.2 = (bf16[256,256]{1,0:T(8,128)(2,1)S(1)}, bf16[256,256]{1,0:T(8,128)(2,1)S(1)}, u32[]{:S(2)}, u32[]{:S(2)}) collective-permute-start(bf16[256,256]{1,0:T(8,128)(2,1)S(1)} %convert_element_type.7.w0), channel_id=1, source_target_pairs={{0,2},{2,4},{4,6},{6,0},{1,3},{3,5},{5,7},{7,1},{8,10},{10,12},{12... | collective-permute-start | bytes 393224 | tf_op jit(solution)/shard_map/ppermute | solution.py:296
  28.6 9.5 %collective-permute-start.1 = (bf16[256,256]{1,0:T(8,128)(2,1)S(1)}, bf16[256,256]{1,0:T(8,128)(2,1)S(1)}, u32[]{:S(2)}, u32[]{:S(2)}) collective-permute-start(bf16[256,256]{1,0:T(8,128)(2,1)S(1)} %convert_element_type.7.w0), channel_id=1, source_target_pairs={{0,4},{2,6},{4,0},{6,2},{1,5},{3,7},{5,1},{7,3},{8,12},{10,14},{12... | collective-permute-start | bytes 393224 | tf_op jit(solution)/shard_map/ppermute | solution.py:296
  31.5 6.6 %collective-permute-start = (bf16[256,256]{1,0:T(8,128)(2,1)S(1)}, bf16[256,256]{1,0:T(8,128)(2,1)S(1)}, u32[]{:S(2)}, u32[]{:S(2)}) collective-permute-start(bf16[256,256]{1,0:T(8,128)(2,1)S(1)} %convert_element_type.7.w0), channel_id=1, source_target_pairs={{0,6},{2,0},{4,2},{6,4},{1,7},{3,1},{5,3},{7,5},{8,14},{10,8},{12,... | collective-permute-start | bytes 393224 | tf_op jit(solution)/shard_map/ppermute | solution.py:296
  81.8 4.6 %collective-permute-start.7 = (f32[256,1152]{1,0:T(8,128)S(1)}, f32[256,1152]{1,0:T(8,128)S(1)}, u32[]{:S(2)}, u32[]{:S(2)}) collective-permute-start(f32[256,1152]{1,0:T(8,128)S(1)} %get-tuple-element.57), channel_id=1, source_target_pairs={{0,1},{1,0},{2,3},{3,2},{4,5},{5,4},{6,7},{7,6},{8,9},{9,8},{10,11... | collective-permute-start | bytes 3538952 | tf_op jit(solution)/shard_map/ppermute | solution.py:288
  87.6 25.0 %copy-start.1 = (f32[32,512]{1,0:T(8,128)S(1)}, f32[32,512]{1,0:T(8,128)}, u32[]{:S(2)}) copy-start(f32[32,512]{1,0:T(8,128)} %h_ref.1) | copy-start | bytes 196612
  87.6 25.0 %all-to-all-start.2 = ((f32[16,136,128]{2,1,0:T(8,128)}), f32[16,136,128]{2,1,0:T(8,128)S(1)}, u32[]{:S(2)}, u32[]{:S(2)}) async-start(f32[16,136,128]{2,1,0:T(8,128)} %pair.2), calls=%async_computation.2 | async-start | bytes 2228224 | tf_op jit(solution)/shard_map/all_to_all | solution.py:284
  92.8 20.7 %collective-permute-start.4 = (f32[264,256]{1,0:T(8,128)}, f32[264,256]{1,0:T(8,128)S(1)}, u32[]{:S(2)}, u32[]{:S(2)}) collective-permute-start(f32[264,256]{1,0:T(8,128)} %get-tuple-element.53), channel_id=1, source_target_pairs={{0,2},{2,4},{4,6},{6,0},{1,3},{3,5},{5,7},{7,1},{8,10},{10,12},{12... | collective-permute-start | bytes 811016 | tf_op jit(solution)/shard_map/ppermute | solution.py:292
  94.5 19.1 %collective-permute-start.5 = (f32[264,256]{1,0:T(8,128)S(1)}, f32[264,256]{1,0:T(8,128)S(1)}, u32[]{:S(2)}, u32[]{:S(2)}) collective-permute-start(f32[264,256]{1,0:T(8,128)S(1)} %get-tuple-element.54), channel_id=1, source_target_pairs={{0,4},{2,6},{4,0},{6,2},{1,5},{3,7},{5,1},{7,3},{8,12},{10,14},{12... | collective-permute-start | bytes 811016 | tf_op jit(solution)/shard_map/ppermute | solution.py:292
  97.4 16.2 %collective-permute-start.6 = (f32[264,256]{1,0:T(8,128)S(1)}, f32[264,256]{1,0:T(8,128)S(1)}, u32[]{:S(2)}, u32[]{:S(2)}) collective-permute-start(f32[264,256]{1,0:T(8,128)S(1)} %get-tuple-element.55), channel_id=1, source_target_pairs={{0,6},{2,0},{4,2},{6,4},{1,7},{3,1},{5,3},{7,5},{8,14},{10,8},{12,... | collective-permute-start | bytes 811016 | tf_op jit(solution)/shard_map/ppermute | solution.py:292
  113.5 14.9 %all-to-all-start.3 = ((bf16[16,32,512]{2,1,0:T(8,128)(2,1)}), bf16[16,32,512]{2,1,0:T(8,128)(2,1)S(1)}, u32[]{:S(2)}, u32[]{:S(2)}) async-start(bf16[16,32,512]{2,1,0:T(8,128)(2,1)} %get-tuple-element.65), calls=%async_computation.3 | async-start | bytes 1048576 | tf_op jit(solution)/shard_map/all_to_all | solution.py:284
  117.3 6.7 %collective-permute-start.10 = (bf16[256,256]{1,0:T(8,128)(2,1)S(1)}, bf16[256,256]{1,0:T(8,128)(2,1)S(1)}, u32[]{:S(2)}, u32[]{:S(2)}) collective-permute-start(bf16[256,256]{1,0:T(8,128)(2,1)S(1)} %get-tuple-element.67.w0), channel_id=1, source_target_pairs={{0,2},{2,4},{4,6},{6,0},{1,3},{3,5},{5,7},{7,1},{8,10},{10,12},{12... | collective-permute-start | bytes 393224 | tf_op jit(solution)/shard_map/ppermute | solution.py:296
  118.9 8.5 %collective-permute-start.9 = (bf16[256,256]{1,0:T(8,128)(2,1)S(1)}, bf16[256,256]{1,0:T(8,128)(2,1)S(1)}, u32[]{:S(2)}, u32[]{:S(2)}) collective-permute-start(bf16[256,256]{1,0:T(8,128)(2,1)S(1)} %get-tuple-element.67.w0), channel_id=1, source_target_pairs={{0,4},{2,6},{4,0},{6,2},{1,5},{3,7},{5,1},{7,3},{8,12},{10,14},{12... | collective-permute-start | bytes 393224 | tf_op jit(solution)/shard_map/ppermute | solution.py:296
  121.9 5.6 %collective-permute-start.8 = (bf16[256,256]{1,0:T(8,128)(2,1)S(1)}, bf16[256,256]{1,0:T(8,128)(2,1)S(1)}, u32[]{:S(2)}, u32[]{:S(2)}) collective-permute-start(bf16[256,256]{1,0:T(8,128)(2,1)S(1)} %get-tuple-element.67.w0), channel_id=1, source_target_pairs={{0,6},{2,0},{4,2},{6,4},{1,7},{3,1},{5,3},{7,5},{8,14},{10,8},{12,... | collective-permute-start | bytes 393224 | tf_op jit(solution)/shard_map/ppermute | solution.py:296
  128.5 1.9 %collective-permute-start.11 = (bf16[8,2,32,512]{3,2,1,0:T(8,128)(2,1)S(1)}, bf16[8,2,32,512]{3,2,1,0:T(8,128)(2,1)S(1)}, u32[]{:S(2)}, u32[]{:S(2)}) collective-permute-start(bf16[8,2,32,512]{3,2,1,0:T(8,128)(2,1)S(1)} %bitcast.10), channel_id=1, source_target_pairs={{0,1},{1,0},{2,3},{3,2},{4,5},{5,4},{6,7},{7,6},{8,9},{9,8},{10,11... | collective-permute-start | bytes 1572872 | tf_op jit(solution)/shard_map/ppermute | solution.py:288
  134.3 4.7 %collective-permute-start.15 = (f32[256,1152]{1,0:T(8,128)S(1)}, f32[256,1152]{1,0:T(8,128)S(1)}, u32[]{:S(2)}, u32[]{:S(2)}) collective-permute-start(f32[256,1152]{1,0:T(8,128)S(1)} %get-tuple-element.80), channel_id=1, source_target_pairs={{0,1},{1,0},{2,3},{3,2},{4,5},{5,4},{6,7},{7,6},{8,9},{9,8},{10,11... | collective-permute-start | bytes 3538952 | tf_op jit(solution)/shard_map/ppermute | solution.py:288
  140.2 25.6 %all-to-all-start.4 = ((f32[16,136,128]{2,1,0:T(8,128)}), f32[16,136,128]{2,1,0:T(8,128)S(1)}, u32[]{:S(2)}, u32[]{:S(2)}) async-start(f32[16,136,128]{2,1,0:T(8,128)} %pair.3), calls=%async_computation.4 | async-start | bytes 2228224 | tf_op jit(solution)/shard_map/all_to_all | solution.py:284
  146.1 20.7 %collective-permute-start.12 = (f32[264,256]{1,0:T(8,128)}, f32[264,256]{1,0:T(8,128)S(1)}, u32[]{:S(2)}, u32[]{:S(2)}) collective-permute-start(f32[264,256]{1,0:T(8,128)} %get-tuple-element.76), channel_id=1, source_target_pairs={{0,2},{2,4},{4,6},{6,0},{1,3},{3,5},{5,7},{7,1},{8,10},{10,12},{12... | collective-permute-start | bytes 811016 | tf_op jit(solution)/shard_map/ppermute | solution.py:292
  147.4 19.4 %collective-permute-start.13 = (f32[264,256]{1,0:T(8,128)S(1)}, f32[264,256]{1,0:T(8,128)S(1)}, u32[]{:S(2)}, u32[]{:S(2)}) collective-permute-start(f32[264,256]{1,0:T(8,128)S(1)} %get-tuple-element.77), channel_id=1, source_target_pairs={{0,4},{2,6},{4,0},{6,2},{1,5},{3,7},{5,1},{7,3},{8,12},{10,14},{12... | collective-permute-start | bytes 811016 | tf_op jit(solution)/shard_map/ppermute | solution.py:292
  150.2 16.6 %collective-permute-start.14 = (f32[264,256]{1,0:T(8,128)S(1)}, f32[264,256]{1,0:T(8,128)S(1)}, u32[]{:S(2)}, u32[]{:S(2)}) collective-permute-start(f32[264,256]{1,0:T(8,128)S(1)} %get-tuple-element.78), channel_id=1, source_target_pairs={{0,6},{2,0},{4,2},{6,4},{1,7},{3,1},{5,3},{7,5},{8,14},{10,8},{12,... | collective-permute-start | bytes 811016 | tf_op jit(solution)/shard_map/ppermute | solution.py:292

commit v9 on v8

--- a/solution.py
+++ b/solution.py
@@ -1,6 +1,5 @@
 import functools
 import math
-import operator
 
 import jax
 import jax.numpy as jnp
@@ -18,7 +17,7 @@
 AXES = ("zh", "x", "zl", "y", "core")
 SIZES = (2, 4, 2, 4, 2)
 TILE = ("zh", "zl", "core", "x")
-RANKS = ("zh", "x", "zl")
+RANKS = ("x", "zh", "zl")
 N_Y = 4
 N_R = 8
 N_P = 16
@@ -100,13 +99,9 @@
     )(record, table)
 
 
-def added(terms):
-    return functools.reduce(operator.add, terms)
-
-
 def sweep_kernel(first, at_ref, s_hbm, h_ref, w0, w1, w2, w3, *refs):
     before, (n0, n1, n2, n3, sums_ref, ht_ref, s_ref, sem) = (() if first else refs[:4]), refs[-8:]
-    blocks, half = h_ref.shape[1], h_ref.shape[3]
+    blocks, half = h_ref.shape[2], h_ref.shape[4]
     rank, span = ht_ref.shape[1], blocks * half
     run = half // 2
     core = at_ref[0 if first else 1]
@@ -124,28 +119,27 @@
     for p in range(2):
         for t, i in pieces:
             fetch(p, t, i).start()
-    h = [h_ref[:, b].reshape(rank, half) for b in range(blocks)]
+    h = [jnp.concatenate([h_ref[x, zh, b] for zh in range(2) for x in range(4)], axis=0) for b in range(blocks)]
     for b in range(blocks):
         ht_ref[b * half : (b + 1) * half, :] = h[b].T
     rowsum = jnp.dot(jnp.ones((8, span), jnp.bfloat16), ht_ref[...], preferred_element_type=jnp.float32)
-    wts = [jnp.concatenate([w[...] for w in pair], axis=0).T for pair in ((w0, w1), (w2, w3))]
-    colsum = added(jnp.sum(wt.astype(jnp.float32), axis=1, keepdims=True) for wt in wts)
-    cuts = [slice(b * half, (b + 1) * half) for b in range(blocks)]
-    recons = [[jnp.dot(ht_ref[cut, :], wt, preferred_element_type=jnp.float32) for cut in cuts] for wt in wts]
+    colsum = jnp.zeros((rank, 1), jnp.float32)
     for p in range(2):
+        wt = jnp.concatenate([w[...] for w in ((w0, w1), (w2, w3))[p]], axis=0).T
+        colsum = colsum + jnp.sum(wt.astype(jnp.float32), axis=1, keepdims=True)
+        recon = jnp.dot(ht_ref[...], wt, preferred_element_type=jnp.float32)
         for t, i in pieces:
             fetch(p, t, i).wait()
-    quotients = [
-        [(s_ref[p, cut].astype(jnp.float32) / recons[p][b]).astype(jnp.bfloat16) for b, cut in enumerate(cuts)]
-        for p in range(2)
-    ]
-    for b, cut in enumerate(cuts):
-        sums_ref[:, cut] = added(
-            lax.dot_general(wts[p], quotients[p][b], (((1,), (1,)), ((), ())), preferred_element_type=jnp.float32)
-            for p in range(2)
-        )
-    for p in range(2):
-        wn = added(jnp.dot(h[b], quotients[p][b], preferred_element_type=jnp.float32) for b in range(blocks))
+        quotient = (s_ref[p].astype(jnp.float32) / recon).astype(jnp.bfloat16)
+        hn = lax.dot_general(wt, quotient, (((1,), (1,)), ((), ())), preferred_element_type=jnp.float32)
+        if p == 0:
+            sums_ref[:, :span] = hn
+        else:
+            sums_ref[:, :span] += hn
+        wn = None
+        for b in range(blocks):
+            part = jnp.dot(h[b], quotient[b * half : (b + 1) * half], preferred_element_type=jnp.float32)
+            wn = part if wn is None else wn + part
         for t in range(2):
             ref = (n0, n1, n2, n3)[2 * p + t]
             part = wn[:, t * rank : (t + 1) * rank]
@@ -160,7 +154,7 @@
 
 def half_sweep(at, spectra, h, ws, before=()):
     frames, rows = spectra.shape
-    blocks, half, rank = h.shape[1], h.shape[3], ws[0].shape[1]
+    blocks, half, rank = h.shape[2], h.shape[4], ws[0].shape[1]
     return pl.pallas_call(
         functools.partial(sweep_kernel, not before),
         in_specs=whole(1, pltpu.SMEM) + whole(1, pl.ANY) + whole(5 + len(before)),
@@ -183,7 +177,7 @@
     half, span = 4 * LANES, a_ref.shape[1] - LANES
     group = lax.broadcasted_iota(jnp.int32, (TAIL, LANES), 1) // each
     for r in range(N_R):
-        rows = slice(r * each, (r + 1) * each)
+        rows, at = slice(r * each, (r + 1) * each), (r % 4 * 2 + r // 4) * 2
         sums = a_ref[rows, span:] + b_ref[rows, span:]
         tail = sums[:TAIL]
         for j in range(1, each // TAIL):
@@ -191,8 +185,8 @@
         for zl in range(2):
             for c in range(4):
                 columns = slice(zl * half + c * LANES, zl * half + (c + 1) * LANES)
-                out_ref[r * 2 + zl, c * each : (c + 1) * each, :] = a_ref[rows, columns] + b_ref[rows, columns]
-            out_ref[r * 2 + zl, 4 * each :, :] = tail
+                out_ref[at + zl, c * each : (c + 1) * each, :] = a_ref[rows, columns] + b_ref[rows, columns]
+            out_ref[at + zl, 4 * each :, :] = tail
 
 
 def pair(a, b, each):
@@ -300,7 +294,7 @@
     record = samples.reshape(samples.shape[2], samples.shape[3])
     core, y = lax.axis_index("core"), lax.axis_index("y")
     at = jnp.stack([1 - core, core, y]).astype(jnp.int32)
-    h_own = exchange(spread(h), RANKS).reshape(N_R, 2, *h.shape)
+    h_own = exchange(spread(h), RANKS).reshape(4, 2, 2, *h.shape)
     energy = energies(record, dft_table())
     frames, rows = energy.shape[4:]
     energy, w_low = lax.optimization_barrier((energy, w.astype(jnp.bfloat16)))
@@ -319,7 +313,7 @@
         if step + 1 < ITERS:
             ws = taken_ahead(w_low)
             ws, h_own = lax.optimization_barrier((ws, exchange(low, RANKS)))
-            h_own = h_own.reshape(N_R, 2, *h.shape)
+            h_own = h_own.reshape(4, 2, 2, *h.shape)
             h_oth = from_sibling(h_own)
     return (w, h)
 

time: 169 us -> 166 us (0.982)
  transfers between devices with their start and end apart: 21 -> 21, of which waited for: 10 -> 11; matrix products, arithmetic and copies ran while one was open for 0% -> 0% of each run, Pallas kernels for 11% -> 11%
where the time goes in v9:
time: 166 us; the launch traced here: 165 us
  waiting for transfers between devices  83 us (50%)
  starting transfers between devices  50.9 us (31%)
  Pallas kernels  30.6 us (18%)
    all_to_all x5, waiting for transfers between devices, exchange(): return lax.all_to_all(x, axes, 0, 0, tiled=True)  72.1 us
    all_to_all x5, starting transfers between devices, exchange(): return lax.all_to_all(x, axes, 0, 0, tiled=True)  28 us
    pallas_call x4, Pallas kernels, half_sweep(): pl.pallas_call(functools.partial(sweep_kernel, not before), in_specs=whol...  16 us
    ppermute x6, starting transfers between devices, taken_ahead(): lax.ppermute(x, 'y', [(i, (i - t) % N_Y) for i in range(N_Y)])  11.6 us
    ppermute x6, starting transfers between devices, sent_ahead(): return lax.ppermute(x, 'y', [(i, (i + t) % N_Y) for i in range(N_Y)])  10.8 us
    ppermute x6, waiting for transfers between devices, taken_ahead(): lax.ppermute(x, 'y', [(i, (i - t) % N_Y) for i in range(N_Y)])  8.91 us
    pallas_call x1, Pallas kernels, energies(): pl.pallas_call(energy_kernel, in_specs=[pl.BlockSpec(memory_space=pl.ANY)...  7.46 us
  transfers between devices with their start and end apart: 21, of which 11 were waited for; matrix products, arithmetic and copies ran while one was open for 0% of the time, Pallas kernels for 11%

profile of v9, /device:TPU:0, one launch (start us, length us, event | category | flops | bytes accessed | tf_op | source)
XLA Modules:
  0.0 165.3 jit_solution(10535966406468430316)
XLA Ops:
  0.6 0.0 copy-start
  0.6 1.8 %spread.1 = bf16[16,32,512]{2,1,0:T(8,128)(2,1)} custom-call(f32[32,512]{1,0:T(8,128)} %h_ref.1), custom_call_target="tpu_custom_call" | custom-call | tf_op jit(solution)/shard_map/spread/pallas_call | solution.py:261
  2.5 8.0 %all-to-all-start.1 = ((bf16[16,32,512]{2,1,0:T(8,128)(2,1)}), bf16[16,32,512]{2,1,0:T(8,128)(2,1)S(1)}, u32[]{:S(2)}, u32[]{:S(2)}) async-start(bf16[16,32,512]{2,1,0:T(8,128)(2,1)} %spread.1), calls=%async_computation.1 | async-start | bytes 1048576 | tf_op jit(solution)/shard_map/all_to_all | solution.py:278
  10.4 0.0 copy-done
  10.5 7.5 %energy.1 = bf16[2,2,2,4,64,1024]{5,4,3,2,1,0:T(8,128)(2,1)} custom-call(bf16[256,16384]{1,0:T(8,128)(2,1)} %bitcast.13, bf16[256,256]{1,0:T(8,128)(2,1)} %constant.14.table_ref), custom_call_target="tpu_custom_call" | custom-call | flops 2147483648 | bytes 12582912 | tf_op jit(solution)/shard_map/energy/pallas_call | solution.py:83
  17.9 4.0 %all-to-all-done.1 = bf16[16,32,512]{2,1,0:T(8,128)(2,1)S(1)} async-done(((bf16[16,32,512]{2,1,0:T(8,128)(2,1)}), bf16[16,32,512]{2,1,0:T(8,128)(2,1)S(1)}, u32[]{:S(2)}, u32[]{:S(2)}) %all-to-all-start.1) | async-done | bytes 524320 | tf_op jit(solution)/shard_map/all_to_all | solution.py:278
  21.9 4.9 %all-to-all-start = ((bf16[32,64,1024]{2,1,0:T(8,128)(2,1)}), bf16[32,64,1024]{2,1,0:T(8,128)(2,1)}, u32[]{:S(2)}, u32[]{:S(2)}) async-start(bf16[32,64,1024]{2,1,0:T(8,128)(2,1)} %bitcast.12), calls=%async_computation | async-start | bytes 8388608 | tf_op jit(solution)/shard_map/all_to_all | solution.py:278
  26.8 0.2 collective-permute-start.3
  27.0 1.6 collective-permute-start.2
  28.6 2.9 %collective-permute-start.1 = (bf16[256,256]{1,0:T(8,128)(2,1)S(1)}, bf16[256,256]{1,0:T(8,128)(2,1)S(1)}, u32[]{:S(2)}, u32[]{:S(2)}) collective-permute-start(bf16[256,256]{1,0:T(8,128)(2,1)S(1)} %convert_element_type.7.w0), channel_id=1, source_target_pairs={{0,4},{2,6},{4,0},{6,2},{1,5},{3,7},{5,1},{7,3},{8,12},{10,14},{12... | collective-permute-start | bytes 393224 | tf_op jit(solution)/shard_map/ppermute | solution.py:290
  31.5 1.3 collective-permute-start
  32.8 0.1 pad_add_fusion.at_ref
  32.9 1.2 collective-permute-done.2.w3
  34.1 4.0 %collective-permute-done.1.w2 = bf16[256,256]{1,0:T(8,128)(2,1)S(1)} collective-permute-done((bf16[256,256]{1,0:T(8,128)(2,1)S(1)}, bf16[256,256]{1,0:T(8,128)(2,1)S(1)}, u32[]{:S(2)}, u32[]{:S(2)}) %collective-permute-start.1) | collective-permute-done | bytes 131104 | tf_op jit(solution)/shard_map/ppermute | solution.py:290
  38.1 0.0 collective-permute-done.w1
  38.1 0.0 collective-permute-done.3.h_ref
  38.1 39.8 %all-to-all-done = bf16[32,64,1024]{2,1,0:T(8,128)(2,1)} async-done(((bf16[32,64,1024]{2,1,0:T(8,128)(2,1)}), bf16[32,64,1024]{2,1,0:T(8,128)(2,1)}, u32[]{:S(2)}, u32[]{:S(2)}) %all-to-all-start) | async-done | bytes 4194336 | tf_op jit(solution)/shard_map/all_to_all | solution.py:278
  77.9 4.0 %sweep_a.2 = (f32[264,256]{1,0:T(8,128)S(1)}, f32[264,256]{1,0:T(8,128)S(1)}, f32[264,256]{1,0:T(8,128)S(1)}, f32[264,256]{1,0:T(8,128)S(1)}, f32[256,1152]{1,0:T(8,128)S(1)}) custom-call(s32[3]{0:T(128)S(1)} %pad_add_fusion.at_ref, bf16[2048,1024]{1,0:T(8,128)(2,1)} %bitcast.5.s_hbm, bf16[4,2,2,32,512]{4,3,2,1,0:T(8,128)(2,1)S(1)} %collective-permute-done.3.h_ref, ...), custom_call_target="tpu_custom_call" | custom-call | flops 1610612736 | bytes 4194304 | tf_op jit(solution)/shard_map/sweep_a/pallas_call | solution.py:158
  81.9 0.1 collective-permute-start.7
  82.0 4.0 %sweep_b.2 = (f32[264,256]{1,0:T(8,128)S(1)}, f32[264,256]{1,0:T(8,128)}, f32[264,256]{1,0:T(8,128)S(1)}, f32[264,256]{1,0:T(8,128)S(1)}, f32[256,1152]{1,0:T(8,128)S(1)}) custom-call(s32[3]{0:T(128)S(1)} %pad_add_fusion.at_ref, bf16[2048,1024]{1,0:T(8,128)(2,1)} %bitcast.5.s_hbm, bf16[4,2,2,32,512]{4,3,2,1,0:T(8,128)(2,1)S(1)} %bitcast.9, ...), custom_call_target="tpu_custom_call" | custom-call | flops 1610612736 | bytes 4194304 | tf_op jit(solution)/shard_map/sweep_b/pallas_call | solution.py:158
  86.0 0.0 collective-permute-done.7.b_ref
  86.0 1.2 pair.2
  87.2 0.0 copy-start.1
  87.2 5.3 %all-to-all-start.2 = ((f32[16,136,128]{2,1,0:T(8,128)}), f32[16,136,128]{2,1,0:T(8,128)S(1)}, u32[]{:S(2)}, u32[]{:S(2)}) async-start(f32[16,136,128]{2,1,0:T(8,128)} %pair.2), calls=%async_computation.2 | async-start | bytes 2228224 | tf_op jit(solution)/shard_map/all_to_all | solution.py:278
  92.4 1.6 collective-permute-start.4
  94.1 2.9 %collective-permute-start.5 = (f32[264,256]{1,0:T(8,128)S(1)}, f32[264,256]{1,0:T(8,128)S(1)}, u32[]{:S(2)}, u32[]{:S(2)}) collective-permute-start(f32[264,256]{1,0:T(8,128)S(1)} %get-tuple-element.54), channel_id=1, source_target_pairs={{0,4},{2,6},{4,0},{6,2},{1,5},{3,7},{5,1},{7,3},{8,12},{10,14},{12... | collective-permute-start | bytes 811016 | tf_op jit(solution)/shard_map/ppermute | solution.py:286
  97.0 1.3 collective-permute-start.6
  98.3 13.2 %all-to-all-done.2.parts_ref = f32[16,136,128]{2,1,0:T(8,128)S(1)} async-done(((f32[16,136,128]{2,1,0:T(8,128)}), f32[16,136,128]{2,1,0:T(8,128)S(1)}, u32[]{:S(2)}, u32[]{:S(2)}) %all-to-all-start.2) | async-done | bytes 1114144 | tf_op jit(solution)/shard_map/all_to_all | solution.py:278
  111.5 0.0 copy-done.1
  111.5 1.0 h_update.2
  112.5 0.0 collective-permute-done.4.p1
  112.5 0.0 collective-permute-done.5.p2
  112.5 0.0 collective-permute-done.6.p3
  112.5 3.8 %all-to-all-start.3 = ((bf16[16,32,512]{2,1,0:T(8,128)(2,1)}), bf16[16,32,512]{2,1,0:T(8,128)(2,1)S(1)}, u32[]{:S(2)}, u32[]{:S(2)}) async-start(bf16[16,32,512]{2,1,0:T(8,128)(2,1)} %get-tuple-element.65), calls=%async_computation.3 | async-start | bytes 1048576 | tf_op jit(solution)/shard_map/all_to_all | solution.py:278
  116.3 0.2 w_update.2
  116.5 1.5 collective-permute-start.10
  118.0 2.9 %collective-permute-start.9 = (bf16[256,256]{1,0:T(8,128)(2,1)S(1)}, bf16[256,256]{1,0:T(8,128)(2,1)S(1)}, u32[]{:S(2)}, u32[]{:S(2)}) collective-permute-start(bf16[256,256]{1,0:T(8,128)(2,1)S(1)} %get-tuple-element.67.w0), channel_id=1, source_target_pairs={{0,4},{2,6},{4,0},{6,2},{1,5},{3,7},{5,1},{7,3},{8,12},{10,14},{12... | collective-permute-start | bytes 393224 | tf_op jit(solution)/shard_map/ppermute | solution.py:290
  120.9 1.3 collective-permute-start.8
  122.2 1.9 %collective-permute-done.10.w3 = bf16[256,256]{1,0:T(8,128)(2,1)S(1)} collective-permute-done((bf16[256,256]{1,0:T(8,128)(2,1)S(1)}, bf16[256,256]{1,0:T(8,128)(2,1)S(1)}, u32[]{:S(2)}, u32[]{:S(2)}) %collective-permute-start.10) | collective-permute-done | bytes 131104 | tf_op jit(solution)/shard_map/ppermute | solution.py:290
  124.1 1.7 %collective-permute-done.9.w2 = bf16[256,256]{1,0:T(8,128)(2,1)S(1)} collective-permute-done((bf16[256,256]{1,0:T(8,128)(2,1)S(1)}, bf16[256,256]{1,0:T(8,128)(2,1)S(1)}, u32[]{:S(2)}, u32[]{:S(2)}) %collective-permute-start.9) | collective-permute-done | bytes 131104 | tf_op jit(solution)/shard_map/ppermute | solution.py:290
  125.9 0.1 collective-permute-done.8.w1
  125.9 1.0 all-to-all-done.3
  126.9 0.0 collective-permute-start.11
  126.9 1.9 %collective-permute-done.11.h_ref = bf16[4,2,2,32,512]{4,3,2,1,0:T(8,128)(2,1)S(1)} collective-permute-done((bf16[4,2,2,32,512]{4,3,2,1,0:T(8,128)(2,1)S(1)}, bf16[4,2,2,32,512]{4,3,2,1,0:T(8,128)(2,1)S(1)}, u32[]{:S(2)}, u32[]{:S(2)}) %collective-permute-start.11) | collective-permute-done | bytes 524320 | tf_op jit(solution)/shard_map/ppermute | solution.py:282
  128.8 4.0 %sweep_a.3 = (f32[264,256]{1,0:T(8,128)S(1)}, f32[264,256]{1,0:T(8,128)S(1)}, f32[264,256]{1,0:T(8,128)S(1)}, f32[264,256]{1,0:T(8,128)S(1)}, f32[256,1152]{1,0:T(8,128)S(1)}) custom-call(s32[3]{0:T(128)S(1)} %pad_add_fusion.at_ref, bf16[2048,1024]{1,0:T(8,128)(2,1)} %bitcast.5.s_hbm, bf16[4,2,2,32,512]{4,3,2,1,0:T(8,128)(2,1)S(1)} %collective-permute-done.11.h_ref, ...), custom_call_target="tpu_custom_call" | custom-call | flops 1610612736 | bytes 4194304 | tf_op jit(solution)/shard_map/sweep_a/pallas_call | solution.py:158
  132.8 0.2 collective-permute-start.15
  133.1 4.0 %sweep_b.3 = (f32[264,256]{1,0:T(8,128)S(1)}, f32[264,256]{1,0:T(8,128)}, f32[264,256]{1,0:T(8,128)S(1)}, f32[264,256]{1,0:T(8,128)S(1)}, f32[256,1152]{1,0:T(8,128)S(1)}) custom-call(s32[3]{0:T(128)S(1)} %pad_add_fusion.at_ref, bf16[2048,1024]{1,0:T(8,128)(2,1)} %bitcast.5.s_hbm, bf16[4,2,2,32,512]{4,3,2,1,0:T(8,128)(2,1)S(1)} %bitcast.11, ...), custom_call_target="tpu_custom_call" | custom-call | flops 1610612736 | bytes 4194304 | tf_op jit(solution)/shard_map/sweep_b/pallas_call | solution.py:158
  137.1 0.0 collective-permute-done.15.b_ref
  137.1 1.1 pair.3
  138.2 6.1 %all-to-all-start.4 = ((f32[16,136,128]{2,1,0:T(8,128)}), f32[16,136,128]{2,1,0:T(8,128)S(1)}, u32[]{:S(2)}, u32[]{:S(2)}) async-start(f32[16,136,128]{2,1,0:T(8,128)} %pair.3), calls=%async_computation.4 | async-start | bytes 2228224 | tf_op jit(solution)/shard_map/all_to_all | solution.py:278
  144.3 1.3 collective-permute-start.12
  145.6 2.8 %collective-permute-start.13 = (f32[264,256]{1,0:T(8,128)S(1)}, f32[264,256]{1,0:T(8,128)S(1)}, u32[]{:S(2)}, u32[]{:S(2)}) collective-permute-start(f32[264,256]{1,0:T(8,128)S(1)} %get-tuple-element.77), channel_id=1, source_target_pairs={{0,4},{2,6},{4,0},{6,2},{1,5},{3,7},{5,1},{7,3},{8,12},{10,14},{12... | collective-permute-start | bytes 811016 | tf_op jit(solution)/shard_map/ppermute | solution.py:286
  148.4 0.8 collective-permute-start.14
  149.3 14.2 %all-to-all-done.4.parts_ref = f32[16,136,128]{2,1,0:T(8,128)S(1)} async-done(((f32[16,136,128]{2,1,0:T(8,128)}), f32[16,136,128]{2,1,0:T(8,128)S(1)}, u32[]{:S(2)}, u32[]{:S(2)}) %all-to-all-start.4) | async-done | bytes 1114144 | tf_op jit(solution)/shard_map/all_to_all | solution.py:278
  163.4 1.0 h_update.3
  164.4 0.0 collective-permute-done.12.p1
  164.4 0.0 collective-permute-done.13.p2
  164.4 0.0 collective-permute-done.14.p3
  164.4 0.9 w_update.3
  (1 shorter events, 0.0 us)
Async XLA Ops:
  0.6 9.8 %copy-start = (f32[256,256]{1,0:T(8,128)S(1)}, f32[256,256]{1,0:T(8,128)}, u32[]{:S(2)}) copy-start(f32[256,256]{1,0:T(8,128)} %w_ref.1) | copy-start | bytes 786436
  2.5 19.5 %all-to-all-start.1 = ((bf16[16,32,512]{2,1,0:T(8,128)(2,1)}), bf16[16,32,512]{2,1,0:T(8,128)(2,1)S(1)}, u32[]{:S(2)}, u32[]{:S(2)}) async-start(bf16[16,32,512]{2,1,0:T(8,128)(2,1)} %spread.1), calls=%async_computation.1 | async-start | bytes 1048576 | tf_op jit(solution)/shard_map/all_to_all | solution.py:278
  21.9 55.9 %all-to-all-start = ((bf16[32,64,1024]{2,1,0:T(8,128)(2,1)}), bf16[32,64,1024]{2,1,0:T(8,128)(2,1)}, u32[]{:S(2)}, u32[]{:S(2)}) async-start(bf16[32,64,1024]{2,1,0:T(8,128)(2,1)} %bitcast.12), calls=%async_computation | async-start | bytes 8388608 | tf_op jit(solution)/shard_map/all_to_all | solution.py:278
  26.8 11.3 %collective-permute-start.3 = (bf16[4,2,2,32,512]{4,3,2,1,0:T(8,128)(2,1)S(1)}, bf16[4,2,2,32,512]{4,3,2,1,0:T(8,128)(2,1)S(1)}, u32[]{:S(2)}, u32[]{:S(2)}) collective-permute-start(bf16[4,2,2,32,512]{4,3,2,1,0:T(8,128)(2,1)S(1)} %bitcast.8), channel_id=1, source_target_pairs={{0,1},{1,0},{2,3},{3,2},{4,5},{5,4},{6,7},{7,6},{8,9},{9,8},{10,11... | collective-permute-start | bytes 1572872 | tf_op jit(solution)/shard_map/ppermute | solution.py:282
  27.0 7.1 %collective-permute-start.2 = (bf16[256,256]{1,0:T(8,128)(2,1)S(1)}, bf16[256,256]{1,0:T(8,128)(2,1)S(1)}, u32[]{:S(2)}, u32[]{:S(2)}) collective-permute-start(bf16[256,256]{1,0:T(8,128)(2,1)S(1)} %convert_element_type.7.w0), channel_id=1, source_target_pairs={{0,2},{2,4},{4,6},{6,0},{1,3},{3,5},{5,7},{7,1},{8,10},{10,12},{12... | collective-permute-start | bytes 393224 | tf_op jit(solution)/shard_map/ppermute | solution.py:290
  28.6 9.5 %collective-permute-start.1 = (bf16[256,256]{1,0:T(8,128)(2,1)S(1)}, bf16[256,256]{1,0:T(8,128)(2,1)S(1)}, u32[]{:S(2)}, u32[]{:S(2)}) collective-permute-start(bf16[256,256]{1,0:T(8,128)(2,1)S(1)} %convert_element_type.7.w0), channel_id=1, source_target_pairs={{0,4},{2,6},{4,0},{6,2},{1,5},{3,7},{5,1},{7,3},{8,12},{10,14},{12... | collective-permute-start | bytes 393224 | tf_op jit(solution)/shard_map/ppermute | solution.py:290
  31.5 6.6 %collective-permute-start = (bf16[256,256]{1,0:T(8,128)(2,1)S(1)}, bf16[256,256]{1,0:T(8,128)(2,1)S(1)}, u32[]{:S(2)}, u32[]{:S(2)}) collective-permute-start(bf16[256,256]{1,0:T(8,128)(2,1)S(1)} %convert_element_type.7.w0), channel_id=1, source_target_pairs={{0,6},{2,0},{4,2},{6,4},{1,7},{3,1},{5,3},{7,5},{8,14},{10,8},{12,... | collective-permute-start | bytes 393224 | tf_op jit(solution)/shard_map/ppermute | solution.py:290
  81.9 4.1 %collective-permute-start.7 = (f32[256,1152]{1,0:T(8,128)S(1)}, f32[256,1152]{1,0:T(8,128)S(1)}, u32[]{:S(2)}, u32[]{:S(2)}) collective-permute-start(f32[256,1152]{1,0:T(8,128)S(1)} %get-tuple-element.57), channel_id=1, source_target_pairs={{0,1},{1,0},{2,3},{3,2},{4,5},{5,4},{6,7},{7,6},{8,9},{9,8},{10,11... | collective-permute-start | bytes 3538952 | tf_op jit(solution)/shard_map/ppermute | solution.py:282
  87.2 24.4 %copy-start.1 = (f32[32,512]{1,0:T(8,128)S(1)}, f32[32,512]{1,0:T(8,128)}, u32[]{:S(2)}) copy-start(f32[32,512]{1,0:T(8,128)} %h_ref.1) | copy-start | bytes 196612
  87.2 24.3 %all-to-all-start.2 = ((f32[16,136,128]{2,1,0:T(8,128)}), f32[16,136,128]{2,1,0:T(8,128)S(1)}, u32[]{:S(2)}, u32[]{:S(2)}) async-start(f32[16,136,128]{2,1,0:T(8,128)} %pair.2), calls=%async_computation.2 | async-start | bytes 2228224 | tf_op jit(solution)/shard_map/all_to_all | solution.py:278
  92.4 20.1 %collective-permute-start.4 = (f32[264,256]{1,0:T(8,128)}, f32[264,256]{1,0:T(8,128)S(1)}, u32[]{:S(2)}, u32[]{:S(2)}) collective-permute-start(f32[264,256]{1,0:T(8,128)} %get-tuple-element.53), channel_id=1, source_target_pairs={{0,2},{2,4},{4,6},{6,0},{1,3},{3,5},{5,7},{7,1},{8,10},{10,12},{12... | collective-permute-start | bytes 811016 | tf_op jit(solution)/shard_map/ppermute | solution.py:286
  94.1 18.4 %collective-permute-start.5 = (f32[264,256]{1,0:T(8,128)S(1)}, f32[264,256]{1,0:T(8,128)S(1)}, u32[]{:S(2)}, u32[]{:S(2)}) collective-permute-start(f32[264,256]{1,0:T(8,128)S(1)} %get-tuple-element.54), channel_id=1, source_target_pairs={{0,4},{2,6},{4,0},{6,2},{1,5},{3,7},{5,1},{7,3},{8,12},{10,14},{12... | collective-permute-start | bytes 811016 | tf_op jit(solution)/shard_map/ppermute | solution.py:286
  97.0 15.6 %collective-permute-start.6 = (f32[264,256]{1,0:T(8,128)S(1)}, f32[264,256]{1,0:T(8,128)S(1)}, u32[]{:S(2)}, u32[]{:S(2)}) collective-permute-start(f32[264,256]{1,0:T(8,128)S(1)} %get-tuple-element.55), channel_id=1, source_target_pairs={{0,6},{2,0},{4,2},{6,4},{1,7},{3,1},{5,3},{7,5},{8,14},{10,8},{12,... | collective-permute-start | bytes 811016 | tf_op jit(solution)/shard_map/ppermute | solution.py:286
  112.5 14.4 %all-to-all-start.3 = ((bf16[16,32,512]{2,1,0:T(8,128)(2,1)}), bf16[16,32,512]{2,1,0:T(8,128)(2,1)S(1)}, u32[]{:S(2)}, u32[]{:S(2)}) async-start(bf16[16,32,512]{2,1,0:T(8,128)(2,1)} %get-tuple-element.65), calls=%async_computation.3 | async-start | bytes 1048576 | tf_op jit(solution)/shard_map/all_to_all | solution.py:278
  116.5 7.7 %collective-permute-start.10 = (bf16[256,256]{1,0:T(8,128)(2,1)S(1)}, bf16[256,256]{1,0:T(8,128)(2,1)S(1)}, u32[]{:S(2)}, u32[]{:S(2)}) collective-permute-start(bf16[256,256]{1,0:T(8,128)(2,1)S(1)} %get-tuple-element.67.w0), channel_id=1, source_target_pairs={{0,2},{2,4},{4,6},{6,0},{1,3},{3,5},{5,7},{7,1},{8,10},{10,12},{12... | collective-permute-start | bytes 393224 | tf_op jit(solution)/shard_map/ppermute | solution.py:290
  118.0 7.9 %collective-permute-start.9 = (bf16[256,256]{1,0:T(8,128)(2,1)S(1)}, bf16[256,256]{1,0:T(8,128)(2,1)S(1)}, u32[]{:S(2)}, u32[]{:S(2)}) collective-permute-start(bf16[256,256]{1,0:T(8,128)(2,1)S(1)} %get-tuple-element.67.w0), channel_id=1, source_target_pairs={{0,4},{2,6},{4,0},{6,2},{1,5},{3,7},{5,1},{7,3},{8,12},{10,14},{12... | collective-permute-start | bytes 393224 | tf_op jit(solution)/shard_map/ppermute | solution.py:290
  120.9 5.1 %collective-permute-start.8 = (bf16[256,256]{1,0:T(8,128)(2,1)S(1)}, bf16[256,256]{1,0:T(8,128)(2,1)S(1)}, u32[]{:S(2)}, u32[]{:S(2)}) collective-permute-start(bf16[256,256]{1,0:T(8,128)(2,1)S(1)} %get-tuple-element.67.w0), channel_id=1, source_target_pairs={{0,6},{2,0},{4,2},{6,4},{1,7},{3,1},{5,3},{7,5},{8,14},{10,8},{12,... | collective-permute-start | bytes 393224 | tf_op jit(solution)/shard_map/ppermute | solution.py:290
  126.9 1.9 %collective-permute-start.11 = (bf16[4,2,2,32,512]{4,3,2,1,0:T(8,128)(2,1)S(1)}, bf16[4,2,2,32,512]{4,3,2,1,0:T(8,128)(2,1)S(1)}, u32[]{:S(2)}, u32[]{:S(2)}) collective-permute-start(bf16[4,2,2,32,512]{4,3,2,1,0:T(8,128)(2,1)S(1)} %bitcast.10), channel_id=1, source_target_pairs={{0,1},{1,0},{2,3},{3,2},{4,5},{5,4},{6,7},{7,6},{8,9},{9,8},{10,11... | collective-permute-start | bytes 1572872 | tf_op jit(solution)/shard_map/ppermute | solution.py:282
  132.8 4.2 %collective-permute-start.15 = (f32[256,1152]{1,0:T(8,128)S(1)}, f32[256,1152]{1,0:T(8,128)S(1)}, u32[]{:S(2)}, u32[]{:S(2)}) collective-permute-start(f32[256,1152]{1,0:T(8,128)S(1)} %get-tuple-element.80), channel_id=1, source_target_pairs={{0,1},{1,0},{2,3},{3,2},{4,5},{5,4},{6,7},{7,6},{8,9},{9,8},{10,11... | collective-permute-start | bytes 3538952 | tf_op jit(solution)/shard_map/ppermute | solution.py:282
  138.2 25.2 %all-to-all-start.4 = ((f32[16,136,128]{2,1,0:T(8,128)}), f32[16,136,128]{2,1,0:T(8,128)S(1)}, u32[]{:S(2)}, u32[]{:S(2)}) async-start(f32[16,136,128]{2,1,0:T(8,128)} %pair.3), calls=%async_computation.4 | async-start | bytes 2228224 | tf_op jit(solution)/shard_map/all_to_all | solution.py:278
  144.3 20.1 %collective-permute-start.12 = (f32[264,256]{1,0:T(8,128)}, f32[264,256]{1,0:T(8,128)S(1)}, u32[]{:S(2)}, u32[]{:S(2)}) collective-permute-start(f32[264,256]{1,0:T(8,128)} %get-tuple-element.76), channel_id=1, source_target_pairs={{0,2},{2,4},{4,6},{6,0},{1,3},{3,5},{5,7},{7,1},{8,10},{10,12},{12... | collective-permute-start | bytes 811016 | tf_op jit(solution)/shard_map/ppermute | solution.py:286
  145.6 18.8 %collective-permute-start.13 = (f32[264,256]{1,0:T(8,128)S(1)}, f32[264,256]{1,0:T(8,128)S(1)}, u32[]{:S(2)}, u32[]{:S(2)}) collective-permute-start(f32[264,256]{1,0:T(8,128)S(1)} %get-tuple-element.77), channel_id=1, source_target_pairs={{0,4},{2,6},{4,0},{6,2},{1,5},{3,7},{5,1},{7,3},{8,12},{10,14},{12... | collective-permute-start | bytes 811016 | tf_op jit(solution)/shard_map/ppermute | solution.py:286
  148.4 16.0 %collective-permute-start.14 = (f32[264,256]{1,0:T(8,128)S(1)}, f32[264,256]{1,0:T(8,128)S(1)}, u32[]{:S(2)}, u32[]{:S(2)}) collective-permute-start(f32[264,256]{1,0:T(8,128)S(1)} %get-tuple-element.78), channel_id=1, source_target_pairs={{0,6},{2,0},{4,2},{6,4},{1,7},{3,1},{5,3},{7,5},{8,14},{10,8},{12,... | collective-permute-start | bytes 811016 | tf_op jit(solution)/shard_map/ppermute | solution.py:286

commit v10 on v9

--- a/solution.py
+++ b/solution.py
@@ -97,6 +97,27 @@
         ),
         name="energy",
     )(record, table)
+
+
+def level(x, high):
+    relative = jnp.where(high == 0.0, 0.0, (x - high) / high)
+    return jnp.clip(jnp.floor(relative * (7.0 * 256.0) + 0.5), -7.0, 7.0) + 7.0
+
+
+def coded(a, b):
+    high_a, high_b = [x.astype(jnp.bfloat16).astype(jnp.float32) for x in (a, b)]
+    return high_a, high_b, level(a, high_a) * 15.0 + level(b, high_b)
+
+
+def decoded(high_a, high_b, code):
+    first = jnp.floor((code + 0.5) * (1.0 / 15.0))
+    second = code - 15.0 * first
+    return [high + high * ((q - 7.0) * (1.0 / (7.0 * 256.0))) for high, q in ((high_a, first), (high_b, second))]
+
+
+def hi_lo(x):
+    high = x.astype(jnp.bfloat16).astype(jnp.float32)
+    return jnp.concatenate([high, x - high], axis=0).astype(jnp.bfloat16)
 
 
 def sweep_kernel(first, at_ref, s_hbm, h_ref, w0, w1, w2, w3, *refs):
@@ -146,9 +167,18 @@
             if first:
                 ref[:rank, :] = part
                 ref[rank:, :] = rowsum
-            else:
-                ref[:rank, :] = part + before[2 * p + t][:rank, :]
-                ref[rank:, :] = rowsum + before[2 * p + t][rank:, :]
+                continue
+            part = part + before[2 * p + t][:rank, :]
+            total = rowsum + before[2 * p + t][rank:, :]
+            if p == 0 and t == 0:
+                ref[:rank, :] = part
+                ref[rank:, :] = total
+                continue
+            high_a, high_b, code = coded(part[: rank // 2], part[rank // 2 :])
+            ref[: rank // 2, :] = high_a.astype(jnp.bfloat16)
+            ref[rank // 2 : rank, :] = high_b.astype(jnp.bfloat16)
+            ref[rank : rank + rank // 2, :] = code.astype(jnp.bfloat16)
+            ref[rank + rank // 2 :, :] = hi_lo(total)
     sums_ref[:, span:] = jnp.broadcast_to(colsum, (rank, LANES))
 
 
@@ -159,7 +189,13 @@
         functools.partial(sweep_kernel, not before),
         in_specs=whole(1, pltpu.SMEM) + whole(1, pl.ANY) + whole(5 + len(before)),
         out_specs=whole(5),
-        out_shape=[jax.ShapeDtypeStruct((rank + 8, rank), jnp.float32)] * 4
+        out_shape=[jax.ShapeDtypeStruct((rank + 8, rank), jnp.float32)]
+        + [
+            jax.ShapeDtypeStruct((rank + rank // 2 + 16, rank), jnp.bfloat16)
+            if before
+            else jax.ShapeDtypeStruct((rank + 8, rank), jnp.float32)
+        ]
+        * 3
         + [jax.ShapeDtypeStruct((rank, blocks * half + LANES), jnp.float32)],
         scratch_shapes=[
             pltpu.VMEM((blocks * half, rank), jnp.bfloat16),
@@ -173,7 +209,7 @@
 
 
 def pair_kernel(a_ref, b_ref, out_ref):
-    each = (out_ref.shape[1] - TAIL) // 4
+    each = (out_ref.shape[1] - 2 * TAIL) // 6
     half, span = 4 * LANES, a_ref.shape[1] - LANES
     group = lax.broadcasted_iota(jnp.int32, (TAIL, LANES), 1) // each
     for r in range(N_R):
@@ -183,10 +219,18 @@
         for j in range(1, each // TAIL):
             tail = jnp.where(group == j, sums[j * TAIL : (j + 1) * TAIL], tail)
         for zl in range(2):
+            parts = []
             for c in range(4):
                 columns = slice(zl * half + c * LANES, zl * half + (c + 1) * LANES)
-                out_ref[at + zl, c * each : (c + 1) * each, :] = a_ref[rows, columns] + b_ref[rows, columns]
-            out_ref[at + zl, 4 * each :, :] = tail
+                parts.append(a_ref[rows, columns] + b_ref[rows, columns])
+            codes = []
+            for c in (0, 2):
+                high_a, high_b, code = coded(parts[c], parts[c + 1])
+                out_ref[at + zl, c * each : (c + 1) * each, :] = high_a.astype(jnp.bfloat16)
+                out_ref[at + zl, (c + 1) * each : (c + 2) * each, :] = high_b.astype(jnp.bfloat16)
+                codes.append(code.astype(jnp.bfloat16))
+            out_ref[at + zl, 4 * each : 6 * each, :] = jnp.concatenate(codes, axis=0)
+            out_ref[at + zl, 6 * each :, :] = hi_lo(tail)
 
 
 def pair(a, b, each):
@@ -194,7 +238,7 @@
         pair_kernel,
         in_specs=whole(2),
         out_specs=whole(1)[0],
-        out_shape=jax.ShapeDtypeStruct((N_P, 4 * each + TAIL, LANES), jnp.float32),
+        out_shape=jax.ShapeDtypeStruct((N_P, 6 * each + 2 * TAIL, LANES), jnp.bfloat16),
         compiler_params=pltpu.CompilerParams(vmem_limit_bytes=12 << 20),
         name="pair",
     )(a, b)
@@ -202,11 +246,15 @@
 
 def h_update_kernel(parts_ref, h_ref, new_ref, low_ref):
     each = h_ref.shape[0]
-    total = parts_ref[0]
-    for i in range(1, N_P):
-        total = total + parts_ref[i]
-    numer = jnp.concatenate([total[c * each : (c + 1) * each] for c in range(4)], axis=1)
-    tail = total[4 * each :]
+    blocks, tail = [0.0] * 4, 0.0
+    for i in range(N_P):
+        part = parts_ref[i].astype(jnp.float32)
+        pieces = [part[c * each : (c + 1) * each] for c in range(6)]
+        values = decoded(*pieces[0:2], pieces[4]) + decoded(*pieces[2:4], pieces[5])
+        blocks = [block + value for block, value in zip(blocks, values)]
+        tail = tail + part[6 * each :]
+    numer = jnp.concatenate(blocks, axis=1)
+    tail = tail[:TAIL] + tail[TAIL:]
     colsum = jnp.concatenate([tail[:, j * each : j * each + 1] for j in range(each // TAIL)], axis=0)
     new = h_ref[...] * numer / colsum
     new_ref[...] = new
@@ -228,8 +276,14 @@
 
 def w_update_kernel(p0, p1, p2, p3, w_ref, new_ref, low_ref):
     rank = w_ref.shape[1]
-    total = (p0[...] + p1[...]) + (p2[...] + p3[...])
-    new = w_ref[...] * total[:rank, :].T / total[rank : rank + 1, :]
+    cut = rank // 2
+    tops, bottoms, rowsum = p0[:cut, :], p0[cut:rank, :], p0[rank : rank + 1, :]
+    for ref in (p1, p2, p3):
+        part = ref[...].astype(jnp.float32)
+        top, bottom = decoded(part[:cut], part[cut:rank], part[rank : rank + cut])
+        tops, bottoms = tops + top, bottoms + bottom
+        rowsum = rowsum + part[rank + cut : rank + cut + 1] + part[rank + cut + 8 : rank + cut + 9]
+    new = w_ref[...] * jnp.concatenate([tops, bottoms], axis=0).T / rowsum
     new_ref[...] = new
     low_ref[...] = new.astype(jnp.bfloat16)
 

time: 166 us -> 161 us (0.970)
  waiting for transfers between devices: 83 us -> 76.3 us
  Pallas kernels: 30.6 us -> 32.4 us
    all_to_all x5, waiting for transfers between devices: 72.1 us -> 65.5 us  [exchange(): return lax.all_to_all(x, axes, 0, 0, tiled=True)]
  transfers between devices with their start and end apart: 21 -> 21, of which waited for: 11 -> 11; matrix products, arithmetic and copies ran while one was open for 0% -> 0% of each run, Pallas kernels for 11% -> 12%
where the time goes in v10:
time: 161 us
  waiting for transfers between devices  76.3 us (47%)
  starting transfers between devices  51.2 us (32%)
  Pallas kernels  32.4 us (20%)
    all_to_all x5, waiting for transfers between devices, exchange(): return lax.all_to_all(x, axes, 0, 0, tiled=True)  65.5 us
    all_to_all x5, starting transfers between devices, exchange(): return lax.all_to_all(x, axes, 0, 0, tiled=True)  28.2 us
    pallas_call x4, Pallas kernels, half_sweep(): pl.pallas_call(functools.partial(sweep_kernel, not before), in_specs=whol...  16.4 us
    ppermute x6, starting transfers between devices, taken_ahead(): lax.ppermute(x, 'y', [(i, (i - t) % N_Y) for i in range(N_Y)])  11.7 us
    ppermute x6, starting transfers between devices, sent_ahead(): return lax.ppermute(x, 'y', [(i, (i + t) % N_Y) for i in range(N_Y)])  10.9 us
    ppermute x6, waiting for transfers between devices, taken_ahead(): lax.ppermute(x, 'y', [(i, (i - t) % N_Y) for i in range(N_Y)])  8.85 us
    pallas_call x1, Pallas kernels, energies(): pl.pallas_call(energy_kernel, in_specs=[pl.BlockSpec(memory_space=pl.ANY)...  7.46 us
  transfers between devices with their start and end apart: 21, of which 11 were waited for; matrix products, arithmetic and copies ran while one was open for 0% of the time, Pallas kernels for 12%

profile of v10, /device:TPU:0, one launch (start us, length us, event | category | flops | bytes accessed | tf_op | source)
XLA Modules:
  0.0 160.8 jit_solution(14814886583670156890)
XLA Ops:
  0.6 0.0 copy-start
  0.6 1.8 %spread.1 = bf16[16,32,512]{2,1,0:T(8,128)(2,1)} custom-call(f32[32,512]{1,0:T(8,128)} %h_ref.1), custom_call_target="tpu_custom_call" | custom-call | tf_op jit(solution)/shard_map/spread/pallas_call | solution.py:315
  2.5 8.0 %all-to-all-start.1 = ((bf16[16,32,512]{2,1,0:T(8,128)(2,1)}), bf16[16,32,512]{2,1,0:T(8,128)(2,1)S(1)}, u32[]{:S(2)}, u32[]{:S(2)}) async-start(bf16[16,32,512]{2,1,0:T(8,128)(2,1)} %spread.1), calls=%async_computation.1 | async-start | bytes 1048576 | tf_op jit(solution)/shard_map/all_to_all | solution.py:332
  10.4 0.0 copy-done
  10.5 7.5 %energy.1 = bf16[2,2,2,4,64,1024]{5,4,3,2,1,0:T(8,128)(2,1)} custom-call(bf16[256,16384]{1,0:T(8,128)(2,1)} %bitcast.13, bf16[256,256]{1,0:T(8,128)(2,1)} %constant.14.table_ref), custom_call_target="tpu_custom_call" | custom-call | flops 2147483648 | bytes 12582912 | tf_op jit(solution)/shard_map/energy/pallas_call | solution.py:83
  17.9 4.0 %all-to-all-done.1 = bf16[16,32,512]{2,1,0:T(8,128)(2,1)S(1)} async-done(((bf16[16,32,512]{2,1,0:T(8,128)(2,1)}), bf16[16,32,512]{2,1,0:T(8,128)(2,1)S(1)}, u32[]{:S(2)}, u32[]{:S(2)}) %all-to-all-start.1) | async-done | bytes 524320 | tf_op jit(solution)/shard_map/all_to_all | solution.py:332
  21.9 4.9 %all-to-all-start = ((bf16[32,64,1024]{2,1,0:T(8,128)(2,1)}), bf16[32,64,1024]{2,1,0:T(8,128)(2,1)}, u32[]{:S(2)}, u32[]{:S(2)}) async-start(bf16[32,64,1024]{2,1,0:T(8,128)(2,1)} %bitcast.12), calls=%async_computation | async-start | bytes 8388608 | tf_op jit(solution)/shard_map/all_to_all | solution.py:332
  26.8 0.2 collective-permute-start.3
  27.0 1.6 collective-permute-start.2
  28.6 2.9 %collective-permute-start.1 = (bf16[256,256]{1,0:T(8,128)(2,1)S(1)}, bf16[256,256]{1,0:T(8,128)(2,1)S(1)}, u32[]{:S(2)}, u32[]{:S(2)}) collective-permute-start(bf16[256,256]{1,0:T(8,128)(2,1)S(1)} %convert_element_type.7.w0), channel_id=1, source_target_pairs={{0,4},{2,6},{4,0},{6,2},{1,5},{3,7},{5,1},{7,3},{8,12},{10,14},{12... | collective-permute-start | bytes 393224 | tf_op jit(solution)/shard_map/ppermute | solution.py:344
  31.5 1.3 collective-permute-start
  32.8 0.1 pad_add_fusion.at_ref
  32.9 1.2 collective-permute-done.2.w3
  34.1 4.0 %collective-permute-done.1.w2 = bf16[256,256]{1,0:T(8,128)(2,1)S(1)} collective-permute-done((bf16[256,256]{1,0:T(8,128)(2,1)S(1)}, bf16[256,256]{1,0:T(8,128)(2,1)S(1)}, u32[]{:S(2)}, u32[]{:S(2)}) %collective-permute-start.1) | collective-permute-done | bytes 131104 | tf_op jit(solution)/shard_map/ppermute | solution.py:344
  38.1 0.0 collective-permute-done.w1
  38.1 0.0 collective-permute-done.3.h_ref
  38.1 39.8 %all-to-all-done = bf16[32,64,1024]{2,1,0:T(8,128)(2,1)} async-done(((bf16[32,64,1024]{2,1,0:T(8,128)(2,1)}), bf16[32,64,1024]{2,1,0:T(8,128)(2,1)}, u32[]{:S(2)}, u32[]{:S(2)}) %all-to-all-start) | async-done | bytes 4194336 | tf_op jit(solution)/shard_map/all_to_all | solution.py:332
  77.9 4.0 %sweep_a.2 = (f32[264,256]{1,0:T(8,128)S(1)}, f32[264,256]{1,0:T(8,128)S(1)}, f32[264,256]{1,0:T(8,128)S(1)}, f32[264,256]{1,0:T(8,128)S(1)}, f32[256,1152]{1,0:T(8,128)S(1)}) custom-call(s32[3]{0:T(128)S(1)} %pad_add_fusion.at_ref, bf16[2048,1024]{1,0:T(8,128)(2,1)} %bitcast.5.s_hbm, bf16[4,2,2,32,512]{4,3,2,1,0:T(8,128)(2,1)S(1)} %collective-permute-done.3.h_ref, ...), custom_call_target="tpu_custom_call" | custom-call | flops 1610612736 | bytes 4194304 | tf_op jit(solution)/shard_map/sweep_a/pallas_call | solution.py:188
  81.9 0.1 collective-permute-start.7
  82.0 4.2 %sweep_b.2 = (f32[264,256]{1,0:T(8,128)S(1)}, bf16[400,256]{1,0:T(8,128)(2,1)S(1)}, bf16[400,256]{1,0:T(8,128)(2,1)S(1)}, bf16[400,256]{1,0:T(8,128)(2,1)S(1)}, f32[256,1152]{1,0:T(8,128)S(1)}) custom-call(s32[3]{0:T(128)S(1)} %pad_add_fusion.at_ref, bf16[2048,1024]{1,0:T(8,128)(2,1)} %bitcast.5.s_hbm, bf16[4,2,2,32,512]{4,3,2,1,0:T(8,128)(2,1)S(1)} %bitcast.9, ...), custom_call_target="tpu_custom_call" | custom-call | flops 1610612736 | bytes 4194304 | tf_op jit(solution)/shard_map/sweep_b/pallas_call | solution.py:188
  86.2 0.0 collective-permute-done.7.b_ref
  86.2 1.4 pair.2
  87.6 0.0 copy-start.1
  87.6 5.3 %all-to-all-start.2 = ((bf16[16,208,128]{2,1,0:T(8,128)(2,1)}), bf16[16,208,128]{2,1,0:T(8,128)(2,1)S(1)}, u32[]{:S(2)}, u32[]{:S(2)}) async-start(bf16[16,208,128]{2,1,0:T(8,128)(2,1)} %pair.2), calls=%async_computation.2 | async-start | bytes 1703936 | tf_op jit(solution)/shard_map/all_to_all | solution.py:332
  92.9 1.6 %collective-permute-start.4 = (bf16[400,256]{1,0:T(8,128)(2,1)S(1)}, bf16[400,256]{1,0:T(8,128)(2,1)S(1)}, u32[]{:S(2)}, u32[]{:S(2)}) collective-permute-start(bf16[400,256]{1,0:T(8,128)(2,1)S(1)} %get-tuple-element.53), channel_id=1, source_target_pairs={{0,2},{2,4},{4,6},{6,0},{1,3},{3,5},{5,7},{7,1},{8,10},{10,12},{12... | collective-permute-start | bytes 614408 | tf_op jit(solution)/shard_map/ppermute | solution.py:340
  94.5 2.9 %collective-permute-start.5 = (bf16[400,256]{1,0:T(8,128)(2,1)S(1)}, bf16[400,256]{1,0:T(8,128)(2,1)S(1)}, u32[]{:S(2)}, u32[]{:S(2)}) collective-permute-start(bf16[400,256]{1,0:T(8,128)(2,1)S(1)} %get-tuple-element.54), channel_id=1, source_target_pairs={{0,4},{2,6},{4,0},{6,2},{1,5},{3,7},{5,1},{7,3},{8,12},{10,14},{12... | collective-permute-start | bytes 614408 | tf_op jit(solution)/shard_map/ppermute | solution.py:340
  97.4 1.3 collective-permute-start.6
  98.8 10.1 %all-to-all-done.2.parts_ref = bf16[16,208,128]{2,1,0:T(8,128)(2,1)S(1)} async-done(((bf16[16,208,128]{2,1,0:T(8,128)(2,1)}), bf16[16,208,128]{2,1,0:T(8,128)(2,1)S(1)}, u32[]{:S(2)}, u32[]{:S(2)}) %all-to-all-start.2) | async-done | bytes 852000 | tf_op jit(solution)/shard_map/all_to_all | solution.py:332
  108.8 0.0 copy-done.1
  108.8 1.3 h_update.2
  110.1 0.0 collective-permute-done.4.p1
  110.1 0.0 collective-permute-done.5.p2
  110.1 0.0 collective-permute-done.6.p3
  110.1 3.6 %all-to-all-start.3 = ((bf16[16,32,512]{2,1,0:T(8,128)(2,1)}), bf16[16,32,512]{2,1,0:T(8,128)(2,1)S(1)}, u32[]{:S(2)}, u32[]{:S(2)}) async-start(bf16[16,32,512]{2,1,0:T(8,128)(2,1)} %get-tuple-element.65), calls=%async_computation.3 | async-start | bytes 1048576 | tf_op jit(solution)/shard_map/all_to_all | solution.py:332
  113.7 0.3 w_update.2
  114.1 1.6 collective-permute-start.10
  115.7 2.9 %collective-permute-start.9 = (bf16[256,256]{1,0:T(8,128)(2,1)S(1)}, bf16[256,256]{1,0:T(8,128)(2,1)S(1)}, u32[]{:S(2)}, u32[]{:S(2)}) collective-permute-start(bf16[256,256]{1,0:T(8,128)(2,1)S(1)} %get-tuple-element.67.w0), channel_id=1, source_target_pairs={{0,4},{2,6},{4,0},{6,2},{1,5},{3,7},{5,1},{7,3},{8,12},{10,14},{12... | collective-permute-start | bytes 393224 | tf_op jit(solution)/shard_map/ppermute | solution.py:344
  118.6 1.3 collective-permute-start.8
  119.9 1.8 %collective-permute-done.10.w3 = bf16[256,256]{1,0:T(8,128)(2,1)S(1)} collective-permute-done((bf16[256,256]{1,0:T(8,128)(2,1)S(1)}, bf16[256,256]{1,0:T(8,128)(2,1)S(1)}, u32[]{:S(2)}, u32[]{:S(2)}) %collective-permute-start.10) | collective-permute-done | bytes 131104 | tf_op jit(solution)/shard_map/ppermute | solution.py:344
  121.7 1.8 %collective-permute-done.9.w2 = bf16[256,256]{1,0:T(8,128)(2,1)S(1)} collective-permute-done((bf16[256,256]{1,0:T(8,128)(2,1)S(1)}, bf16[256,256]{1,0:T(8,128)(2,1)S(1)}, u32[]{:S(2)}, u32[]{:S(2)}) %collective-permute-start.9) | collective-permute-done | bytes 131104 | tf_op jit(solution)/shard_map/ppermute | solution.py:344
  123.5 0.1 collective-permute-done.8.w1
  123.6 0.8 all-to-all-done.3
  124.4 0.0 collective-permute-start.11
  124.4 1.9 %collective-permute-done.11.h_ref = bf16[4,2,2,32,512]{4,3,2,1,0:T(8,128)(2,1)S(1)} collective-permute-done((bf16[4,2,2,32,512]{4,3,2,1,0:T(8,128)(2,1)S(1)}, bf16[4,2,2,32,512]{4,3,2,1,0:T(8,128)(2,1)S(1)}, u32[]{:S(2)}, u32[]{:S(2)}) %collective-permute-start.11) | collective-permute-done | bytes 524320 | tf_op jit(solution)/shard_map/ppermute | solution.py:336
  126.3 4.0 %sweep_a.3 = (f32[264,256]{1,0:T(8,128)S(1)}, f32[264,256]{1,0:T(8,128)S(1)}, f32[264,256]{1,0:T(8,128)S(1)}, f32[264,256]{1,0:T(8,128)S(1)}, f32[256,1152]{1,0:T(8,128)S(1)}) custom-call(s32[3]{0:T(128)S(1)} %pad_add_fusion.at_ref, bf16[2048,1024]{1,0:T(8,128)(2,1)} %bitcast.5.s_hbm, bf16[4,2,2,32,512]{4,3,2,1,0:T(8,128)(2,1)S(1)} %collective-permute-done.11.h_ref, ...), custom_call_target="tpu_custom_call" | custom-call | flops 1610612736 | bytes 4194304 | tf_op jit(solution)/shard_map/sweep_a/pallas_call | solution.py:188
  130.3 0.2 collective-permute-start.15
  130.5 4.2 %sweep_b.3 = (f32[264,256]{1,0:T(8,128)S(1)}, bf16[400,256]{1,0:T(8,128)(2,1)S(1)}, bf16[400,256]{1,0:T(8,128)(2,1)S(1)}, bf16[400,256]{1,0:T(8,128)(2,1)S(1)}, f32[256,1152]{1,0:T(8,128)S(1)}) custom-call(s32[3]{0:T(128)S(1)} %pad_add_fusion.at_ref, bf16[2048,1024]{1,0:T(8,128)(2,1)} %bitcast.5.s_hbm, bf16[4,2,2,32,512]{4,3,2,1,0:T(8,128)(2,1)S(1)} %bitcast.11, ...), custom_call_target="tpu_custom_call" | custom-call | flops 1610612736 | bytes 4194304 | tf_op jit(solution)/shard_map/sweep_b/pallas_call | solution.py:188
  134.7 0.0 collective-permute-done.15.b_ref
  134.7 1.4 pair.3
  136.1 6.4 %all-to-all-start.4 = ((bf16[16,208,128]{2,1,0:T(8,128)(2,1)}), bf16[16,208,128]{2,1,0:T(8,128)(2,1)S(1)}, u32[]{:S(2)}, u32[]{:S(2)}) async-start(bf16[16,208,128]{2,1,0:T(8,128)(2,1)} %pair.3), calls=%async_computation.4 | async-start | bytes 1703936 | tf_op jit(solution)/shard_map/all_to_all | solution.py:332
  142.5 1.2 collective-permute-start.12
  143.7 2.9 %collective-permute-start.13 = (bf16[400,256]{1,0:T(8,128)(2,1)S(1)}, bf16[400,256]{1,0:T(8,128)(2,1)S(1)}, u32[]{:S(2)}, u32[]{:S(2)}) collective-permute-start(bf16[400,256]{1,0:T(8,128)(2,1)S(1)} %get-tuple-element.77), channel_id=1, source_target_pairs={{0,4},{2,6},{4,0},{6,2},{1,5},{3,7},{5,1},{7,3},{8,12},{10,14},{12... | collective-permute-start | bytes 614408 | tf_op jit(solution)/shard_map/ppermute | solution.py:340
  146.6 0.9 collective-permute-start.14
  147.6 10.9 %all-to-all-done.4.parts_ref = bf16[16,208,128]{2,1,0:T(8,128)(2,1)S(1)} async-done(((bf16[16,208,128]{2,1,0:T(8,128)(2,1)}), bf16[16,208,128]{2,1,0:T(8,128)(2,1)S(1)}, u32[]{:S(2)}, u32[]{:S(2)}) %all-to-all-start.4) | async-done | bytes 852000 | tf_op jit(solution)/shard_map/all_to_all | solution.py:332
  158.5 1.2 h_update.3
  159.7 0.0 collective-permute-done.12.p1
  159.7 0.0 collective-permute-done.13.p2
  159.7 0.0 collective-permute-done.14.p3
  159.7 1.1 w_update.3
  (1 shorter events, 0.0 us)
Async XLA Ops:
  0.6 9.8 %copy-start = (f32[256,256]{1,0:T(8,128)S(1)}, f32[256,256]{1,0:T(8,128)}, u32[]{:S(2)}) copy-start(f32[256,256]{1,0:T(8,128)} %w_ref.1) | copy-start | bytes 786436
  2.5 19.5 %all-to-all-start.1 = ((bf16[16,32,512]{2,1,0:T(8,128)(2,1)}), bf16[16,32,512]{2,1,0:T(8,128)(2,1)S(1)}, u32[]{:S(2)}, u32[]{:S(2)}) async-start(bf16[16,32,512]{2,1,0:T(8,128)(2,1)} %spread.1), calls=%async_computation.1 | async-start | bytes 1048576 | tf_op jit(solution)/shard_map/all_to_all | solution.py:332
  21.9 55.9 %all-to-all-start = ((bf16[32,64,1024]{2,1,0:T(8,128)(2,1)}), bf16[32,64,1024]{2,1,0:T(8,128)(2,1)}, u32[]{:S(2)}, u32[]{:S(2)}) async-start(bf16[32,64,1024]{2,1,0:T(8,128)(2,1)} %bitcast.12), calls=%async_computation | async-start | bytes 8388608 | tf_op jit(solution)/shard_map/all_to_all | solution.py:332
  26.8 11.3 %collective-permute-start.3 = (bf16[4,2,2,32,512]{4,3,2,1,0:T(8,128)(2,1)S(1)}, bf16[4,2,2,32,512]{4,3,2,1,0:T(8,128)(2,1)S(1)}, u32[]{:S(2)}, u32[]{:S(2)}) collective-permute-start(bf16[4,2,2,32,512]{4,3,2,1,0:T(8,128)(2,1)S(1)} %bitcast.8), channel_id=1, source_target_pairs={{0,1},{1,0},{2,3},{3,2},{4,5},{5,4},{6,7},{7,6},{8,9},{9,8},{10,11... | collective-permute-start | bytes 1572872 | tf_op jit(solution)/shard_map/ppermute | solution.py:336
  27.0 7.1 %collective-permute-start.2 = (bf16[256,256]{1,0:T(8,128)(2,1)S(1)}, bf16[256,256]{1,0:T(8,128)(2,1)S(1)}, u32[]{:S(2)}, u32[]{:S(2)}) collective-permute-start(bf16[256,256]{1,0:T(8,128)(2,1)S(1)} %convert_element_type.7.w0), channel_id=1, source_target_pairs={{0,2},{2,4},{4,6},{6,0},{1,3},{3,5},{5,7},{7,1},{8,10},{10,12},{12... | collective-permute-start | bytes 393224 | tf_op jit(solution)/shard_map/ppermute | solution.py:344
  28.6 9.5 %collective-permute-start.1 = (bf16[256,256]{1,0:T(8,128)(2,1)S(1)}, bf16[256,256]{1,0:T(8,128)(2,1)S(1)}, u32[]{:S(2)}, u32[]{:S(2)}) collective-permute-start(bf16[256,256]{1,0:T(8,128)(2,1)S(1)} %convert_element_type.7.w0), channel_id=1, source_target_pairs={{0,4},{2,6},{4,0},{6,2},{1,5},{3,7},{5,1},{7,3},{8,12},{10,14},{12... | collective-permute-start | bytes 393224 | tf_op jit(solution)/shard_map/ppermute | solution.py:344
  31.5 6.6 %collective-permute-start = (bf16[256,256]{1,0:T(8,128)(2,1)S(1)}, bf16[256,256]{1,0:T(8,128)(2,1)S(1)}, u32[]{:S(2)}, u32[]{:S(2)}) collective-permute-start(bf16[256,256]{1,0:T(8,128)(2,1)S(1)} %convert_element_type.7.w0), channel_id=1, source_target_pairs={{0,6},{2,0},{4,2},{6,4},{1,7},{3,1},{5,3},{7,5},{8,14},{10,8},{12,... | collective-permute-start | bytes 393224 | tf_op jit(solution)/shard_map/ppermute | solution.py:344
  81.9 4.3 %collective-permute-start.7 = (f32[256,1152]{1,0:T(8,128)S(1)}, f32[256,1152]{1,0:T(8,128)S(1)}, u32[]{:S(2)}, u32[]{:S(2)}) collective-permute-start(f32[256,1152]{1,0:T(8,128)S(1)} %get-tuple-element.57), channel_id=1, source_target_pairs={{0,1},{1,0},{2,3},{3,2},{4,5},{5,4},{6,7},{7,6},{8,9},{9,8},{10,11... | collective-permute-start | bytes 3538952 | tf_op jit(solution)/shard_map/ppermute | solution.py:336
  87.6 21.2 %copy-start.1 = (f32[32,512]{1,0:T(8,128)S(1)}, f32[32,512]{1,0:T(8,128)}, u32[]{:S(2)}) copy-start(f32[32,512]{1,0:T(8,128)} %h_ref.1) | copy-start | bytes 196612
  87.6 21.2 %all-to-all-start.2 = ((bf16[16,208,128]{2,1,0:T(8,128)(2,1)}), bf16[16,208,128]{2,1,0:T(8,128)(2,1)S(1)}, u32[]{:S(2)}, u32[]{:S(2)}) async-start(bf16[16,208,128]{2,1,0:T(8,128)(2,1)} %pair.2), calls=%async_computation.2 | async-start | bytes 1703936 | tf_op jit(solution)/shard_map/all_to_all | solution.py:332
  92.9 17.2 %collective-permute-start.4 = (bf16[400,256]{1,0:T(8,128)(2,1)S(1)}, bf16[400,256]{1,0:T(8,128)(2,1)S(1)}, u32[]{:S(2)}, u32[]{:S(2)}) collective-permute-start(bf16[400,256]{1,0:T(8,128)(2,1)S(1)} %get-tuple-element.53), channel_id=1, source_target_pairs={{0,2},{2,4},{4,6},{6,0},{1,3},{3,5},{5,7},{7,1},{8,10},{10,12},{12... | collective-permute-start | bytes 614408 | tf_op jit(solution)/shard_map/ppermute | solution.py:340
  94.5 15.6 %collective-permute-start.5 = (bf16[400,256]{1,0:T(8,128)(2,1)S(1)}, bf16[400,256]{1,0:T(8,128)(2,1)S(1)}, u32[]{:S(2)}, u32[]{:S(2)}) collective-permute-start(bf16[400,256]{1,0:T(8,128)(2,1)S(1)} %get-tuple-element.54), channel_id=1, source_target_pairs={{0,4},{2,6},{4,0},{6,2},{1,5},{3,7},{5,1},{7,3},{8,12},{10,14},{12... | collective-permute-start | bytes 614408 | tf_op jit(solution)/shard_map/ppermute | solution.py:340
  97.4 12.7 %collective-permute-start.6 = (bf16[400,256]{1,0:T(8,128)(2,1)S(1)}, bf16[400,256]{1,0:T(8,128)(2,1)S(1)}, u32[]{:S(2)}, u32[]{:S(2)}) collective-permute-start(bf16[400,256]{1,0:T(8,128)(2,1)S(1)} %get-tuple-element.55), channel_id=1, source_target_pairs={{0,6},{2,0},{4,2},{6,4},{1,7},{3,1},{5,3},{7,5},{8,14},{10,8},{12,... | collective-permute-start | bytes 614408 | tf_op jit(solution)/shard_map/ppermute | solution.py:340
  110.1 14.3 %all-to-all-start.3 = ((bf16[16,32,512]{2,1,0:T(8,128)(2,1)}), bf16[16,32,512]{2,1,0:T(8,128)(2,1)S(1)}, u32[]{:S(2)}, u32[]{:S(2)}) async-start(bf16[16,32,512]{2,1,0:T(8,128)(2,1)} %get-tuple-element.65), calls=%async_computation.3 | async-start | bytes 1048576 | tf_op jit(solution)/shard_map/all_to_all | solution.py:332
  114.1 7.7 %collective-permute-start.10 = (bf16[256,256]{1,0:T(8,128)(2,1)S(1)}, bf16[256,256]{1,0:T(8,128)(2,1)S(1)}, u32[]{:S(2)}, u32[]{:S(2)}) collective-permute-start(bf16[256,256]{1,0:T(8,128)(2,1)S(1)} %get-tuple-element.67.w0), channel_id=1, source_target_pairs={{0,2},{2,4},{4,6},{6,0},{1,3},{3,5},{5,7},{7,1},{8,10},{10,12},{12... | collective-permute-start | bytes 393224 | tf_op jit(solution)/shard_map/ppermute | solution.py:344
  115.7 7.9 %collective-permute-start.9 = (bf16[256,256]{1,0:T(8,128)(2,1)S(1)}, bf16[256,256]{1,0:T(8,128)(2,1)S(1)}, u32[]{:S(2)}, u32[]{:S(2)}) collective-permute-start(bf16[256,256]{1,0:T(8,128)(2,1)S(1)} %get-tuple-element.67.w0), channel_id=1, source_target_pairs={{0,4},{2,6},{4,0},{6,2},{1,5},{3,7},{5,1},{7,3},{8,12},{10,14},{12... | collective-permute-start | bytes 393224 | tf_op jit(solution)/shard_map/ppermute | solution.py:344
  118.6 5.0 %collective-permute-start.8 = (bf16[256,256]{1,0:T(8,128)(2,1)S(1)}, bf16[256,256]{1,0:T(8,128)(2,1)S(1)}, u32[]{:S(2)}, u32[]{:S(2)}) collective-permute-start(bf16[256,256]{1,0:T(8,128)(2,1)S(1)} %get-tuple-element.67.w0), channel_id=1, source_target_pairs={{0,6},{2,0},{4,2},{6,4},{1,7},{3,1},{5,3},{7,5},{8,14},{10,8},{12,... | collective-permute-start | bytes 393224 | tf_op jit(solution)/shard_map/ppermute | solution.py:344
  124.4 1.9 %collective-permute-start.11 = (bf16[4,2,2,32,512]{4,3,2,1,0:T(8,128)(2,1)S(1)}, bf16[4,2,2,32,512]{4,3,2,1,0:T(8,128)(2,1)S(1)}, u32[]{:S(2)}, u32[]{:S(2)}) collective-permute-start(bf16[4,2,2,32,512]{4,3,2,1,0:T(8,128)(2,1)S(1)} %bitcast.10), channel_id=1, source_target_pairs={{0,1},{1,0},{2,3},{3,2},{4,5},{5,4},{6,7},{7,6},{8,9},{9,8},{10,11... | collective-permute-start | bytes 1572872 | tf_op jit(solution)/shard_map/ppermute | solution.py:336
  130.3 4.4 %collective-permute-start.15 = (f32[256,1152]{1,0:T(8,128)S(1)}, f32[256,1152]{1,0:T(8,128)S(1)}, u32[]{:S(2)}, u32[]{:S(2)}) collective-permute-start(f32[256,1152]{1,0:T(8,128)S(1)} %get-tuple-element.80), channel_id=1, source_target_pairs={{0,1},{1,0},{2,3},{3,2},{4,5},{5,4},{6,7},{7,6},{8,9},{9,8},{10,11... | collective-permute-start | bytes 3538952 | tf_op jit(solution)/shard_map/ppermute | solution.py:336
  136.1 22.4 %all-to-all-start.4 = ((bf16[16,208,128]{2,1,0:T(8,128)(2,1)}), bf16[16,208,128]{2,1,0:T(8,128)(2,1)S(1)}, u32[]{:S(2)}, u32[]{:S(2)}) async-start(bf16[16,208,128]{2,1,0:T(8,128)(2,1)} %pair.3), calls=%async_computation.4 | async-start | bytes 1703936 | tf_op jit(solution)/shard_map/all_to_all | solution.py:332
  142.5 17.2 %collective-permute-start.12 = (bf16[400,256]{1,0:T(8,128)(2,1)S(1)}, bf16[400,256]{1,0:T(8,128)(2,1)S(1)}, u32[]{:S(2)}, u32[]{:S(2)}) collective-permute-start(bf16[400,256]{1,0:T(8,128)(2,1)S(1)} %get-tuple-element.76), channel_id=1, source_target_pairs={{0,2},{2,4},{4,6},{6,0},{1,3},{3,5},{5,7},{7,1},{8,10},{10,12},{12... | collective-permute-start | bytes 614408 | tf_op jit(solution)/shard_map/ppermute | solution.py:340
  143.7 16.0 %collective-permute-start.13 = (bf16[400,256]{1,0:T(8,128)(2,1)S(1)}, bf16[400,256]{1,0:T(8,128)(2,1)S(1)}, u32[]{:S(2)}, u32[]{:S(2)}) collective-permute-start(bf16[400,256]{1,0:T(8,128)(2,1)S(1)} %get-tuple-element.77), channel_id=1, source_target_pairs={{0,4},{2,6},{4,0},{6,2},{1,5},{3,7},{5,1},{7,3},{8,12},{10,14},{12... | collective-permute-start | bytes 614408 | tf_op jit(solution)/shard_map/ppermute | solution.py:340
  146.6 13.1 %collective-permute-start.14 = (bf16[400,256]{1,0:T(8,128)(2,1)S(1)}, bf16[400,256]{1,0:T(8,128)(2,1)S(1)}, u32[]{:S(2)}, u32[]{:S(2)}) collective-permute-start(bf16[400,256]{1,0:T(8,128)(2,1)S(1)} %get-tuple-element.78), channel_id=1, source_target_pairs={{0,6},{2,0},{4,2},{6,4},{1,7},{3,1},{5,3},{7,5},{8,14},{10,8},{12,... | collective-permute-start | bytes 614408 | tf_op jit(solution)/shard_map/ppermute | solution.py:340

commit v11 on v10

--- a/solution.py
+++ b/solution.py
@@ -244,7 +244,7 @@
     )(a, b)
 
 
-def h_update_kernel(parts_ref, h_ref, new_ref, low_ref):
+def h_update_kernel(parts_ref, h_ref, new_ref, *low_refs):
     each = h_ref.shape[0]
     blocks, tail = [0.0] * 4, 0.0
     for i in range(N_P):
@@ -259,22 +259,24 @@
     new = h_ref[...] * numer / colsum
     new_ref[...] = new
     low = new.astype(jnp.bfloat16)
-    for i in range(N_P):
-        low_ref[i] = low
-
-
-def h_update(parts, h):
+    for low_ref in low_refs:
+        for i in range(N_P):
+            low_ref[i] = low
+
+
+def h_update(parts, h, more):
     return pl.pallas_call(
         h_update_kernel,
         in_specs=whole(2),
-        out_specs=whole(2),
-        out_shape=[jax.ShapeDtypeStruct(h.shape, jnp.float32), jax.ShapeDtypeStruct((N_P, *h.shape), jnp.bfloat16)],
+        out_specs=whole(1 + more),
+        out_shape=[jax.ShapeDtypeStruct(h.shape, jnp.float32)]
+        + [jax.ShapeDtypeStruct((N_P, *h.shape), jnp.bfloat16)] * more,
         compiler_params=pltpu.CompilerParams(vmem_limit_bytes=12 << 20),
         name="h_update",
     )(parts, h)
 
 
-def w_update_kernel(p0, p1, p2, p3, w_ref, new_ref, low_ref):
+def w_update_kernel(p0, p1, p2, p3, w_ref, new_ref, *low_refs):
     rank = w_ref.shape[1]
     cut = rank // 2
     tops, bottoms, rowsum = p0[:cut, :], p0[cut:rank, :], p0[rank : rank + 1, :]
@@ -285,15 +287,16 @@
         rowsum = rowsum + part[rank + cut : rank + cut + 1] + part[rank + cut + 8 : rank + cut + 9]
     new = w_ref[...] * jnp.concatenate([tops, bottoms], axis=0).T / rowsum
     new_ref[...] = new
-    low_ref[...] = new.astype(jnp.bfloat16)
-
-
-def w_update(parts, w):
+    for low_ref in low_refs:
+        low_ref[...] = new.astype(jnp.bfloat16)
+
+
+def w_update(parts, w, more):
     return pl.pallas_call(
         w_update_kernel,
         in_specs=whole(5),
-        out_specs=whole(2),
-        out_shape=[jax.ShapeDtypeStruct(w.shape, jnp.float32), jax.ShapeDtypeStruct(w.shape, jnp.bfloat16)],
+        out_specs=whole(1 + more),
+        out_shape=[jax.ShapeDtypeStruct(w.shape, jnp.float32)] + [jax.ShapeDtypeStruct(w.shape, jnp.bfloat16)] * more,
         compiler_params=pltpu.CompilerParams(vmem_limit_bytes=12 << 20),
         name="w_update",
     )(*parts, w)
@@ -361,12 +364,14 @@
         n0, n1, n2, n3, s_own = half_sweep(at, spectra, h_own, ws, parts)
         w_parts = [n0] + [sent_ahead(n, t + 1) for t, n in enumerate((n1, n2, n3))]
         h_parts = exchange(pair(s_own, s_got, h.shape[0]), RANKS)
-        h, low = h_update(h_parts, h)
-        w_parts, low, h = lax.optimization_barrier((w_parts, low, h))
-        w, w_low = w_update(w_parts, w)
-        if step + 1 < ITERS:
-            ws = taken_ahead(w_low)
-            ws, h_own = lax.optimization_barrier((ws, exchange(low, RANKS)))
+        more = step + 1 < ITERS
+        h, *low = h_update(h_parts, h, more)
+        if low:
+            w_parts, low, h = lax.optimization_barrier((w_parts, low, h))
+        w, *w_low = w_update(w_parts, w, more)
+        if more:
+            ws = taken_ahead(*w_low)
+            ws, h_own = lax.optimization_barrier((ws, exchange(*low, RANKS)))
             h_own = h_own.reshape(4, 2, 2, *h.shape)
             h_oth = from_sibling(h_own)
     return (w, h)

time: 161 us -> 160 us (level)
    all_to_all x5, waiting for transfers between devices: 65.5 us -> 56 us  [exchange(): return lax.all_to_all(x, axes, 0, 0, tiled=True)]
    ppermute x6, waiting for transfers between devices: 0.02 us -> 8.52 us  [sent_ahead(): return lax.ppermute(x, 'y', [(i, (i + t) % N_Y) for i in range(N_Y)])]
  transfers between devices with their start and end apart: 21 -> 21, of which waited for: 11 -> 13; matrix products, arithmetic and copies ran while one was open for 0% -> 0% of each run, Pallas kernels for 12% -> 12%
where the time goes in v11:
time: 160 us; the launch traced here: 159 us
  waiting for transfers between devices  75.3 us (47%)
  starting transfers between devices  51.1 us (32%)
  Pallas kernels  32.1 us (20%)
    all_to_all x5, waiting for transfers between devices, exchange(): return lax.all_to_all(x, axes, 0, 0, tiled=True)  56 us
    all_to_all x5, starting transfers between devices, exchange(): return lax.all_to_all(x, axes, 0, 0, tiled=True)  28.1 us
    pallas_call x4, Pallas kernels, half_sweep(): pl.pallas_call(functools.partial(sweep_kernel, not before), in_specs=whol...  16.4 us
    ppermute x6, starting transfers between devices, taken_ahead(): lax.ppermute(x, 'y', [(i, (i - t) % N_Y) for i in range(N_Y)])  11.7 us
    ppermute x6, starting transfers between devices, sent_ahead(): return lax.ppermute(x, 'y', [(i, (i + t) % N_Y) for i in range(N_Y)])  10.9 us
    ppermute x6, waiting for transfers between devices, taken_ahead(): lax.ppermute(x, 'y', [(i, (i - t) % N_Y) for i in range(N_Y)])  8.84 us
    ppermute x6, waiting for transfers between devices, sent_ahead(): return lax.ppermute(x, 'y', [(i, (i + t) % N_Y) for i in range(N_Y)])  8.52 us
    pallas_call x1, Pallas kernels, energies(): pl.pallas_call(energy_kernel, in_specs=[pl.BlockSpec(memory_space=pl.ANY)...  7.46 us
  transfers between devices with their start and end apart: 21, of which 13 were waited for; matrix products, arithmetic and copies ran while one was open for 0% of the time, Pallas kernels for 12%

profile of v11, /device:TPU:0, one launch (start us, length us, event | category | flops | bytes accessed | tf_op | source)
XLA Modules:
  0.0 159.5 jit_solution(10938525140973864777)
XLA Ops:
  0.6 0.0 copy-start
  0.6 1.8 %spread.1 = bf16[16,32,512]{2,1,0:T(8,128)(2,1)} custom-call(f32[32,512]{1,0:T(8,128)} %h_ref.1), custom_call_target="tpu_custom_call" | custom-call | tf_op jit(solution)/shard_map/spread/pallas_call | solution.py:318
  2.5 8.0 %all-to-all-start.1 = ((bf16[16,32,512]{2,1,0:T(8,128)(2,1)}), bf16[16,32,512]{2,1,0:T(8,128)(2,1)S(1)}, u32[]{:S(2)}, u32[]{:S(2)}) async-start(bf16[16,32,512]{2,1,0:T(8,128)(2,1)} %spread.1), calls=%async_computation.1 | async-start | bytes 1048576 | tf_op jit(solution)/shard_map/all_to_all | solution.py:335
  10.5 0.0 copy-done
  10.5 7.5 %energy.1 = bf16[2,2,2,4,64,1024]{5,4,3,2,1,0:T(8,128)(2,1)} custom-call(bf16[256,16384]{1,0:T(8,128)(2,1)} %bitcast.13, bf16[256,256]{1,0:T(8,128)(2,1)} %constant.14.table_ref), custom_call_target="tpu_custom_call" | custom-call | flops 2147483648 | bytes 12582912 | tf_op jit(solution)/shard_map/energy/pallas_call | solution.py:83
  18.0 4.0 %all-to-all-done.1 = bf16[16,32,512]{2,1,0:T(8,128)(2,1)S(1)} async-done(((bf16[16,32,512]{2,1,0:T(8,128)(2,1)}), bf16[16,32,512]{2,1,0:T(8,128)(2,1)S(1)}, u32[]{:S(2)}, u32[]{:S(2)}) %all-to-all-start.1) | async-done | bytes 524320 | tf_op jit(solution)/shard_map/all_to_all | solution.py:335
  21.9 4.9 %all-to-all-start = ((bf16[32,64,1024]{2,1,0:T(8,128)(2,1)}), bf16[32,64,1024]{2,1,0:T(8,128)(2,1)}, u32[]{:S(2)}, u32[]{:S(2)}) async-start(bf16[32,64,1024]{2,1,0:T(8,128)(2,1)} %bitcast.12), calls=%async_computation | async-start | bytes 8388608 | tf_op jit(solution)/shard_map/all_to_all | solution.py:335
  26.8 0.2 collective-permute-start.3
  27.0 1.6 collective-permute-start.2
  28.6 2.9 %collective-permute-start.1 = (bf16[256,256]{1,0:T(8,128)(2,1)S(1)}, bf16[256,256]{1,0:T(8,128)(2,1)S(1)}, u32[]{:S(2)}, u32[]{:S(2)}) collective-permute-start(bf16[256,256]{1,0:T(8,128)(2,1)S(1)} %convert_element_type.7.w0), channel_id=1, source_target_pairs={{0,4},{2,6},{4,0},{6,2},{1,5},{3,7},{5,1},{7,3},{8,12},{10,14},{12... | collective-permute-start | bytes 393224 | tf_op jit(solution)/shard_map/ppermute | solution.py:347
  31.5 1.3 collective-permute-start
  32.8 0.1 pad_add_fusion.at_ref
  32.9 1.2 collective-permute-done.2.w3
  34.1 4.0 %collective-permute-done.1.w2 = bf16[256,256]{1,0:T(8,128)(2,1)S(1)} collective-permute-done((bf16[256,256]{1,0:T(8,128)(2,1)S(1)}, bf16[256,256]{1,0:T(8,128)(2,1)S(1)}, u32[]{:S(2)}, u32[]{:S(2)}) %collective-permute-start.1) | collective-permute-done | bytes 131104 | tf_op jit(solution)/shard_map/ppermute | solution.py:347
  38.1 0.0 collective-permute-done.w1
  38.1 0.0 collective-permute-done.3.h_ref
  38.1 39.8 %all-to-all-done = bf16[32,64,1024]{2,1,0:T(8,128)(2,1)} async-done(((bf16[32,64,1024]{2,1,0:T(8,128)(2,1)}), bf16[32,64,1024]{2,1,0:T(8,128)(2,1)}, u32[]{:S(2)}, u32[]{:S(2)}) %all-to-all-start) | async-done | bytes 4194336 | tf_op jit(solution)/shard_map/all_to_all | solution.py:335
  77.9 4.0 %sweep_a.2 = (f32[264,256]{1,0:T(8,128)S(1)}, f32[264,256]{1,0:T(8,128)S(1)}, f32[264,256]{1,0:T(8,128)S(1)}, f32[264,256]{1,0:T(8,128)S(1)}, f32[256,1152]{1,0:T(8,128)S(1)}) custom-call(s32[3]{0:T(128)S(1)} %pad_add_fusion.at_ref, bf16[2048,1024]{1,0:T(8,128)(2,1)} %bitcast.5.s_hbm, bf16[4,2,2,32,512]{4,3,2,1,0:T(8,128)(2,1)S(1)} %collective-permute-done.3.h_ref, ...), custom_call_target="tpu_custom_call" | custom-call | flops 1610612736 | bytes 4194304 | tf_op jit(solution)/shard_map/sweep_a/pallas_call | solution.py:188
  81.9 0.1 collective-permute-start.7
  82.0 4.2 %sweep_b.2 = (f32[264,256]{1,0:T(8,128)S(1)}, bf16[400,256]{1,0:T(8,128)(2,1)S(1)}, bf16[400,256]{1,0:T(8,128)(2,1)S(1)}, bf16[400,256]{1,0:T(8,128)(2,1)S(1)}, f32[256,1152]{1,0:T(8,128)S(1)}) custom-call(s32[3]{0:T(128)S(1)} %pad_add_fusion.at_ref, bf16[2048,1024]{1,0:T(8,128)(2,1)} %bitcast.5.s_hbm, bf16[4,2,2,32,512]{4,3,2,1,0:T(8,128)(2,1)S(1)} %bitcast.9, ...), custom_call_target="tpu_custom_call" | custom-call | flops 1610612736 | bytes 4194304 | tf_op jit(solution)/shard_map/sweep_b/pallas_call | solution.py:188
  86.2 0.0 collective-permute-done.7.b_ref
  86.2 1.4 pair.2
  87.6 0.0 copy-start.1
  87.6 5.3 %all-to-all-start.2 = ((bf16[16,208,128]{2,1,0:T(8,128)(2,1)}), bf16[16,208,128]{2,1,0:T(8,128)(2,1)S(1)}, u32[]{:S(2)}, u32[]{:S(2)}) async-start(bf16[16,208,128]{2,1,0:T(8,128)(2,1)} %pair.2), calls=%async_computation.2 | async-start | bytes 1703936 | tf_op jit(solution)/shard_map/all_to_all | solution.py:335
  92.9 1.7 %collective-permute-start.4 = (bf16[400,256]{1,0:T(8,128)(2,1)S(1)}, bf16[400,256]{1,0:T(8,128)(2,1)S(1)}, u32[]{:S(2)}, u32[]{:S(2)}) collective-permute-start(bf16[400,256]{1,0:T(8,128)(2,1)S(1)} %get-tuple-element.46), channel_id=1, source_target_pairs={{0,2},{2,4},{4,6},{6,0},{1,3},{3,5},{5,7},{7,1},{8,10},{10,12},{12... | collective-permute-start | bytes 614408 | tf_op jit(solution)/shard_map/ppermute | solution.py:343
  94.5 2.9 %collective-permute-start.5 = (bf16[400,256]{1,0:T(8,128)(2,1)S(1)}, bf16[400,256]{1,0:T(8,128)(2,1)S(1)}, u32[]{:S(2)}, u32[]{:S(2)}) collective-permute-start(bf16[400,256]{1,0:T(8,128)(2,1)S(1)} %get-tuple-element.47), channel_id=1, source_target_pairs={{0,4},{2,6},{4,0},{6,2},{1,5},{3,7},{5,1},{7,3},{8,12},{10,14},{12... | collective-permute-start | bytes 614408 | tf_op jit(solution)/shard_map/ppermute | solution.py:343
  97.5 1.3 collective-permute-start.6
  98.8 10.1 %all-to-all-done.2.parts_ref = bf16[16,208,128]{2,1,0:T(8,128)(2,1)S(1)} async-done(((bf16[16,208,128]{2,1,0:T(8,128)(2,1)}), bf16[16,208,128]{2,1,0:T(8,128)(2,1)S(1)}, u32[]{:S(2)}, u32[]{:S(2)}) %all-to-all-start.2) | async-done | bytes 852000 | tf_op jit(solution)/shard_map/all_to_all | solution.py:335
  108.9 0.0 copy-done.1
  108.9 1.2 h_update.2
  110.1 0.0 collective-permute-done.4.p1
  110.1 0.0 collective-permute-done.5.p2
  110.1 0.0 collective-permute-done.6.p3
  110.1 3.6 %all-to-all-start.3 = ((bf16[16,32,512]{2,1,0:T(8,128)(2,1)}), bf16[16,32,512]{2,1,0:T(8,128)(2,1)S(1)}, u32[]{:S(2)}, u32[]{:S(2)}) async-start(bf16[16,32,512]{2,1,0:T(8,128)(2,1)} %get-tuple-element.58), calls=%async_computation.3 | async-start | bytes 1048576 | tf_op jit(solution)/shard_map/all_to_all | solution.py:335
  113.7 0.3 w_update.2
  114.1 1.6 collective-permute-start.10
  115.7 2.9 %collective-permute-start.9 = (bf16[256,256]{1,0:T(8,128)(2,1)S(1)}, bf16[256,256]{1,0:T(8,128)(2,1)S(1)}, u32[]{:S(2)}, u32[]{:S(2)}) collective-permute-start(bf16[256,256]{1,0:T(8,128)(2,1)S(1)} %get-tuple-element.60.w0), channel_id=1, source_target_pairs={{0,4},{2,6},{4,0},{6,2},{1,5},{3,7},{5,1},{7,3},{8,12},{10,14},{12... | collective-permute-start | bytes 393224 | tf_op jit(solution)/shard_map/ppermute | solution.py:347
  118.6 1.3 collective-permute-start.8
  119.9 1.8 %collective-permute-done.10.w3 = bf16[256,256]{1,0:T(8,128)(2,1)S(1)} collective-permute-done((bf16[256,256]{1,0:T(8,128)(2,1)S(1)}, bf16[256,256]{1,0:T(8,128)(2,1)S(1)}, u32[]{:S(2)}, u32[]{:S(2)}) %collective-permute-start.10) | collective-permute-done | bytes 131104 | tf_op jit(solution)/shard_map/ppermute | solution.py:347
  121.7 1.8 %collective-permute-done.9.w2 = bf16[256,256]{1,0:T(8,128)(2,1)S(1)} collective-permute-done((bf16[256,256]{1,0:T(8,128)(2,1)S(1)}, bf16[256,256]{1,0:T(8,128)(2,1)S(1)}, u32[]{:S(2)}, u32[]{:S(2)}) %collective-permute-start.9) | collective-permute-done | bytes 131104 | tf_op jit(solution)/shard_map/ppermute | solution.py:347
  123.5 0.1 collective-permute-done.8.w1
  123.6 0.8 all-to-all-done.3
  124.4 0.0 collective-permute-start.11
  124.4 1.9 %collective-permute-done.11.h_ref = bf16[4,2,2,32,512]{4,3,2,1,0:T(8,128)(2,1)S(1)} collective-permute-done((bf16[4,2,2,32,512]{4,3,2,1,0:T(8,128)(2,1)S(1)}, bf16[4,2,2,32,512]{4,3,2,1,0:T(8,128)(2,1)S(1)}, u32[]{:S(2)}, u32[]{:S(2)}) %collective-permute-start.11) | collective-permute-done | bytes 524320 | tf_op jit(solution)/shard_map/ppermute | solution.py:339
  126.3 4.0 %sweep_a.3 = (f32[264,256]{1,0:T(8,128)S(1)}, f32[264,256]{1,0:T(8,128)S(1)}, f32[264,256]{1,0:T(8,128)S(1)}, f32[264,256]{1,0:T(8,128)S(1)}, f32[256,1152]{1,0:T(8,128)S(1)}) custom-call(s32[3]{0:T(128)S(1)} %pad_add_fusion.at_ref, bf16[2048,1024]{1,0:T(8,128)(2,1)} %bitcast.5.s_hbm, bf16[4,2,2,32,512]{4,3,2,1,0:T(8,128)(2,1)S(1)} %collective-permute-done.11.h_ref, ...), custom_call_target="tpu_custom_call" | custom-call | flops 1610612736 | bytes 4194304 | tf_op jit(solution)/shard_map/sweep_a/pallas_call | solution.py:188
  130.3 0.2 collective-permute-start.15
  130.5 4.2 %sweep_b.3 = (f32[264,256]{1,0:T(8,128)S(1)}, bf16[400,256]{1,0:T(8,128)(2,1)S(1)}, bf16[400,256]{1,0:T(8,128)(2,1)S(1)}, bf16[400,256]{1,0:T(8,128)(2,1)S(1)}, f32[256,1152]{1,0:T(8,128)S(1)}) custom-call(s32[3]{0:T(128)S(1)} %pad_add_fusion.at_ref, bf16[2048,1024]{1,0:T(8,128)(2,1)} %bitcast.5.s_hbm, bf16[4,2,2,32,512]{4,3,2,1,0:T(8,128)(2,1)S(1)} %bitcast.11, ...), custom_call_target="tpu_custom_call" | custom-call | flops 1610612736 | bytes 4194304 | tf_op jit(solution)/shard_map/sweep_b/pallas_call | solution.py:188
  134.8 0.0 collective-permute-done.15.b_ref
  134.8 1.4 pair.3
  136.2 6.4 %all-to-all-start.4 = ((bf16[16,208,128]{2,1,0:T(8,128)(2,1)}), bf16[16,208,128]{2,1,0:T(8,128)(2,1)S(1)}, u32[]{:S(2)}, u32[]{:S(2)}) async-start(bf16[16,208,128]{2,1,0:T(8,128)(2,1)} %pair.3), calls=%async_computation.4 | async-start | bytes 1703936 | tf_op jit(solution)/shard_map/all_to_all | solution.py:335
  142.5 1.2 collective-permute-start.12
  143.7 2.9 %collective-permute-start.13 = (bf16[400,256]{1,0:T(8,128)(2,1)S(1)}, bf16[400,256]{1,0:T(8,128)(2,1)S(1)}, u32[]{:S(2)}, u32[]{:S(2)}) collective-permute-start(bf16[400,256]{1,0:T(8,128)(2,1)S(1)} %get-tuple-element.70), channel_id=1, source_target_pairs={{0,4},{2,6},{4,0},{6,2},{1,5},{3,7},{5,1},{7,3},{8,12},{10,14},{12... | collective-permute-start | bytes 614408 | tf_op jit(solution)/shard_map/ppermute | solution.py:343
  146.6 0.9 collective-permute-start.14
  147.5 3.4 %collective-permute-done.12.p1 = bf16[400,256]{1,0:T(8,128)(2,1)S(1)} collective-permute-done((bf16[400,256]{1,0:T(8,128)(2,1)S(1)}, bf16[400,256]{1,0:T(8,128)(2,1)S(1)}, u32[]{:S(2)}, u32[]{:S(2)}) %collective-permute-start.12) | collective-permute-done | bytes 204832 | tf_op jit(solution)/shard_map/ppermute | solution.py:343
  150.9 5.1 %collective-permute-done.13.p2 = bf16[400,256]{1,0:T(8,128)(2,1)S(1)} collective-permute-done((bf16[400,256]{1,0:T(8,128)(2,1)S(1)}, bf16[400,256]{1,0:T(8,128)(2,1)S(1)}, u32[]{:S(2)}, u32[]{:S(2)}) %collective-permute-start.13) | collective-permute-done | bytes 204832 | tf_op jit(solution)/shard_map/ppermute | solution.py:343
  156.0 0.0 collective-permute-done.14.p3
  156.0 1.0 w_update.3
  157.1 1.4 all-to-all-done.4.parts_ref
  158.5 1.0 h_update.3
  (1 shorter events, 0.0 us)
Async XLA Ops:
  0.6 9.8 %copy-start = (f32[256,256]{1,0:T(8,128)S(1)}, f32[256,256]{1,0:T(8,128)}, u32[]{:S(2)}) copy-start(f32[256,256]{1,0:T(8,128)} %w_ref.1) | copy-start | bytes 786436
  2.5 19.5 %all-to-all-start.1 = ((bf16[16,32,512]{2,1,0:T(8,128)(2,1)}), bf16[16,32,512]{2,1,0:T(8,128)(2,1)S(1)}, u32[]{:S(2)}, u32[]{:S(2)}) async-start(bf16[16,32,512]{2,1,0:T(8,128)(2,1)} %spread.1), calls=%async_computation.1 | async-start | bytes 1048576 | tf_op jit(solution)/shard_map/all_to_all | solution.py:335
  21.9 55.9 %all-to-all-start = ((bf16[32,64,1024]{2,1,0:T(8,128)(2,1)}), bf16[32,64,1024]{2,1,0:T(8,128)(2,1)}, u32[]{:S(2)}, u32[]{:S(2)}) async-start(bf16[32,64,1024]{2,1,0:T(8,128)(2,1)} %bitcast.12), calls=%async_computation | async-start | bytes 8388608 | tf_op jit(solution)/shard_map/all_to_all | solution.py:335
  26.8 11.3 %collective-permute-start.3 = (bf16[4,2,2,32,512]{4,3,2,1,0:T(8,128)(2,1)S(1)}, bf16[4,2,2,32,512]{4,3,2,1,0:T(8,128)(2,1)S(1)}, u32[]{:S(2)}, u32[]{:S(2)}) collective-permute-start(bf16[4,2,2,32,512]{4,3,2,1,0:T(8,128)(2,1)S(1)} %bitcast.8), channel_id=1, source_target_pairs={{0,1},{1,0},{2,3},{3,2},{4,5},{5,4},{6,7},{7,6},{8,9},{9,8},{10,11... | collective-permute-start | bytes 1572872 | tf_op jit(solution)/shard_map/ppermute | solution.py:339
  27.0 7.1 %collective-permute-start.2 = (bf16[256,256]{1,0:T(8,128)(2,1)S(1)}, bf16[256,256]{1,0:T(8,128)(2,1)S(1)}, u32[]{:S(2)}, u32[]{:S(2)}) collective-permute-start(bf16[256,256]{1,0:T(8,128)(2,1)S(1)} %convert_element_type.7.w0), channel_id=1, source_target_pairs={{0,2},{2,4},{4,6},{6,0},{1,3},{3,5},{5,7},{7,1},{8,10},{10,12},{12... | collective-permute-start | bytes 393224 | tf_op jit(solution)/shard_map/ppermute | solution.py:347
  28.6 9.5 %collective-permute-start.1 = (bf16[256,256]{1,0:T(8,128)(2,1)S(1)}, bf16[256,256]{1,0:T(8,128)(2,1)S(1)}, u32[]{:S(2)}, u32[]{:S(2)}) collective-permute-start(bf16[256,256]{1,0:T(8,128)(2,1)S(1)} %convert_element_type.7.w0), channel_id=1, source_target_pairs={{0,4},{2,6},{4,0},{6,2},{1,5},{3,7},{5,1},{7,3},{8,12},{10,14},{12... | collective-permute-start | bytes 393224 | tf_op jit(solution)/shard_map/ppermute | solution.py:347
  31.5 6.6 %collective-permute-start = (bf16[256,256]{1,0:T(8,128)(2,1)S(1)}, bf16[256,256]{1,0:T(8,128)(2,1)S(1)}, u32[]{:S(2)}, u32[]{:S(2)}) collective-permute-start(bf16[256,256]{1,0:T(8,128)(2,1)S(1)} %convert_element_type.7.w0), channel_id=1, source_target_pairs={{0,6},{2,0},{4,2},{6,4},{1,7},{3,1},{5,3},{7,5},{8,14},{10,8},{12,... | collective-permute-start | bytes 393224 | tf_op jit(solution)/shard_map/ppermute | solution.py:347
  81.9 4.3 %collective-permute-start.7 = (f32[256,1152]{1,0:T(8,128)S(1)}, f32[256,1152]{1,0:T(8,128)S(1)}, u32[]{:S(2)}, u32[]{:S(2)}) collective-permute-start(f32[256,1152]{1,0:T(8,128)S(1)} %get-tuple-element.50), channel_id=1, source_target_pairs={{0,1},{1,0},{2,3},{3,2},{4,5},{5,4},{6,7},{7,6},{8,9},{9,8},{10,11... | collective-permute-start | bytes 3538952 | tf_op jit(solution)/shard_map/ppermute | solution.py:339
  87.6 21.2 %copy-start.1 = (f32[32,512]{1,0:T(8,128)S(1)}, f32[32,512]{1,0:T(8,128)}, u32[]{:S(2)}) copy-start(f32[32,512]{1,0:T(8,128)} %h_ref.1) | copy-start | bytes 196612
  87.6 21.2 %all-to-all-start.2 = ((bf16[16,208,128]{2,1,0:T(8,128)(2,1)}), bf16[16,208,128]{2,1,0:T(8,128)(2,1)S(1)}, u32[]{:S(2)}, u32[]{:S(2)}) async-start(bf16[16,208,128]{2,1,0:T(8,128)(2,1)} %pair.2), calls=%async_computation.2 | async-start | bytes 1703936 | tf_op jit(solution)/shard_map/all_to_all | solution.py:335
  92.9 17.2 %collective-permute-start.4 = (bf16[400,256]{1,0:T(8,128)(2,1)S(1)}, bf16[400,256]{1,0:T(8,128)(2,1)S(1)}, u32[]{:S(2)}, u32[]{:S(2)}) collective-permute-start(bf16[400,256]{1,0:T(8,128)(2,1)S(1)} %get-tuple-element.46), channel_id=1, source_target_pairs={{0,2},{2,4},{4,6},{6,0},{1,3},{3,5},{5,7},{7,1},{8,10},{10,12},{12... | collective-permute-start | bytes 614408 | tf_op jit(solution)/shard_map/ppermute | solution.py:343
  94.5 15.6 %collective-permute-start.5 = (bf16[400,256]{1,0:T(8,128)(2,1)S(1)}, bf16[400,256]{1,0:T(8,128)(2,1)S(1)}, u32[]{:S(2)}, u32[]{:S(2)}) collective-permute-start(bf16[400,256]{1,0:T(8,128)(2,1)S(1)} %get-tuple-element.47), channel_id=1, source_target_pairs={{0,4},{2,6},{4,0},{6,2},{1,5},{3,7},{5,1},{7,3},{8,12},{10,14},{12... | collective-permute-start | bytes 614408 | tf_op jit(solution)/shard_map/ppermute | solution.py:343
  97.5 12.7 %collective-permute-start.6 = (bf16[400,256]{1,0:T(8,128)(2,1)S(1)}, bf16[400,256]{1,0:T(8,128)(2,1)S(1)}, u32[]{:S(2)}, u32[]{:S(2)}) collective-permute-start(bf16[400,256]{1,0:T(8,128)(2,1)S(1)} %get-tuple-element.48), channel_id=1, source_target_pairs={{0,6},{2,0},{4,2},{6,4},{1,7},{3,1},{5,3},{7,5},{8,14},{10,8},{12,... | collective-permute-start | bytes 614408 | tf_op jit(solution)/shard_map/ppermute | solution.py:343
  110.1 14.3 %all-to-all-start.3 = ((bf16[16,32,512]{2,1,0:T(8,128)(2,1)}), bf16[16,32,512]{2,1,0:T(8,128)(2,1)S(1)}, u32[]{:S(2)}, u32[]{:S(2)}) async-start(bf16[16,32,512]{2,1,0:T(8,128)(2,1)} %get-tuple-element.58), calls=%async_computation.3 | async-start | bytes 1048576 | tf_op jit(solution)/shard_map/all_to_all | solution.py:335
  114.1 7.7 %collective-permute-start.10 = (bf16[256,256]{1,0:T(8,128)(2,1)S(1)}, bf16[256,256]{1,0:T(8,128)(2,1)S(1)}, u32[]{:S(2)}, u32[]{:S(2)}) collective-permute-start(bf16[256,256]{1,0:T(8,128)(2,1)S(1)} %get-tuple-element.60.w0), channel_id=1, source_target_pairs={{0,2},{2,4},{4,6},{6,0},{1,3},{3,5},{5,7},{7,1},{8,10},{10,12},{12... | collective-permute-start | bytes 393224 | tf_op jit(solution)/shard_map/ppermute | solution.py:347
  115.7 7.8 %collective-permute-start.9 = (bf16[256,256]{1,0:T(8,128)(2,1)S(1)}, bf16[256,256]{1,0:T(8,128)(2,1)S(1)}, u32[]{:S(2)}, u32[]{:S(2)}) collective-permute-start(bf16[256,256]{1,0:T(8,128)(2,1)S(1)} %get-tuple-element.60.w0), channel_id=1, source_target_pairs={{0,4},{2,6},{4,0},{6,2},{1,5},{3,7},{5,1},{7,3},{8,12},{10,14},{12... | collective-permute-start | bytes 393224 | tf_op jit(solution)/shard_map/ppermute | solution.py:347
  118.6 5.0 %collective-permute-start.8 = (bf16[256,256]{1,0:T(8,128)(2,1)S(1)}, bf16[256,256]{1,0:T(8,128)(2,1)S(1)}, u32[]{:S(2)}, u32[]{:S(2)}) collective-permute-start(bf16[256,256]{1,0:T(8,128)(2,1)S(1)} %get-tuple-element.60.w0), channel_id=1, source_target_pairs={{0,6},{2,0},{4,2},{6,4},{1,7},{3,1},{5,3},{7,5},{8,14},{10,8},{12,... | collective-permute-start | bytes 393224 | tf_op jit(solution)/shard_map/ppermute | solution.py:347
  124.4 1.9 %collective-permute-start.11 = (bf16[4,2,2,32,512]{4,3,2,1,0:T(8,128)(2,1)S(1)}, bf16[4,2,2,32,512]{4,3,2,1,0:T(8,128)(2,1)S(1)}, u32[]{:S(2)}, u32[]{:S(2)}) collective-permute-start(bf16[4,2,2,32,512]{4,3,2,1,0:T(8,128)(2,1)S(1)} %bitcast.10), channel_id=1, source_target_pairs={{0,1},{1,0},{2,3},{3,2},{4,5},{5,4},{6,7},{7,6},{8,9},{9,8},{10,11... | collective-permute-start | bytes 1572872 | tf_op jit(solution)/shard_map/ppermute | solution.py:339
  130.3 4.4 %collective-permute-start.15 = (f32[256,1152]{1,0:T(8,128)S(1)}, f32[256,1152]{1,0:T(8,128)S(1)}, u32[]{:S(2)}, u32[]{:S(2)}) collective-permute-start(f32[256,1152]{1,0:T(8,128)S(1)} %get-tuple-element.74), channel_id=1, source_target_pairs={{0,1},{1,0},{2,3},{3,2},{4,5},{5,4},{6,7},{7,6},{8,9},{9,8},{10,11... | collective-permute-start | bytes 3538952 | tf_op jit(solution)/shard_map/ppermute | solution.py:339
  136.2 22.3 %all-to-all-start.4 = ((bf16[16,208,128]{2,1,0:T(8,128)(2,1)}), bf16[16,208,128]{2,1,0:T(8,128)(2,1)S(1)}, u32[]{:S(2)}, u32[]{:S(2)}) async-start(bf16[16,208,128]{2,1,0:T(8,128)(2,1)} %pair.3), calls=%async_computation.4 | async-start | bytes 1703936 | tf_op jit(solution)/shard_map/all_to_all | solution.py:335
  142.5 8.4 %collective-permute-start.12 = (bf16[400,256]{1,0:T(8,128)(2,1)S(1)}, bf16[400,256]{1,0:T(8,128)(2,1)S(1)}, u32[]{:S(2)}, u32[]{:S(2)}) collective-permute-start(bf16[400,256]{1,0:T(8,128)(2,1)S(1)} %get-tuple-element.69), channel_id=1, source_target_pairs={{0,2},{2,4},{4,6},{6,0},{1,3},{3,5},{5,7},{7,1},{8,10},{10,12},{12... | collective-permute-start | bytes 614408 | tf_op jit(solution)/shard_map/ppermute | solution.py:343
  143.7 12.4 %collective-permute-start.13 = (bf16[400,256]{1,0:T(8,128)(2,1)S(1)}, bf16[400,256]{1,0:T(8,128)(2,1)S(1)}, u32[]{:S(2)}, u32[]{:S(2)}) collective-permute-start(bf16[400,256]{1,0:T(8,128)(2,1)S(1)} %get-tuple-element.70), channel_id=1, source_target_pairs={{0,4},{2,6},{4,0},{6,2},{1,5},{3,7},{5,1},{7,3},{8,12},{10,14},{12... | collective-permute-start | bytes 614408 | tf_op jit(solution)/shard_map/ppermute | solution.py:343
  146.6 9.4 %collective-permute-start.14 = (bf16[400,256]{1,0:T(8,128)(2,1)S(1)}, bf16[400,256]{1,0:T(8,128)(2,1)S(1)}, u32[]{:S(2)}, u32[]{:S(2)}) collective-permute-start(bf16[400,256]{1,0:T(8,128)(2,1)S(1)} %get-tuple-element.71), channel_id=1, source_target_pairs={{0,6},{2,0},{4,2},{6,4},{1,7},{3,1},{5,3},{7,5},{8,14},{10,8},{12,... | collective-permute-start | bytes 614408 | tf_op jit(solution)/shard_map/ppermute | solution.py:343

commit v12 on v11

--- a/solution.py
+++ b/solution.py
@@ -354,8 +354,7 @@
     h_own = exchange(spread(h), RANKS).reshape(4, 2, 2, *h.shape)
     energy = energies(record, dft_table())
     frames, rows = energy.shape[4:]
-    energy, w_low = lax.optimization_barrier((energy, w.astype(jnp.bfloat16)))
-    ws = taken_ahead(w_low)
+    energy, ws = lax.optimization_barrier((energy, taken_ahead(w.astype(jnp.bfloat16))))
     h_oth = from_sibling(h_own)
     spectra = exchange(energy.reshape(2 * N_P, frames, rows), TILE).reshape(2 * N_P * frames, rows)
     for step in range(ITERS):

time: 160 us -> 164 us (1.025)
  waiting for transfers between devices: 75.3 us -> 80.9 us
  starting transfers between devices: 51.1 us -> 49.3 us
    all_to_all x5, waiting for transfers between devices: 56 us -> 62.4 us  [exchange(): return lax.all_to_all(x, axes, 0, 0, tiled=True)]
    ppermute x6, waiting for transfers between devices: 8.84 us -> 5.68 us  [taken_ahead(): lax.ppermute(x, 'y', [(i, (i - t) % N_Y) for i in range(N_Y)])]
    all_to_all x5, starting transfers between devices: 28.1 us -> 31.2 us  [exchange(): return lax.all_to_all(x, axes, 0, 0, tiled=True)]
    ppermute x6, starting transfers between devices: 11.7 us -> 8.79 us  [taken_ahead(): lax.ppermute(x, 'y', [(i, (i - t) % N_Y) for i in range(N_Y)])]
    ppermute x6, starting transfers between devices: 10.9 us -> 8.73 us  [sent_ahead(): return lax.ppermute(x, 'y', [(i, (i + t) % N_Y) for i in range(N_Y)])]
  transfers between devices with their start and end apart: 21 -> 21, of which waited for: 13 -> 11; matrix products, arithmetic and copies ran while one was open for 0% -> 0% of each run, Pallas kernels for 12% -> 11%
where the time goes in v12:
time: 164 us; the launch traced here: 163 us
  waiting for transfers between devices  80.9 us (49%)
  starting transfers between devices  49.3 us (30%)
  Pallas kernels  32.1 us (20%)
    all_to_all x5, waiting for transfers between devices, exchange(): return lax.all_to_all(x, axes, 0, 0, tiled=True)  62.4 us
    all_to_all x5, starting transfers between devices, exchange(): return lax.all_to_all(x, axes, 0, 0, tiled=True)  31.2 us
    pallas_call x4, Pallas kernels, half_sweep(): pl.pallas_call(functools.partial(sweep_kernel, not before), in_specs=whol...  16.4 us
    ppermute x6, waiting for transfers between devices, sent_ahead(): return lax.ppermute(x, 'y', [(i, (i + t) % N_Y) for i in range(N_Y)])  9.33 us
    ppermute x6, starting transfers between devices, taken_ahead(): lax.ppermute(x, 'y', [(i, (i - t) % N_Y) for i in range(N_Y)])  8.79 us
    ppermute x6, starting transfers between devices, sent_ahead(): return lax.ppermute(x, 'y', [(i, (i + t) % N_Y) for i in range(N_Y)])  8.73 us
    pallas_call x1, Pallas kernels, energies(): pl.pallas_call(energy_kernel, in_specs=[pl.BlockSpec(memory_space=pl.ANY)...  7.43 us
    ppermute x6, waiting for transfers between devices, taken_ahead(): lax.ppermute(x, 'y', [(i, (i - t) % N_Y) for i in range(N_Y)])  5.68 us
  transfers between devices with their start and end apart: 21, of which 11 were waited for; matrix products, arithmetic and copies ran while one was open for 0% of the time, Pallas kernels for 11%

profile of v12, /device:TPU:0, one launch (start us, length us, event | category | flops | bytes accessed | tf_op | source)
XLA Modules:
  0.0 163.2 jit_solution(3271794673338007667)
XLA Ops:
  0.6 0.0 copy-start
  0.6 1.8 %spread.1 = bf16[16,32,512]{2,1,0:T(8,128)(2,1)} custom-call(f32[32,512]{1,0:T(8,128)} %h_ref.1), custom_call_target="tpu_custom_call" | custom-call | tf_op jit(solution)/shard_map/spread/pallas_call | solution.py:318
  2.5 8.0 %all-to-all-start.1 = ((bf16[16,32,512]{2,1,0:T(8,128)(2,1)}), bf16[16,32,512]{2,1,0:T(8,128)(2,1)S(1)}, u32[]{:S(2)}, u32[]{:S(2)}) async-start(bf16[16,32,512]{2,1,0:T(8,128)(2,1)} %spread.1), calls=%async_computation.1 | async-start | bytes 1048576 | tf_op jit(solution)/shard_map/all_to_all | solution.py:335
  10.5 0.0 copy-done
  10.5 3.1 %collective-permute-start = (bf16[256,256]{1,0:T(8,128)(2,1)S(1)}, bf16[256,256]{1,0:T(8,128)(2,1)S(1)}, u32[]{:S(2)}, u32[]{:S(2)}) collective-permute-start(bf16[256,256]{1,0:T(8,128)(2,1)S(1)} %convert_element_type.7.w0), channel_id=1, source_target_pairs={{0,6},{2,0},{4,2},{6,4},{1,7},{3,1},{5,3},{7,5},{8,14},{10,8},{12,... | collective-permute-start | bytes 393224 | tf_op jit(solution)/shard_map/ppermute | solution.py:347
  13.6 0.6 collective-permute-start.1
  14.2 1.0 collective-permute-start.2
  15.2 7.4 %energy.1 = bf16[2,2,2,4,64,1024]{5,4,3,2,1,0:T(8,128)(2,1)} custom-call(bf16[256,16384]{1,0:T(8,128)(2,1)} %bitcast.13, bf16[256,256]{1,0:T(8,128)(2,1)} %constant.14.table_ref), custom_call_target="tpu_custom_call" | custom-call | flops 2147483648 | bytes 12582912 | tf_op jit(solution)/shard_map/energy/pallas_call | solution.py:83
  22.6 0.0 collective-permute-done.w1
  22.6 0.0 collective-permute-done.1.w2
  22.6 0.0 collective-permute-done.2.w3
  22.6 0.0 all-to-all-done.1
  22.7 7.6 %all-to-all-start = ((bf16[32,64,1024]{2,1,0:T(8,128)(2,1)}), bf16[32,64,1024]{2,1,0:T(8,128)(2,1)}, u32[]{:S(2)}, u32[]{:S(2)}) async-start(bf16[32,64,1024]{2,1,0:T(8,128)(2,1)} %bitcast.12), calls=%async_computation | async-start | bytes 8388608 | tf_op jit(solution)/shard_map/all_to_all | solution.py:335
  30.3 0.3 collective-permute-start.3
  30.6 0.1 pad_add_fusion.at_ref
  30.7 1.6 %collective-permute-done.3.h_ref = bf16[4,2,2,32,512]{4,3,2,1,0:T(8,128)(2,1)S(1)} collective-permute-done((bf16[4,2,2,32,512]{4,3,2,1,0:T(8,128)(2,1)S(1)}, bf16[4,2,2,32,512]{4,3,2,1,0:T(8,128)(2,1)S(1)}, u32[]{:S(2)}, u32[]{:S(2)}) %collective-permute-start.3) | collective-permute-done | bytes 524320 | tf_op jit(solution)/shard_map/ppermute | solution.py:339
  32.3 49.1 %all-to-all-done = bf16[32,64,1024]{2,1,0:T(8,128)(2,1)} async-done(((bf16[32,64,1024]{2,1,0:T(8,128)(2,1)}), bf16[32,64,1024]{2,1,0:T(8,128)(2,1)}, u32[]{:S(2)}, u32[]{:S(2)}) %all-to-all-start) | async-done | bytes 4194336 | tf_op jit(solution)/shard_map/all_to_all | solution.py:335
  81.4 4.0 %sweep_a.2 = (f32[264,256]{1,0:T(8,128)S(1)}, f32[264,256]{1,0:T(8,128)S(1)}, f32[264,256]{1,0:T(8,128)S(1)}, f32[264,256]{1,0:T(8,128)S(1)}, f32[256,1152]{1,0:T(8,128)S(1)}) custom-call(s32[3]{0:T(128)S(1)} %pad_add_fusion.at_ref, bf16[2048,1024]{1,0:T(8,128)(2,1)} %bitcast.5.s_hbm, bf16[4,2,2,32,512]{4,3,2,1,0:T(8,128)(2,1)S(1)} %collective-permute-done.3.h_ref, ...), custom_call_target="tpu_custom_call" | custom-call | flops 1610612736 | bytes 4194304 | tf_op jit(solution)/shard_map/sweep_a/pallas_call | solution.py:188
  85.4 0.1 collective-permute-start.7
  85.5 4.2 %sweep_b.2 = (f32[264,256]{1,0:T(8,128)S(1)}, bf16[400,256]{1,0:T(8,128)(2,1)S(1)}, bf16[400,256]{1,0:T(8,128)(2,1)S(1)}, bf16[400,256]{1,0:T(8,128)(2,1)S(1)}, f32[256,1152]{1,0:T(8,128)S(1)}) custom-call(s32[3]{0:T(128)S(1)} %pad_add_fusion.at_ref, bf16[2048,1024]{1,0:T(8,128)(2,1)} %bitcast.5.s_hbm, bf16[4,2,2,32,512]{4,3,2,1,0:T(8,128)(2,1)S(1)} %bitcast.9, ...), custom_call_target="tpu_custom_call" | custom-call | flops 1610612736 | bytes 4194304 | tf_op jit(solution)/shard_map/sweep_b/pallas_call | solution.py:188
  89.7 0.0 collective-permute-done.7.b_ref
  89.7 1.4 pair.2
  91.1 0.0 copy-start.1
  91.1 5.3 %all-to-all-start.2 = ((bf16[16,208,128]{2,1,0:T(8,128)(2,1)}), bf16[16,208,128]{2,1,0:T(8,128)(2,1)S(1)}, u32[]{:S(2)}, u32[]{:S(2)}) async-start(bf16[16,208,128]{2,1,0:T(8,128)(2,1)} %pair.2), calls=%async_computation.2 | async-start | bytes 1703936 | tf_op jit(solution)/shard_map/all_to_all | solution.py:335
  96.4 2.0 %collective-permute-start.4 = (bf16[400,256]{1,0:T(8,128)(2,1)S(1)}, bf16[400,256]{1,0:T(8,128)(2,1)S(1)}, u32[]{:S(2)}, u32[]{:S(2)}) collective-permute-start(bf16[400,256]{1,0:T(8,128)(2,1)S(1)} %get-tuple-element.52), channel_id=1, source_target_pairs={{0,2},{2,4},{4,6},{6,0},{1,3},{3,5},{5,7},{7,1},{8,10},{10,12},{12... | collective-permute-start | bytes 614408 | tf_op jit(solution)/shard_map/ppermute | solution.py:343
  98.4 1.8 %collective-permute-start.5 = (bf16[400,256]{1,0:T(8,128)(2,1)S(1)}, bf16[400,256]{1,0:T(8,128)(2,1)S(1)}, u32[]{:S(2)}, u32[]{:S(2)}) collective-permute-start(bf16[400,256]{1,0:T(8,128)(2,1)S(1)} %get-tuple-element.53), channel_id=1, source_target_pairs={{0,4},{2,6},{4,0},{6,2},{1,5},{3,7},{5,1},{7,3},{8,12},{10,14},{12... | collective-permute-start | bytes 614408 | tf_op jit(solution)/shard_map/ppermute | solution.py:343
  100.2 0.9 collective-permute-start.6
  101.1 11.2 %all-to-all-done.2.parts_ref = bf16[16,208,128]{2,1,0:T(8,128)(2,1)S(1)} async-done(((bf16[16,208,128]{2,1,0:T(8,128)(2,1)}), bf16[16,208,128]{2,1,0:T(8,128)(2,1)S(1)}, u32[]{:S(2)}, u32[]{:S(2)}) %all-to-all-start.2) | async-done | bytes 852000 | tf_op jit(solution)/shard_map/all_to_all | solution.py:335
  112.3 0.0 copy-done.1
  112.3 1.2 h_update.2
  113.6 0.0 collective-permute-done.4.p1
  113.6 0.0 collective-permute-done.5.p2
  113.6 0.0 collective-permute-done.6.p3
  113.6 3.6 %all-to-all-start.3 = ((bf16[16,32,512]{2,1,0:T(8,128)(2,1)}), bf16[16,32,512]{2,1,0:T(8,128)(2,1)S(1)}, u32[]{:S(2)}, u32[]{:S(2)}) async-start(bf16[16,32,512]{2,1,0:T(8,128)(2,1)} %get-tuple-element.64), calls=%async_computation.3 | async-start | bytes 1048576 | tf_op jit(solution)/shard_map/all_to_all | solution.py:335
  117.2 0.3 w_update.2
  117.5 2.0 %collective-permute-start.10 = (bf16[256,256]{1,0:T(8,128)(2,1)S(1)}, bf16[256,256]{1,0:T(8,128)(2,1)S(1)}, u32[]{:S(2)}, u32[]{:S(2)}) collective-permute-start(bf16[256,256]{1,0:T(8,128)(2,1)S(1)} %get-tuple-element.66.w0), channel_id=1, source_target_pairs={{0,2},{2,4},{4,6},{6,0},{1,3},{3,5},{5,7},{7,1},{8,10},{10,12},{12... | collective-permute-start | bytes 393224 | tf_op jit(solution)/shard_map/ppermute | solution.py:347
  119.5 1.3 collective-permute-start.8
  120.8 0.8 collective-permute-start.9
  121.6 2.7 %collective-permute-done.10.w3 = bf16[256,256]{1,0:T(8,128)(2,1)S(1)} collective-permute-done((bf16[256,256]{1,0:T(8,128)(2,1)S(1)}, bf16[256,256]{1,0:T(8,128)(2,1)S(1)}, u32[]{:S(2)}, u32[]{:S(2)}) %collective-permute-start.10) | collective-permute-done | bytes 131104 | tf_op jit(solution)/shard_map/ppermute | solution.py:347
  124.3 0.8 collective-permute-done.8.w1
  125.1 2.2 %collective-permute-done.9.w2 = bf16[256,256]{1,0:T(8,128)(2,1)S(1)} collective-permute-done((bf16[256,256]{1,0:T(8,128)(2,1)S(1)}, bf16[256,256]{1,0:T(8,128)(2,1)S(1)}, u32[]{:S(2)}, u32[]{:S(2)}) %collective-permute-start.9) | collective-permute-done | bytes 131104 | tf_op jit(solution)/shard_map/ppermute | solution.py:347
  127.3 0.5 all-to-all-done.3
  127.9 0.0 collective-permute-start.11
  127.9 1.9 %collective-permute-done.11.h_ref = bf16[4,2,2,32,512]{4,3,2,1,0:T(8,128)(2,1)S(1)} collective-permute-done((bf16[4,2,2,32,512]{4,3,2,1,0:T(8,128)(2,1)S(1)}, bf16[4,2,2,32,512]{4,3,2,1,0:T(8,128)(2,1)S(1)}, u32[]{:S(2)}, u32[]{:S(2)}) %collective-permute-start.11) | collective-permute-done | bytes 524320 | tf_op jit(solution)/shard_map/ppermute | solution.py:339
  129.8 4.0 %sweep_a.3 = (f32[264,256]{1,0:T(8,128)S(1)}, f32[264,256]{1,0:T(8,128)S(1)}, f32[264,256]{1,0:T(8,128)S(1)}, f32[264,256]{1,0:T(8,128)S(1)}, f32[256,1152]{1,0:T(8,128)S(1)}) custom-call(s32[3]{0:T(128)S(1)} %pad_add_fusion.at_ref, bf16[2048,1024]{1,0:T(8,128)(2,1)} %bitcast.5.s_hbm, bf16[4,2,2,32,512]{4,3,2,1,0:T(8,128)(2,1)S(1)} %collective-permute-done.11.h_ref, ...), custom_call_target="tpu_custom_call" | custom-call | flops 1610612736 | bytes 4194304 | tf_op jit(solution)/shard_map/sweep_a/pallas_call | solution.py:188
  133.8 0.2 collective-permute-start.15
  134.0 4.2 %sweep_b.3 = (f32[264,256]{1,0:T(8,128)S(1)}, bf16[400,256]{1,0:T(8,128)(2,1)S(1)}, bf16[400,256]{1,0:T(8,128)(2,1)S(1)}, bf16[400,256]{1,0:T(8,128)(2,1)S(1)}, f32[256,1152]{1,0:T(8,128)S(1)}) custom-call(s32[3]{0:T(128)S(1)} %pad_add_fusion.at_ref, bf16[2048,1024]{1,0:T(8,128)(2,1)} %bitcast.5.s_hbm, bf16[4,2,2,32,512]{4,3,2,1,0:T(8,128)(2,1)S(1)} %bitcast.11, ...), custom_call_target="tpu_custom_call" | custom-call | flops 1610612736 | bytes 4194304 | tf_op jit(solution)/shard_map/sweep_b/pallas_call | solution.py:188
  138.2 0.0 collective-permute-done.15.b_ref
  138.2 1.4 pair.3
  139.6 6.7 %all-to-all-start.4 = ((bf16[16,208,128]{2,1,0:T(8,128)(2,1)}), bf16[16,208,128]{2,1,0:T(8,128)(2,1)S(1)}, u32[]{:S(2)}, u32[]{:S(2)}) async-start(bf16[16,208,128]{2,1,0:T(8,128)(2,1)} %pair.3), calls=%async_computation.4 | async-start | bytes 1703936 | tf_op jit(solution)/shard_map/all_to_all | solution.py:335
  146.3 0.7 collective-permute-start.12
  147.0 2.4 %collective-permute-start.13 = (bf16[400,256]{1,0:T(8,128)(2,1)S(1)}, bf16[400,256]{1,0:T(8,128)(2,1)S(1)}, u32[]{:S(2)}, u32[]{:S(2)}) collective-permute-start(bf16[400,256]{1,0:T(8,128)(2,1)S(1)} %get-tuple-element.76), channel_id=1, source_target_pairs={{0,4},{2,6},{4,0},{6,2},{1,5},{3,7},{5,1},{7,3},{8,12},{10,14},{12... | collective-permute-start | bytes 614408 | tf_op jit(solution)/shard_map/ppermute | solution.py:343
  149.4 0.9 collective-permute-start.14
  150.3 8.7 %collective-permute-done.12.p1 = bf16[400,256]{1,0:T(8,128)(2,1)S(1)} collective-permute-done((bf16[400,256]{1,0:T(8,128)(2,1)S(1)}, bf16[400,256]{1,0:T(8,128)(2,1)S(1)}, u32[]{:S(2)}, u32[]{:S(2)}) %collective-permute-start.12) | collective-permute-done | bytes 204832 | tf_op jit(solution)/shard_map/ppermute | solution.py:343
  159.0 0.0 collective-permute-done.13.p2
  159.0 0.6 collective-permute-done.14.p3
  159.6 1.0 w_update.3
  160.7 1.6 all-to-all-done.4.parts_ref
  162.2 1.0 h_update.3
  (1 shorter events, 0.0 us)
Async XLA Ops:
  0.6 9.8 %copy-start = (f32[256,256]{1,0:T(8,128)S(1)}, f32[256,256]{1,0:T(8,128)}, u32[]{:S(2)}) copy-start(f32[256,256]{1,0:T(8,128)} %w_ref.1) | copy-start | bytes 786436
  2.5 20.2 %all-to-all-start.1 = ((bf16[16,32,512]{2,1,0:T(8,128)(2,1)}), bf16[16,32,512]{2,1,0:T(8,128)(2,1)S(1)}, u32[]{:S(2)}, u32[]{:S(2)}) async-start(bf16[16,32,512]{2,1,0:T(8,128)(2,1)} %spread.1), calls=%async_computation.1 | async-start | bytes 1048576 | tf_op jit(solution)/shard_map/all_to_all | solution.py:335
  10.5 12.1 %collective-permute-start = (bf16[256,256]{1,0:T(8,128)(2,1)S(1)}, bf16[256,256]{1,0:T(8,128)(2,1)S(1)}, u32[]{:S(2)}, u32[]{:S(2)}) collective-permute-start(bf16[256,256]{1,0:T(8,128)(2,1)S(1)} %convert_element_type.7.w0), channel_id=1, source_target_pairs={{0,6},{2,0},{4,2},{6,4},{1,7},{3,1},{5,3},{7,5},{8,14},{10,8},{12,... | collective-permute-start | bytes 393224 | tf_op jit(solution)/shard_map/ppermute | solution.py:347
  13.6 9.1 %collective-permute-start.1 = (bf16[256,256]{1,0:T(8,128)(2,1)S(1)}, bf16[256,256]{1,0:T(8,128)(2,1)S(1)}, u32[]{:S(2)}, u32[]{:S(2)}) collective-permute-start(bf16[256,256]{1,0:T(8,128)(2,1)S(1)} %convert_element_type.7.w0), channel_id=1, source_target_pairs={{0,4},{2,6},{4,0},{6,2},{1,5},{3,7},{5,1},{7,3},{8,12},{10,14},{12... | collective-permute-start | bytes 393224 | tf_op jit(solution)/shard_map/ppermute | solution.py:347
  14.2 8.4 %collective-permute-start.2 = (bf16[256,256]{1,0:T(8,128)(2,1)S(1)}, bf16[256,256]{1,0:T(8,128)(2,1)S(1)}, u32[]{:S(2)}, u32[]{:S(2)}) collective-permute-start(bf16[256,256]{1,0:T(8,128)(2,1)S(1)} %convert_element_type.7.w0), channel_id=1, source_target_pairs={{0,2},{2,4},{4,6},{6,0},{1,3},{3,5},{5,7},{7,1},{8,10},{10,12},{12... | collective-permute-start | bytes 393224 | tf_op jit(solution)/shard_map/ppermute | solution.py:347
  22.7 58.7 %all-to-all-start = ((bf16[32,64,1024]{2,1,0:T(8,128)(2,1)}), bf16[32,64,1024]{2,1,0:T(8,128)(2,1)}, u32[]{:S(2)}, u32[]{:S(2)}) async-start(bf16[32,64,1024]{2,1,0:T(8,128)(2,1)} %bitcast.12), calls=%async_computation | async-start | bytes 8388608 | tf_op jit(solution)/shard_map/all_to_all | solution.py:335
  30.3 2.0 %collective-permute-start.3 = (bf16[4,2,2,32,512]{4,3,2,1,0:T(8,128)(2,1)S(1)}, bf16[4,2,2,32,512]{4,3,2,1,0:T(8,128)(2,1)S(1)}, u32[]{:S(2)}, u32[]{:S(2)}) collective-permute-start(bf16[4,2,2,32,512]{4,3,2,1,0:T(8,128)(2,1)S(1)} %bitcast.8), channel_id=1, source_target_pairs={{0,1},{1,0},{2,3},{3,2},{4,5},{5,4},{6,7},{7,6},{8,9},{9,8},{10,11... | collective-permute-start | bytes 1572872 | tf_op jit(solution)/shard_map/ppermute | solution.py:339
  85.4 4.3 %collective-permute-start.7 = (f32[256,1152]{1,0:T(8,128)S(1)}, f32[256,1152]{1,0:T(8,128)S(1)}, u32[]{:S(2)}, u32[]{:S(2)}) collective-permute-start(f32[256,1152]{1,0:T(8,128)S(1)} %get-tuple-element.56), channel_id=1, source_target_pairs={{0,1},{1,0},{2,3},{3,2},{4,5},{5,4},{6,7},{7,6},{8,9},{9,8},{10,11... | collective-permute-start | bytes 3538952 | tf_op jit(solution)/shard_map/ppermute | solution.py:339
  91.1 21.2 %copy-start.1 = (f32[32,512]{1,0:T(8,128)S(1)}, f32[32,512]{1,0:T(8,128)}, u32[]{:S(2)}) copy-start(f32[32,512]{1,0:T(8,128)} %h_ref.1) | copy-start | bytes 196612
  91.1 21.2 %all-to-all-start.2 = ((bf16[16,208,128]{2,1,0:T(8,128)(2,1)}), bf16[16,208,128]{2,1,0:T(8,128)(2,1)S(1)}, u32[]{:S(2)}, u32[]{:S(2)}) async-start(bf16[16,208,128]{2,1,0:T(8,128)(2,1)} %pair.2), calls=%async_computation.2 | async-start | bytes 1703936 | tf_op jit(solution)/shard_map/all_to_all | solution.py:335
  96.4 17.2 %collective-permute-start.4 = (bf16[400,256]{1,0:T(8,128)(2,1)S(1)}, bf16[400,256]{1,0:T(8,128)(2,1)S(1)}, u32[]{:S(2)}, u32[]{:S(2)}) collective-permute-start(bf16[400,256]{1,0:T(8,128)(2,1)S(1)} %get-tuple-element.52), channel_id=1, source_target_pairs={{0,2},{2,4},{4,6},{6,0},{1,3},{3,5},{5,7},{7,1},{8,10},{10,12},{12... | collective-permute-start | bytes 614408 | tf_op jit(solution)/shard_map/ppermute | solution.py:343
  98.4 15.2 %collective-permute-start.5 = (bf16[400,256]{1,0:T(8,128)(2,1)S(1)}, bf16[400,256]{1,0:T(8,128)(2,1)S(1)}, u32[]{:S(2)}, u32[]{:S(2)}) collective-permute-start(bf16[400,256]{1,0:T(8,128)(2,1)S(1)} %get-tuple-element.53), channel_id=1, source_target_pairs={{0,4},{2,6},{4,0},{6,2},{1,5},{3,7},{5,1},{7,3},{8,12},{10,14},{12... | collective-permute-start | bytes 614408 | tf_op jit(solution)/shard_map/ppermute | solution.py:343
  100.2 13.4 %collective-permute-start.6 = (bf16[400,256]{1,0:T(8,128)(2,1)S(1)}, bf16[400,256]{1,0:T(8,128)(2,1)S(1)}, u32[]{:S(2)}, u32[]{:S(2)}) collective-permute-start(bf16[400,256]{1,0:T(8,128)(2,1)S(1)} %get-tuple-element.54), channel_id=1, source_target_pairs={{0,6},{2,0},{4,2},{6,4},{1,7},{3,1},{5,3},{7,5},{8,14},{10,8},{12,... | collective-permute-start | bytes 614408 | tf_op jit(solution)/shard_map/ppermute | solution.py:343
  113.6 14.3 %all-to-all-start.3 = ((bf16[16,32,512]{2,1,0:T(8,128)(2,1)}), bf16[16,32,512]{2,1,0:T(8,128)(2,1)S(1)}, u32[]{:S(2)}, u32[]{:S(2)}) async-start(bf16[16,32,512]{2,1,0:T(8,128)(2,1)} %get-tuple-element.64), calls=%async_computation.3 | async-start | bytes 1048576 | tf_op jit(solution)/shard_map/all_to_all | solution.py:335
  117.5 6.8 %collective-permute-start.10 = (bf16[256,256]{1,0:T(8,128)(2,1)S(1)}, bf16[256,256]{1,0:T(8,128)(2,1)S(1)}, u32[]{:S(2)}, u32[]{:S(2)}) collective-permute-start(bf16[256,256]{1,0:T(8,128)(2,1)S(1)} %get-tuple-element.66.w0), channel_id=1, source_target_pairs={{0,2},{2,4},{4,6},{6,0},{1,3},{3,5},{5,7},{7,1},{8,10},{10,12},{12... | collective-permute-start | bytes 393224 | tf_op jit(solution)/shard_map/ppermute | solution.py:347
  119.5 5.6 %collective-permute-start.8 = (bf16[256,256]{1,0:T(8,128)(2,1)S(1)}, bf16[256,256]{1,0:T(8,128)(2,1)S(1)}, u32[]{:S(2)}, u32[]{:S(2)}) collective-permute-start(bf16[256,256]{1,0:T(8,128)(2,1)S(1)} %get-tuple-element.66.w0), channel_id=1, source_target_pairs={{0,6},{2,0},{4,2},{6,4},{1,7},{3,1},{5,3},{7,5},{8,14},{10,8},{12,... | collective-permute-start | bytes 393224 | tf_op jit(solution)/shard_map/ppermute | solution.py:347
  120.8 6.5 %collective-permute-start.9 = (bf16[256,256]{1,0:T(8,128)(2,1)S(1)}, bf16[256,256]{1,0:T(8,128)(2,1)S(1)}, u32[]{:S(2)}, u32[]{:S(2)}) collective-permute-start(bf16[256,256]{1,0:T(8,128)(2,1)S(1)} %get-tuple-element.66.w0), channel_id=1, source_target_pairs={{0,4},{2,6},{4,0},{6,2},{1,5},{3,7},{5,1},{7,3},{8,12},{10,14},{12... | collective-permute-start | bytes 393224 | tf_op jit(solution)/shard_map/ppermute | solution.py:347
  127.9 1.9 %collective-permute-start.11 = (bf16[4,2,2,32,512]{4,3,2,1,0:T(8,128)(2,1)S(1)}, bf16[4,2,2,32,512]{4,3,2,1,0:T(8,128)(2,1)S(1)}, u32[]{:S(2)}, u32[]{:S(2)}) collective-permute-start(bf16[4,2,2,32,512]{4,3,2,1,0:T(8,128)(2,1)S(1)} %bitcast.10), channel_id=1, source_target_pairs={{0,1},{1,0},{2,3},{3,2},{4,5},{5,4},{6,7},{7,6},{8,9},{9,8},{10,11... | collective-permute-start | bytes 1572872 | tf_op jit(solution)/shard_map/ppermute | solution.py:339
  133.8 4.4 %collective-permute-start.15 = (f32[256,1152]{1,0:T(8,128)S(1)}, f32[256,1152]{1,0:T(8,128)S(1)}, u32[]{:S(2)}, u32[]{:S(2)}) collective-permute-start(f32[256,1152]{1,0:T(8,128)S(1)} %get-tuple-element.80), channel_id=1, source_target_pairs={{0,1},{1,0},{2,3},{3,2},{4,5},{5,4},{6,7},{7,6},{8,9},{9,8},{10,11... | collective-permute-start | bytes 3538952 | tf_op jit(solution)/shard_map/ppermute | solution.py:339
  139.6 22.6 %all-to-all-start.4 = ((bf16[16,208,128]{2,1,0:T(8,128)(2,1)}), bf16[16,208,128]{2,1,0:T(8,128)(2,1)S(1)}, u32[]{:S(2)}, u32[]{:S(2)}) async-start(bf16[16,208,128]{2,1,0:T(8,128)(2,1)} %pair.3), calls=%async_computation.4 | async-start | bytes 1703936 | tf_op jit(solution)/shard_map/all_to_all | solution.py:335
  146.3 12.7 %collective-permute-start.12 = (bf16[400,256]{1,0:T(8,128)(2,1)S(1)}, bf16[400,256]{1,0:T(8,128)(2,1)S(1)}, u32[]{:S(2)}, u32[]{:S(2)}) collective-permute-start(bf16[400,256]{1,0:T(8,128)(2,1)S(1)} %get-tuple-element.75), channel_id=1, source_target_pairs={{0,2},{2,4},{4,6},{6,0},{1,3},{3,5},{5,7},{7,1},{8,10},{10,12},{12... | collective-permute-start | bytes 614408 | tf_op jit(solution)/shard_map/ppermute | solution.py:343
  147.0 12.0 %collective-permute-start.13 = (bf16[400,256]{1,0:T(8,128)(2,1)S(1)}, bf16[400,256]{1,0:T(8,128)(2,1)S(1)}, u32[]{:S(2)}, u32[]{:S(2)}) collective-permute-start(bf16[400,256]{1,0:T(8,128)(2,1)S(1)} %get-tuple-element.76), channel_id=1, source_target_pairs={{0,4},{2,6},{4,0},{6,2},{1,5},{3,7},{5,1},{7,3},{8,12},{10,14},{12... | collective-permute-start | bytes 614408 | tf_op jit(solution)/shard_map/ppermute | solution.py:343
  149.4 10.2 %collective-permute-start.14 = (bf16[400,256]{1,0:T(8,128)(2,1)S(1)}, bf16[400,256]{1,0:T(8,128)(2,1)S(1)}, u32[]{:S(2)}, u32[]{:S(2)}) collective-permute-start(bf16[400,256]{1,0:T(8,128)(2,1)S(1)} %get-tuple-element.77), channel_id=1, source_target_pairs={{0,6},{2,0},{4,2},{6,4},{1,7},{3,1},{5,3},{7,5},{8,14},{10,8},{12,... | collective-permute-start | bytes 614408 | tf_op jit(solution)/shard_map/ppermute | solution.py:343

commit v13 on v11

--- a/solution.py
+++ b/solution.py
@@ -350,7 +350,7 @@
 def local(samples, w, h):
     record = samples.reshape(samples.shape[2], samples.shape[3])
     core, y = lax.axis_index("core"), lax.axis_index("y")
-    at = jnp.stack([1 - core, core, y]).astype(jnp.int32)
+    ats = [jnp.stack(order).astype(jnp.int32) for order in ([1 - core, core, y], [core, 1 - core, y])]
     h_own = exchange(spread(h), RANKS).reshape(4, 2, 2, *h.shape)
     energy = energies(record, dft_table())
     frames, rows = energy.shape[4:]
@@ -359,9 +359,13 @@
     h_oth = from_sibling(h_own)
     spectra = exchange(energy.reshape(2 * N_P, frames, rows), TILE).reshape(2 * N_P * frames, rows)
     for step in range(ITERS):
-        *parts, s_oth = half_sweep(at, spectra, h_oth, ws)
+        sibling_first = step == 0
+        halves = (h_oth, h_own) if sibling_first else (h_own, h_oth)
+        at = ats[0 if sibling_first else 1]
+        *parts, s_first = half_sweep(at, spectra, halves[0], ws)
+        n0, n1, n2, n3, s_second = half_sweep(at, spectra, halves[1], ws, parts)
+        s_oth, s_own = (s_first, s_second) if sibling_first else (s_second, s_first)
         s_got = from_sibling(s_oth)
-        n0, n1, n2, n3, s_own = half_sweep(at, spectra, h_own, ws, parts)
         w_parts = [n0] + [sent_ahead(n, t + 1) for t, n in enumerate((n1, n2, n3))]
         h_parts = exchange(pair(s_own, s_got, h.shape[0]), RANKS)
         more = step + 1 < ITERS

time: 160 us -> 161 us (level)
  transfers between devices with their start and end apart: 21 -> 21, of which waited for: 13 -> 13; matrix products, arithmetic and copies ran while one was open for 0% -> 0% of each run, Pallas kernels for 12% -> 11%
where the time goes in v13:
time: 161 us; the launch traced here: 160 us
  waiting for transfers between devices  75.9 us (47%)
  starting transfers between devices  51.6 us (32%)
  Pallas kernels  32.1 us (20%)
    all_to_all x5, waiting for transfers between devices, exchange(): return lax.all_to_all(x, axes, 0, 0, tiled=True)  56.1 us
    all_to_all x5, starting transfers between devices, exchange(): return lax.all_to_all(x, axes, 0, 0, tiled=True)  28.1 us
    pallas_call x4, Pallas kernels, half_sweep(): pl.pallas_call(functools.partial(sweep_kernel, not before), in_specs=whol...  16.4 us
    ppermute x6, starting transfers between devices, taken_ahead(): lax.ppermute(x, 'y', [(i, (i - t) % N_Y) for i in range(N_Y)])  11.7 us
    ppermute x6, starting transfers between devices, sent_ahead(): return lax.ppermute(x, 'y', [(i, (i + t) % N_Y) for i in range(N_Y)])  10.9 us
    ppermute x6, waiting for transfers between devices, taken_ahead(): lax.ppermute(x, 'y', [(i, (i - t) % N_Y) for i in range(N_Y)])  8.85 us
    ppermute x6, waiting for transfers between devices, sent_ahead(): return lax.ppermute(x, 'y', [(i, (i + t) % N_Y) for i in range(N_Y)])  8.49 us
    pallas_call x1, Pallas kernels, energies(): pl.pallas_call(energy_kernel, in_specs=[pl.BlockSpec(memory_space=pl.ANY)...  7.44 us
  transfers between devices with their start and end apart: 21, of which 13 were waited for; matrix products, arithmetic and copies ran while one was open for 0% of the time, Pallas kernels for 11%

profile of v13, /device:TPU:0, one launch (start us, length us, event | category | flops | bytes accessed | tf_op | source)
XLA Modules:
  0.0 160.5 jit_solution(7979688091168946347)
XLA Ops:
  0.6 0.0 copy-start
  0.6 1.8 %spread.1 = bf16[16,32,512]{2,1,0:T(8,128)(2,1)} custom-call(f32[32,512]{1,0:T(8,128)} %h_ref.1), custom_call_target="tpu_custom_call" | custom-call | tf_op jit(solution)/shard_map/spread/pallas_call | solution.py:318
  2.5 8.0 %all-to-all-start.1 = ((bf16[16,32,512]{2,1,0:T(8,128)(2,1)}), bf16[16,32,512]{2,1,0:T(8,128)(2,1)S(1)}, u32[]{:S(2)}, u32[]{:S(2)}) async-start(bf16[16,32,512]{2,1,0:T(8,128)(2,1)} %spread.1), calls=%async_computation.1 | async-start | bytes 1048576 | tf_op jit(solution)/shard_map/all_to_all | solution.py:335
  10.5 0.0 copy-done
  10.5 7.4 %energy.1 = bf16[2,2,2,4,64,1024]{5,4,3,2,1,0:T(8,128)(2,1)} custom-call(bf16[256,16384]{1,0:T(8,128)(2,1)} %bitcast.13, bf16[256,256]{1,0:T(8,128)(2,1)} %constant.14.table_ref), custom_call_target="tpu_custom_call" | custom-call | flops 2147483648 | bytes 12582912 | tf_op jit(solution)/shard_map/energy/pallas_call | solution.py:83
  17.9 4.0 %all-to-all-done.1 = bf16[16,32,512]{2,1,0:T(8,128)(2,1)S(1)} async-done(((bf16[16,32,512]{2,1,0:T(8,128)(2,1)}), bf16[16,32,512]{2,1,0:T(8,128)(2,1)S(1)}, u32[]{:S(2)}, u32[]{:S(2)}) %all-to-all-start.1) | async-done | bytes 524320 | tf_op jit(solution)/shard_map/all_to_all | solution.py:335
  21.9 4.9 %all-to-all-start = ((bf16[32,64,1024]{2,1,0:T(8,128)(2,1)}), bf16[32,64,1024]{2,1,0:T(8,128)(2,1)}, u32[]{:S(2)}, u32[]{:S(2)}) async-start(bf16[32,64,1024]{2,1,0:T(8,128)(2,1)} %bitcast.12), calls=%async_computation | async-start | bytes 8388608 | tf_op jit(solution)/shard_map/all_to_all | solution.py:335
  26.8 0.2 collective-permute-start.3
  27.0 1.6 collective-permute-start.2
  28.6 2.9 %collective-permute-start.1 = (bf16[256,256]{1,0:T(8,128)(2,1)S(1)}, bf16[256,256]{1,0:T(8,128)(2,1)S(1)}, u32[]{:S(2)}, u32[]{:S(2)}) collective-permute-start(bf16[256,256]{1,0:T(8,128)(2,1)S(1)} %convert_element_type.7.w0), channel_id=1, source_target_pairs={{0,4},{2,6},{4,0},{6,2},{1,5},{3,7},{5,1},{7,3},{8,12},{10,14},{12... | collective-permute-start | bytes 393224 | tf_op jit(solution)/shard_map/ppermute | solution.py:347
  31.5 1.3 collective-permute-start
  32.8 0.1 add_add_fusion.1.at_ref
  32.9 1.2 collective-permute-done.2.w3
  34.1 4.0 %collective-permute-done.1.w2 = bf16[256,256]{1,0:T(8,128)(2,1)S(1)} collective-permute-done((bf16[256,256]{1,0:T(8,128)(2,1)S(1)}, bf16[256,256]{1,0:T(8,128)(2,1)S(1)}, u32[]{:S(2)}, u32[]{:S(2)}) %collective-permute-start.1) | collective-permute-done | bytes 131104 | tf_op jit(solution)/shard_map/ppermute | solution.py:347
  38.1 0.0 collective-permute-done.w1
  38.1 0.0 collective-permute-done.3.h_ref
  38.1 39.8 %all-to-all-done = bf16[32,64,1024]{2,1,0:T(8,128)(2,1)} async-done(((bf16[32,64,1024]{2,1,0:T(8,128)(2,1)}), bf16[32,64,1024]{2,1,0:T(8,128)(2,1)}, u32[]{:S(2)}, u32[]{:S(2)}) %all-to-all-start) | async-done | bytes 4194336 | tf_op jit(solution)/shard_map/all_to_all | solution.py:335
  77.9 4.0 %sweep_a.2 = (f32[264,256]{1,0:T(8,128)S(1)}, f32[264,256]{1,0:T(8,128)S(1)}, f32[264,256]{1,0:T(8,128)S(1)}, f32[264,256]{1,0:T(8,128)S(1)}, f32[256,1152]{1,0:T(8,128)S(1)}) custom-call(s32[3]{0:T(128)S(1)} %add_add_fusion.1.at_ref, bf16[2048,1024]{1,0:T(8,128)(2,1)} %bitcast.5.s_hbm, bf16[4,2,2,32,512]{4,3,2,1,0:T(8,128)(2,1)S(1)} %collective-permute-done.3.h_ref, ...), custom_call_target="tpu_custom_call" | custom-call | flops 1610612736 | bytes 4194304 | tf_op jit(solution)/shard_map/sweep_a/pallas_call | solution.py:188
  81.9 0.1 collective-permute-start.7
  82.0 4.2 %sweep_b.2 = (f32[264,256]{1,0:T(8,128)S(1)}, bf16[400,256]{1,0:T(8,128)(2,1)S(1)}, bf16[400,256]{1,0:T(8,128)(2,1)S(1)}, bf16[400,256]{1,0:T(8,128)(2,1)S(1)}, f32[256,1152]{1,0:T(8,128)S(1)}) custom-call(s32[3]{0:T(128)S(1)} %add_add_fusion.1.at_ref, bf16[2048,1024]{1,0:T(8,128)(2,1)} %bitcast.5.s_hbm, bf16[4,2,2,32,512]{4,3,2,1,0:T(8,128)(2,1)S(1)} %bitcast.9, ...), custom_call_target="tpu_custom_call" | custom-call | flops 1610612736 | bytes 4194304 | tf_op jit(solution)/shard_map/sweep_b/pallas_call | solution.py:188
  86.2 0.0 collective-permute-done.7.b_ref
  86.2 1.4 pair.2
  87.6 0.0 copy-start.1
  87.6 5.3 %all-to-all-start.2 = ((bf16[16,208,128]{2,1,0:T(8,128)(2,1)}), bf16[16,208,128]{2,1,0:T(8,128)(2,1)S(1)}, u32[]{:S(2)}, u32[]{:S(2)}) async-start(bf16[16,208,128]{2,1,0:T(8,128)(2,1)} %pair.2), calls=%async_computation.2 | async-start | bytes 1703936 | tf_op jit(solution)/shard_map/all_to_all | solution.py:335
  92.9 1.6 %collective-permute-start.4 = (bf16[400,256]{1,0:T(8,128)(2,1)S(1)}, bf16[400,256]{1,0:T(8,128)(2,1)S(1)}, u32[]{:S(2)}, u32[]{:S(2)}) collective-permute-start(bf16[400,256]{1,0:T(8,128)(2,1)S(1)} %get-tuple-element.46), channel_id=1, source_target_pairs={{0,2},{2,4},{4,6},{6,0},{1,3},{3,5},{5,7},{7,1},{8,10},{10,12},{12... | collective-permute-start | bytes 614408 | tf_op jit(solution)/shard_map/ppermute | solution.py:343
  94.5 2.9 %collective-permute-start.5 = (bf16[400,256]{1,0:T(8,128)(2,1)S(1)}, bf16[400,256]{1,0:T(8,128)(2,1)S(1)}, u32[]{:S(2)}, u32[]{:S(2)}) collective-permute-start(bf16[400,256]{1,0:T(8,128)(2,1)S(1)} %get-tuple-element.47), channel_id=1, source_target_pairs={{0,4},{2,6},{4,0},{6,2},{1,5},{3,7},{5,1},{7,3},{8,12},{10,14},{12... | collective-permute-start | bytes 614408 | tf_op jit(solution)/shard_map/ppermute | solution.py:343
  97.4 1.3 collective-permute-start.6
  98.8 10.1 %all-to-all-done.2.parts_ref = bf16[16,208,128]{2,1,0:T(8,128)(2,1)S(1)} async-done(((bf16[16,208,128]{2,1,0:T(8,128)(2,1)}), bf16[16,208,128]{2,1,0:T(8,128)(2,1)S(1)}, u32[]{:S(2)}, u32[]{:S(2)}) %all-to-all-start.2) | async-done | bytes 852000 | tf_op jit(solution)/shard_map/all_to_all | solution.py:335
  108.8 0.0 copy-done.1
  108.8 1.2 h_update.2
  110.1 0.0 collective-permute-done.4.p1
  110.1 0.0 collective-permute-done.5.p2
  110.1 0.0 collective-permute-done.6.p3
  110.1 3.6 %all-to-all-start.3 = ((bf16[16,32,512]{2,1,0:T(8,128)(2,1)}), bf16[16,32,512]{2,1,0:T(8,128)(2,1)S(1)}, u32[]{:S(2)}, u32[]{:S(2)}) async-start(bf16[16,32,512]{2,1,0:T(8,128)(2,1)} %get-tuple-element.58), calls=%async_computation.3 | async-start | bytes 1048576 | tf_op jit(solution)/shard_map/all_to_all | solution.py:335
  113.7 0.3 w_update.2
  114.1 1.6 collective-permute-start.10
  115.7 2.9 %collective-permute-start.9 = (bf16[256,256]{1,0:T(8,128)(2,1)S(1)}, bf16[256,256]{1,0:T(8,128)(2,1)S(1)}, u32[]{:S(2)}, u32[]{:S(2)}) collective-permute-start(bf16[256,256]{1,0:T(8,128)(2,1)S(1)} %get-tuple-element.60.w0), channel_id=1, source_target_pairs={{0,4},{2,6},{4,0},{6,2},{1,5},{3,7},{5,1},{7,3},{8,12},{10,14},{12... | collective-permute-start | bytes 393224 | tf_op jit(solution)/shard_map/ppermute | solution.py:347
  118.6 1.3 collective-permute-start.8
  119.9 1.8 %collective-permute-done.10.w3 = bf16[256,256]{1,0:T(8,128)(2,1)S(1)} collective-permute-done((bf16[256,256]{1,0:T(8,128)(2,1)S(1)}, bf16[256,256]{1,0:T(8,128)(2,1)S(1)}, u32[]{:S(2)}, u32[]{:S(2)}) %collective-permute-start.10) | collective-permute-done | bytes 131104 | tf_op jit(solution)/shard_map/ppermute | solution.py:347
  121.7 1.8 %collective-permute-done.9.w2 = bf16[256,256]{1,0:T(8,128)(2,1)S(1)} collective-permute-done((bf16[256,256]{1,0:T(8,128)(2,1)S(1)}, bf16[256,256]{1,0:T(8,128)(2,1)S(1)}, u32[]{:S(2)}, u32[]{:S(2)}) %collective-permute-start.9) | collective-permute-done | bytes 131104 | tf_op jit(solution)/shard_map/ppermute | solution.py:347
  123.5 0.1 collective-permute-done.8.w1
  123.6 0.8 all-to-all-done.3
  124.4 0.0 collective-permute-start.11
  124.4 0.1 add_add_fusion.at_ref
  124.4 4.0 %sweep_a.3 = (f32[264,256]{1,0:T(8,128)S(1)}, f32[264,256]{1,0:T(8,128)S(1)}, f32[264,256]{1,0:T(8,128)S(1)}, f32[264,256]{1,0:T(8,128)S(1)}, f32[256,1152]{1,0:T(8,128)S(1)}) custom-call(s32[3]{0:T(128)S(1)} %add_add_fusion.at_ref, bf16[2048,1024]{1,0:T(8,128)(2,1)} %bitcast.5.s_hbm, bf16[4,2,2,32,512]{4,3,2,1,0:T(8,128)(2,1)S(1)} %bitcast.11, ...), custom_call_target="tpu_custom_call" | custom-call | flops 1610612736 | bytes 4194304 | tf_op jit(solution)/shard_map/sweep_a/pallas_call | solution.py:188
  128.5 0.0 collective-permute-done.11.h_ref
  128.5 4.2 %sweep_b.3 = (f32[264,256]{1,0:T(8,128)S(1)}, bf16[400,256]{1,0:T(8,128)(2,1)S(1)}, bf16[400,256]{1,0:T(8,128)(2,1)S(1)}, bf16[400,256]{1,0:T(8,128)(2,1)S(1)}, f32[256,1152]{1,0:T(8,128)S(1)}) custom-call(s32[3]{0:T(128)S(1)} %add_add_fusion.at_ref, bf16[2048,1024]{1,0:T(8,128)(2,1)} %bitcast.5.s_hbm, ...), custom_call_target="tpu_custom_call" | custom-call | flops 1610612736 | bytes 4194304 | tf_op jit(solution)/shard_map/sweep_b/pallas_call | solution.py:188
  132.7 0.6 collective-permute-start.15
  133.3 2.5 %collective-permute-done.15.b_ref = f32[256,1152]{1,0:T(8,128)S(1)} collective-permute-done((f32[256,1152]{1,0:T(8,128)S(1)}, f32[256,1152]{1,0:T(8,128)S(1)}, u32[]{:S(2)}, u32[]{:S(2)}) %collective-permute-start.15) | collective-permute-done | bytes 1179680 | tf_op jit(solution)/shard_map/ppermute | solution.py:339
  135.7 1.4 pair.3
  137.1 6.4 %all-to-all-start.4 = ((bf16[16,208,128]{2,1,0:T(8,128)(2,1)}), bf16[16,208,128]{2,1,0:T(8,128)(2,1)S(1)}, u32[]{:S(2)}, u32[]{:S(2)}) async-start(bf16[16,208,128]{2,1,0:T(8,128)(2,1)} %pair.3), calls=%async_computation.4 | async-start | bytes 1703936 | tf_op jit(solution)/shard_map/all_to_all | solution.py:335
  143.5 1.2 collective-permute-start.12
  144.7 2.9 %collective-permute-start.13 = (bf16[400,256]{1,0:T(8,128)(2,1)S(1)}, bf16[400,256]{1,0:T(8,128)(2,1)S(1)}, u32[]{:S(2)}, u32[]{:S(2)}) collective-permute-start(bf16[400,256]{1,0:T(8,128)(2,1)S(1)} %get-tuple-element.70), channel_id=1, source_target_pairs={{0,4},{2,6},{4,0},{6,2},{1,5},{3,7},{5,1},{7,3},{8,12},{10,14},{12... | collective-permute-start | bytes 614408 | tf_op jit(solution)/shard_map/ppermute | solution.py:343
  147.6 0.9 collective-permute-start.14
  148.5 3.4 %collective-permute-done.12.p1 = bf16[400,256]{1,0:T(8,128)(2,1)S(1)} collective-permute-done((bf16[400,256]{1,0:T(8,128)(2,1)S(1)}, bf16[400,256]{1,0:T(8,128)(2,1)S(1)}, u32[]{:S(2)}, u32[]{:S(2)}) %collective-permute-start.12) | collective-permute-done | bytes 204832 | tf_op jit(solution)/shard_map/ppermute | solution.py:343
  152.0 5.1 %collective-permute-done.13.p2 = bf16[400,256]{1,0:T(8,128)(2,1)S(1)} collective-permute-done((bf16[400,256]{1,0:T(8,128)(2,1)S(1)}, bf16[400,256]{1,0:T(8,128)(2,1)S(1)}, u32[]{:S(2)}, u32[]{:S(2)}) %collective-permute-start.13) | collective-permute-done | bytes 204832 | tf_op jit(solution)/shard_map/ppermute | solution.py:343
  157.0 0.0 collective-permute-done.14.p3
  157.0 1.0 w_update.3
  158.1 1.4 all-to-all-done.4.parts_ref
  159.5 1.0 h_update.3
  (1 shorter events, 0.0 us)
Async XLA Ops:
  0.6 9.8 %copy-start = (f32[256,256]{1,0:T(8,128)S(1)}, f32[256,256]{1,0:T(8,128)}, u32[]{:S(2)}) copy-start(f32[256,256]{1,0:T(8,128)} %w_ref.1) | copy-start | bytes 786436
  2.5 19.5 %all-to-all-start.1 = ((bf16[16,32,512]{2,1,0:T(8,128)(2,1)}), bf16[16,32,512]{2,1,0:T(8,128)(2,1)S(1)}, u32[]{:S(2)}, u32[]{:S(2)}) async-start(bf16[16,32,512]{2,1,0:T(8,128)(2,1)} %spread.1), calls=%async_computation.1 | async-start | bytes 1048576 | tf_op jit(solution)/shard_map/all_to_all | solution.py:335
  21.9 55.9 %all-to-all-start = ((bf16[32,64,1024]{2,1,0:T(8,128)(2,1)}), bf16[32,64,1024]{2,1,0:T(8,128)(2,1)}, u32[]{:S(2)}, u32[]{:S(2)}) async-start(bf16[32,64,1024]{2,1,0:T(8,128)(2,1)} %bitcast.12), calls=%async_computation | async-start | bytes 8388608 | tf_op jit(solution)/shard_map/all_to_all | solution.py:335
  26.8 11.3 %collective-permute-start.3 = (bf16[4,2,2,32,512]{4,3,2,1,0:T(8,128)(2,1)S(1)}, bf16[4,2,2,32,512]{4,3,2,1,0:T(8,128)(2,1)S(1)}, u32[]{:S(2)}, u32[]{:S(2)}) collective-permute-start(bf16[4,2,2,32,512]{4,3,2,1,0:T(8,128)(2,1)S(1)} %bitcast.8), channel_id=1, source_target_pairs={{0,1},{1,0},{2,3},{3,2},{4,5},{5,4},{6,7},{7,6},{8,9},{9,8},{10,11... | collective-permute-start | bytes 1572872 | tf_op jit(solution)/shard_map/ppermute | solution.py:339
  27.0 7.1 %collective-permute-start.2 = (bf16[256,256]{1,0:T(8,128)(2,1)S(1)}, bf16[256,256]{1,0:T(8,128)(2,1)S(1)}, u32[]{:S(2)}, u32[]{:S(2)}) collective-permute-start(bf16[256,256]{1,0:T(8,128)(2,1)S(1)} %convert_element_type.7.w0), channel_id=1, source_target_pairs={{0,2},{2,4},{4,6},{6,0},{1,3},{3,5},{5,7},{7,1},{8,10},{10,12},{12... | collective-permute-start | bytes 393224 | tf_op jit(solution)/shard_map/ppermute | solution.py:347
  28.6 9.5 %collective-permute-start.1 = (bf16[256,256]{1,0:T(8,128)(2,1)S(1)}, bf16[256,256]{1,0:T(8,128)(2,1)S(1)}, u32[]{:S(2)}, u32[]{:S(2)}) collective-permute-start(bf16[256,256]{1,0:T(8,128)(2,1)S(1)} %convert_element_type.7.w0), channel_id=1, source_target_pairs={{0,4},{2,6},{4,0},{6,2},{1,5},{3,7},{5,1},{7,3},{8,12},{10,14},{12... | collective-permute-start | bytes 393224 | tf_op jit(solution)/shard_map/ppermute | solution.py:347
  31.5 6.6 %collective-permute-start = (bf16[256,256]{1,0:T(8,128)(2,1)S(1)}, bf16[256,256]{1,0:T(8,128)(2,1)S(1)}, u32[]{:S(2)}, u32[]{:S(2)}) collective-permute-start(bf16[256,256]{1,0:T(8,128)(2,1)S(1)} %convert_element_type.7.w0), channel_id=1, source_target_pairs={{0,6},{2,0},{4,2},{6,4},{1,7},{3,1},{5,3},{7,5},{8,14},{10,8},{12,... | collective-permute-start | bytes 393224 | tf_op jit(solution)/shard_map/ppermute | solution.py:347
  81.9 4.3 %collective-permute-start.7 = (f32[256,1152]{1,0:T(8,128)S(1)}, f32[256,1152]{1,0:T(8,128)S(1)}, u32[]{:S(2)}, u32[]{:S(2)}) collective-permute-start(f32[256,1152]{1,0:T(8,128)S(1)} %get-tuple-element.50), channel_id=1, source_target_pairs={{0,1},{1,0},{2,3},{3,2},{4,5},{5,4},{6,7},{7,6},{8,9},{9,8},{10,11... | collective-permute-start | bytes 3538952 | tf_op jit(solution)/shard_map/ppermute | solution.py:339
  87.6 21.2 %copy-start.1 = (f32[32,512]{1,0:T(8,128)S(1)}, f32[32,512]{1,0:T(8,128)}, u32[]{:S(2)}) copy-start(f32[32,512]{1,0:T(8,128)} %h_ref.1) | copy-start | bytes 196612
  87.6 21.2 %all-to-all-start.2 = ((bf16[16,208,128]{2,1,0:T(8,128)(2,1)}), bf16[16,208,128]{2,1,0:T(8,128)(2,1)S(1)}, u32[]{:S(2)}, u32[]{:S(2)}) async-start(bf16[16,208,128]{2,1,0:T(8,128)(2,1)} %pair.2), calls=%async_computation.2 | async-start | bytes 1703936 | tf_op jit(solution)/shard_map/all_to_all | solution.py:335
  92.9 17.2 %collective-permute-start.4 = (bf16[400,256]{1,0:T(8,128)(2,1)S(1)}, bf16[400,256]{1,0:T(8,128)(2,1)S(1)}, u32[]{:S(2)}, u32[]{:S(2)}) collective-permute-start(bf16[400,256]{1,0:T(8,128)(2,1)S(1)} %get-tuple-element.46), channel_id=1, source_target_pairs={{0,2},{2,4},{4,6},{6,0},{1,3},{3,5},{5,7},{7,1},{8,10},{10,12},{12... | collective-permute-start | bytes 614408 | tf_op jit(solution)/shard_map/ppermute | solution.py:343
  94.5 15.6 %collective-permute-start.5 = (bf16[400,256]{1,0:T(8,128)(2,1)S(1)}, bf16[400,256]{1,0:T(8,128)(2,1)S(1)}, u32[]{:S(2)}, u32[]{:S(2)}) collective-permute-start(bf16[400,256]{1,0:T(8,128)(2,1)S(1)} %get-tuple-element.47), channel_id=1, source_target_pairs={{0,4},{2,6},{4,0},{6,2},{1,5},{3,7},{5,1},{7,3},{8,12},{10,14},{12... | collective-permute-start | bytes 614408 | tf_op jit(solution)/shard_map/ppermute | solution.py:343
  97.4 12.7 %collective-permute-start.6 = (bf16[400,256]{1,0:T(8,128)(2,1)S(1)}, bf16[400,256]{1,0:T(8,128)(2,1)S(1)}, u32[]{:S(2)}, u32[]{:S(2)}) collective-permute-start(bf16[400,256]{1,0:T(8,128)(2,1)S(1)} %get-tuple-element.48), channel_id=1, source_target_pairs={{0,6},{2,0},{4,2},{6,4},{1,7},{3,1},{5,3},{7,5},{8,14},{10,8},{12,... | collective-permute-start | bytes 614408 | tf_op jit(solution)/shard_map/ppermute | solution.py:343
  110.1 14.3 %all-to-all-start.3 = ((bf16[16,32,512]{2,1,0:T(8,128)(2,1)}), bf16[16,32,512]{2,1,0:T(8,128)(2,1)S(1)}, u32[]{:S(2)}, u32[]{:S(2)}) async-start(bf16[16,32,512]{2,1,0:T(8,128)(2,1)} %get-tuple-element.58), calls=%async_computation.3 | async-start | bytes 1048576 | tf_op jit(solution)/shard_map/all_to_all | solution.py:335
  114.1 7.7 %collective-permute-start.10 = (bf16[256,256]{1,0:T(8,128)(2,1)S(1)}, bf16[256,256]{1,0:T(8,128)(2,1)S(1)}, u32[]{:S(2)}, u32[]{:S(2)}) collective-permute-start(bf16[256,256]{1,0:T(8,128)(2,1)S(1)} %get-tuple-element.60.w0), channel_id=1, source_target_pairs={{0,2},{2,4},{4,6},{6,0},{1,3},{3,5},{5,7},{7,1},{8,10},{10,12},{12... | collective-permute-start | bytes 393224 | tf_op jit(solution)/shard_map/ppermute | solution.py:347
  115.7 7.8 %collective-permute-start.9 = (bf16[256,256]{1,0:T(8,128)(2,1)S(1)}, bf16[256,256]{1,0:T(8,128)(2,1)S(1)}, u32[]{:S(2)}, u32[]{:S(2)}) collective-permute-start(bf16[256,256]{1,0:T(8,128)(2,1)S(1)} %get-tuple-element.60.w0), channel_id=1, source_target_pairs={{0,4},{2,6},{4,0},{6,2},{1,5},{3,7},{5,1},{7,3},{8,12},{10,14},{12... | collective-permute-start | bytes 393224 | tf_op jit(solution)/shard_map/ppermute | solution.py:347
  118.6 5.0 %collective-permute-start.8 = (bf16[256,256]{1,0:T(8,128)(2,1)S(1)}, bf16[256,256]{1,0:T(8,128)(2,1)S(1)}, u32[]{:S(2)}, u32[]{:S(2)}) collective-permute-start(bf16[256,256]{1,0:T(8,128)(2,1)S(1)} %get-tuple-element.60.w0), channel_id=1, source_target_pairs={{0,6},{2,0},{4,2},{6,4},{1,7},{3,1},{5,3},{7,5},{8,14},{10,8},{12,... | collective-permute-start | bytes 393224 | tf_op jit(solution)/shard_map/ppermute | solution.py:347
  124.4 4.1 %collective-permute-start.11 = (bf16[4,2,2,32,512]{4,3,2,1,0:T(8,128)(2,1)S(1)}, bf16[4,2,2,32,512]{4,3,2,1,0:T(8,128)(2,1)S(1)}, u32[]{:S(2)}, u32[]{:S(2)}) collective-permute-start(bf16[4,2,2,32,512]{4,3,2,1,0:T(8,128)(2,1)S(1)} %bitcast.10), channel_id=1, source_target_pairs={{0,1},{1,0},{2,3},{3,2},{4,5},{5,4},{6,7},{7,6},{8,9},{9,8},{10,11... | collective-permute-start | bytes 1572872 | tf_op jit(solution)/shard_map/ppermute | solution.py:339
  132.7 3.0 %collective-permute-start.15 = (f32[256,1152]{1,0:T(8,128)S(1)}, f32[256,1152]{1,0:T(8,128)S(1)}, u32[]{:S(2)}, u32[]{:S(2)}) collective-permute-start(f32[256,1152]{1,0:T(8,128)S(1)} %get-tuple-element.74), channel_id=1, source_target_pairs={{0,1},{1,0},{2,3},{3,2},{4,5},{5,4},{6,7},{7,6},{8,9},{9,8},{10,11... | collective-permute-start | bytes 3538952 | tf_op jit(solution)/shard_map/ppermute | solution.py:339
  137.1 22.3 %all-to-all-start.4 = ((bf16[16,208,128]{2,1,0:T(8,128)(2,1)}), bf16[16,208,128]{2,1,0:T(8,128)(2,1)S(1)}, u32[]{:S(2)}, u32[]{:S(2)}) async-start(bf16[16,208,128]{2,1,0:T(8,128)(2,1)} %pair.3), calls=%async_computation.4 | async-start | bytes 1703936 | tf_op jit(solution)/shard_map/all_to_all | solution.py:335
  143.5 8.4 %collective-permute-start.12 = (bf16[400,256]{1,0:T(8,128)(2,1)S(1)}, bf16[400,256]{1,0:T(8,128)(2,1)S(1)}, u32[]{:S(2)}, u32[]{:S(2)}) collective-permute-start(bf16[400,256]{1,0:T(8,128)(2,1)S(1)} %get-tuple-element.69), channel_id=1, source_target_pairs={{0,2},{2,4},{4,6},{6,0},{1,3},{3,5},{5,7},{7,1},{8,10},{10,12},{12... | collective-permute-start | bytes 614408 | tf_op jit(solution)/shard_map/ppermute | solution.py:343
  144.7 12.3 %collective-permute-start.13 = (bf16[400,256]{1,0:T(8,128)(2,1)S(1)}, bf16[400,256]{1,0:T(8,128)(2,1)S(1)}, u32[]{:S(2)}, u32[]{:S(2)}) collective-permute-start(bf16[400,256]{1,0:T(8,128)(2,1)S(1)} %get-tuple-element.70), channel_id=1, source_target_pairs={{0,4},{2,6},{4,0},{6,2},{1,5},{3,7},{5,1},{7,3},{8,12},{10,14},{12... | collective-permute-start | bytes 614408 | tf_op jit(solution)/shard_map/ppermute | solution.py:343
  147.6 9.4 %collective-permute-start.14 = (bf16[400,256]{1,0:T(8,128)(2,1)S(1)}, bf16[400,256]{1,0:T(8,128)(2,1)S(1)}, u32[]{:S(2)}, u32[]{:S(2)}) collective-permute-start(bf16[400,256]{1,0:T(8,128)(2,1)S(1)} %get-tuple-element.71), channel_id=1, source_target_pairs={{0,6},{2,0},{4,2},{6,4},{1,7},{3,1},{5,3},{7,5},{8,14},{10,8},{12,... | collective-permute-start | bytes 614408 | tf_op jit(solution)/shard_map/ppermute | solution.py:343

commit v14 on v11

--- a/solution.py
+++ b/solution.py
@@ -244,7 +244,7 @@
     )(a, b)
 
 
-def h_update_kernel(parts_ref, h_ref, new_ref, *low_refs):
+def h_update_kernel(parts_ref, h_ref, new_ref, *refs):
     each = h_ref.shape[0]
     blocks, tail = [0.0] * 4, 0.0
     for i in range(N_P):
@@ -258,19 +258,24 @@
     colsum = jnp.concatenate([tail[:, j * each : j * each + 1] for j in range(each // TAIL)], axis=0)
     new = h_ref[...] * numer / colsum
     new_ref[...] = new
-    low = new.astype(jnp.bfloat16)
-    for low_ref in low_refs:
-        for i in range(N_P):
-            low_ref[i] = low
+    if refs:
+        out_hbm, low_ref, sem = refs
+        low_ref[...] = new.astype(jnp.bfloat16)
+        puts = [pltpu.make_async_copy(low_ref, out_hbm.at[i], sem.at[i]) for i in range(N_P)]
+        for put in puts:
+            put.start()
+        for put in puts:
+            put.wait()
 
 
 def h_update(parts, h, more):
     return pl.pallas_call(
         h_update_kernel,
         in_specs=whole(2),
-        out_specs=whole(1 + more),
+        out_specs=whole(1) + whole(1, pl.ANY) * more,
         out_shape=[jax.ShapeDtypeStruct(h.shape, jnp.float32)]
         + [jax.ShapeDtypeStruct((N_P, *h.shape), jnp.bfloat16)] * more,
+        scratch_shapes=[pltpu.VMEM(h.shape, jnp.bfloat16), pltpu.SemaphoreType.DMA((N_P,))] * more,
         compiler_params=pltpu.CompilerParams(vmem_limit_bytes=12 << 20),
         name="h_update",
     )(parts, h)

time: 160 us -> 160 us (level)
  no operation moved by 1% of the time
where the time goes in v14:
time: 160 us
  waiting for transfers between devices  75.3 us (47%)
  starting transfers between devices  51.1 us (32%)
  Pallas kernels  32.2 us (20%)
    all_to_all x5, waiting for transfers between devices, exchange(): return lax.all_to_all(x, axes, 0, 0, tiled=True)  56.1 us
    all_to_all x5, starting transfers between devices, exchange(): return lax.all_to_all(x, axes, 0, 0, tiled=True)  28.1 us
    pallas_call x4, Pallas kernels, half_sweep(): pl.pallas_call(functools.partial(sweep_kernel, not before), in_specs=whol...  16.4 us
    ppermute x6, starting transfers between devices, taken_ahead(): lax.ppermute(x, 'y', [(i, (i - t) % N_Y) for i in range(N_Y)])  11.7 us
    ppermute x6, starting transfers between devices, sent_ahead(): return lax.ppermute(x, 'y', [(i, (i + t) % N_Y) for i in range(N_Y)])  10.9 us
    ppermute x6, waiting for transfers between devices, taken_ahead(): lax.ppermute(x, 'y', [(i, (i - t) % N_Y) for i in range(N_Y)])  8.81 us
    ppermute x6, waiting for transfers between devices, sent_ahead(): return lax.ppermute(x, 'y', [(i, (i + t) % N_Y) for i in range(N_Y)])  8.52 us
    pallas_call x1, Pallas kernels, energies(): pl.pallas_call(energy_kernel, in_specs=[pl.BlockSpec(memory_space=pl.ANY)...  7.46 us
  transfers between devices with their start and end apart: 21, of which 13 were waited for; matrix products, arithmetic and copies ran while one was open for 0% of the time, Pallas kernels for 12%

profile of v14, /device:TPU:0, one launch (start us, length us, event | category | flops | bytes accessed | tf_op | source)
XLA Modules:
  0.0 159.6 jit_solution(18380359979132510780)
XLA Ops:
  0.6 0.0 copy-start
  0.6 1.8 %spread.1 = bf16[16,32,512]{2,1,0:T(8,128)(2,1)} custom-call(f32[32,512]{1,0:T(8,128)} %h_ref.1), custom_call_target="tpu_custom_call" | custom-call | tf_op jit(solution)/shard_map/spread/pallas_call | solution.py:323
  2.5 8.0 %all-to-all-start.1 = ((bf16[16,32,512]{2,1,0:T(8,128)(2,1)}), bf16[16,32,512]{2,1,0:T(8,128)(2,1)S(1)}, u32[]{:S(2)}, u32[]{:S(2)}) async-start(bf16[16,32,512]{2,1,0:T(8,128)(2,1)} %spread.1), calls=%async_computation.1 | async-start | bytes 1048576 | tf_op jit(solution)/shard_map/all_to_all | solution.py:340
  10.5 0.0 copy-done
  10.5 7.5 %energy.1 = bf16[2,2,2,4,64,1024]{5,4,3,2,1,0:T(8,128)(2,1)} custom-call(bf16[256,16384]{1,0:T(8,128)(2,1)} %bitcast.13, bf16[256,256]{1,0:T(8,128)(2,1)} %constant.14.table_ref), custom_call_target="tpu_custom_call" | custom-call | flops 2147483648 | bytes 12582912 | tf_op jit(solution)/shard_map/energy/pallas_call | solution.py:83
  18.0 4.0 %all-to-all-done.1 = bf16[16,32,512]{2,1,0:T(8,128)(2,1)S(1)} async-done(((bf16[16,32,512]{2,1,0:T(8,128)(2,1)}), bf16[16,32,512]{2,1,0:T(8,128)(2,1)S(1)}, u32[]{:S(2)}, u32[]{:S(2)}) %all-to-all-start.1) | async-done | bytes 524320 | tf_op jit(solution)/shard_map/all_to_all | solution.py:340
  21.9 4.9 %all-to-all-start = ((bf16[32,64,1024]{2,1,0:T(8,128)(2,1)}), bf16[32,64,1024]{2,1,0:T(8,128)(2,1)}, u32[]{:S(2)}, u32[]{:S(2)}) async-start(bf16[32,64,1024]{2,1,0:T(8,128)(2,1)} %bitcast.12), calls=%async_computation | async-start | bytes 8388608 | tf_op jit(solution)/shard_map/all_to_all | solution.py:340
  26.8 0.2 collective-permute-start.3
  27.0 1.6 collective-permute-start.2
  28.6 2.9 %collective-permute-start.1 = (bf16[256,256]{1,0:T(8,128)(2,1)S(1)}, bf16[256,256]{1,0:T(8,128)(2,1)S(1)}, u32[]{:S(2)}, u32[]{:S(2)}) collective-permute-start(bf16[256,256]{1,0:T(8,128)(2,1)S(1)} %convert_element_type.7.w0), channel_id=1, source_target_pairs={{0,4},{2,6},{4,0},{6,2},{1,5},{3,7},{5,1},{7,3},{8,12},{10,14},{12... | collective-permute-start | bytes 393224 | tf_op jit(solution)/shard_map/ppermute | solution.py:352
  31.5 1.3 collective-permute-start
  32.8 0.1 pad_add_fusion.at_ref
  32.9 1.2 collective-permute-done.2.w3
  34.1 4.0 %collective-permute-done.1.w2 = bf16[256,256]{1,0:T(8,128)(2,1)S(1)} collective-permute-done((bf16[256,256]{1,0:T(8,128)(2,1)S(1)}, bf16[256,256]{1,0:T(8,128)(2,1)S(1)}, u32[]{:S(2)}, u32[]{:S(2)}) %collective-permute-start.1) | collective-permute-done | bytes 131104 | tf_op jit(solution)/shard_map/ppermute | solution.py:352
  38.1 0.0 collective-permute-done.w1
  38.1 0.0 collective-permute-done.3.h_ref
  38.1 39.8 %all-to-all-done = bf16[32,64,1024]{2,1,0:T(8,128)(2,1)} async-done(((bf16[32,64,1024]{2,1,0:T(8,128)(2,1)}), bf16[32,64,1024]{2,1,0:T(8,128)(2,1)}, u32[]{:S(2)}, u32[]{:S(2)}) %all-to-all-start) | async-done | bytes 4194336 | tf_op jit(solution)/shard_map/all_to_all | solution.py:340
  77.9 4.0 %sweep_a.2 = (f32[264,256]{1,0:T(8,128)S(1)}, f32[264,256]{1,0:T(8,128)S(1)}, f32[264,256]{1,0:T(8,128)S(1)}, f32[264,256]{1,0:T(8,128)S(1)}, f32[256,1152]{1,0:T(8,128)S(1)}) custom-call(s32[3]{0:T(128)S(1)} %pad_add_fusion.at_ref, bf16[2048,1024]{1,0:T(8,128)(2,1)} %bitcast.5.s_hbm, bf16[4,2,2,32,512]{4,3,2,1,0:T(8,128)(2,1)S(1)} %collective-permute-done.3.h_ref, ...), custom_call_target="tpu_custom_call" | custom-call | flops 1610612736 | bytes 4194304 | tf_op jit(solution)/shard_map/sweep_a/pallas_call | solution.py:188
  81.9 0.1 collective-permute-start.7
  82.0 4.2 %sweep_b.2 = (f32[264,256]{1,0:T(8,128)S(1)}, bf16[400,256]{1,0:T(8,128)(2,1)S(1)}, bf16[400,256]{1,0:T(8,128)(2,1)S(1)}, bf16[400,256]{1,0:T(8,128)(2,1)S(1)}, f32[256,1152]{1,0:T(8,128)S(1)}) custom-call(s32[3]{0:T(128)S(1)} %pad_add_fusion.at_ref, bf16[2048,1024]{1,0:T(8,128)(2,1)} %bitcast.5.s_hbm, bf16[4,2,2,32,512]{4,3,2,1,0:T(8,128)(2,1)S(1)} %bitcast.9, ...), custom_call_target="tpu_custom_call" | custom-call | flops 1610612736 | bytes 4194304 | tf_op jit(solution)/shard_map/sweep_b/pallas_call | solution.py:188
  86.2 0.0 collective-permute-done.7.b_ref
  86.2 1.4 pair.2
  87.6 0.0 copy-start.1
  87.6 5.3 %all-to-all-start.2 = ((bf16[16,208,128]{2,1,0:T(8,128)(2,1)}), bf16[16,208,128]{2,1,0:T(8,128)(2,1)S(1)}, u32[]{:S(2)}, u32[]{:S(2)}) async-start(bf16[16,208,128]{2,1,0:T(8,128)(2,1)} %pair.2), calls=%async_computation.2 | async-start | bytes 1703936 | tf_op jit(solution)/shard_map/all_to_all | solution.py:340
  92.9 1.7 %collective-permute-start.4 = (bf16[400,256]{1,0:T(8,128)(2,1)S(1)}, bf16[400,256]{1,0:T(8,128)(2,1)S(1)}, u32[]{:S(2)}, u32[]{:S(2)}) collective-permute-start(bf16[400,256]{1,0:T(8,128)(2,1)S(1)} %get-tuple-element.46), channel_id=1, source_target_pairs={{0,2},{2,4},{4,6},{6,0},{1,3},{3,5},{5,7},{7,1},{8,10},{10,12},{12... | collective-permute-start | bytes 614408 | tf_op jit(solution)/shard_map/ppermute | solution.py:348
  94.5 2.9 %collective-permute-start.5 = (bf16[400,256]{1,0:T(8,128)(2,1)S(1)}, bf16[400,256]{1,0:T(8,128)(2,1)S(1)}, u32[]{:S(2)}, u32[]{:S(2)}) collective-permute-start(bf16[400,256]{1,0:T(8,128)(2,1)S(1)} %get-tuple-element.47), channel_id=1, source_target_pairs={{0,4},{2,6},{4,0},{6,2},{1,5},{3,7},{5,1},{7,3},{8,12},{10,14},{12... | collective-permute-start | bytes 614408 | tf_op jit(solution)/shard_map/ppermute | solution.py:348
  97.5 1.3 collective-permute-start.6
  98.8 10.1 %all-to-all-done.2.parts_ref = bf16[16,208,128]{2,1,0:T(8,128)(2,1)S(1)} async-done(((bf16[16,208,128]{2,1,0:T(8,128)(2,1)}), bf16[16,208,128]{2,1,0:T(8,128)(2,1)S(1)}, u32[]{:S(2)}, u32[]{:S(2)}) %all-to-all-start.2) | async-done | bytes 852000 | tf_op jit(solution)/shard_map/all_to_all | solution.py:340
  108.9 0.0 copy-done.1
  108.9 1.4 h_update.2
  110.2 0.0 collective-permute-done.4.p1
  110.2 0.0 collective-permute-done.5.p2
  110.2 0.0 collective-permute-done.6.p3
  110.2 3.6 %all-to-all-start.3 = ((bf16[16,32,512]{2,1,0:T(8,128)(2,1)}), bf16[16,32,512]{2,1,0:T(8,128)(2,1)S(1)}, u32[]{:S(2)}, u32[]{:S(2)}) async-start(bf16[16,32,512]{2,1,0:T(8,128)(2,1)} %get-tuple-element.58), calls=%async_computation.3 | async-start | bytes 1048576 | tf_op jit(solution)/shard_map/all_to_all | solution.py:340
  113.8 0.3 w_update.2
  114.2 1.6 %collective-permute-start.10 = (bf16[256,256]{1,0:T(8,128)(2,1)S(1)}, bf16[256,256]{1,0:T(8,128)(2,1)S(1)}, u32[]{:S(2)}, u32[]{:S(2)}) collective-permute-start(bf16[256,256]{1,0:T(8,128)(2,1)S(1)} %get-tuple-element.60.w0), channel_id=1, source_target_pairs={{0,2},{2,4},{4,6},{6,0},{1,3},{3,5},{5,7},{7,1},{8,10},{10,12},{12... | collective-permute-start | bytes 393224 | tf_op jit(solution)/shard_map/ppermute | solution.py:352
  115.8 2.9 %collective-permute-start.9 = (bf16[256,256]{1,0:T(8,128)(2,1)S(1)}, bf16[256,256]{1,0:T(8,128)(2,1)S(1)}, u32[]{:S(2)}, u32[]{:S(2)}) collective-permute-start(bf16[256,256]{1,0:T(8,128)(2,1)S(1)} %get-tuple-element.60.w0), channel_id=1, source_target_pairs={{0,4},{2,6},{4,0},{6,2},{1,5},{3,7},{5,1},{7,3},{8,12},{10,14},{12... | collective-permute-start | bytes 393224 | tf_op jit(solution)/shard_map/ppermute | solution.py:352
  118.7 1.3 collective-permute-start.8
  120.1 1.8 %collective-permute-done.10.w3 = bf16[256,256]{1,0:T(8,128)(2,1)S(1)} collective-permute-done((bf16[256,256]{1,0:T(8,128)(2,1)S(1)}, bf16[256,256]{1,0:T(8,128)(2,1)S(1)}, u32[]{:S(2)}, u32[]{:S(2)}) %collective-permute-start.10) | collective-permute-done | bytes 131104 | tf_op jit(solution)/shard_map/ppermute | solution.py:352
  121.8 1.8 %collective-permute-done.9.w2 = bf16[256,256]{1,0:T(8,128)(2,1)S(1)} collective-permute-done((bf16[256,256]{1,0:T(8,128)(2,1)S(1)}, bf16[256,256]{1,0:T(8,128)(2,1)S(1)}, u32[]{:S(2)}, u32[]{:S(2)}) %collective-permute-start.9) | collective-permute-done | bytes 131104 | tf_op jit(solution)/shard_map/ppermute | solution.py:352
  123.6 0.1 collective-permute-done.8.w1
  123.7 0.9 all-to-all-done.3
  124.5 0.0 collective-permute-start.11
  124.6 1.9 %collective-permute-done.11.h_ref = bf16[4,2,2,32,512]{4,3,2,1,0:T(8,128)(2,1)S(1)} collective-permute-done((bf16[4,2,2,32,512]{4,3,2,1,0:T(8,128)(2,1)S(1)}, bf16[4,2,2,32,512]{4,3,2,1,0:T(8,128)(2,1)S(1)}, u32[]{:S(2)}, u32[]{:S(2)}) %collective-permute-start.11) | collective-permute-done | bytes 524320 | tf_op jit(solution)/shard_map/ppermute | solution.py:344
  126.5 4.0 %sweep_a.3 = (f32[264,256]{1,0:T(8,128)S(1)}, f32[264,256]{1,0:T(8,128)S(1)}, f32[264,256]{1,0:T(8,128)S(1)}, f32[264,256]{1,0:T(8,128)S(1)}, f32[256,1152]{1,0:T(8,128)S(1)}) custom-call(s32[3]{0:T(128)S(1)} %pad_add_fusion.at_ref, bf16[2048,1024]{1,0:T(8,128)(2,1)} %bitcast.5.s_hbm, bf16[4,2,2,32,512]{4,3,2,1,0:T(8,128)(2,1)S(1)} %collective-permute-done.11.h_ref, ...), custom_call_target="tpu_custom_call" | custom-call | flops 1610612736 | bytes 4194304 | tf_op jit(solution)/shard_map/sweep_a/pallas_call | solution.py:188
  130.5 0.2 collective-permute-start.15
  130.7 4.2 %sweep_b.3 = (f32[264,256]{1,0:T(8,128)S(1)}, bf16[400,256]{1,0:T(8,128)(2,1)S(1)}, bf16[400,256]{1,0:T(8,128)(2,1)S(1)}, bf16[400,256]{1,0:T(8,128)(2,1)S(1)}, f32[256,1152]{1,0:T(8,128)S(1)}) custom-call(s32[3]{0:T(128)S(1)} %pad_add_fusion.at_ref, bf16[2048,1024]{1,0:T(8,128)(2,1)} %bitcast.5.s_hbm, bf16[4,2,2,32,512]{4,3,2,1,0:T(8,128)(2,1)S(1)} %bitcast.11, ...), custom_call_target="tpu_custom_call" | custom-call | flops 1610612736 | bytes 4194304 | tf_op jit(solution)/shard_map/sweep_b/pallas_call | solution.py:188
  134.9 0.0 collective-permute-done.15.b_ref
  134.9 1.4 pair.3
  136.3 6.4 %all-to-all-start.4 = ((bf16[16,208,128]{2,1,0:T(8,128)(2,1)}), bf16[16,208,128]{2,1,0:T(8,128)(2,1)S(1)}, u32[]{:S(2)}, u32[]{:S(2)}) async-start(bf16[16,208,128]{2,1,0:T(8,128)(2,1)} %pair.3), calls=%async_computation.4 | async-start | bytes 1703936 | tf_op jit(solution)/shard_map/all_to_all | solution.py:340
  142.7 1.1 collective-permute-start.12
  143.8 3.0 %collective-permute-start.13 = (bf16[400,256]{1,0:T(8,128)(2,1)S(1)}, bf16[400,256]{1,0:T(8,128)(2,1)S(1)}, u32[]{:S(2)}, u32[]{:S(2)}) collective-permute-start(bf16[400,256]{1,0:T(8,128)(2,1)S(1)} %get-tuple-element.70), channel_id=1, source_target_pairs={{0,4},{2,6},{4,0},{6,2},{1,5},{3,7},{5,1},{7,3},{8,12},{10,14},{12... | collective-permute-start | bytes 614408 | tf_op jit(solution)/shard_map/ppermute | solution.py:348
  146.7 0.9 collective-permute-start.14
  147.7 3.4 %collective-permute-done.12.p1 = bf16[400,256]{1,0:T(8,128)(2,1)S(1)} collective-permute-done((bf16[400,256]{1,0:T(8,128)(2,1)S(1)}, bf16[400,256]{1,0:T(8,128)(2,1)S(1)}, u32[]{:S(2)}, u32[]{:S(2)}) %collective-permute-start.12) | collective-permute-done | bytes 204832 | tf_op jit(solution)/shard_map/ppermute | solution.py:348
  151.1 5.1 %collective-permute-done.13.p2 = bf16[400,256]{1,0:T(8,128)(2,1)S(1)} collective-permute-done((bf16[400,256]{1,0:T(8,128)(2,1)S(1)}, bf16[400,256]{1,0:T(8,128)(2,1)S(1)}, u32[]{:S(2)}, u32[]{:S(2)}) %collective-permute-start.13) | collective-permute-done | bytes 204832 | tf_op jit(solution)/shard_map/ppermute | solution.py:348
  156.2 0.0 collective-permute-done.14.p3
  156.2 1.0 w_update.3
  157.2 1.4 all-to-all-done.4.parts_ref
  158.6 1.0 h_update.3
  (1 shorter events, 0.0 us)
Async XLA Ops:
  0.6 9.8 %copy-start = (f32[256,256]{1,0:T(8,128)S(1)}, f32[256,256]{1,0:T(8,128)}, u32[]{:S(2)}) copy-start(f32[256,256]{1,0:T(8,128)} %w_ref.1) | copy-start | bytes 786436
  2.5 19.5 %all-to-all-start.1 = ((bf16[16,32,512]{2,1,0:T(8,128)(2,1)}), bf16[16,32,512]{2,1,0:T(8,128)(2,1)S(1)}, u32[]{:S(2)}, u32[]{:S(2)}) async-start(bf16[16,32,512]{2,1,0:T(8,128)(2,1)} %spread.1), calls=%async_computation.1 | async-start | bytes 1048576 | tf_op jit(solution)/shard_map/all_to_all | solution.py:340
  21.9 55.9 %all-to-all-start = ((bf16[32,64,1024]{2,1,0:T(8,128)(2,1)}), bf16[32,64,1024]{2,1,0:T(8,128)(2,1)}, u32[]{:S(2)}, u32[]{:S(2)}) async-start(bf16[32,64,1024]{2,1,0:T(8,128)(2,1)} %bitcast.12), calls=%async_computation | async-start | bytes 8388608 | tf_op jit(solution)/shard_map/all_to_all | solution.py:340
  26.8 11.3 %collective-permute-start.3 = (bf16[4,2,2,32,512]{4,3,2,1,0:T(8,128)(2,1)S(1)}, bf16[4,2,2,32,512]{4,3,2,1,0:T(8,128)(2,1)S(1)}, u32[]{:S(2)}, u32[]{:S(2)}) collective-permute-start(bf16[4,2,2,32,512]{4,3,2,1,0:T(8,128)(2,1)S(1)} %bitcast.8), channel_id=1, source_target_pairs={{0,1},{1,0},{2,3},{3,2},{4,5},{5,4},{6,7},{7,6},{8,9},{9,8},{10,11... | collective-permute-start | bytes 1572872 | tf_op jit(solution)/shard_map/ppermute | solution.py:344
  27.0 7.1 %collective-permute-start.2 = (bf16[256,256]{1,0:T(8,128)(2,1)S(1)}, bf16[256,256]{1,0:T(8,128)(2,1)S(1)}, u32[]{:S(2)}, u32[]{:S(2)}) collective-permute-start(bf16[256,256]{1,0:T(8,128)(2,1)S(1)} %convert_element_type.7.w0), channel_id=1, source_target_pairs={{0,2},{2,4},{4,6},{6,0},{1,3},{3,5},{5,7},{7,1},{8,10},{10,12},{12... | collective-permute-start | bytes 393224 | tf_op jit(solution)/shard_map/ppermute | solution.py:352
  28.6 9.5 %collective-permute-start.1 = (bf16[256,256]{1,0:T(8,128)(2,1)S(1)}, bf16[256,256]{1,0:T(8,128)(2,1)S(1)}, u32[]{:S(2)}, u32[]{:S(2)}) collective-permute-start(bf16[256,256]{1,0:T(8,128)(2,1)S(1)} %convert_element_type.7.w0), channel_id=1, source_target_pairs={{0,4},{2,6},{4,0},{6,2},{1,5},{3,7},{5,1},{7,3},{8,12},{10,14},{12... | collective-permute-start | bytes 393224 | tf_op jit(solution)/shard_map/ppermute | solution.py:352
  31.5 6.6 %collective-permute-start = (bf16[256,256]{1,0:T(8,128)(2,1)S(1)}, bf16[256,256]{1,0:T(8,128)(2,1)S(1)}, u32[]{:S(2)}, u32[]{:S(2)}) collective-permute-start(bf16[256,256]{1,0:T(8,128)(2,1)S(1)} %convert_element_type.7.w0), channel_id=1, source_target_pairs={{0,6},{2,0},{4,2},{6,4},{1,7},{3,1},{5,3},{7,5},{8,14},{10,8},{12,... | collective-permute-start | bytes 393224 | tf_op jit(solution)/shard_map/ppermute | solution.py:352
  81.9 4.3 %collective-permute-start.7 = (f32[256,1152]{1,0:T(8,128)S(1)}, f32[256,1152]{1,0:T(8,128)S(1)}, u32[]{:S(2)}, u32[]{:S(2)}) collective-permute-start(f32[256,1152]{1,0:T(8,128)S(1)} %get-tuple-element.50), channel_id=1, source_target_pairs={{0,1},{1,0},{2,3},{3,2},{4,5},{5,4},{6,7},{7,6},{8,9},{9,8},{10,11... | collective-permute-start | bytes 3538952 | tf_op jit(solution)/shard_map/ppermute | solution.py:344
  87.6 21.2 %copy-start.1 = (f32[32,512]{1,0:T(8,128)S(1)}, f32[32,512]{1,0:T(8,128)}, u32[]{:S(2)}) copy-start(f32[32,512]{1,0:T(8,128)} %h_ref.1) | copy-start | bytes 196612
  87.6 21.2 %all-to-all-start.2 = ((bf16[16,208,128]{2,1,0:T(8,128)(2,1)}), bf16[16,208,128]{2,1,0:T(8,128)(2,1)S(1)}, u32[]{:S(2)}, u32[]{:S(2)}) async-start(bf16[16,208,128]{2,1,0:T(8,128)(2,1)} %pair.2), calls=%async_computation.2 | async-start | bytes 1703936 | tf_op jit(solution)/shard_map/all_to_all | solution.py:340
  92.9 17.3 %collective-permute-start.4 = (bf16[400,256]{1,0:T(8,128)(2,1)S(1)}, bf16[400,256]{1,0:T(8,128)(2,1)S(1)}, u32[]{:S(2)}, u32[]{:S(2)}) collective-permute-start(bf16[400,256]{1,0:T(8,128)(2,1)S(1)} %get-tuple-element.46), channel_id=1, source_target_pairs={{0,2},{2,4},{4,6},{6,0},{1,3},{3,5},{5,7},{7,1},{8,10},{10,12},{12... | collective-permute-start | bytes 614408 | tf_op jit(solution)/shard_map/ppermute | solution.py:348
  94.5 15.7 %collective-permute-start.5 = (bf16[400,256]{1,0:T(8,128)(2,1)S(1)}, bf16[400,256]{1,0:T(8,128)(2,1)S(1)}, u32[]{:S(2)}, u32[]{:S(2)}) collective-permute-start(bf16[400,256]{1,0:T(8,128)(2,1)S(1)} %get-tuple-element.47), channel_id=1, source_target_pairs={{0,4},{2,6},{4,0},{6,2},{1,5},{3,7},{5,1},{7,3},{8,12},{10,14},{12... | collective-permute-start | bytes 614408 | tf_op jit(solution)/shard_map/ppermute | solution.py:348
  97.5 12.8 %collective-permute-start.6 = (bf16[400,256]{1,0:T(8,128)(2,1)S(1)}, bf16[400,256]{1,0:T(8,128)(2,1)S(1)}, u32[]{:S(2)}, u32[]{:S(2)}) collective-permute-start(bf16[400,256]{1,0:T(8,128)(2,1)S(1)} %get-tuple-element.48), channel_id=1, source_target_pairs={{0,6},{2,0},{4,2},{6,4},{1,7},{3,1},{5,3},{7,5},{8,14},{10,8},{12,... | collective-permute-start | bytes 614408 | tf_op jit(solution)/shard_map/ppermute | solution.py:348
  110.2 14.3 %all-to-all-start.3 = ((bf16[16,32,512]{2,1,0:T(8,128)(2,1)}), bf16[16,32,512]{2,1,0:T(8,128)(2,1)S(1)}, u32[]{:S(2)}, u32[]{:S(2)}) async-start(bf16[16,32,512]{2,1,0:T(8,128)(2,1)} %get-tuple-element.58), calls=%async_computation.3 | async-start | bytes 1048576 | tf_op jit(solution)/shard_map/all_to_all | solution.py:340
  114.2 7.7 %collective-permute-start.10 = (bf16[256,256]{1,0:T(8,128)(2,1)S(1)}, bf16[256,256]{1,0:T(8,128)(2,1)S(1)}, u32[]{:S(2)}, u32[]{:S(2)}) collective-permute-start(bf16[256,256]{1,0:T(8,128)(2,1)S(1)} %get-tuple-element.60.w0), channel_id=1, source_target_pairs={{0,2},{2,4},{4,6},{6,0},{1,3},{3,5},{5,7},{7,1},{8,10},{10,12},{12... | collective-permute-start | bytes 393224 | tf_op jit(solution)/shard_map/ppermute | solution.py:352
  115.8 7.8 %collective-permute-start.9 = (bf16[256,256]{1,0:T(8,128)(2,1)S(1)}, bf16[256,256]{1,0:T(8,128)(2,1)S(1)}, u32[]{:S(2)}, u32[]{:S(2)}) collective-permute-start(bf16[256,256]{1,0:T(8,128)(2,1)S(1)} %get-tuple-element.60.w0), channel_id=1, source_target_pairs={{0,4},{2,6},{4,0},{6,2},{1,5},{3,7},{5,1},{7,3},{8,12},{10,14},{12... | collective-permute-start | bytes 393224 | tf_op jit(solution)/shard_map/ppermute | solution.py:352
  118.7 5.0 %collective-permute-start.8 = (bf16[256,256]{1,0:T(8,128)(2,1)S(1)}, bf16[256,256]{1,0:T(8,128)(2,1)S(1)}, u32[]{:S(2)}, u32[]{:S(2)}) collective-permute-start(bf16[256,256]{1,0:T(8,128)(2,1)S(1)} %get-tuple-element.60.w0), channel_id=1, source_target_pairs={{0,6},{2,0},{4,2},{6,4},{1,7},{3,1},{5,3},{7,5},{8,14},{10,8},{12,... | collective-permute-start | bytes 393224 | tf_op jit(solution)/shard_map/ppermute | solution.py:352
  124.5 1.9 %collective-permute-start.11 = (bf16[4,2,2,32,512]{4,3,2,1,0:T(8,128)(2,1)S(1)}, bf16[4,2,2,32,512]{4,3,2,1,0:T(8,128)(2,1)S(1)}, u32[]{:S(2)}, u32[]{:S(2)}) collective-permute-start(bf16[4,2,2,32,512]{4,3,2,1,0:T(8,128)(2,1)S(1)} %bitcast.10), channel_id=1, source_target_pairs={{0,1},{1,0},{2,3},{3,2},{4,5},{5,4},{6,7},{7,6},{8,9},{9,8},{10,11... | collective-permute-start | bytes 1572872 | tf_op jit(solution)/shard_map/ppermute | solution.py:344
  130.5 4.4 %collective-permute-start.15 = (f32[256,1152]{1,0:T(8,128)S(1)}, f32[256,1152]{1,0:T(8,128)S(1)}, u32[]{:S(2)}, u32[]{:S(2)}) collective-permute-start(f32[256,1152]{1,0:T(8,128)S(1)} %get-tuple-element.74), channel_id=1, source_target_pairs={{0,1},{1,0},{2,3},{3,2},{4,5},{5,4},{6,7},{7,6},{8,9},{9,8},{10,11... | collective-permute-start | bytes 3538952 | tf_op jit(solution)/shard_map/ppermute | solution.py:344
  136.3 22.3 %all-to-all-start.4 = ((bf16[16,208,128]{2,1,0:T(8,128)(2,1)}), bf16[16,208,128]{2,1,0:T(8,128)(2,1)S(1)}, u32[]{:S(2)}, u32[]{:S(2)}) async-start(bf16[16,208,128]{2,1,0:T(8,128)(2,1)} %pair.3), calls=%async_computation.4 | async-start | bytes 1703936 | tf_op jit(solution)/shard_map/all_to_all | solution.py:340
  142.7 8.4 %collective-permute-start.12 = (bf16[400,256]{1,0:T(8,128)(2,1)S(1)}, bf16[400,256]{1,0:T(8,128)(2,1)S(1)}, u32[]{:S(2)}, u32[]{:S(2)}) collective-permute-start(bf16[400,256]{1,0:T(8,128)(2,1)S(1)} %get-tuple-element.69), channel_id=1, source_target_pairs={{0,2},{2,4},{4,6},{6,0},{1,3},{3,5},{5,7},{7,1},{8,10},{10,12},{12... | collective-permute-start | bytes 614408 | tf_op jit(solution)/shard_map/ppermute | solution.py:348
  143.8 12.4 %collective-permute-start.13 = (bf16[400,256]{1,0:T(8,128)(2,1)S(1)}, bf16[400,256]{1,0:T(8,128)(2,1)S(1)}, u32[]{:S(2)}, u32[]{:S(2)}) collective-permute-start(bf16[400,256]{1,0:T(8,128)(2,1)S(1)} %get-tuple-element.70), channel_id=1, source_target_pairs={{0,4},{2,6},{4,0},{6,2},{1,5},{3,7},{5,1},{7,3},{8,12},{10,14},{12... | collective-permute-start | bytes 614408 | tf_op jit(solution)/shard_map/ppermute | solution.py:348
  146.7 9.4 %collective-permute-start.14 = (bf16[400,256]{1,0:T(8,128)(2,1)S(1)}, bf16[400,256]{1,0:T(8,128)(2,1)S(1)}, u32[]{:S(2)}, u32[]{:S(2)}) collective-permute-start(bf16[400,256]{1,0:T(8,128)(2,1)S(1)} %get-tuple-element.71), channel_id=1, source_target_pairs={{0,6},{2,0},{4,2},{6,4},{1,7},{3,1},{5,3},{7,5},{8,14},{10,8},{12,... | collective-permute-start | bytes 614408 | tf_op jit(solution)/shard_map/ppermute | solution.py:348
